TPU v7x, 256 devices: a whole 4x4x8 slice. The times are simulated.
256 devices in a mesh: dp: 16 (over y, z_hi), mp: 16 (over x, z_lo, core).
Axes of the slice: x: 4, y: 4, z: 8 (z_hi: 4, z_lo: 2; z = z_hi * 2 + z_lo), core: 2. Of those that a mesh axis runs over, the one named last changes fastest.
Arguments:
- tokens: bfloat16 [4096, 4096], P('dp', 'mp'), may hold values from -6 to 6
- norm_gain: float32 [4096], P('mp'), may hold values from 0.75 to 7.5
- w_gate: bfloat16 [4096, 6144], P('dp', 'mp'), may hold values from -0.09375 to 0.09375
- w_up: bfloat16 [4096, 6144], P('dp', 'mp'), may hold values from -0.09375 to 0.09375
- cotangent: bfloat16 [4096, 6144], P('dp', 'mp'), may hold values from -0.09375 to 0.09375
- decay_mask: int32 [2, 4096], replicated, may hold values 0 or 1
- radius: float32 [1], replicated, may hold values from 12.8 to 38.4
Outputs:
- grad_gain: float32 [4096], P('mp')
- grad_gate: float32 [4096, 6144], P('dp', 'mp')
- grad_up: float32 [4096, 6144], P('dp', 'mp')
Inputs may be any that keep to these rules, and one draw needn't show every extreme that they name: `decay_mask`: 1 marks a row that is perturbed.
All inputs are finite; a program needn't handle non-finite values.
Results may differ from a plain program's by a relative error of at most 0.024.
Values may be sent and summed in bfloat16 or wider, within the bound.
No kernel may reach another device: no remote copies, remote signals or barrier semaphores. Data moves between devices by JAX's collectives and lax.ppermute only.
A program may use at most 64 MiB of HBM per device.

v0:
```python
import jax
import jax.numpy as jnp
from jax import lax
from jax.sharding import PartitionSpec as P


def activation(value):
    return jax.nn.gelu(value, approximate=True)


def fetch_weights(part_gate, part_up):
    return (
        lax.all_gather(part_gate, "dp", axis=0, tiled=True),
        lax.all_gather(part_up, "dp", axis=0, tiled=True),
    )


def one_pass(scaled_rows, gain_part, full_gate, full_up, cotangent):
    hidden_width = full_gate.shape[1]
    normed_part = (scaled_rows * gain_part[None, :]).astype(jnp.bfloat16)
    normed = lax.all_gather(normed_part, "mp", axis=1, tiled=True)
    pre_gate = jnp.dot(normed, full_gate, preferred_element_type=jnp.float32)
    pre_up = jnp.dot(normed, full_up, preferred_element_type=jnp.float32)
    activated, back_fn = jax.vjp(activation, pre_gate)
    upstream = cotangent.astype(jnp.float32)
    d_up = (upstream * activated).astype(jnp.bfloat16)
    d_gate = back_fn(upstream * pre_up)[0].astype(jnp.bfloat16)
    feature_term = lax.dot_general(
        d_gate, full_gate, (((1,), (1,)), ((), ())), preferred_element_type=jnp.float32
    )
    feature_term = feature_term + lax.dot_general(
        d_up, full_up, (((1,), (1,)), ((), ())), preferred_element_type=jnp.float32
    )
    d_norm = lax.psum_scatter(
        feature_term.astype(jnp.bfloat16), "mp", scatter_dimension=1, tiled=True
    ).astype(jnp.float32)
    d_gain = lax.psum(jnp.sum(d_norm * scaled_rows, axis=0), "dp")
    stacked = jnp.concatenate([d_gate, d_up], axis=1)
    both = lax.psum_scatter(
        lax.dot_general(
            normed, stacked, (((0,), (0,)), ((), ())), preferred_element_type=jnp.float32
        ).astype(jnp.bfloat16),
        "dp",
        scatter_dimension=0,
        tiled=True,
    ).astype(jnp.float32)
    return (d_gain, both[:, :hidden_width], both[:, hidden_width:])


def body(tokens, norm_gain, w_gate, w_up, cotangent, decay_mask, radius):
    values = tokens.astype(jnp.float32)
    width = values.shape[1] * lax.axis_size("mp")
    row_total = lax.psum(jnp.sum(values * values, axis=1), "mp")
    scaled_rows = values * lax.rsqrt(row_total / width + 1e-06)[:, None]
    groups = decay_mask.astype(jnp.float32)
    local_rows = w_gate.shape[0]
    first_row = lax.axis_index("dp") * local_rows
    local_groups = lax.dynamic_slice_in_dim(groups, first_row, local_rows, 1)
    gate_mask = local_groups[0][:, None]
    up_mask = local_groups[1][:, None]
    full_gate, full_up = fetch_weights(w_gate, w_up)
    asc_gain, asc_gate_f, asc_up_f = one_pass(scaled_rows, norm_gain, full_gate, full_up, cotangent)
    gate_low = asc_gate_f.astype(jnp.bfloat16)
    up_low = asc_up_f.astype(jnp.bfloat16)
    gate_wide = gate_low.astype(jnp.float32)
    up_wide = up_low.astype(jnp.float32)
    matrix_part = jnp.sum(gate_mask * gate_wide * gate_wide) + jnp.sum(up_mask * up_wide * up_wide)
    total = lax.psum(matrix_part, ("dp", "mp"))
    factor = radius[0] / (jnp.sqrt(total) + 1e-12)
    new_gate = (w_gate.astype(jnp.float32) + factor * gate_mask * gate_wide).astype(jnp.bfloat16)
    new_up = (w_up.astype(jnp.float32) + factor * up_mask * up_wide).astype(jnp.bfloat16)
    next_gate, next_up = fetch_weights(new_gate, new_up)
    return one_pass(scaled_rows, norm_gain, next_gate, next_up, cotangent)


def solution(mesh):
    placed = (P("dp", "mp"), P("mp"), P("dp", "mp"), P("dp", "mp"), P("dp", "mp"), P(), P())
    return jax.shard_map(
        body,
        mesh=mesh,
        in_specs=placed,
        out_specs=(P("mp"), P("dp", "mp"), P("dp", "mp")),
        check_vma=False,
    )
```

profile of v0, /device:TPU:4, one launch (start us, length us, event | category | flops | bytes accessed | tf_op | source)
XLA Modules:
  0.0 741.1 jit_solution(15227484376641133650)
XLA Ops:
  7.2 0.0 all-gather.6.cloned.1.call-start
  7.2 1.0 fusion.33
  8.2 23.6 %psum.21 = f32[256]{0:T(256)S(1)} all-reduce(f32[256]{0:T(256)S(1)} %fusion.33), channel_id=1, replica_groups=mesh['dp'=16,'mp'=16] {'mp'}, use_global_device_ids=true, to_apply=%region_1.0 | all-reduce | flops 256 | bytes 2048 | tf_op jit(solution)/shard_map/psum | solution.py:53
  31.9 1.7 fusion.31
  33.6 0.0 all-gather.6.cloned.1.call-update
  33.6 0.0 all-gather.10.cloned.1.call-start
  33.6 0.7 all-gather.10.cloned.1.call-update
  34.3 0.0 all-gather.8.cloned.1.call-start
  34.4 0.7 all-gather.8.cloned.1.call-update
  35.1 0.0 copy-start.6
  35.1 0.0 reduce-scatter.4.cloned.1.call-start
  35.1 44.3 %all-gather.6.cloned.1.call-done = bf16[256,4096]{1,0:T(8,128)(2,1)} async-done(((bf16[256,256]{1,0:T(8,128)(2,1)}), bf16[256,4096]{1,0:T(8,128)(2,1)}) %all-gather.6.cloned.1.call-update) | async-done | bytes 2097168 | tf_op jit(solution)/shard_map/all_gather | solution.py:21
  79.4 70.9 %all-gather.10.cloned.1.call-done = bf16[4096,384]{1,0:T(8,128)(2,1)} async-done(((bf16[256,384]{1,0:T(8,128)(2,1)}), bf16[4096,384]{1,0:T(8,128)(2,1)}) %all-gather.10.cloned.1.call-update) | async-done | bytes 3145744 | tf_op jit(solution)/shard_map/all_gather | solution.py:13
  150.3 3.9 fusion.21
  154.2 64.3 %all-gather.8.cloned.1.call-done = bf16[4096,384]{1,0:T(8,128)(2,1)} async-done(((bf16[256,384]{1,0:T(8,128)(2,1)}), bf16[4096,384]{1,0:T(8,128)(2,1)}) %all-gather.8.cloned.1.call-update) | async-done | bytes 3145744 | tf_op jit(solution)/shard_map/all_gather | solution.py:14
  218.5 0.0 copy-done.6
  218.5 0.0 copy-done
  218.5 3.3 fusion.11
  221.8 4.5 convolution_convert_fusion.1
  226.4 0.0 reduce-scatter.4.cloned.1.call-update
  226.4 0.0 all-gather.14.cloned.1.call-start
  226.5 0.8 dynamic-slice_convert_fusion
  227.3 107.5 %reduce-scatter.4.cloned.1.call-done = bf16[256,768]{1,0:T(8,128)(2,1)} async-done(((bf16[4096,768]{1,0:T(8,128)(2,1)}), bf16[256,768]{1,0:T(8,128)(2,1)}) %reduce-scatter.4.cloned.1.call-update) | async-done | bytes 393232 | tf_op jit(solution)/shard_map/reduce_scatter | solution.py:39
  334.8 1.9 fusion.20
  338.6 73.6 %psum.22 = f32[]{:T(128)} all-reduce(f32[]{:T(128)S(6)} %add.55), channel_id=1, replica_groups=mesh['dp'=16,'mp'=16] {'dp','mp'}, use_global_device_ids=true, to_apply=%region_5.0 | all-reduce | flops 1 | bytes 8 | tf_op jit(solution)/shard_map/psum | solution.py:68
  413.0 0.0 copy-done.4
  413.0 0.0 copy-done.5
  413.0 2.0 fusion.4
  414.9 0.0 all-gather.14.cloned.1.call-update
  415.0 0.0 all-gather.12.cloned.1.call-start
  415.0 0.5 all-gather.12.cloned.1.call-update
  415.6 0.0 reduce-scatter.6.cloned.1.call-start
  415.6 64.0 %all-gather.14.cloned.1.call-done = bf16[4096,384]{1,0:T(8,128)(2,1)} async-done(((bf16[256,384]{1,0:T(8,128)(2,1)}), bf16[4096,384]{1,0:T(8,128)(2,1)}) %all-gather.14.cloned.1.call-update) | async-done | bytes 3145744 | tf_op jit(solution)/shard_map/all_gather | solution.py:13
  479.6 3.3 fusion.22
  482.9 65.4 %all-gather.12.cloned.1.call-done = bf16[4096,384]{1,0:T(8,128)(2,1)} async-done(((bf16[256,384]{1,0:T(8,128)(2,1)}), bf16[4096,384]{1,0:T(8,128)(2,1)}) %all-gather.12.cloned.1.call-update) | async-done | bytes 3145744 | tf_op jit(solution)/shard_map/all_gather | solution.py:14
  548.3 3.5 fusion.18
  551.8 1.3 fusion.38
  553.1 0.6 copy-done.2
  553.7 2.7 fusion
  556.4 0.0 reduce-scatter.6.cloned.1.call-update
  556.4 0.0 reduce-scatter.8.cloned.1.call-start
  556.4 4.5 convolution_convert_fusion
  561.0 0.0 reduce-scatter.8.cloned.1.call-update
  561.0 50.3 %reduce-scatter.6.cloned.1.call-done = bf16[256,256]{1,0:T(8,128)(2,1)} async-done(((bf16[256,4096]{1,0:T(8,128)(2,1)}), bf16[256,256]{1,0:T(8,128)(2,1)}) %reduce-scatter.6.cloned.1.call-update) | async-done | bytes 131088 | tf_op jit(solution)/shard_map/reduce_scatter | solution.py:34
  611.4 1.0 fusion.32
  612.4 45.8 %psum.23 = f32[256]{0:T(256)} all-reduce(f32[256]{0:T(256)S(1)} %fusion.32), channel_id=1, replica_groups=mesh['dp'=16,'mp'=16] {'dp'}, use_global_device_ids=true, to_apply=%region_8.0 | all-reduce | flops 256 | bytes 2048 | tf_op jit(solution)/shard_map/psum | solution.py:37
  658.2 74.2 %reduce-scatter.8.cloned.1.call-done = bf16[256,768]{1,0:T(8,128)(2,1)} async-done(((bf16[4096,768]{1,0:T(8,128)(2,1)}), bf16[256,768]{1,0:T(8,128)(2,1)}) %reduce-scatter.8.cloned.1.call-update) | async-done | bytes 393232 | tf_op jit(solution)/shard_map/reduce_scatter | solution.py:39
  732.4 1.9 fusion.36
  (11 shorter events, 0.0 us)
Async XLA Ops:
  7.2 72.2 %all-gather.6.cloned.1.call-start = ((), (), s32[]{:S(2)}) async-start(), calls=%async_computation.3 | async-start | bytes 2228224 | tf_op jit(solution)/shard_map/all_gather | solution.py:21
  33.6 116.7 %all-gather.10.cloned.1.call-start = ((), (), s32[]{:S(2)}) async-start(), calls=%async_computation.5 | async-start | bytes 3342336 | tf_op jit(solution)/shard_map/all_gather | solution.py:13
  34.3 184.2 %all-gather.8.cloned.1.call-start = ((), (), s32[]{:S(2)}) async-start(), calls=%async_computation.4 | async-start | bytes 3342336 | tf_op jit(solution)/shard_map/all_gather | solution.py:14
  35.1 183.4 %copy-start.6 = (bf16[256,384]{1,0:T(8,128)(2,1)S(1)}, bf16[256,384]{1,0:T(8,128)(2,1)}, u32[]{:S(2)}) copy-start(bf16[256,384]{1,0:T(8,128)(2,1)} %param.11) | copy-start | bytes 589828
  35.1 299.7 %reduce-scatter.4.cloned.1.call-start = ((), (), s32[]{:S(2)}) async-start(), calls=%async_computation.6 | async-start | bytes 6684672 | tf_op jit(solution)/shard_map/reduce_scatter | solution.py:39
  79.4 139.1 %copy-start = (bf16[256,4096]{1,0:T(8,128)(2,1)S(1)}, bf16[256,4096]{1,0:T(8,128)(2,1)}, u32[]{:S(2)}) copy-start(bf16[256,4096]{1,0:T(8,128)(2,1)} %all-gather.6.cloned.1.call-done) | copy-start | bytes 6291460
  226.4 186.6 %copy-start.4 = (bf16[256,384]{1,0:T(8,128)(2,1)S(1)}, bf16[256,384]{1,0:T(8,128)(2,1)}, u32[]{:S(2)}) copy-start(bf16[256,384]{1,0:T(8,128)(2,1)} %param.9) | copy-start | bytes 589828
  226.4 186.6 %copy-start.5 = (bf16[256,384]{1,0:T(8,128)(2,1)S(1)}, bf16[256,384]{1,0:T(8,128)(2,1)}, u32[]{:S(2)}) copy-start(bf16[256,384]{1,0:T(8,128)(2,1)} %param.10) | copy-start | bytes 589828
  226.4 253.2 %all-gather.14.cloned.1.call-start = ((), (), s32[]{:S(2)}) async-start(), calls=%async_computation.8 | async-start | bytes 3342336 | tf_op jit(solution)/shard_map/all_gather | solution.py:13
  415.0 133.3 %all-gather.12.cloned.1.call-start = ((), (), s32[]{:S(2)}) async-start(), calls=%async_computation.7 | async-start | bytes 3342336 | tf_op jit(solution)/shard_map/all_gather | solution.py:14
  415.6 195.8 %reduce-scatter.6.cloned.1.call-start = ((), (), s32[]{:S(2)}) async-start(), calls=%async_computation.9 | async-start | bytes 2228224 | tf_op jit(solution)/shard_map/reduce_scatter | solution.py:34
  548.3 3.5 copy-start.1
  551.8 1.9 copy-start.2
  556.4 176.0 %reduce-scatter.8.cloned.1.call-start = ((), (), s32[]{:S(2)}) async-start(), calls=%async_computation.10 | async-start | bytes 6684672 | tf_op jit(solution)/shard_map/reduce_scatter | solution.py:39
  561.0 50.4 %copy-start.3 = (bf16[256,256]{1,0:T(8,128)(2,1)S(1)}, bf16[256,256]{1,0:T(8,128)(2,1)}, u32[]{:S(2)}) copy-start(bf16[256,256]{1,0:T(8,128)(2,1)} %param.7) | copy-start | bytes 393220
Sparse Core Ops, SparseCore 0:
  33.7 45.6 all-gather.5
  81.9 68.3 all-gather.9
  152.8 65.7 all-gather.7
  226.5 108.1 reduce-scatter.3
  415.1 64.4 all-gather.13
  482.5 65.7 all-gather.11
  556.5 54.8 reduce-scatter.5
  615.1 117.2 reduce-scatter.7
where the time goes:
time: 742 us; the launch traced here: 741 us
  waiting for transfers between devices  543 us (73%)
  blocking collectives  143 us (19%)
  matrix products  27.1 us (4%)
  between operations  16.9 us (2%)
  other arithmetic  8.34 us (1%)
    reduce_scatter x2, waiting for transfers between devices, one_pass(): lax.psum_scatter(lax.dot_general(normed, stacked, (((0,), (0,)), ((), ())...  182 us
    all_gather x2, waiting for transfers between devices, fetch_weights(): lax.all_gather(part_gate, 'dp', axis=0, tiled=True)  135 us
    all_gather x2, waiting for transfers between devices, fetch_weights(): lax.all_gather(part_up, 'dp', axis=0, tiled=True)  130 us
    psum x1, blocking collectives, body(): total = lax.psum(matrix_part, ('dp', 'mp'))  73.6 us
    reduce_scatter x1, waiting for transfers between devices, one_pass(): lax.psum_scatter(feature_term.astype(jnp.bfloat16), 'mp', scatter_dimensi...  50.3 us
    psum x1, blocking collectives, one_pass(): d_gain = lax.psum(jnp.sum(d_norm * scaled_rows, axis=0), 'dp')  45.8 us
    all_gather x1, waiting for transfers between devices, one_pass(): normed = lax.all_gather(normed_part, 'mp', axis=1, tiled=True)  44.3 us
    psum x1, blocking collectives, body(): row_total = lax.psum(jnp.sum(values * values, axis=1), 'mp')  23.6 us
  transfers between devices with their start and end apart: 8, of which 8 were waited for; matrix products, arithmetic and copies ran while one was open for 2% of the time, Pallas kernels for 0%

commit v1 on v0

v1 whole, which is shorter than its diff:
```python
import functools
import jax
import jax.numpy as jnp
from jax import lax
from jax.experimental import pallas as pl
from jax.experimental.pallas import tpu as pltpu
from jax.sharding import Mesh, PartitionSpec as P

SIZES = (4, 4, 4, 2, 2)
NAMES = ("y", "zh", "x", "zl", "c")
DP, MP = ("y", "zh"), ("x", "zl", "c")
BLK = 256
SUB = 96
ROWS = 2 * SUB
NB = 16
PACK = BLK + 16
KC = 0.7978845608
KB = 0.044715
BF = jnp.bfloat16
F32 = jnp.float32
NT = (((1,), (1,)), ((), ()))
NN = (((1,), (0,)), ((), ()))

GROUPS = (
    ((0, 0),),
    ((0, 1), (1, 0), (3, 0)),
    ((1, 1), (3, 1), (2, 0), (2, 1)),
)
PLACE = {b: (g, i) for g, grp in enumerate(GROUPS) for i, b in enumerate(grp)}


def from_z(value, dzh, lz):
    pairs = []
    for zh in range(4):
        for zl in range(2):
            pairs.append((((zh + dzh) % 4) * 2 + (zl ^ lz), zh * 2 + zl))
    return lax.ppermute(value, ("zh", "zl"), pairs)


def other_core(value):
    return lax.ppermute(value, "c", [(0, 1), (1, 0)])


def shape(dims, dtype):
    return jax.ShapeDtypeStruct(dims, dtype)


def call(kernel, out_shape, in_specs, out_specs, grid=(), scratch=(), flops=10**6, nbytes=10**6):
    return pl.pallas_call(
        kernel,
        out_shape=out_shape,
        grid=grid,
        in_specs=in_specs,
        out_specs=out_specs,
        scratch_shapes=scratch,
        compiler_params=pltpu.CompilerParams(vmem_limit_bytes=32 * 1024 * 1024),
        cost_estimate=pl.CostEstimate(flops=flops, bytes_accessed=nbytes, transcendentals=0),
    )


SMEM = pl.BlockSpec(memory_space=pltpu.SMEM)


def whole(dims):
    return pl.BlockSpec(dims, lambda *_: (0,) * len(dims))


def by_x(dims):
    return pl.BlockSpec((1,) + dims, lambda i: (i,) + (0,) * len(dims))


def split3(value):
    hi = value.astype(BF)
    left = value - hi.astype(F32)
    mid = left.astype(BF)
    return [hi, mid, (left - mid.astype(F32)).astype(BF)]


def row(ref_rows, at):
    rows = ref_rows.astype(F32)
    return rows[at : at + 1] + rows[at + 1 : at + 2] + rows[at + 2 : at + 3]


def start_kernel(tokens, gain, w_gate, w_up, cot, pack, pieces):
    values = tokens[...].astype(F32)
    squares = jnp.sum((values * values).T, axis=0, keepdims=True)
    pack[0:BLK, :] = tokens[...]
    extra = split3(gain[...]) + split3(squares)
    tail = jnp.concatenate([e.astype(F32) for e in extra] + [jnp.zeros((10, BLK), F32)], axis=0)
    pack[BLK:PACK, :] = tail.astype(BF)
    for i, ref in enumerate((w_gate, w_up, cot)):
        turned = ref[...].astype(F32).T.astype(BF)
        for q in range(4):
            pieces[q, SUB * i : SUB * (i + 1), :] = turned[SUB * q : SUB * (q + 1), :]


def pre_kernel(parts, with_gain, ids, w, *refs):
    toks = refs[: len(parts)]
    out, sq = refs[len(parts)], refs[len(parts) + 1]
    gabs = refs[len(parts) + 2] if with_gain else None
    x, zh, zl, c = pl.program_id(0), ids[1], ids[3], ids[4]

    @pl.when(x == 0)
    def _():
        out[...] = jnp.zeros_like(out)
        sq[...] = jnp.zeros_like(sq)

    scaled, sums, squares = {}, {}, {}
    for (grp, g), ref in zip(parts, toks):
        for i, (k, l) in enumerate(GROUPS[grp]):
            tail = ref[0, i, BLK:PACK, :]
            if (l, g) not in scaled:
                gain = row(tail, 0)
                at = (zl ^ l) * 2 + (c ^ g)
                wv = w[0, at]
                scaled[l, g] = (wv.astype(F32) * gain).astype(BF)
                if gabs is not None:
                    gabs[x * 4 + at] = jnp.broadcast_to(gain, (8, BLK))
            term = lax.dot_general(scaled[l, g], ref[0, i, 0:BLK, :], NT, preferred_element_type=F32)
            sums[k] = sums[k] + term if k in sums else term
            s = row(tail, 3)
            squares[k] = squares[k] + s if k in squares else s
    for k, total in sums.items():
        out[k] += total
        sq[k] += jnp.broadcast_to(squares[k], (8, BLK))


def pre2_kernel(parts, ids, asc, mask, gabs, *refs):
    toks, out = refs[: len(parts)], refs[len(parts)]
    x, zl, c = pl.program_id(0), ids[3], ids[4]

    @pl.when(x == 0)
    def _():
        out[...] = jnp.zeros_like(out)

    scaled, sums = {}, {}
    for (grp, g), ref in zip(parts, toks):
        for i, (k, l) in enumerate(GROUPS[grp]):
            if (l, g) not in scaled:
                at = (zl ^ l) * 2 + (c ^ g)
                fb = x * 4 + at
                scaled[l, g] = (asc[0, at].astype(F32) * mask_rows(mask[fb]) * gabs[fb][0:1]).astype(BF)
            term = lax.dot_general(scaled[l, g], ref[0, i, 0:BLK, :], NT, preferred_element_type=F32)
            sums[k] = sums[k] + term if k in sums else term
    for k, total in sums.items():
        out[k] += total


def mask_rows(m):
    return jnp.concatenate(
        [jnp.broadcast_to(m[0:1, :], (SUB, BLK)), jnp.broadcast_to(m[1:2, :], (SUB, BLK))], axis=0
    )


def hidden_grads(pre, r, cot):
    gate = pre[0:SUB] * r
    up = pre[SUB:ROWS] * r
    u = cot.astype(F32)
    inner = KC * (gate + KB * gate * gate * gate)
    t = jnp.tanh(inner)
    act = 0.5 * gate * (1.0 + t)
    slope = 0.5 * (1.0 + t) + 0.5 * gate * (1.0 - t * t) * KC * (1.0 + 3.0 * KB * gate * gate)
    return jnp.concatenate([u * up * slope * r, u * act * r], axis=0).astype(BF)


def fill_grads(ids, d, pres, sqs, pieces):
    zh = ids[1]
    for k in range(4):
        pre, sq = pres(k), sqs[0][k][0:1]
        for s in sqs[1:]:
            sq = sq + s[k][0:1]
        r = lax.rsqrt(sq / (NB * BLK) + 1e-06)
        d[k] = hidden_grads(pre, r, pieces[lax.rem(zh + k, 4), ROWS : ROWS + SUB, :])


def outer_terms(parts, d, toks):
    where = {p: ref for p, ref in zip(parts, toks)}
    for l in range(2):
        for g in range(2):
            total = None
            for k in range(4):
                grp, i = PLACE[k, l]
                term = lax.dot_general(d[k], where[grp, g][0, i, 0:BLK, :], NN, preferred_element_type=F32)
                total = term if total is None else total + term
            yield l, g, total


def outer1_kernel(parts, ids, p0, p1, p2, s0, s1, s2, pieces, *refs):
    toks, out, d = refs[: len(parts)], refs[len(parts)], refs[len(parts) + 1]
    zl, c = ids[3], ids[4]

    @pl.when(pl.program_id(0) == 0)
    def _():
        fill_grads(ids, d, lambda k: p0[k] + p1[k] + p2[k], (s0, s1, s2), pieces)

    for l, g, total in outer_terms(parts, d, toks):
        out[0, (zl ^ l) * 2 + (c ^ g)] = total.astype(BF)


def outer2_kernel(parts, factor, ids, p0, p1, p2, s0, s1, s2, pieces, pa, w, asc, mask, *refs):
    toks, out, dgp, d = refs[: len(parts)], refs[len(parts)], refs[len(parts) + 1], refs[len(parts) + 2]
    x, zh, zl, c = pl.program_id(0), ids[1], ids[3], ids[4]
    f = factor[0]

    @pl.when(x == 0)
    def _():
        fill_grads(ids, d, lambda k: p0[k] + p1[k] + p2[k] + f * pa[k], (s0, s1, s2), pieces)

    for l, g, total in outer_terms(parts, d, toks):
        at = (zl ^ l) * 2 + (c ^ g)
        out[0, at] = total.astype(BF)
        fb = x * 4 + at
        wv = w[0, at].astype(F32)
        wv = wv + f * mask_rows(mask[fb]) * asc[0, at].astype(F32)
        dgp[pl.ds(fb, 1), :] = jnp.sum(wv * total, axis=0, keepdims=True)


def ascent_kernel(ids, terms, gabs, mask, asc, part):
    y = ids[0]
    acc = jnp.zeros((8, BLK), F32)
    for h in range(4):
        total = terms[0, h].astype(F32)
        for j in range(1, 4):
            total = total + terms[j, h].astype(F32)
        low = (total * gabs[y * 4 + h][0:1]).astype(BF)
        asc[h] = low
        wide = low.astype(F32)
        acc = acc + jnp.sum((mask_rows(mask[y * 4 + h]) * wide * wide).reshape(ROWS // 8, 8, BLK), axis=0)
    part[...] = acc[:, 0:128] + acc[:, 128:256]


def final_kernel(ids, gabs, sums, gate, up):
    g = gabs[ids[0] * 4 + ids[1]][0:1]
    tg = jnp.concatenate([sums[q, 0:SUB, :].astype(F32) for q in range(4)], axis=0) * g
    tu = jnp.concatenate([sums[q, SUB:ROWS, :].astype(F32) for q in range(4)], axis=0) * g
    gate[...] = tg.T
    up[...] = tu.T


def spread(value, axes):
    n = 16
    return lax.all_to_all(jnp.broadcast_to(value[None], (n,) + value.shape), axes, 0, 0, tiled=True)


def body(tokens, norm_gain, w_gate, w_up, cotangent, decay_mask, radius):
    ids = jnp.stack([lax.axis_index(n) for n in NAMES]).astype(jnp.int32)
    mask = decay_mask.astype(F32).reshape(2, NB, BLK).transpose(1, 0, 2)

    pack, pieces = call(
        start_kernel,
        (shape((PACK, BLK), BF), shape((4, 3 * SUB, BLK), BF)),
        [whole((BLK, BLK)), whole((1, BLK))] + [whole((BLK, 4 * SUB))] * 3,
        (whole((PACK, BLK)), whole((4, 3 * SUB, BLK))),
    )(tokens, norm_gain[None, :], w_gate, w_up, cotangent)

    own = []
    for grp in GROUPS:
        blocks = [pack if b == (0, 0) else from_z(pack, *b) for b in grp]
        own.append(jnp.stack(blocks))
    mine = [lax.all_gather(v, "x", axis=0, tiled=False) for v in own]
    theirs = [other_core(v) for v in mine]
    toks = {(grp, g): (mine, theirs)[g][grp] for grp in range(3) for g in range(2)}

    pieces = lax.all_to_all(pieces, "zh", 0, 0, tiled=True)
    weights = lax.all_to_all(jnp.broadcast_to(pieces[None, :, :ROWS], (4, 4, ROWS, BLK)), "y", 0, 0, tiled=True)

    pshape, sshape, gshape = shape((4, ROWS, BLK), F32), shape((4, 8, BLK), F32), shape((NB, 8, BLK), F32)
    wspec = by_x((4, ROWS, BLK))

    def tok_spec(grp):
        return by_x((len(GROUPS[grp]), PACK, BLK))

    def pre(parts, with_gain):
        outs = [pshape, sshape] + ([gshape] if with_gain else [])
        blocks = sum(len(GROUPS[p[0]]) for p in parts)
        return call(
            functools.partial(pre_kernel, parts, with_gain),
            outs,
            [SMEM, wspec] + [tok_spec(p[0]) for p in parts],
            [whole(s.shape) for s in outs],
            (4,),
            flops=blocks * 4 * 2 * ROWS * BLK * BLK,
            nbytes=blocks * 4 * 2 * PACK * BLK,
        )(ids, weights, *[toks[p] for p in parts])

    p0, s0, gabs = pre(((0, 0), (1, 0), (0, 1), (1, 1)), True)
    p1, s1 = pre(((2, 0),), False)
    p2, s2 = pre(((2, 1),), False)
    parts = ((0, 0), (1, 0), (2, 0), (0, 1), (1, 1), (2, 1))
    tok_specs = [tok_spec(p[0]) for p in parts]
    tok_refs = [toks[p] for p in parts]
    cost = {"flops": 64 * 2 * ROWS * BLK * BLK, "nbytes": 12 * 10**6}
    oshape = shape((4, 4, ROWS, BLK), BF)
    dscratch = [pltpu.VMEM((4, ROWS, BLK), BF)]
    first_specs = [whole(pshape.shape)] * 3 + [whole(sshape.shape)] * 3 + [whole(pieces.shape)]
    out1 = call(
        functools.partial(outer1_kernel, parts),
        oshape,
        [SMEM] + first_specs + tok_specs,
        by_x((4, ROWS, BLK)),
        (4,),
        dscratch,
        **cost,
    )(ids, p0, p1, p2, s0, s1, s2, pieces, *tok_refs)
    terms = lax.all_to_all(out1, "y", 0, 0, tiled=True)
    asc, part = call(
        ascent_kernel,
        (shape((4, ROWS, BLK), BF), shape((8, 128), F32)),
        [SMEM, whole(oshape.shape), whole(gshape.shape), whole((NB, 2, BLK))],
        (whole((4, ROWS, BLK)), whole((8, 128))),
    )(ids, terms, gabs, mask)
    ascs = lax.all_gather(asc, "y", axis=0, tiled=False)
    part = jnp.sum(spread(part, MP), axis=0)
    total = jnp.sum(spread(part, DP))
    factor = (radius[0] / (jnp.sqrt(total) + 1e-12))[None]
    pa = call(
        functools.partial(pre2_kernel, parts),
        pshape,
        [SMEM, wspec, whole((NB, 2, BLK)), whole(gshape.shape)] + tok_specs,
        whole(pshape.shape),
        (4,),
        **cost,
    )(ids, ascs, mask, gabs, *tok_refs)
    out2, dgp = call(
        functools.partial(outer2_kernel, parts),
        (oshape, shape((NB, BLK), F32)),
        [SMEM, SMEM] + first_specs + [whole(pshape.shape), wspec, wspec, whole((NB, 2, BLK))] + tok_specs,
        (by_x((4, ROWS, BLK)), whole((NB, BLK))),
        (4,),
        dscratch,
        **cost,
    )(factor, ids, p0, p1, p2, s0, s1, s2, pieces, pa, weights, ascs, mask, *tok_refs)
    sums = lax.psum_scatter(out2, "y", scatter_dimension=0, tiled=False)
    dg = jnp.sum(lax.all_to_all(dgp, MP, 0, 0, tiled=True), axis=0)
    grad_gain = jnp.sum(spread(dg, DP).reshape(16, BLK), axis=0)
    sums = lax.all_to_all(sums, "zh", 0, 0, tiled=True)
    out = shape((BLK, 4 * SUB), F32)
    grad_gate, grad_up = call(
        final_kernel,
        (out, out),
        [SMEM, whole(gshape.shape), whole((4, ROWS, BLK))],
        (whole((BLK, 4 * SUB)), whole((BLK, 4 * SUB))),
    )(ids, gabs, sums)
    return grad_gain, grad_gate, grad_up


def solution(mesh):
    fine = Mesh(mesh.devices.reshape(SIZES), NAMES)
    both = P(DP, MP)
    return jax.shard_map(
        body,
        mesh=fine,
        in_specs=(both, P(MP), both, both, both, P(), P()),
        out_specs=(P(MP), both, both),
        check_vma=False,
    )
```

time: 742 us -> 279 us (0.38)
  waiting for transfers between devices: 543 us -> 116 us
  blocking collectives: 143 us -> 48.4 us
  starting transfers between devices: 0.32 us -> 47.6 us
  Pallas kernels: 0 us -> 30.5 us
  matrix products: 27.1 us -> 0 us
  local copies, waits for them, and re-layouts: 2.56 us -> 15.2 us
    all_gather x5 -> x3, waiting for transfers between devices: 309 us -> 43 us  [the longest x2 43 us: body(): mine = [lax.all_gather(v, 'x', axis=0, tiled=False) for v in own]]
    reduce_scatter x3 -> x1, waiting for transfers between devices: 232 us -> 1.79 us  [body(): sums = lax.psum_scatter(out2, 'y', scatter_dimension=0, tiled=False)]
    psum x3 -> x0, blocking collectives: 143 us -> none  [the longest x1 73.6 us: body(): total = lax.psum(matrix_part, ('dp', 'mp'))]
    all_to_all x0 -> x5, waiting for transfers between devices: none -> 49.3 us  [the longest x1 20.5 us: body(): terms = lax.all_to_all(out1, 'y', 0, 0, tiled=True)]
    all_to_all x0 -> x3, blocking collectives: none -> 35 us  [the longest x2 26.3 us: spread(): lax.all_to_all(jnp.broadcast_to(value[None], (n,) + value.shape), axes, 0...]
    pallas_call x0 -> x9, Pallas kernels: none -> 30.5 us  [the longest x3 9.82 us: pre(): call(functools.partial(pre_kernel, parts, with_gain), outs, [SMEM, wspec]...]
    all_to_all x0 -> x5, starting transfers between devices: none -> 30 us  [the longest x1 7.09 us: spread(): lax.all_to_all(jnp.broadcast_to(value[None], (n,) + value.shape), axes, 0...]
    dot_general x8 -> x0, matrix products: 27.1 us -> none  [the longest x2 9.09 us: one_pass(): lax.dot_general(normed, stacked, (((0,), (0,)), ((), ())), preferred_elem...]
  transfers between devices with their start and end apart: 8 -> 19, of which waited for: 8 -> 14; matrix products, arithmetic and copies ran while one was open for 2% -> 2% of each run, Pallas kernels for 0% -> 2%
where the time goes in v1:
time: 279 us; the launch traced here: 278 us
  waiting for transfers between devices  116 us (42%)
  blocking collectives  48.4 us (17%)
  starting transfers between devices  47.6 us (17%)
  Pallas kernels  30.5 us (11%)
  between operations  15.5 us (6%)
  local copies, waits for them, and re-layouts  15.2 us (5%)
  other arithmetic  4.68 us (2%)
    all_gather x2, waiting for transfers between devices, body(): mine = [lax.all_gather(v, 'x', axis=0, tiled=False) for v in own]  43 us
    all_to_all x2, blocking collectives, spread(): lax.all_to_all(jnp.broadcast_to(value[None], (n,) + value.shape), axes, 0...  26.3 us
    ppermute x7, waiting for transfers between devices, from_z(): return lax.ppermute(value, ('zh', 'zl'), pairs)  22.3 us
    all_to_all x1, waiting for transfers between devices, body(): terms = lax.all_to_all(out1, 'y', 0, 0, tiled=True)  20.5 us
    ppermute x7, starting transfers between devices, from_z(): return lax.ppermute(value, ('zh', 'zl'), pairs)  17.3 us
    all_gather x1, blocking collectives, body(): mine = [lax.all_gather(v, 'x', axis=0, tiled=False) for v in own]  13.4 us
    unnamed x50, local copies, waits for them, and re-layouts  13 us
    all_to_all x1, waiting for transfers between devices, body(): sums = lax.all_to_all(sums, 'zh', 0, 0, tiled=True)  11.5 us
  transfers between devices with their start and end apart: 19, of which 14 were waited for; matrix products, arithmetic and copies ran while one was open for 2% of the time, Pallas kernels for 2%

profile of v1, /device:TPU:4, one launch (start us, length us, event | category | flops | bytes accessed | tf_op | source)
XLA Modules:
  0.0 278.3 jit_solution(2218193052365120952)
XLA Ops:
  7.2 0.9 copy-done.19
  8.1 0.9 copy-done.20
  9.1 0.9 copy-done.21
  10.0 0.9 copy-done.22
  11.6 1.2 shard_map.94
  12.8 6.7 %collective-permute-start.8 = (bf16[272,256]{1,0:T(8,128)(2,1)S(1)}, bf16[272,256]{1,0:T(8,128)(2,1)S(1)}, u32[]{:S(2)}, u32[]{:S(2)}) collective-permute-start(bf16[272,256]{1,0:T(8,128)(2,1)S(1)} %get-tuple-element.19), channel_id=1, source_target_pairs={{34,0},{32,2},{50,16},{48,18},{2,32},{0,34},{18,48},{16,50},{35,1}... | collective-permute-start | bytes 417800 | tf_op jit(solution)/shard_map/ppermute | solution.py:37
  19.9 2.0 collective-permute-start.6
  22.0 2.1 collective-permute-start.5
  24.1 5.6 %collective-permute-done.8 = bf16[272,256]{1,0:T(8,128)(2,1)S(1)} collective-permute-done((bf16[272,256]{1,0:T(8,128)(2,1)S(1)}, bf16[272,256]{1,0:T(8,128)(2,1)S(1)}, u32[]{:S(2)}, u32[]{:S(2)}) %collective-permute-start.8) | collective-permute-done | bytes 139296 | tf_op jit(solution)/shard_map/ppermute | solution.py:37
  29.7 5.4 %collective-permute-done.7 = bf16[272,256]{1,0:T(8,128)(2,1)S(1)} collective-permute-done((bf16[272,256]{1,0:T(8,128)(2,1)S(1)}, bf16[272,256]{1,0:T(8,128)(2,1)S(1)}, u32[]{:S(2)}, u32[]{:S(2)}) %collective-permute-start.7) | collective-permute-done | bytes 139296 | tf_op jit(solution)/shard_map/ppermute | solution.py:37
  35.1 2.1 collective-permute-done.6
  38.4 2.3 collective-permute-start.2
  40.7 1.9 collective-permute-start.1
  42.6 1.7 collective-permute-start
  44.3 1.4 collective-permute-done.2
  45.7 3.8 %collective-permute-done.1 = bf16[272,256]{1,0:T(8,128)(2,1)S(1)} collective-permute-done((bf16[272,256]{1,0:T(8,128)(2,1)S(1)}, bf16[272,256]{1,0:T(8,128)(2,1)S(1)}, u32[]{:S(2)}, u32[]{:S(2)}) %collective-permute-start.1) | collective-permute-done | bytes 139296 | tf_op jit(solution)/shard_map/ppermute | solution.py:37
  49.5 3.8 %collective-permute-done = bf16[272,256]{1,0:T(8,128)(2,1)S(1)} collective-permute-done((bf16[272,256]{1,0:T(8,128)(2,1)S(1)}, bf16[272,256]{1,0:T(8,128)(2,1)S(1)}, u32[]{:S(2)}, u32[]{:S(2)}) %collective-permute-start) | collective-permute-done | bytes 139296 | tf_op jit(solution)/shard_map/ppermute | solution.py:37
  54.2 18.3 %all-gather.10.cloned.1.call-done = bf16[16,272,256]{2,1,0:T(8,128)(2,1)} async-done(((bf16[4,272,256]{2,1,0:T(8,128)(2,1)}), bf16[16,272,256]{2,1,0:T(8,128)(2,1)}) %all-gather.10.cloned.1.call-update) | async-done | bytes 2228240 | tf_op jit(solution)/shard_map/all_gather | solution.py:260
  72.5 7.0 %all-to-all-start = ((bf16[4,288,256]{2,1,0:T(8,128)(2,1)}), bf16[4,288,256]{2,1,0:T(8,128)(2,1)S(1)}, u32[]{:S(2)}, u32[]{:S(2)}) async-start(bf16[4,288,256]{2,1,0:T(8,128)(2,1)} %get-tuple-element.18), calls=%async_computation | async-start | bytes 1179648 | tf_op jit(solution)/shard_map/all_to_all | solution.py:264
  79.5 24.7 %all-gather.8.cloned.1.call-done = bf16[12,272,256]{2,1,0:T(8,128)(2,1)} async-done(((bf16[3,272,256]{2,1,0:T(8,128)(2,1)}), bf16[12,272,256]{2,1,0:T(8,128)(2,1)}) %all-gather.8.cloned.1.call-update) | async-done | bytes 1671184 | tf_op jit(solution)/shard_map/all_gather | solution.py:260
  104.2 1.4 broadcast_in_dim.13
  105.5 4.3 %all-to-all-start.1 = ((bf16[4,4,192,256]{3,2,1,0:T(8,128)(2,1)}), bf16[4,4,192,256]{3,2,1,0:T(8,128)(2,1)S(1)}, u32[]{:S(2)}, u32[]{:S(2)}) async-start(bf16[4,4,192,256]{3,2,1,0:T(8,128)(2,1)} %broadcast_in_dim.13), calls=%async_computation.1 | async-start | bytes 3145728 | tf_op jit(solution)/shard_map/all_to_all | solution.py:265
  109.8 13.4 %all-gather = bf16[1088,256]{1,0:T(8,128)(2,1)} all-gather(bf16[272,256]{1,0:T(8,128)(2,1)S(1)} %get-tuple-element.19), channel_id=2, replica_groups=mesh['y'=4,'zh'=4,'x'=4,'zl'=2,'c'=2] {'x'}, dimensions={0}, use_global_device_ids=true | all-gather | bytes 696320 | tf_op jit(solution)/shard_map/all_gather | solution.py:260
  123.3 7.9 %all-to-all-done.1.w = bf16[4,4,192,256]{3,2,1,0:T(8,128)(2,1)S(1)} async-done(((bf16[4,4,192,256]{3,2,1,0:T(8,128)(2,1)}), bf16[4,4,192,256]{3,2,1,0:T(8,128)(2,1)S(1)}, u32[]{:S(2)}, u32[]{:S(2)}) %all-to-all-start.1) | async-done | bytes 1572896 | tf_op jit(solution)/shard_map/all_to_all | solution.py:265
  131.2 1.6 copy-done
  132.8 2.0 shard_map.96
  134.9 4.2 %shard_map.95 = (f32[4,192,256]{2,1,0:T(8,128)S(1)}, f32[4,8,256]{2,1,0:T(8,128)S(1)}, f32[16,8,256]{2,1,0:T(8,128)S(1)}) custom-call(s32[5]{0:T(128)S(1)} %stack.50.ids, bf16[4,4,192,256]{3,2,1,0:T(8,128)(2,1)S(1)} %all-to-all-done.1.w, bf16[4,1,272,256]{3,2,1,0:T(8,128)(2,1)} %bitcast.7.refs_0_, bf16[4,3,272,256]{3,2,1,0:T(8,128)(2,1)S(1)} %bitcast.31, ...), custom_call_target="tpu_custom_call" | custom-call | flops 805306368 | bytes 4456448 | tf_op jit(solution)/shard_map/pallas_call | solution.py:276
  139.2 3.6 %shard_map.97 = (f32[4,192,256]{2,1,0:T(8,128)S(1)}, f32[4,8,256]{2,1,0:T(8,128)S(1)}) custom-call(s32[5]{0:T(128)S(1)} %stack.50.ids, bf16[4,4,192,256]{3,2,1,0:T(8,128)(2,1)S(1)} %all-to-all-done.1.w, bf16[4,4,272,256]{3,2,1,0:T(8,128)(2,1)} %collective-permute-done.9.refs_0_.refs_5_), custom_call_target="tpu_custom_call" | custom-call | flops 402653184 | bytes 2228224 | tf_op jit(solution)/shard_map/pallas_call | solution.py:276
  142.8 5.1 %shard_map.98 = bf16[4,4,192,256]{3,2,1,0:T(8,128)(2,1)S(1)} custom-call(s32[5]{0:T(128)S(1)} %stack.50.ids, f32[4,192,256]{2,1,0:T(8,128)S(1)} %get-tuple-element.20.p0, f32[4,192,256]{2,1,0:T(8,128)S(1)} %get-tuple-element.21.p1, f32[4,192,256]{2,1,0:T(8,128)S(1)} %get-tuple-element.22.p2, f32[4,8,256]{2,1,0:T(8,128)S(1)} %get-tuple-element.23.s0, ...), custom_call_target="tpu_custom_call" | custom-call | flops 1610612736 | bytes 12000000 | tf_op jit(solution)/shard_map/pallas_call | solution.py:296
  147.9 1.2 copy-done.8
  149.9 4.5 %all-to-all-start.2 = ((bf16[4,4,192,256]{3,2,1,0:T(8,128)(2,1)}), bf16[4,4,192,256]{3,2,1,0:T(8,128)(2,1)}, u32[]{:S(2)}, u32[]{:S(2)}) async-start(bf16[4,4,192,256]{3,2,1,0:T(8,128)(2,1)} %copy-done.8), calls=%async_computation.2 | async-start | bytes 3145728 | tf_op jit(solution)/shard_map/all_to_all | solution.py:305
  154.5 20.5 %all-to-all-done.2.terms = bf16[4,4,192,256]{3,2,1,0:T(8,128)(2,1)} async-done(((bf16[4,4,192,256]{3,2,1,0:T(8,128)(2,1)}), bf16[4,4,192,256]{3,2,1,0:T(8,128)(2,1)}, u32[]{:S(2)}, u32[]{:S(2)}) %all-to-all-start.2) | async-done | bytes 1572896 | tf_op jit(solution)/shard_map/all_to_all | solution.py:305
  175.1 1.8 shard_map.99
  177.6 9.6 %all_to_all.45 = f32[16,8,128]{2,1,0:T(8,128)} all-to-all(f32[16,8,128]{2,1,0:T(8,128)S(1)} %broadcast_in_dim.14), channel_id=1, replica_groups=mesh['y'=4,'zh'=4,'x'=4,'zl'=2,'c'=2] {'x','zl','c'}, dimensions={0} | all-to-all | bytes 131072 | tf_op jit(solution)/shard_map/all_to_all | solution.py:242
  188.7 7.1 %all-to-all-start.4 = ((f32[16,8,128]{2,1,0:T(8,128)}), f32[16,8,128]{2,1,0:T(8,128)}, u32[]{:S(2)}, u32[]{:S(2)}) async-start(f32[16,8,128]{2,1,0:T(8,128)} %broadcast_in_dim.15), calls=%async_computation.4 | async-start | bytes 131072 | tf_op jit(solution)/shard_map/all_to_all | solution.py:242
  196.7 9.4 %all-to-all-done.4 = f32[16,8,128]{2,1,0:T(8,128)} async-done(((f32[16,8,128]{2,1,0:T(8,128)}), f32[16,8,128]{2,1,0:T(8,128)}, u32[]{:S(2)}, u32[]{:S(2)}) %all-to-all-start.4) | async-done | bytes 65568 | tf_op jit(solution)/shard_map/all_to_all | solution.py:242
  206.1 1.5 reduce_sum.37
  208.3 1.6 copy-done.2
  209.9 1.4 copy-done.9
  211.3 5.9 %shard_map.100.pa = f32[4,192,256]{2,1,0:T(8,128)S(1)} custom-call(s32[5]{0:T(128)S(1)} %stack.50.ids, bf16[4,4,192,256]{3,2,1,0:T(8,128)(2,1)S(1)} %bitcast.35, f32[16,2,256]{2,1,0:T(2,128)S(1)} %bitcast.38, f32[16,8,256]{2,1,0:T(8,128)S(1)} %get-tuple-element.26.gabs, bf16[4,1,272,256]{3,2,1,0:T(8,128)(2,1)} %bitcast.7.refs_0_, ...), custom_call_target="tpu_custom_call" | custom-call | flops 1610612736 | bytes 12000000 | tf_op jit(solution)/shard_map/pallas_call | solution.py:316
  217.3 5.2 %shard_map.101 = (bf16[4,4,192,256]{3,2,1,0:T(8,128)(2,1)S(1)}, f32[16,256]{1,0:T(8,128)S(1)}) custom-call(f32[1]{0:T(128)} %bitcast.19.factor, s32[5]{0:T(128)S(1)} %stack.50.ids, f32[4,192,256]{2,1,0:T(8,128)S(1)} %copy-done.14, f32[4,192,256]{2,1,0:T(8,128)S(1)} %copy-done.12, f32[4,192,256]{2,1,0:T(8,128)S(1)} %copy-done.16, ...), custom_call_target="tpu_custom_call" | custom-call | flops 1610612736 | bytes 12000000 | tf_op jit(solution)/shard_map/pallas_call | solution.py:324
  222.5 1.2 copy-done.17
  223.7 8.6 %all_to_all.46 = f32[16,1,256]{2,1,0:T(1,128)S(1)} all-to-all(f32[16,1,256]{2,1,0:T(1,128)S(1)} %copy.12), channel_id=1, replica_groups=mesh['y'=4,'zh'=4,'x'=4,'zl'=2,'c'=2] {'x','zl','c'}, dimensions={0} | all-to-all | bytes 32768 | tf_op jit(solution)/shard_map/all_to_all | solution.py:334
  232.4 16.7 %all_to_all.47 = f32[16,1,256]{2,1,0:T(1,128)S(1)} all-to-all(f32[16,1,256]{2,1,0:T(1,128)S(1)} %broadcast_in_dim.17), channel_id=1, replica_groups=mesh['y'=4,'zh'=4,'x'=4,'zl'=2,'c'=2] {'y','zh'}, dimensions={0} | all-to-all | bytes 32768 | tf_op jit(solution)/shard_map/all_to_all | solution.py:242
  249.2 1.8 reduce-scatter.2.cloned.1.call-done
  250.9 7.1 %all-to-all-start.7 = ((bf16[4,192,256]{2,1,0:T(8,128)(2,1)}), bf16[4,192,256]{2,1,0:T(8,128)(2,1)S(1)}, u32[]{:S(2)}, u32[]{:S(2)}) async-start(bf16[4,192,256]{2,1,0:T(8,128)(2,1)} %bitcast.42), calls=%async_computation.8 | async-start | bytes 786432 | tf_op jit(solution)/shard_map/all_to_all | solution.py:336
  258.6 11.5 %all-to-all-done.7.sums = bf16[4,192,256]{2,1,0:T(8,128)(2,1)S(1)} async-done(((bf16[4,192,256]{2,1,0:T(8,128)(2,1)}), bf16[4,192,256]{2,1,0:T(8,128)(2,1)S(1)}, u32[]{:S(2)}, u32[]{:S(2)}) %all-to-all-start.7) | async-done | bytes 393248 | tf_op jit(solution)/shard_map/all_to_all | solution.py:336
  270.1 1.6 shard_map.102
  (71 shorter events, 7.5 us)
Async XLA Ops:
  7.2 65.3 %all-gather.10.cloned.1.call-start = ((), (), s32[]{:S(2)}) async-start(), calls=%async_computation.11 | async-start | bytes 2785280 | tf_op jit(solution)/shard_map/all_gather | solution.py:260
  7.2 0.9 copy-start.19
  8.1 0.9 copy-start.20
  9.1 0.9 copy-start.21
  10.0 0.9 copy-start.22
  10.9 0.7 copy-start.23
  12.8 17.0 %collective-permute-start.8 = (bf16[272,256]{1,0:T(8,128)(2,1)S(1)}, bf16[272,256]{1,0:T(8,128)(2,1)S(1)}, u32[]{:S(2)}, u32[]{:S(2)}) collective-permute-start(bf16[272,256]{1,0:T(8,128)(2,1)S(1)} %get-tuple-element.19), channel_id=1, source_target_pairs={{34,0},{32,2},{50,16},{48,18},{2,32},{0,34},{18,48},{16,50},{35,1}... | collective-permute-start | bytes 417800 | tf_op jit(solution)/shard_map/ppermute | solution.py:37
  19.5 15.6 %collective-permute-start.7 = (bf16[272,256]{1,0:T(8,128)(2,1)S(1)}, bf16[272,256]{1,0:T(8,128)(2,1)S(1)}, u32[]{:S(2)}, u32[]{:S(2)}) collective-permute-start(bf16[272,256]{1,0:T(8,128)(2,1)S(1)} %get-tuple-element.19), channel_id=1, source_target_pairs={{32,0},{34,2},{48,16},{50,18},{0,32},{2,34},{16,48},{18,50},{33,1}... | collective-permute-start | bytes 417800 | tf_op jit(solution)/shard_map/ppermute | solution.py:37
  19.9 17.3 %collective-permute-start.6 = (bf16[272,256]{1,0:T(8,128)(2,1)S(1)}, bf16[272,256]{1,0:T(8,128)(2,1)S(1)}, u32[]{:S(2)}, u32[]{:S(2)}) collective-permute-start(bf16[272,256]{1,0:T(8,128)(2,1)S(1)} %get-tuple-element.19), channel_id=1, source_target_pairs={{50,0},{48,2},{2,16},{0,18},{18,32},{16,34},{34,48},{32,50},{51,1}... | collective-permute-start | bytes 417800 | tf_op jit(solution)/shard_map/ppermute | solution.py:37
  22.0 15.4 %collective-permute-start.5 = (bf16[272,256]{1,0:T(8,128)(2,1)S(1)}, bf16[272,256]{1,0:T(8,128)(2,1)S(1)}, u32[]{:S(2)}, u32[]{:S(2)}) collective-permute-start(bf16[272,256]{1,0:T(8,128)(2,1)S(1)} %get-tuple-element.19), channel_id=1, source_target_pairs={{18,0},{16,2},{34,16},{32,18},{50,32},{48,34},{2,48},{0,50},{19,1}... | collective-permute-start | bytes 417800 | tf_op jit(solution)/shard_map/ppermute | solution.py:37
  38.3 65.8 %all-gather.8.cloned.1.call-start = ((), (), s32[]{:S(2)}) async-start(), calls=%async_computation.10 | async-start | bytes 2088960 | tf_op jit(solution)/shard_map/all_gather | solution.py:260
  38.4 7.4 %collective-permute-start.2 = (bf16[272,256]{1,0:T(8,128)(2,1)S(1)}, bf16[272,256]{1,0:T(8,128)(2,1)S(1)}, u32[]{:S(2)}, u32[]{:S(2)}) collective-permute-start(bf16[272,256]{1,0:T(8,128)(2,1)S(1)} %get-tuple-element.19), channel_id=1, source_target_pairs={{48,0},{50,2},{0,16},{2,18},{16,32},{18,34},{32,48},{34,50},{49,1}... | collective-permute-start | bytes 417800 | tf_op jit(solution)/shard_map/ppermute | solution.py:37
  40.7 8.8 %collective-permute-start.1 = (bf16[272,256]{1,0:T(8,128)(2,1)S(1)}, bf16[272,256]{1,0:T(8,128)(2,1)S(1)}, u32[]{:S(2)}, u32[]{:S(2)}) collective-permute-start(bf16[272,256]{1,0:T(8,128)(2,1)S(1)} %get-tuple-element.19), channel_id=1, source_target_pairs={{16,0},{18,2},{32,16},{34,18},{48,32},{50,34},{0,48},{2,50},{17,1}... | collective-permute-start | bytes 417800 | tf_op jit(solution)/shard_map/ppermute | solution.py:37
  42.6 10.7 %collective-permute-start = (bf16[272,256]{1,0:T(8,128)(2,1)S(1)}, bf16[272,256]{1,0:T(8,128)(2,1)S(1)}, u32[]{:S(2)}, u32[]{:S(2)}) collective-permute-start(bf16[272,256]{1,0:T(8,128)(2,1)S(1)} %get-tuple-element.19), channel_id=1, source_target_pairs={{2,0},{0,2},{18,16},{16,18},{34,32},{32,34},{50,48},{48,50},{3,1},... | collective-permute-start | bytes 417800 | tf_op jit(solution)/shard_map/ppermute | solution.py:37
  72.5 66.7 %collective-permute-start.9 = (bf16[4,4,272,256]{3,2,1,0:T(8,128)(2,1)}, bf16[4,4,272,256]{3,2,1,0:T(8,128)(2,1)}, u32[]{:S(2)}, u32[]{:S(2)}) collective-permute-start(bf16[4,4,272,256]{3,2,1,0:T(8,128)(2,1)} %bitcast.25), channel_id=1, source_target_pairs={{0,1},{1,0},{2,3},{3,2},{4,5},{5,4},{6,7},{7,6},{8,9},{9,8},{10,11... | collective-permute-start | bytes 6684680 | tf_op jit(solution)/shard_map/ppermute | solution.py:41
  72.5 31.7 %all-to-all-start = ((bf16[4,288,256]{2,1,0:T(8,128)(2,1)}), bf16[4,288,256]{2,1,0:T(8,128)(2,1)S(1)}, u32[]{:S(2)}, u32[]{:S(2)}) async-start(bf16[4,288,256]{2,1,0:T(8,128)(2,1)} %get-tuple-element.18), calls=%async_computation | async-start | bytes 1179648 | tf_op jit(solution)/shard_map/all_to_all | solution.py:264
  104.1 30.7 %collective-permute-start.4 = (bf16[4,3,272,256]{3,2,1,0:T(8,128)(2,1)}, bf16[4,3,272,256]{3,2,1,0:T(8,128)(2,1)}, u32[]{:S(2)}, u32[]{:S(2)}) collective-permute-start(bf16[4,3,272,256]{3,2,1,0:T(8,128)(2,1)} %bitcast.30), channel_id=1, source_target_pairs={{0,1},{1,0},{2,3},{3,2},{4,5},{5,4},{6,7},{7,6},{8,9},{9,8},{10,11... | collective-permute-start | bytes 5013512 | tf_op jit(solution)/shard_map/ppermute | solution.py:41
  104.1 1.4 copy-start.5
  105.5 25.7 %all-to-all-start.1 = ((bf16[4,4,192,256]{3,2,1,0:T(8,128)(2,1)}), bf16[4,4,192,256]{3,2,1,0:T(8,128)(2,1)S(1)}, u32[]{:S(2)}, u32[]{:S(2)}) async-start(bf16[4,4,192,256]{3,2,1,0:T(8,128)(2,1)} %broadcast_in_dim.13), calls=%async_computation.1 | async-start | bytes 3145728 | tf_op jit(solution)/shard_map/all_to_all | solution.py:265
  123.2 11.7 %collective-permute-start.3 = (bf16[4,1,272,256]{3,2,1,0:T(8,128)(2,1)}, bf16[4,1,272,256]{3,2,1,0:T(8,128)(2,1)}, u32[]{:S(2)}, u32[]{:S(2)}) collective-permute-start(bf16[4,1,272,256]{3,2,1,0:T(8,128)(2,1)} %bitcast.7.refs_0_), channel_id=1, source_target_pairs={{0,1},{1,0},{2,3},{3,2},{4,5},{5,4},{6,7},{7,6},{8,9},{9,8},{10,11... | collective-permute-start | bytes 1671176 | tf_op jit(solution)/shard_map/ppermute | solution.py:41
  131.2 1.6 copy-start
  132.8 2.0 copy-start.4
  134.9 7.9 %copy-start.11 = (f32[4,192,256]{2,1,0:T(8,128)}, f32[4,192,256]{2,1,0:T(8,128)S(1)}, u32[]{:S(2)}) copy-start(f32[4,192,256]{2,1,0:T(8,128)S(1)} %get-tuple-element.21.p1) | copy-start | bytes 2359300
  139.1 3.7 %copy-start.13 = (f32[4,192,256]{2,1,0:T(8,128)}, f32[4,192,256]{2,1,0:T(8,128)S(1)}, u32[]{:S(2)}) copy-start(f32[4,192,256]{2,1,0:T(8,128)S(1)} %get-tuple-element.20.p0) | copy-start | bytes 2359300
  139.1 3.7 %copy-start.1 = (bf16[16,272,256]{2,1,0:T(8,128)(2,1)S(1)}, bf16[16,272,256]{2,1,0:T(8,128)(2,1)}, u32[]{:S(2)}) copy-start(bf16[16,272,256]{2,1,0:T(8,128)(2,1)} %all-gather.10.cloned.1.call-done) | copy-start | bytes 6684676
  139.1 3.7 %copy-start.6 = (bf16[4,288,256]{2,1,0:T(8,128)(2,1)S(1)}, bf16[4,288,256]{2,1,0:T(8,128)(2,1)}, u32[]{:S(2)}) copy-start(bf16[4,288,256]{2,1,0:T(8,128)(2,1)} %copy-done.5) | copy-start | bytes 1769476
  147.9 1.2 copy-start.8
  149.1 0.9 copy-start.15
  149.9 4.6 %copy-start.24 = (s32[2,4096]{1,0:T(2,128)S(1)}, s32[2,4096]{1,0:T(2,128)}, u32[]{:S(2)}) copy-start(s32[2,4096]{1,0:T(2,128)} %param.12) | copy-start | bytes 98308
  149.9 25.1 %all-to-all-start.2 = ((bf16[4,4,192,256]{3,2,1,0:T(8,128)(2,1)}), bf16[4,4,192,256]{3,2,1,0:T(8,128)(2,1)}, u32[]{:S(2)}, u32[]{:S(2)}) async-start(bf16[4,4,192,256]{3,2,1,0:T(8,128)(2,1)} %copy-done.8), calls=%async_computation.2 | async-start | bytes 3145728 | tf_op jit(solution)/shard_map/all_to_all | solution.py:305
  154.4 53.8 %all-gather.12.cloned.1.call-start = ((), (), s32[]{:S(2)}) async-start(), calls=%async_computation.12 | async-start | bytes 1966080 | tf_op jit(solution)/shard_map/all_gather | solution.py:312
  176.8 0.7 copy-start.18
  188.7 17.3 %all-to-all-start.4 = ((f32[16,8,128]{2,1,0:T(8,128)}), f32[16,8,128]{2,1,0:T(8,128)}, u32[]{:S(2)}, u32[]{:S(2)}) async-start(f32[16,8,128]{2,1,0:T(8,128)} %broadcast_in_dim.15), calls=%async_computation.4 | async-start | bytes 131072 | tf_op jit(solution)/shard_map/all_to_all | solution.py:242
  195.8 55.1 %reduce-scatter.2.cloned.1.call-start = ((), (), s32[]{:S(2)}) async-start(), calls=%async_computation.9 | async-start | bytes 1966080 | tf_op jit(solution)/shard_map/reduce_scatter | solution.py:333
  208.3 1.6 copy-start.2
  209.9 1.4 copy-start.9
  211.3 5.9 %copy-start.3 = (bf16[16,272,256]{2,1,0:T(8,128)(2,1)S(1)}, bf16[16,272,256]{2,1,0:T(8,128)(2,1)}, u32[]{:S(2)}) copy-start(bf16[16,272,256]{2,1,0:T(8,128)(2,1)} %all-gather.10.cloned.1.call-done) | copy-start | bytes 6684676
  211.3 5.9 %copy-start.7 = (bf16[4,288,256]{2,1,0:T(8,128)(2,1)S(1)}, bf16[4,288,256]{2,1,0:T(8,128)(2,1)}, u32[]{:S(2)}) copy-start(bf16[4,288,256]{2,1,0:T(8,128)(2,1)} %copy-done.5) | copy-start | bytes 1769476
  211.3 5.9 %copy-start.10 = (bf16[16,192,256]{2,1,0:T(8,128)(2,1)S(1)}, bf16[16,192,256]{2,1,0:T(8,128)(2,1)}, u32[]{:S(2)}) copy-start(bf16[16,192,256]{2,1,0:T(8,128)(2,1)} %all-gather.12.cloned.1.call-done) | copy-start | bytes 4718596
  211.3 5.9 %copy-start.12 = (f32[4,192,256]{2,1,0:T(8,128)S(1)}, f32[4,192,256]{2,1,0:T(8,128)}, u32[]{:S(2)}) copy-start(f32[4,192,256]{2,1,0:T(8,128)} %copy-done.11) | copy-start | bytes 2359300
  211.3 5.9 %copy-start.14 = (f32[4,192,256]{2,1,0:T(8,128)S(1)}, f32[4,192,256]{2,1,0:T(8,128)}, u32[]{:S(2)}) copy-start(f32[4,192,256]{2,1,0:T(8,128)} %copy-done.13) | copy-start | bytes 2359300
  211.3 5.9 %copy-start.16 = (f32[4,192,256]{2,1,0:T(8,128)S(1)}, f32[4,192,256]{2,1,0:T(8,128)}, u32[]{:S(2)}) copy-start(f32[4,192,256]{2,1,0:T(8,128)} %copy-done.15) | copy-start | bytes 2359300
  222.5 1.2 copy-start.17
  250.9 19.2 %all-to-all-start.7 = ((bf16[4,192,256]{2,1,0:T(8,128)(2,1)}), bf16[4,192,256]{2,1,0:T(8,128)(2,1)S(1)}, u32[]{:S(2)}, u32[]{:S(2)}) async-start(bf16[4,192,256]{2,1,0:T(8,128)(2,1)} %bitcast.42), calls=%async_computation.8 | async-start | bytes 786432 | tf_op jit(solution)/shard_map/all_to_all | solution.py:336
Sparse Core Ops, SparseCore 0:
  38.4 33.9 all-gather.9
  74.3 29.8 all-gather.7
  177.7 29.2 all-gather.11
  223.8 27.0 reduce-scatter.1

commit v2 on v1

--- a/solution.py
+++ b/solution.py
@@ -23,8 +23,9 @@
 
 GROUPS = (
     ((0, 0),),
-    ((0, 1), (1, 0), (3, 0)),
-    ((1, 1), (3, 1), (2, 0), (2, 1)),
+    ((0, 1),),
+    ((1, 0), (3, 0), (2, 0)),
+    ((1, 1), (3, 1), (2, 1)),
 )
 PLACE = {b: (g, i) for g, grp in enumerate(GROUPS) for i, b in enumerate(grp)}
 
@@ -56,6 +57,14 @@
         compiler_params=pltpu.CompilerParams(vmem_limit_bytes=32 * 1024 * 1024),
         cost_estimate=pl.CostEstimate(flops=flops, bytes_accessed=nbytes, transcendentals=0),
     )
+
+
+def hbm(dims, dtype):
+    return pltpu.HBM(dims, dtype)
+
+
+def in_hbm(value):
+    return pltpu.with_memory_space_constraint(value, pltpu.HBM)
 
 
 SMEM = pl.BlockSpec(memory_space=pltpu.SMEM)
@@ -248,21 +257,29 @@
 
     pack, pieces = call(
         start_kernel,
-        (shape((PACK, BLK), BF), shape((4, 3 * SUB, BLK), BF)),
+        (hbm((PACK, BLK), BF), hbm((4, 3 * SUB, BLK), BF)),
         [whole((BLK, BLK)), whole((1, BLK))] + [whole((BLK, 4 * SUB))] * 3,
         (whole((PACK, BLK)), whole((4, 3 * SUB, BLK))),
-    )(tokens, norm_gain[None, :], w_gate, w_up, cotangent)
-
-    own = []
-    for grp in GROUPS:
-        blocks = [pack if b == (0, 0) else from_z(pack, *b) for b in grp]
-        own.append(jnp.stack(blocks))
-    mine = [lax.all_gather(v, "x", axis=0, tiled=False) for v in own]
+    )(in_hbm(tokens), norm_gain[None, :], in_hbm(w_gate), in_hbm(w_up), in_hbm(cotangent))
+
+    def after(value, *others):
+        return lax.optimization_barrier((value,) + others)[0]
+
+    def over_x(value):
+        return lax.all_to_all(jnp.broadcast_to(value[None], (4,) + value.shape), "x", 0, 0, tiled=True)
+
+    mid = jnp.stack([from_z(pack, k, 0) for k, _ in GROUPS[2]])
+    mid_x = lax.all_gather(mid, "x", axis=0, tiled=False)
+    near = from_z(pack, 0, 1)
+    own_x = over_x(pack[None])
+    far_x = lax.all_gather(from_z(mid, 0, 1), "x", axis=0, tiled=False)
+    near_x = over_x(near[None])
+    pieces = lax.all_to_all(after(pieces, mid), "zh", 0, 0, tiled=True)
+    weights = lax.all_to_all(jnp.broadcast_to(pieces[None, :, :ROWS], (4, 4, ROWS, BLK)), "y", 0, 0, tiled=True)
+    weights = in_hbm(weights)
+    mine = [own_x, near_x, mid_x, far_x]
     theirs = [other_core(v) for v in mine]
-    toks = {(grp, g): (mine, theirs)[g][grp] for grp in range(3) for g in range(2)}
-
-    pieces = lax.all_to_all(pieces, "zh", 0, 0, tiled=True)
-    weights = lax.all_to_all(jnp.broadcast_to(pieces[None, :, :ROWS], (4, 4, ROWS, BLK)), "y", 0, 0, tiled=True)
+    toks = {(grp, g): in_hbm((mine, theirs)[g][grp]) for grp in range(len(GROUPS)) for g in range(2)}
 
     pshape, sshape, gshape = shape((4, ROWS, BLK), F32), shape((4, 8, BLK), F32), shape((NB, 8, BLK), F32)
     wspec = by_x((4, ROWS, BLK))
@@ -283,14 +300,14 @@
             nbytes=blocks * 4 * 2 * PACK * BLK,
         )(ids, weights, *[toks[p] for p in parts])
 
-    p0, s0, gabs = pre(((0, 0), (1, 0), (0, 1), (1, 1)), True)
-    p1, s1 = pre(((2, 0),), False)
-    p2, s2 = pre(((2, 1),), False)
-    parts = ((0, 0), (1, 0), (2, 0), (0, 1), (1, 1), (2, 1))
+    p0, s0, gabs = pre(tuple((grp, g) for g in range(2) for grp in (0, 1, 2)), True)
+    p1, s1 = pre(((3, 0),), False)
+    p2, s2 = pre(((3, 1),), False)
+    parts = tuple((grp, g) for g in range(2) for grp in range(len(GROUPS)))
     tok_specs = [tok_spec(p[0]) for p in parts]
     tok_refs = [toks[p] for p in parts]
     cost = {"flops": 64 * 2 * ROWS * BLK * BLK, "nbytes": 12 * 10**6}
-    oshape = shape((4, 4, ROWS, BLK), BF)
+    oshape = hbm((4, 4, ROWS, BLK), BF)
     dscratch = [pltpu.VMEM((4, ROWS, BLK), BF)]
     first_specs = [whole(pshape.shape)] * 3 + [whole(sshape.shape)] * 3 + [whole(pieces.shape)]
     out1 = call(
@@ -305,11 +322,11 @@
     terms = lax.all_to_all(out1, "y", 0, 0, tiled=True)
     asc, part = call(
         ascent_kernel,
-        (shape((4, ROWS, BLK), BF), shape((8, 128), F32)),
+        (hbm((4, ROWS, BLK), BF), shape((8, 128), F32)),
         [SMEM, whole(oshape.shape), whole(gshape.shape), whole((NB, 2, BLK))],
         (whole((4, ROWS, BLK)), whole((8, 128))),
     )(ids, terms, gabs, mask)
-    ascs = lax.all_gather(asc, "y", axis=0, tiled=False)
+    ascs = in_hbm(lax.all_gather(asc, "y", axis=0, tiled=False))
     part = jnp.sum(spread(part, MP), axis=0)
     total = jnp.sum(spread(part, DP))
     factor = (radius[0] / (jnp.sqrt(total) + 1e-12))[None]
@@ -334,7 +351,7 @@
     dg = jnp.sum(lax.all_to_all(dgp, MP, 0, 0, tiled=True), axis=0)
     grad_gain = jnp.sum(spread(dg, DP).reshape(16, BLK), axis=0)
     sums = lax.all_to_all(sums, "zh", 0, 0, tiled=True)
-    out = shape((BLK, 4 * SUB), F32)
+    out = hbm((BLK, 4 * SUB), F32)
     grad_gate, grad_up = call(
         final_kernel,
         (out, out),

time: 279 us -> 277 us (level)
  blocking collectives: 48.4 us -> 36.1 us
  local copies, waits for them, and re-layouts: 15.2 us -> 7.45 us
  Pallas kernels: 30.5 us -> 38 us
  waiting for transfers between devices: 116 us -> 123 us
  starting transfers between devices: 47.6 us -> 54.2 us
    all_gather x3, waiting for transfers between devices: 43 us -> 9.38 us  [the longest x1 8.41 us: body(): far_x = lax.all_gather(from_z(mid, 0, 1), 'x', axis=0, tiled=False)]
    all_to_all x1 -> x3, waiting for transfers between devices: 0.01 us -> 15.8 us  [the longest x2 13.2 us: over_x(): lax.all_to_all(jnp.broadcast_to(value[None], (4,) + value.shape), 'x', 0,...]
    all_gather x1 -> x0, blocking collectives: 13.4 us -> none  [body(): mine = [lax.all_gather(v, 'x', axis=0, tiled=False) for v in own]]
    ppermute x7 -> x5, waiting for transfers between devices: 22.3 us -> 35.2 us  [from_z(): return lax.ppermute(value, ('zh', 'zl'), pairs)]
    all_to_all x1, waiting for transfers between devices: 7.92 us -> 20.1 us  [body(): lax.all_to_all(jnp.broadcast_to(pieces[None, :, :ROWS], (4, 4, ROWS, BLK)...]
    all_to_all x1 -> x3, starting transfers between devices: 7.01 us -> 17.2 us  [the longest x2 12.1 us: over_x(): lax.all_to_all(jnp.broadcast_to(value[None], (4,) + value.shape), 'x', 0,...]
    unnamed x50 -> x18, local copies, waits for them, and re-layouts: 13 us -> 3.57 us
    ppermute x7 -> x5, starting transfers between devices: 17.3 us -> 13 us  [from_z(): return lax.ppermute(value, ('zh', 'zl'), pairs)]
  transfers between devices with their start and end apart: 19 -> 20, of which waited for: 14 -> 15; matrix products, arithmetic and copies ran while one was open for 2% -> 2% of each run, Pallas kernels for 2% -> 3%
where the time goes in v2:
time: 277 us; the launch traced here: 276 us
  waiting for transfers between devices  123 us (44%)
  starting transfers between devices  54.2 us (20%)
  Pallas kernels  38 us (14%)
  blocking collectives  36.1 us (13%)
  between operations  15.3 us (6%)
  local copies, waits for them, and re-layouts  7.45 us (3%)
    ppermute x5, waiting for transfers between devices, from_z(): return lax.ppermute(value, ('zh', 'zl'), pairs)  35.2 us
    all_to_all x2, blocking collectives, spread(): lax.all_to_all(jnp.broadcast_to(value[None], (n,) + value.shape), axes, 0...  26.6 us
    all_to_all x1, waiting for transfers between devices, body(): lax.all_to_all(jnp.broadcast_to(pieces[None, :, :ROWS], (4, 4, ROWS, BLK)...  20.1 us
    all_to_all x1, waiting for transfers between devices, body(): terms = lax.all_to_all(out1, 'y', 0, 0, tiled=True)  19.7 us
    all_to_all x2, waiting for transfers between devices, over_x(): lax.all_to_all(jnp.broadcast_to(value[None], (4,) + value.shape), 'x', 0,...  13.2 us
    ppermute x5, starting transfers between devices, from_z(): return lax.ppermute(value, ('zh', 'zl'), pairs)  13 us
    all_to_all x2, starting transfers between devices, over_x(): lax.all_to_all(jnp.broadcast_to(value[None], (4,) + value.shape), 'x', 0,...  12.1 us
    pallas_call x3, Pallas kernels, pre(): call(functools.partial(pre_kernel, parts, with_gain), outs, [SMEM, wspec]...  11.9 us
  transfers between devices with their start and end apart: 20, of which 15 were waited for; matrix products, arithmetic and copies ran while one was open for 2% of the time, Pallas kernels for 3%

profile of v2, /device:TPU:4, one launch (start us, length us, event | category | flops | bytes accessed | tf_op | source)
XLA Modules:
  0.0 276.4 jit_solution(7961238622443763220)
XLA Ops:
  7.2 0.7 copy-done.4
  7.9 2.3 shard_map.94
  10.2 7.2 %collective-permute-start.2 = (bf16[272,256]{1,0:T(8,128)(2,1)}, bf16[272,256]{1,0:T(8,128)(2,1)S(1)}, u32[]{:S(2)}, u32[]{:S(2)}) collective-permute-start(bf16[272,256]{1,0:T(8,128)(2,1)} %get-tuple-element.20), channel_id=1, source_target_pairs={{32,0},{34,2},{48,16},{50,18},{0,32},{2,34},{16,48},{18,50},{33,1}... | collective-permute-start | bytes 417800 | tf_op jit(solution)/shard_map/ppermute | solution.py:38
  17.4 1.5 collective-permute-start.1
  18.9 2.7 collective-permute-start
  21.5 2.9 %collective-permute-done.2 = bf16[272,256]{1,0:T(8,128)(2,1)S(1)} collective-permute-done((bf16[272,256]{1,0:T(8,128)(2,1)}, bf16[272,256]{1,0:T(8,128)(2,1)S(1)}, u32[]{:S(2)}, u32[]{:S(2)}) %collective-permute-start.2) | collective-permute-done | bytes 139296 | tf_op jit(solution)/shard_map/ppermute | solution.py:38
  24.4 3.4 %collective-permute-done.1 = bf16[272,256]{1,0:T(8,128)(2,1)S(1)} collective-permute-done((bf16[272,256]{1,0:T(8,128)(2,1)}, bf16[272,256]{1,0:T(8,128)(2,1)S(1)}, u32[]{:S(2)}, u32[]{:S(2)}) %collective-permute-start.1) | collective-permute-done | bytes 139296 | tf_op jit(solution)/shard_map/ppermute | solution.py:38
  27.8 3.1 %collective-permute-done = bf16[272,256]{1,0:T(8,128)(2,1)S(1)} collective-permute-done((bf16[272,256]{1,0:T(8,128)(2,1)}, bf16[272,256]{1,0:T(8,128)(2,1)S(1)}, u32[]{:S(2)}, u32[]{:S(2)}) %collective-permute-start) | collective-permute-done | bytes 139296 | tf_op jit(solution)/shard_map/ppermute | solution.py:38
  30.9 0.8 pad_maximum_fusion
  32.1 11.5 %collective-permute-done.7 = bf16[3,272,256]{2,1,0:T(8,128)(2,1)S(1)} collective-permute-done((bf16[3,272,256]{2,1,0:T(8,128)(2,1)}, bf16[3,272,256]{2,1,0:T(8,128)(2,1)S(1)}, u32[]{:S(2)}, u32[]{:S(2)}) %collective-permute-start.7) | collective-permute-done | bytes 417824 | tf_op jit(solution)/shard_map/ppermute | solution.py:38
  43.6 0.8 copy-done.6
  44.4 0.8 broadcast_in_dim.18
  45.2 4.8 %all-to-all-start.2 = ((bf16[4,1,272,256]{3,2,1,0:T(8,128)(2,1)}), bf16[4,1,272,256]{3,2,1,0:T(8,128)(2,1)}, u32[]{:S(2)}, u32[]{:S(2)}) async-start(bf16[4,1,272,256]{3,2,1,0:T(8,128)(2,1)} %broadcast_in_dim.18), calls=%async_computation.2 | async-start | bytes 1114112 | tf_op jit(solution)/shard_map/all_to_all | solution.py:269
  50.0 12.6 %all-to-all-done.2.refs_0_ = bf16[4,1,272,256]{3,2,1,0:T(8,128)(2,1)} async-done(((bf16[4,1,272,256]{3,2,1,0:T(8,128)(2,1)}), bf16[4,1,272,256]{3,2,1,0:T(8,128)(2,1)}, u32[]{:S(2)}, u32[]{:S(2)}) %all-to-all-start.2) | async-done | bytes 557088 | tf_op jit(solution)/shard_map/all_to_all | solution.py:269
  62.6 5.1 %all-to-all-start = ((bf16[4,288,256]{2,1,0:T(8,128)(2,1)}), bf16[4,288,256]{2,1,0:T(8,128)(2,1)S(1)}, u32[]{:S(2)}, u32[]{:S(2)}) async-start(bf16[4,288,256]{2,1,0:T(8,128)(2,1)} %get-tuple-element.21), calls=%async_computation | async-start | bytes 1179648 | tf_op jit(solution)/shard_map/all_to_all | solution.py:277
  67.8 1.3 collective-permute-start.3
  69.1 14.4 %collective-permute-done.3 = bf16[272,256]{1,0:T(8,128)(2,1)S(1)} collective-permute-done((bf16[272,256]{1,0:T(8,128)(2,1)S(1)}, bf16[272,256]{1,0:T(8,128)(2,1)S(1)}, u32[]{:S(2)}, u32[]{:S(2)}) %collective-permute-start.3) | collective-permute-done | bytes 139296 | tf_op jit(solution)/shard_map/ppermute | solution.py:38
  83.5 2.6 all-to-all-done.pieces
  86.1 0.8 broadcast_in_dim.19
  86.9 7.3 %all-to-all-start.3 = ((bf16[4,1,272,256]{3,2,1,0:T(8,128)(2,1)}), bf16[4,1,272,256]{3,2,1,0:T(8,128)(2,1)}, u32[]{:S(2)}, u32[]{:S(2)}) async-start(bf16[4,1,272,256]{3,2,1,0:T(8,128)(2,1)} %broadcast_in_dim.19), calls=%async_computation.3 | async-start | bytes 1114112 | tf_op jit(solution)/shard_map/all_to_all | solution.py:269
  94.2 8.4 %all-gather.9.cloned.1.call-done = bf16[12,272,256]{2,1,0:T(8,128)(2,1)} async-done(((bf16[3,272,256]{2,1,0:T(8,128)(2,1)}), bf16[12,272,256]{2,1,0:T(8,128)(2,1)}) %all-gather.9.cloned.1.call-update) | async-done | bytes 1671184 | tf_op jit(solution)/shard_map/all_gather | solution.py:275
  103.2 1.4 broadcast_in_dim.17
  104.6 4.3 %all-to-all-start.1 = ((bf16[4,4,192,256]{3,2,1,0:T(8,128)(2,1)}), bf16[4,4,192,256]{3,2,1,0:T(8,128)(2,1)S(1)}, u32[]{:S(2)}, u32[]{:S(2)}) async-start(bf16[4,4,192,256]{3,2,1,0:T(8,128)(2,1)} %broadcast_in_dim.17), calls=%async_computation.1 | async-start | bytes 3145728 | tf_op jit(solution)/shard_map/all_to_all | solution.py:278
  109.5 20.1 %all-to-all-done.1.w = bf16[4,4,192,256]{3,2,1,0:T(8,128)(2,1)S(1)} async-done(((bf16[4,4,192,256]{3,2,1,0:T(8,128)(2,1)}), bf16[4,4,192,256]{3,2,1,0:T(8,128)(2,1)S(1)}, u32[]{:S(2)}, u32[]{:S(2)}) %all-to-all-start.1) | async-done | bytes 1572896 | tf_op jit(solution)/shard_map/all_to_all | solution.py:278
  129.7 1.2 copy-done.5
  130.9 3.3 %shard_map.96 = (f32[4,192,256]{2,1,0:T(8,128)S(1)}, f32[4,8,256]{2,1,0:T(8,128)S(1)}) custom-call(s32[5]{0:T(128)S(1)} %stack.35.ids, bf16[4,4,192,256]{3,2,1,0:T(8,128)(2,1)} %copy-done.5, bf16[4,3,272,256]{3,2,1,0:T(8,128)(2,1)} %bitcast.31), custom_call_target="tpu_custom_call" | custom-call | flops 301989888 | bytes 1671168 | tf_op jit(solution)/shard_map/pallas_call | solution.py:293
  134.2 5.0 %shard_map.95 = (f32[4,192,256]{2,1,0:T(8,128)S(1)}, f32[4,8,256]{2,1,0:T(8,128)S(1)}, f32[16,8,256]{2,1,0:T(8,128)S(1)}) custom-call(s32[5]{0:T(128)S(1)} %stack.35.ids, bf16[4,4,192,256]{3,2,1,0:T(8,128)(2,1)} %copy-done.5, bf16[4,1,272,256]{3,2,1,0:T(8,128)(2,1)} %all-to-all-done.2.refs_0_, bf16[4,1,272,256]{3,2,1,0:T(8,128)(2,1)} %all-to-all-done.3.refs_1_, ...), custom_call_target="tpu_custom_call" | custom-call | flops 1006632960 | bytes 5570560 | tf_op jit(solution)/shard_map/pallas_call | solution.py:293
  139.3 3.6 %shard_map.97 = (f32[4,192,256]{2,1,0:T(8,128)S(1)}, f32[4,8,256]{2,1,0:T(8,128)S(1)}) custom-call(s32[5]{0:T(128)S(1)} %stack.35.ids, bf16[4,4,192,256]{3,2,1,0:T(8,128)(2,1)} %copy-done.5, bf16[4,3,272,256]{3,2,1,0:T(8,128)(2,1)} %collective-permute-done.8.refs_0_.refs_7_), custom_call_target="tpu_custom_call" | custom-call | flops 301989888 | bytes 1671168 | tf_op jit(solution)/shard_map/pallas_call | solution.py:293
  142.9 6.7 %shard_map.98 = bf16[4,4,192,256]{3,2,1,0:T(8,128)(2,1)} custom-call(s32[5]{0:T(128)S(1)} %stack.35.ids, f32[4,192,256]{2,1,0:T(8,128)S(1)} %get-tuple-element.22.p0, f32[4,192,256]{2,1,0:T(8,128)S(1)} %get-tuple-element.23.p1, f32[4,192,256]{2,1,0:T(8,128)S(1)} %get-tuple-element.24.p2, f32[4,8,256]{2,1,0:T(8,128)S(1)} %get-tuple-element.25.s0, ...), custom_call_target="tpu_custom_call" | custom-call | flops 1610612736 | bytes 12000000 | tf_op jit(solution)/shard_map/pallas_call | solution.py:313
  149.6 0.9 copy-done.2
  150.5 3.7 %all-to-all-start.4 = ((bf16[4,4,192,256]{3,2,1,0:T(8,128)(2,1)}), bf16[4,4,192,256]{3,2,1,0:T(8,128)(2,1)S(1)}, u32[]{:S(2)}, u32[]{:S(2)}) async-start(bf16[4,4,192,256]{3,2,1,0:T(8,128)(2,1)} %shard_map.98), calls=%async_computation.4 | async-start | bytes 3145728 | tf_op jit(solution)/shard_map/all_to_all | solution.py:322
  154.3 19.7 %all-to-all-done.4.terms = bf16[4,4,192,256]{3,2,1,0:T(8,128)(2,1)S(1)} async-done(((bf16[4,4,192,256]{3,2,1,0:T(8,128)(2,1)}), bf16[4,4,192,256]{3,2,1,0:T(8,128)(2,1)S(1)}, u32[]{:S(2)}, u32[]{:S(2)}) %all-to-all-start.4) | async-done | bytes 1572896 | tf_op jit(solution)/shard_map/all_to_all | solution.py:322
  174.0 1.6 shard_map.99
  175.6 9.6 %all_to_all.55 = f32[16,8,128]{2,1,0:T(8,128)S(1)} all-to-all(f32[16,8,128]{2,1,0:T(8,128)S(1)} %broadcast_in_dim.20), channel_id=1, replica_groups=mesh['y'=4,'zh'=4,'x'=4,'zl'=2,'c'=2] {'x','zl','c'}, dimensions={0} | all-to-all | bytes 131072 | tf_op jit(solution)/shard_map/all_to_all | solution.py:251
  185.2 0.6 broadcast_in_dim.21
  185.8 8.3 %all-to-all-start.6 = ((f32[16,8,128]{2,1,0:T(8,128)}), f32[16,8,128]{2,1,0:T(8,128)S(1)}, u32[]{:S(2)}, u32[]{:S(2)}) async-start(f32[16,8,128]{2,1,0:T(8,128)} %broadcast_in_dim.21), calls=%async_computation.6 | async-start | bytes 131072 | tf_op jit(solution)/shard_map/all_to_all | solution.py:251
  194.9 9.5 %all-to-all-done.6 = f32[16,8,128]{2,1,0:T(8,128)S(1)} async-done(((f32[16,8,128]{2,1,0:T(8,128)}), f32[16,8,128]{2,1,0:T(8,128)S(1)}, u32[]{:S(2)}, u32[]{:S(2)}) %all-to-all-start.6) | async-done | bytes 65568 | tf_op jit(solution)/shard_map/all_to_all | solution.py:251
  204.3 0.6 reduce_sum.37
  205.7 1.0 all-gather.11.cloned.1.call-done
  206.7 6.4 %shard_map.100.pa = f32[4,192,256]{2,1,0:T(8,128)S(1)} custom-call(s32[5]{0:T(128)S(1)} %stack.35.ids, bf16[4,4,192,256]{3,2,1,0:T(8,128)(2,1)} %bitcast.35, f32[16,2,256]{2,1,0:T(2,128)S(1)} %bitcast.21, f32[16,8,256]{2,1,0:T(8,128)S(1)} %get-tuple-element.28.gabs, bf16[4,1,272,256]{3,2,1,0:T(8,128)(2,1)} %all-to-all-done.2.refs_0_, ...), custom_call_target="tpu_custom_call" | custom-call | flops 1610612736 | bytes 12000000 | tf_op jit(solution)/shard_map/pallas_call | solution.py:333
  213.1 7.5 %shard_map.101 = (bf16[4,4,192,256]{3,2,1,0:T(8,128)(2,1)}, f32[16,256]{1,0:T(8,128)S(1)}) custom-call(f32[1]{0:T(128)} %bitcast.14.factor, s32[5]{0:T(128)S(1)} %stack.35.ids, f32[4,192,256]{2,1,0:T(8,128)S(1)} %copy-done.1, f32[4,192,256]{2,1,0:T(8,128)S(1)} %get-tuple-element.23.p1, f32[4,192,256]{2,1,0:T(8,128)S(1)} %copy-done.3, ...), custom_call_target="tpu_custom_call" | custom-call | flops 1610612736 | bytes 12000000 | tf_op jit(solution)/shard_map/pallas_call | solution.py:341
  220.6 9.4 %all_to_all.56 = f32[16,1,256]{2,1,0:T(1,128)S(1)} all-to-all(f32[16,1,256]{2,1,0:T(1,128)S(1)} %copy.12), channel_id=1, replica_groups=mesh['y'=4,'zh'=4,'x'=4,'zl'=2,'c'=2] {'x','zl','c'}, dimensions={0} | all-to-all | bytes 32768 | tf_op jit(solution)/shard_map/all_to_all | solution.py:351
  230.1 17.1 %all_to_all.57 = f32[16,1,256]{2,1,0:T(1,128)S(1)} all-to-all(f32[16,1,256]{2,1,0:T(1,128)S(1)} %broadcast_in_dim.23), channel_id=1, replica_groups=mesh['y'=4,'zh'=4,'x'=4,'zl'=2,'c'=2] {'y','zh'}, dimensions={0} | all-to-all | bytes 32768 | tf_op jit(solution)/shard_map/all_to_all | solution.py:251
  247.2 1.9 reduce-scatter.2.cloned.1.call-done
  249.1 7.1 %all-to-all-start.9 = ((bf16[4,192,256]{2,1,0:T(8,128)(2,1)}), bf16[4,192,256]{2,1,0:T(8,128)(2,1)S(1)}, u32[]{:S(2)}, u32[]{:S(2)}) async-start(bf16[4,192,256]{2,1,0:T(8,128)(2,1)} %bitcast.37), calls=%async_computation.10 | async-start | bytes 786432 | tf_op jit(solution)/shard_map/all_to_all | solution.py:353
  256.1 0.6 reduce_sum.39
  256.7 11.5 %all-to-all-done.9.sums = bf16[4,192,256]{2,1,0:T(8,128)(2,1)S(1)} async-done(((bf16[4,192,256]{2,1,0:T(8,128)(2,1)}), bf16[4,192,256]{2,1,0:T(8,128)(2,1)S(1)}, u32[]{:S(2)}, u32[]{:S(2)}) %all-to-all-start.9) | async-done | bytes 393248 | tf_op jit(solution)/shard_map/all_to_all | solution.py:353
  268.2 1.6 shard_map.102
  (41 shorter events, 1.9 us)
Async XLA Ops:
  7.2 61.9 %all-gather.7.cloned.1.call-start = ((), (), s32[]{:S(2)}) async-start(), calls=%async_computation.12 | async-start | bytes 2088960 | tf_op jit(solution)/shard_map/all_gather | solution.py:272
  7.2 0.7 copy-start.4
  10.2 34.2 %copy-start.7 = (bf16[272,256]{1,0:T(8,128)(2,1)S(1)}, bf16[272,256]{1,0:T(8,128)(2,1)}, u32[]{:S(2)}) copy-start(bf16[272,256]{1,0:T(8,128)(2,1)} %get-tuple-element.20) | copy-start | bytes 417796
  10.2 14.2 %collective-permute-start.2 = (bf16[272,256]{1,0:T(8,128)(2,1)}, bf16[272,256]{1,0:T(8,128)(2,1)S(1)}, u32[]{:S(2)}, u32[]{:S(2)}) collective-permute-start(bf16[272,256]{1,0:T(8,128)(2,1)} %get-tuple-element.20), channel_id=1, source_target_pairs={{32,0},{34,2},{48,16},{50,18},{0,32},{2,34},{16,48},{18,50},{33,1}... | collective-permute-start | bytes 417800 | tf_op jit(solution)/shard_map/ppermute | solution.py:38
  17.4 10.4 %collective-permute-start.1 = (bf16[272,256]{1,0:T(8,128)(2,1)}, bf16[272,256]{1,0:T(8,128)(2,1)S(1)}, u32[]{:S(2)}, u32[]{:S(2)}) collective-permute-start(bf16[272,256]{1,0:T(8,128)(2,1)} %get-tuple-element.20), channel_id=1, source_target_pairs={{48,0},{50,2},{0,16},{2,18},{16,32},{18,34},{32,48},{34,50},{49,1}... | collective-permute-start | bytes 417800 | tf_op jit(solution)/shard_map/ppermute | solution.py:38
  18.9 12.0 %collective-permute-start = (bf16[272,256]{1,0:T(8,128)(2,1)}, bf16[272,256]{1,0:T(8,128)(2,1)S(1)}, u32[]{:S(2)}, u32[]{:S(2)}) collective-permute-start(bf16[272,256]{1,0:T(8,128)(2,1)} %get-tuple-element.20), channel_id=1, source_target_pairs={{16,0},{18,2},{32,16},{34,18},{48,32},{50,34},{0,48},{2,50},{17,1}... | collective-permute-start | bytes 417800 | tf_op jit(solution)/shard_map/ppermute | solution.py:38
  31.7 70.9 %all-gather.9.cloned.1.call-start = ((), (), s32[]{:S(2)}) async-start(), calls=%async_computation.13 | async-start | bytes 2088960 | tf_op jit(solution)/shard_map/all_gather | solution.py:275
  31.8 11.8 %collective-permute-start.7 = (bf16[3,272,256]{2,1,0:T(8,128)(2,1)}, bf16[3,272,256]{2,1,0:T(8,128)(2,1)S(1)}, u32[]{:S(2)}, u32[]{:S(2)}) collective-permute-start(bf16[3,272,256]{2,1,0:T(8,128)(2,1)} %pad_maximum_fusion), channel_id=1, source_target_pairs={{2,0},{0,2},{18,16},{16,18},{34,32},{32,34},{50,48},{48,50},{3,1},... | collective-permute-start | bytes 1253384 | tf_op jit(solution)/shard_map/ppermute | solution.py:38
  43.6 0.8 copy-start.6
  45.2 17.4 %all-to-all-start.2 = ((bf16[4,1,272,256]{3,2,1,0:T(8,128)(2,1)}), bf16[4,1,272,256]{3,2,1,0:T(8,128)(2,1)}, u32[]{:S(2)}, u32[]{:S(2)}) async-start(bf16[4,1,272,256]{3,2,1,0:T(8,128)(2,1)} %broadcast_in_dim.18), calls=%async_computation.2 | async-start | bytes 1114112 | tf_op jit(solution)/shard_map/all_to_all | solution.py:269
  62.6 23.5 %all-to-all-start = ((bf16[4,288,256]{2,1,0:T(8,128)(2,1)}), bf16[4,288,256]{2,1,0:T(8,128)(2,1)S(1)}, u32[]{:S(2)}, u32[]{:S(2)}) async-start(bf16[4,288,256]{2,1,0:T(8,128)(2,1)} %get-tuple-element.21), calls=%async_computation | async-start | bytes 1179648 | tf_op jit(solution)/shard_map/all_to_all | solution.py:277
  67.8 15.7 %collective-permute-start.3 = (bf16[272,256]{1,0:T(8,128)(2,1)S(1)}, bf16[272,256]{1,0:T(8,128)(2,1)S(1)}, u32[]{:S(2)}, u32[]{:S(2)}) collective-permute-start(bf16[272,256]{1,0:T(8,128)(2,1)S(1)} %copy-done.7), channel_id=1, source_target_pairs={{2,0},{0,2},{18,16},{16,18},{34,32},{32,34},{50,48},{48,50},{3,1},... | collective-permute-start | bytes 417800 | tf_op jit(solution)/shard_map/ppermute | solution.py:38
  69.1 65.1 %collective-permute-start.6 = (bf16[4,3,272,256]{3,2,1,0:T(8,128)(2,1)}, bf16[4,3,272,256]{3,2,1,0:T(8,128)(2,1)}, u32[]{:S(2)}, u32[]{:S(2)}) collective-permute-start(bf16[4,3,272,256]{3,2,1,0:T(8,128)(2,1)} %bitcast.25), channel_id=1, source_target_pairs={{0,1},{1,0},{2,3},{3,2},{4,5},{5,4},{6,7},{7,6},{8,9},{9,8},{10,11... | collective-permute-start | bytes 5013512 | tf_op jit(solution)/shard_map/ppermute | solution.py:42
  86.9 16.3 %all-to-all-start.3 = ((bf16[4,1,272,256]{3,2,1,0:T(8,128)(2,1)}), bf16[4,1,272,256]{3,2,1,0:T(8,128)(2,1)}, u32[]{:S(2)}, u32[]{:S(2)}) async-start(bf16[4,1,272,256]{3,2,1,0:T(8,128)(2,1)} %broadcast_in_dim.19), calls=%async_computation.3 | async-start | bytes 1114112 | tf_op jit(solution)/shard_map/all_to_all | solution.py:269
  102.6 36.6 %collective-permute-start.8 = (bf16[4,3,272,256]{3,2,1,0:T(8,128)(2,1)}, bf16[4,3,272,256]{3,2,1,0:T(8,128)(2,1)}, u32[]{:S(2)}, u32[]{:S(2)}) collective-permute-start(bf16[4,3,272,256]{3,2,1,0:T(8,128)(2,1)} %bitcast.30), channel_id=1, source_target_pairs={{0,1},{1,0},{2,3},{3,2},{4,5},{5,4},{6,7},{7,6},{8,9},{9,8},{10,11... | collective-permute-start | bytes 5013512 | tf_op jit(solution)/shard_map/ppermute | solution.py:42
  104.6 25.0 %all-to-all-start.1 = ((bf16[4,4,192,256]{3,2,1,0:T(8,128)(2,1)}), bf16[4,4,192,256]{3,2,1,0:T(8,128)(2,1)S(1)}, u32[]{:S(2)}, u32[]{:S(2)}) async-start(bf16[4,4,192,256]{3,2,1,0:T(8,128)(2,1)} %broadcast_in_dim.17), calls=%async_computation.1 | async-start | bytes 3145728 | tf_op jit(solution)/shard_map/all_to_all | solution.py:278
  108.9 25.3 %collective-permute-start.4 = (bf16[4,1,272,256]{3,2,1,0:T(8,128)(2,1)}, bf16[4,1,272,256]{3,2,1,0:T(8,128)(2,1)}, u32[]{:S(2)}, u32[]{:S(2)}) collective-permute-start(bf16[4,1,272,256]{3,2,1,0:T(8,128)(2,1)} %all-to-all-done.2.refs_0_), channel_id=1, source_target_pairs={{0,1},{1,0},{2,3},{3,2},{4,5},{5,4},{6,7},{7,6},{8,9},{9,8},{10,11... | collective-permute-start | bytes 1671176 | tf_op jit(solution)/shard_map/ppermute | solution.py:42
  108.9 25.3 %collective-permute-start.5 = (bf16[4,1,272,256]{3,2,1,0:T(8,128)(2,1)}, bf16[4,1,272,256]{3,2,1,0:T(8,128)(2,1)}, u32[]{:S(2)}, u32[]{:S(2)}) collective-permute-start(bf16[4,1,272,256]{3,2,1,0:T(8,128)(2,1)} %all-to-all-done.3.refs_1_), channel_id=1, source_target_pairs={{0,1},{1,0},{2,3},{3,2},{4,5},{5,4},{6,7},{7,6},{8,9},{9,8},{10,11... | collective-permute-start | bytes 1671176 | tf_op jit(solution)/shard_map/ppermute | solution.py:42
  129.6 1.2 copy-start.5
  139.2 3.6 %copy-start = (f32[4,192,256]{2,1,0:T(8,128)}, f32[4,192,256]{2,1,0:T(8,128)S(1)}, u32[]{:S(2)}) copy-start(f32[4,192,256]{2,1,0:T(8,128)S(1)} %get-tuple-element.22.p0) | copy-start | bytes 2359300
  149.6 0.9 copy-start.2
  150.5 3.8 %copy-start.8 = (s32[2,4096]{1,0:T(2,128)S(1)}, s32[2,4096]{1,0:T(2,128)}, u32[]{:S(2)}) copy-start(s32[2,4096]{1,0:T(2,128)} %param.12) | copy-start | bytes 98308
  150.5 23.5 %all-to-all-start.4 = ((bf16[4,4,192,256]{3,2,1,0:T(8,128)(2,1)}), bf16[4,4,192,256]{3,2,1,0:T(8,128)(2,1)S(1)}, u32[]{:S(2)}, u32[]{:S(2)}) async-start(bf16[4,4,192,256]{3,2,1,0:T(8,128)(2,1)} %shard_map.98), calls=%async_computation.4 | async-start | bytes 3145728 | tf_op jit(solution)/shard_map/all_to_all | solution.py:322
  154.2 52.5 %all-gather.11.cloned.1.call-start = ((), (), s32[]{:S(2)}) async-start(), calls=%async_computation.14 | async-start | bytes 1966080 | tf_op jit(solution)/shard_map/all_gather | solution.py:329
  185.8 18.5 %all-to-all-start.6 = ((f32[16,8,128]{2,1,0:T(8,128)}), f32[16,8,128]{2,1,0:T(8,128)S(1)}, u32[]{:S(2)}, u32[]{:S(2)}) async-start(f32[16,8,128]{2,1,0:T(8,128)} %broadcast_in_dim.21), calls=%async_computation.6 | async-start | bytes 131072 | tf_op jit(solution)/shard_map/all_to_all | solution.py:251
  194.2 54.9 %reduce-scatter.2.cloned.1.call-start = ((), (), s32[]{:S(2)}) async-start(), calls=%async_computation.11 | async-start | bytes 1966080 | tf_op jit(solution)/shard_map/reduce_scatter | solution.py:350
  206.7 6.4 %copy-start.1 = (f32[4,192,256]{2,1,0:T(8,128)S(1)}, f32[4,192,256]{2,1,0:T(8,128)}, u32[]{:S(2)}) copy-start(f32[4,192,256]{2,1,0:T(8,128)} %copy-done) | copy-start | bytes 2359300
  206.7 6.4 %copy-start.3 = (f32[4,192,256]{2,1,0:T(8,128)S(1)}, f32[4,192,256]{2,1,0:T(8,128)}, u32[]{:S(2)}) copy-start(f32[4,192,256]{2,1,0:T(8,128)} %copy-done.2) | copy-start | bytes 2359300
  249.1 19.2 %all-to-all-start.9 = ((bf16[4,192,256]{2,1,0:T(8,128)(2,1)}), bf16[4,192,256]{2,1,0:T(8,128)(2,1)S(1)}, u32[]{:S(2)}, u32[]{:S(2)}) async-start(bf16[4,192,256]{2,1,0:T(8,128)(2,1)} %bitcast.37), calls=%async_computation.10 | async-start | bytes 786432 | tf_op jit(solution)/shard_map/all_to_all | solution.py:353
Sparse Core Ops, SparseCore 0:
  31.9 34.3 all-gather.6
  68.1 34.4 all-gather.8
  175.7 30.8 all-gather.10
  220.7 28.3 reduce-scatter.1

commit v3 on v2

--- a/solution.py
+++ b/solution.py
@@ -90,7 +90,7 @@
     return rows[at : at + 1] + rows[at + 1 : at + 2] + rows[at + 2 : at + 3]
 
 
-def start_kernel(tokens, gain, w_gate, w_up, cot, pack, pieces):
+def start_kernel(ids, tokens, gain, w_gate, w_up, cot, pack, p0, p1, p2, p3, turned):
     values = tokens[...].astype(F32)
     squares = jnp.sum((values * values).T, axis=0, keepdims=True)
     pack[0:BLK, :] = tokens[...]
@@ -98,9 +98,10 @@
     tail = jnp.concatenate([e.astype(F32) for e in extra] + [jnp.zeros((10, BLK), F32)], axis=0)
     pack[BLK:PACK, :] = tail.astype(BF)
     for i, ref in enumerate((w_gate, w_up, cot)):
-        turned = ref[...].astype(F32).T.astype(BF)
-        for q in range(4):
-            pieces[q, SUB * i : SUB * (i + 1), :] = turned[SUB * q : SUB * (q + 1), :]
+        turned[i] = ref[...].astype(F32).T.astype(BF)
+        for k, to in enumerate((p0, p1, p2, p3)):
+            q = pl.multiple_of(lax.rem(ids[1] - k + 4, 4) * SUB, SUB)
+            to[SUB * i : SUB * (i + 1), :] = turned[i, pl.ds(q, SUB), :]
 
 
 def pre_kernel(parts, with_gain, ids, w, *refs):
@@ -121,7 +122,7 @@
             if (l, g) not in scaled:
                 gain = row(tail, 0)
                 at = (zl ^ l) * 2 + (c ^ g)
-                wv = w[0, at]
+                wv = w[0, lax.rem(at - zh + 4, 4)]
                 scaled[l, g] = (wv.astype(F32) * gain).astype(BF)
                 if gabs is not None:
                     gabs[x * 4 + at] = jnp.broadcast_to(gain, (8, BLK))
@@ -173,13 +174,12 @@
 
 
 def fill_grads(ids, d, pres, sqs, pieces):
-    zh = ids[1]
     for k in range(4):
         pre, sq = pres(k), sqs[0][k][0:1]
         for s in sqs[1:]:
             sq = sq + s[k][0:1]
         r = lax.rsqrt(sq / (NB * BLK) + 1e-06)
-        d[k] = hidden_grads(pre, r, pieces[lax.rem(zh + k, 4), ROWS : ROWS + SUB, :])
+        d[k] = hidden_grads(pre, r, pieces[k][ROWS : ROWS + SUB, :])
 
 
 def outer_terms(parts, d, toks):
@@ -194,32 +194,32 @@
             yield l, g, total
 
 
-def outer1_kernel(parts, ids, p0, p1, p2, s0, s1, s2, pieces, *refs):
+def outer1_kernel(parts, ids, p0, p1, p2, s0, s1, s2, c0, c1, c2, c3, *refs):
     toks, out, d = refs[: len(parts)], refs[len(parts)], refs[len(parts) + 1]
     zl, c = ids[3], ids[4]
 
     @pl.when(pl.program_id(0) == 0)
     def _():
-        fill_grads(ids, d, lambda k: p0[k] + p1[k] + p2[k], (s0, s1, s2), pieces)
+        fill_grads(ids, d, lambda k: p0[k] + p1[k] + p2[k], (s0, s1, s2), (c0, c1, c2, c3))
 
     for l, g, total in outer_terms(parts, d, toks):
         out[0, (zl ^ l) * 2 + (c ^ g)] = total.astype(BF)
 
 
-def outer2_kernel(parts, factor, ids, p0, p1, p2, s0, s1, s2, pieces, pa, w, asc, mask, *refs):
+def outer2_kernel(parts, factor, ids, p0, p1, p2, s0, s1, s2, c0, c1, c2, c3, pa, w, asc, mask, *refs):
     toks, out, dgp, d = refs[: len(parts)], refs[len(parts)], refs[len(parts) + 1], refs[len(parts) + 2]
     x, zh, zl, c = pl.program_id(0), ids[1], ids[3], ids[4]
     f = factor[0]
 
     @pl.when(x == 0)
     def _():
-        fill_grads(ids, d, lambda k: p0[k] + p1[k] + p2[k] + f * pa[k], (s0, s1, s2), pieces)
+        fill_grads(ids, d, lambda k: p0[k] + p1[k] + p2[k] + f * pa[k], (s0, s1, s2), (c0, c1, c2, c3))
 
     for l, g, total in outer_terms(parts, d, toks):
         at = (zl ^ l) * 2 + (c ^ g)
         out[0, at] = total.astype(BF)
         fb = x * 4 + at
-        wv = w[0, at].astype(F32)
+        wv = w[0, lax.rem(at - zh + 4, 4)].astype(F32)
         wv = wv + f * mask_rows(mask[fb]) * asc[0, at].astype(F32)
         dgp[pl.ds(fb, 1), :] = jnp.sum(wv * total, axis=0, keepdims=True)
 
@@ -255,12 +255,14 @@
     ids = jnp.stack([lax.axis_index(n) for n in NAMES]).astype(jnp.int32)
     mask = decay_mask.astype(F32).reshape(2, NB, BLK).transpose(1, 0, 2)
 
-    pack, pieces = call(
+    piece = hbm((3 * SUB, BLK), BF)
+    pack, *pieces = call(
         start_kernel,
-        (hbm((PACK, BLK), BF), hbm((4, 3 * SUB, BLK), BF)),
-        [whole((BLK, BLK)), whole((1, BLK))] + [whole((BLK, 4 * SUB))] * 3,
-        (whole((PACK, BLK)), whole((4, 3 * SUB, BLK))),
-    )(in_hbm(tokens), norm_gain[None, :], in_hbm(w_gate), in_hbm(w_up), in_hbm(cotangent))
+        (hbm((PACK, BLK), BF),) + (piece,) * 4,
+        [SMEM, whole((BLK, BLK)), whole((1, BLK))] + [whole((BLK, 4 * SUB))] * 3,
+        (whole((PACK, BLK)),) + (whole(piece.shape),) * 4,
+        scratch=[pltpu.VMEM((3, 4 * SUB, BLK), BF)],
+    )(ids, in_hbm(tokens), norm_gain[None, :], in_hbm(w_gate), in_hbm(w_up), in_hbm(cotangent))
 
     def after(value, *others):
         return lax.optimization_barrier((value,) + others)[0]
@@ -268,24 +270,26 @@
     def over_x(value):
         return lax.all_to_all(jnp.broadcast_to(value[None], (4,) + value.shape), "x", 0, 0, tiled=True)
 
-    mid = jnp.stack([from_z(pack, k, 0) for k, _ in GROUPS[2]])
-    mid_x = lax.all_gather(mid, "x", axis=0, tiled=False)
+    mids = [from_z(pack, k, 0) for k, _ in GROUPS[2]]
     near = from_z(pack, 0, 1)
     own_x = over_x(pack[None])
-    far_x = lax.all_gather(from_z(mid, 0, 1), "x", axis=0, tiled=False)
-    near_x = over_x(near[None])
-    pieces = lax.all_to_all(after(pieces, mid), "zh", 0, 0, tiled=True)
-    weights = lax.all_to_all(jnp.broadcast_to(pieces[None, :, :ROWS], (4, 4, ROWS, BLK)), "y", 0, 0, tiled=True)
-    weights = in_hbm(weights)
-    mine = [own_x, near_x, mid_x, far_x]
-    theirs = [other_core(v) for v in mine]
-    toks = {(grp, g): in_hbm((mine, theirs)[g][grp]) for grp in range(len(GROUPS)) for g in range(2)}
+    pieces = [pieces[0]] + [from_z(pieces[k], k, 0) for k in range(1, 4)]
+    part_w = jnp.stack([p[:ROWS] for p in pieces])
+    weights = in_hbm(lax.all_gather(part_w, "y", axis=0, tiled=False))
+    mid_x = over_x(after(jnp.stack(mids + [near]), own_x))
+    far = from_z(jnp.stack(mids), 0, 1)
+    far_x = over_x(after(far, part_w, mid_x))
+    toks = {}
+    for g in range(2):
+        o, m, f = [in_hbm(other_core(v) if g else v) for v in (own_x, mid_x, far_x)]
+        toks.update({(0, g): o, (1, g): m, (2, g): m, (3, g): f})
 
     pshape, sshape, gshape = shape((4, ROWS, BLK), F32), shape((4, 8, BLK), F32), shape((NB, 8, BLK), F32)
     wspec = by_x((4, ROWS, BLK))
 
     def tok_spec(grp):
-        return by_x((len(GROUPS[grp]), PACK, BLK))
+        at = 3 if grp == 1 else 0
+        return pl.BlockSpec((1, len(GROUPS[grp]), PACK, BLK), lambda i: (i, at, 0, 0))
 
     def pre(parts, with_gain):
         outs = [pshape, sshape] + ([gshape] if with_gain else [])
@@ -309,7 +313,7 @@
     cost = {"flops": 64 * 2 * ROWS * BLK * BLK, "nbytes": 12 * 10**6}
     oshape = hbm((4, 4, ROWS, BLK), BF)
     dscratch = [pltpu.VMEM((4, ROWS, BLK), BF)]
-    first_specs = [whole(pshape.shape)] * 3 + [whole(sshape.shape)] * 3 + [whole(pieces.shape)]
+    first_specs = [whole(pshape.shape)] * 3 + [whole(sshape.shape)] * 3 + [whole(piece.shape)] * 4
     out1 = call(
         functools.partial(outer1_kernel, parts),
         oshape,
@@ -318,7 +322,7 @@
         (4,),
         dscratch,
         **cost,
-    )(ids, p0, p1, p2, s0, s1, s2, pieces, *tok_refs)
+    )(ids, p0, p1, p2, s0, s1, s2, *pieces, *tok_refs)
     terms = lax.all_to_all(out1, "y", 0, 0, tiled=True)
     asc, part = call(
         ascent_kernel,
@@ -346,7 +350,7 @@
         (4,),
         dscratch,
         **cost,
-    )(factor, ids, p0, p1, p2, s0, s1, s2, pieces, pa, weights, ascs, mask, *tok_refs)
+    )(factor, ids, p0, p1, p2, s0, s1, s2, *pieces, pa, weights, ascs, mask, *tok_refs)
     sums = lax.psum_scatter(out2, "y", scatter_dimension=0, tiled=False)
     dg = jnp.sum(lax.all_to_all(dgp, MP, 0, 0, tiled=True), axis=0)
     grad_gain = jnp.sum(spread(dg, DP).reshape(16, BLK), axis=0)

time: 277 us -> 258 us (0.931)
  waiting for transfers between devices: 123 us -> 102 us
  local copies, waits for them, and re-layouts: 7.45 us -> 10.3 us
    all_to_all x2 -> x0, waiting for transfers between devices: 22.8 us -> none  [the longest x1 20.1 us: body(): lax.all_to_all(jnp.broadcast_to(pieces[None, :, :ROWS], (4, 4, ROWS, BLK)...]
    all_to_all x2 -> x0, starting transfers between devices: 9.41 us -> none  [the longest x1 5.12 us: body(): pieces = lax.all_to_all(after(pieces, mid), 'zh', 0, 0, tiled=True)]
    ppermute x5 -> x8, waiting for transfers between devices: 35.2 us -> 28.3 us  [from_z(): return lax.ppermute(value, ('zh', 'zl'), pairs)]
    all_gather x2 -> x1, waiting for transfers between devices: 8.41 us -> 13.5 us  [body(): weights = in_hbm(lax.all_gather(part_w, 'y', axis=0, tiled=False))]
    all_to_all x2 -> x3, starting transfers between devices: 12.1 us -> 17.1 us  [over_x(): lax.all_to_all(jnp.broadcast_to(value[None], (4,) + value.shape), 'x', 0,...]
    ppermute x5 -> x8, starting transfers between devices: 13 us -> 17.2 us  [from_z(): return lax.ppermute(value, ('zh', 'zl'), pairs)]
    all_to_all x2 -> x3, waiting for transfers between devices: 13.2 us -> 16.6 us  [over_x(): lax.all_to_all(jnp.broadcast_to(value[None], (4,) + value.shape), 'x', 0,...]
    broadcast_in_dim x2 -> x3, local copies, waits for them, and re-layouts: 1.69 us -> 4.69 us  [over_x(): jnp.broadcast_to(value[None], (4,) + value.shape)]
  transfers between devices with their start and end apart: 20 -> 20, of which waited for: 15 -> 13; matrix products, arithmetic and copies ran while one was open for 2% -> 2% of each run, Pallas kernels for 3% -> 3%
where the time goes in v3:
time: 258 us; the launch traced here: 257 us
  waiting for transfers between devices  102 us (40%)
  starting transfers between devices  52.4 us (20%)
  Pallas kernels  37.8 us (15%)
  blocking collectives  36 us (14%)
  between operations  15.4 us (6%)
  local copies, waits for them, and re-layouts  10.3 us (4%)
  other arithmetic  2.96 us (1%)
    ppermute x8, waiting for transfers between devices, from_z(): return lax.ppermute(value, ('zh', 'zl'), pairs)  28.3 us
    all_to_all x2, blocking collectives, spread(): lax.all_to_all(jnp.broadcast_to(value[None], (n,) + value.shape), axes, 0...  26.6 us
    all_to_all x1, waiting for transfers between devices, body(): terms = lax.all_to_all(out1, 'y', 0, 0, tiled=True)  20.1 us
    ppermute x8, starting transfers between devices, from_z(): return lax.ppermute(value, ('zh', 'zl'), pairs)  17.2 us
    all_to_all x3, starting transfers between devices, over_x(): lax.all_to_all(jnp.broadcast_to(value[None], (4,) + value.shape), 'x', 0,...  17.1 us
    all_to_all x3, waiting for transfers between devices, over_x(): lax.all_to_all(jnp.broadcast_to(value[None], (4,) + value.shape), 'x', 0,...  16.6 us
    all_gather x1, waiting for transfers between devices, body(): weights = in_hbm(lax.all_gather(part_w, 'y', axis=0, tiled=False))  13.5 us
    all_to_all x1, waiting for transfers between devices, body(): sums = lax.all_to_all(sums, 'zh', 0, 0, tiled=True)  11.7 us
  transfers between devices with their start and end apart: 20, of which 13 were waited for; matrix products, arithmetic and copies ran while one was open for 2% of the time, Pallas kernels for 3%

profile of v3, /device:TPU:4, one launch (start us, length us, event | category | flops | bytes accessed | tf_op | source)
XLA Modules:
  0.0 257.3 jit_solution(10903434141798622859)
XLA Ops:
  7.3 0.7 copy-done.14
  7.9 2.4 shard_map.94
  10.3 1.8 broadcast_in_dim.17
  12.1 5.7 %all-to-all-start = ((bf16[4,1,272,256]{3,2,1,0:T(8,128)(2,1)}), bf16[4,1,272,256]{3,2,1,0:T(8,128)(2,1)S(1)}, u32[]{:S(2)}, u32[]{:S(2)}) async-start(bf16[4,1,272,256]{3,2,1,0:T(8,128)(2,1)} %broadcast_in_dim.17), calls=%async_computation | async-start | bytes 1114112 | tf_op jit(solution)/shard_map/all_to_all | solution.py:271
  17.8 1.0 collective-permute-start.6
  18.9 6.3 %collective-permute-start.5 = (bf16[272,256]{1,0:T(8,128)(2,1)S(1)}, bf16[272,256]{1,0:T(8,128)(2,1)S(1)}, u32[]{:S(2)}, u32[]{:S(2)}) collective-permute-start(bf16[272,256]{1,0:T(8,128)(2,1)S(1)} %copy-done.17), channel_id=1, source_target_pairs={{32,0},{34,2},{48,16},{50,18},{0,32},{2,34},{16,48},{18,50},{33,1}... | collective-permute-start | bytes 417800 | tf_op jit(solution)/shard_map/ppermute | solution.py:38
  25.2 1.5 collective-permute-start.4
  26.6 2.7 %collective-permute-start.3 = (bf16[272,256]{1,0:T(8,128)(2,1)S(1)}, bf16[272,256]{1,0:T(8,128)(2,1)S(1)}, u32[]{:S(2)}, u32[]{:S(2)}) collective-permute-start(bf16[272,256]{1,0:T(8,128)(2,1)S(1)} %copy-done.17), channel_id=1, source_target_pairs={{16,0},{18,2},{32,16},{34,18},{48,32},{50,34},{0,48},{2,50},{17,1}... | collective-permute-start | bytes 417800 | tf_op jit(solution)/shard_map/ppermute | solution.py:38
  29.3 8.7 %collective-permute-done.5 = bf16[272,256]{1,0:T(8,128)(2,1)S(1)} collective-permute-done((bf16[272,256]{1,0:T(8,128)(2,1)S(1)}, bf16[272,256]{1,0:T(8,128)(2,1)S(1)}, u32[]{:S(2)}, u32[]{:S(2)}) %collective-permute-start.5) | collective-permute-done | bytes 139296 | tf_op jit(solution)/shard_map/ppermute | solution.py:38
  38.0 1.1 collective-permute-done.4
  39.1 1.6 broadcast_in_dim.18
  40.7 4.9 %all-to-all-start.1 = ((bf16[4,4,272,256]{3,2,1,0:T(8,128)(2,1)}), bf16[4,4,272,256]{3,2,1,0:T(8,128)(2,1)}, u32[]{:S(2)}, u32[]{:S(2)}) async-start(bf16[4,4,272,256]{3,2,1,0:T(8,128)(2,1)} %broadcast_in_dim.18), calls=%async_computation.1 | async-start | bytes 4456448 | tf_op jit(solution)/shard_map/all_to_all | solution.py:271
  45.6 2.2 collective-permute-start
  47.9 2.5 collective-permute-start.1
  50.4 0.9 collective-permute-start.2
  51.5 5.5 %collective-permute-done.c1 = bf16[288,256]{1,0:T(8,128)(2,1)S(1)} collective-permute-done((bf16[288,256]{1,0:T(8,128)(2,1)S(1)}, bf16[288,256]{1,0:T(8,128)(2,1)S(1)}, u32[]{:S(2)}, u32[]{:S(2)}) %collective-permute-start) | collective-permute-done | bytes 147488 | tf_op jit(solution)/shard_map/ppermute | solution.py:38
  57.0 5.0 %collective-permute-done.1.c2 = bf16[288,256]{1,0:T(8,128)(2,1)S(1)} collective-permute-done((bf16[288,256]{1,0:T(8,128)(2,1)S(1)}, bf16[288,256]{1,0:T(8,128)(2,1)S(1)}, u32[]{:S(2)}, u32[]{:S(2)}) %collective-permute-start.1) | collective-permute-done | bytes 147488 | tf_op jit(solution)/shard_map/ppermute | solution.py:38
  62.1 2.4 collective-permute-done.2.c3
  64.5 0.8 pad_maximum_fusion.2
  65.3 5.6 %collective-permute-done.9 = bf16[3,272,256]{2,1,0:T(8,128)(2,1)S(1)} collective-permute-done((bf16[3,272,256]{2,1,0:T(8,128)(2,1)S(1)}, bf16[3,272,256]{2,1,0:T(8,128)(2,1)S(1)}, u32[]{:S(2)}, u32[]{:S(2)}) %collective-permute-start.9) | collective-permute-done | bytes 417824 | tf_op jit(solution)/shard_map/ppermute | solution.py:38
  70.8 1.3 broadcast_in_dim.19
  72.1 6.5 %all-to-all-start.2 = ((bf16[4,3,272,256]{3,2,1,0:T(8,128)(2,1)}), bf16[4,3,272,256]{3,2,1,0:T(8,128)(2,1)}, u32[]{:S(2)}, u32[]{:S(2)}) async-start(bf16[4,3,272,256]{3,2,1,0:T(8,128)(2,1)} %broadcast_in_dim.19), calls=%async_computation.2 | async-start | bytes 3342336 | tf_op jit(solution)/shard_map/all_to_all | solution.py:271
  78.6 0.7 all-gather.5.cloned.1.call-update
  79.4 16.6 %all-to-all-done.2.refs_0_.refs_3_ = bf16[4,3,272,256]{3,2,1,0:T(8,128)(2,1)} async-done(((bf16[4,3,272,256]{3,2,1,0:T(8,128)(2,1)}), bf16[4,3,272,256]{3,2,1,0:T(8,128)(2,1)}, u32[]{:S(2)}, u32[]{:S(2)}) %all-to-all-start.2) | async-done | bytes 1671200 | tf_op jit(solution)/shard_map/all_to_all | solution.py:271
  96.6 13.5 %all-gather.5.cloned.1.call-done = bf16[16,192,256]{2,1,0:T(8,128)(2,1)} async-done(((bf16[4,192,256]{2,1,0:T(8,128)(2,1)}), bf16[16,192,256]{2,1,0:T(8,128)(2,1)}) %all-gather.5.cloned.1.call-update) | async-done | bytes 1572880 | tf_op jit(solution)/shard_map/all_gather | solution.py:278
  110.0 3.3 %shard_map.96 = (f32[4,192,256]{2,1,0:T(8,128)S(1)}, f32[4,8,256]{2,1,0:T(8,128)S(1)}) custom-call(s32[5]{0:T(128)S(1)} %stack.59.ids, bf16[4,4,192,256]{3,2,1,0:T(8,128)(2,1)} %bitcast.33, bf16[4,3,272,256]{3,2,1,0:T(8,128)(2,1)} %all-to-all-done.2.refs_0_.refs_3_), custom_call_target="tpu_custom_call" | custom-call | flops 301989888 | bytes 1671168 | tf_op jit(solution)/shard_map/pallas_call | solution.py:297
  113.4 0.8 copy-done.16
  114.2 5.0 %shard_map.95 = (f32[4,192,256]{2,1,0:T(8,128)S(1)}, f32[4,8,256]{2,1,0:T(8,128)S(1)}, f32[16,8,256]{2,1,0:T(8,128)S(1)}) custom-call(s32[5]{0:T(128)S(1)} %stack.59.ids, bf16[4,4,192,256]{3,2,1,0:T(8,128)(2,1)} %bitcast.34, bf16[4,1,272,256]{3,2,1,0:T(8,128)(2,1)} %copy-done.15, bf16[4,4,272,256]{3,2,1,0:T(8,128)(2,1)} %all-to-all-done.1.refs_1_.refs_2_, ...), custom_call_target="tpu_custom_call" | custom-call | flops 1006632960 | bytes 5570560 | tf_op jit(solution)/shard_map/pallas_call | solution.py:297
  119.2 3.3 %shard_map.97 = (f32[4,192,256]{2,1,0:T(8,128)S(1)}, f32[4,8,256]{2,1,0:T(8,128)S(1)}) custom-call(s32[5]{0:T(128)S(1)} %stack.59.ids, bf16[4,4,192,256]{3,2,1,0:T(8,128)(2,1)} %bitcast.35, bf16[4,3,272,256]{3,2,1,0:T(8,128)(2,1)} %collective-permute-done.10.refs_0_.refs_7_), custom_call_target="tpu_custom_call" | custom-call | flops 301989888 | bytes 1671168 | tf_op jit(solution)/shard_map/pallas_call | solution.py:297
  122.6 6.7 %shard_map.98 = bf16[4,4,192,256]{3,2,1,0:T(8,128)(2,1)} custom-call(s32[5]{0:T(128)S(1)} %stack.59.ids, f32[4,192,256]{2,1,0:T(8,128)S(1)} %get-tuple-element.29.p0, f32[4,192,256]{2,1,0:T(8,128)S(1)} %get-tuple-element.31.p1, f32[4,192,256]{2,1,0:T(8,128)S(1)} %get-tuple-element.32.p2, f32[4,8,256]{2,1,0:T(8,128)S(1)} %get-tuple-element.33.s0, ...), custom_call_target="tpu_custom_call" | custom-call | flops 1610612736 | bytes 12000000 | tf_op jit(solution)/shard_map/pallas_call | solution.py:317
  129.3 0.9 copy-done
  130.2 3.6 %all-to-all-start.3 = ((bf16[4,4,192,256]{3,2,1,0:T(8,128)(2,1)}), bf16[4,4,192,256]{3,2,1,0:T(8,128)(2,1)S(1)}, u32[]{:S(2)}, u32[]{:S(2)}) async-start(bf16[4,4,192,256]{3,2,1,0:T(8,128)(2,1)} %shard_map.98), calls=%async_computation.3 | async-start | bytes 3145728 | tf_op jit(solution)/shard_map/all_to_all | solution.py:326
  133.8 0.8 convert_element_type.3
  134.6 20.1 %all-to-all-done.3.terms = bf16[4,4,192,256]{3,2,1,0:T(8,128)(2,1)S(1)} async-done(((bf16[4,4,192,256]{3,2,1,0:T(8,128)(2,1)}), bf16[4,4,192,256]{3,2,1,0:T(8,128)(2,1)S(1)}, u32[]{:S(2)}, u32[]{:S(2)}) %all-to-all-start.3) | async-done | bytes 1572896 | tf_op jit(solution)/shard_map/all_to_all | solution.py:326
  155.3 1.6 shard_map.99
  157.5 0.7 broadcast_in_dim.20
  158.2 9.5 %all_to_all.50 = f32[16,8,128]{2,1,0:T(8,128)S(1)} all-to-all(f32[16,8,128]{2,1,0:T(8,128)S(1)} %broadcast_in_dim.20), channel_id=1, replica_groups=mesh['y'=4,'zh'=4,'x'=4,'zl'=2,'c'=2] {'x','zl','c'}, dimensions={0} | all-to-all | bytes 131072 | tf_op jit(solution)/shard_map/all_to_all | solution.py:251
  167.7 0.6 broadcast_in_dim.21
  168.3 6.8 %all-to-all-start.5 = ((f32[16,8,128]{2,1,0:T(8,128)}), f32[16,8,128]{2,1,0:T(8,128)S(1)}, u32[]{:S(2)}, u32[]{:S(2)}) async-start(f32[16,8,128]{2,1,0:T(8,128)} %broadcast_in_dim.21), calls=%async_computation.5 | async-start | bytes 131072 | tf_op jit(solution)/shard_map/all_to_all | solution.py:251
  176.0 9.3 %all-to-all-done.5 = f32[16,8,128]{2,1,0:T(8,128)S(1)} async-done(((f32[16,8,128]{2,1,0:T(8,128)}), f32[16,8,128]{2,1,0:T(8,128)S(1)}, u32[]{:S(2)}, u32[]{:S(2)}) %all-to-all-start.5) | async-done | bytes 65568 | tf_op jit(solution)/shard_map/all_to_all | solution.py:251
  187.5 6.4 %shard_map.100.pa = f32[4,192,256]{2,1,0:T(8,128)S(1)} custom-call(s32[5]{0:T(128)S(1)} %copy-done.11, bf16[4,4,192,256]{3,2,1,0:T(8,128)(2,1)} %bitcast.37, f32[16,2,256]{2,1,0:T(2,128)S(1)} %bitcast.29, f32[16,8,256]{2,1,0:T(8,128)S(1)} %get-tuple-element.36.gabs, bf16[4,1,272,256]{3,2,1,0:T(8,128)(2,1)} %copy-done.15, ...), custom_call_target="tpu_custom_call" | custom-call | flops 1610612736 | bytes 12000000 | tf_op jit(solution)/shard_map/pallas_call | solution.py:337
  194.0 7.5 %shard_map.101 = (bf16[4,4,192,256]{3,2,1,0:T(8,128)(2,1)}, f32[16,256]{1,0:T(8,128)S(1)}) custom-call(f32[1]{0:T(128)} %bitcast.18.factor, s32[5]{0:T(128)S(1)} %copy-done.11, f32[4,192,256]{2,1,0:T(8,128)S(1)} %get-tuple-element.29.p0, f32[4,192,256]{2,1,0:T(8,128)S(1)} %get-tuple-element.31.p1, f32[4,192,256]{2,1,0:T(8,128)S(1)} %copy-done.1, ...), custom_call_target="tpu_custom_call" | custom-call | flops 1610612736 | bytes 12000000 | tf_op jit(solution)/shard_map/pallas_call | solution.py:345
  201.6 9.4 %all_to_all.51 = f32[16,1,256]{2,1,0:T(1,128)S(1)} all-to-all(f32[16,1,256]{2,1,0:T(1,128)S(1)} %copy.12), channel_id=1, replica_groups=mesh['y'=4,'zh'=4,'x'=4,'zl'=2,'c'=2] {'x','zl','c'}, dimensions={0} | all-to-all | bytes 32768 | tf_op jit(solution)/shard_map/all_to_all | solution.py:355
  211.0 17.1 %all_to_all.52 = f32[16,1,256]{2,1,0:T(1,128)S(1)} all-to-all(f32[16,1,256]{2,1,0:T(1,128)S(1)} %broadcast_in_dim.23), channel_id=1, replica_groups=mesh['y'=4,'zh'=4,'x'=4,'zl'=2,'c'=2] {'y','zh'}, dimensions={0} | all-to-all | bytes 32768 | tf_op jit(solution)/shard_map/all_to_all | solution.py:251
  228.1 1.9 reduce-scatter.2.cloned.1.call-done
  230.0 6.9 %all-to-all-start.8 = ((bf16[4,192,256]{2,1,0:T(8,128)(2,1)}), bf16[4,192,256]{2,1,0:T(8,128)(2,1)S(1)}, u32[]{:S(2)}, u32[]{:S(2)}) async-start(bf16[4,192,256]{2,1,0:T(8,128)(2,1)} %bitcast.45), calls=%async_computation.9 | async-start | bytes 786432 | tf_op jit(solution)/shard_map/all_to_all | solution.py:357
  237.5 11.7 %all-to-all-done.8.sums = bf16[4,192,256]{2,1,0:T(8,128)(2,1)S(1)} async-done(((bf16[4,192,256]{2,1,0:T(8,128)(2,1)}), bf16[4,192,256]{2,1,0:T(8,128)(2,1)S(1)}, u32[]{:S(2)}, u32[]{:S(2)}) %all-to-all-start.8) | async-done | bytes 393248 | tf_op jit(solution)/shard_map/all_to_all | solution.py:357
  249.2 1.6 shard_map.102
  (69 shorter events, 4.7 us)
Async XLA Ops:
  7.3 115.3 %copy-start.9 = (s32[5]{0:T(128)}, s32[5]{0:T(128)S(1)}, u32[]{:S(2)}) copy-start(s32[5]{0:T(128)S(1)} %stack.59.ids) | copy-start | bytes 64
  7.3 0.7 copy-start.14
  10.3 7.5 %copy-start.17 = (bf16[272,256]{1,0:T(8,128)(2,1)S(1)}, bf16[272,256]{1,0:T(8,128)(2,1)}, u32[]{:S(2)}) copy-start(bf16[272,256]{1,0:T(8,128)(2,1)} %get-tuple-element.27) | copy-start | bytes 417796
  12.1 27.0 %all-to-all-start = ((bf16[4,1,272,256]{3,2,1,0:T(8,128)(2,1)}), bf16[4,1,272,256]{3,2,1,0:T(8,128)(2,1)S(1)}, u32[]{:S(2)}, u32[]{:S(2)}) async-start(bf16[4,1,272,256]{3,2,1,0:T(8,128)(2,1)} %broadcast_in_dim.17), calls=%async_computation | async-start | bytes 1114112 | tf_op jit(solution)/shard_map/all_to_all | solution.py:271
  17.8 11.5 %collective-permute-start.6 = (bf16[272,256]{1,0:T(8,128)(2,1)S(1)}, bf16[272,256]{1,0:T(8,128)(2,1)S(1)}, u32[]{:S(2)}, u32[]{:S(2)}) collective-permute-start(bf16[272,256]{1,0:T(8,128)(2,1)S(1)} %copy-done.17), channel_id=1, source_target_pairs={{2,0},{0,2},{18,16},{16,18},{34,32},{32,34},{50,48},{48,50},{3,1},... | collective-permute-start | bytes 417800 | tf_op jit(solution)/shard_map/ppermute | solution.py:38
  18.9 19.1 %collective-permute-start.5 = (bf16[272,256]{1,0:T(8,128)(2,1)S(1)}, bf16[272,256]{1,0:T(8,128)(2,1)S(1)}, u32[]{:S(2)}, u32[]{:S(2)}) collective-permute-start(bf16[272,256]{1,0:T(8,128)(2,1)S(1)} %copy-done.17), channel_id=1, source_target_pairs={{32,0},{34,2},{48,16},{50,18},{0,32},{2,34},{16,48},{18,50},{33,1}... | collective-permute-start | bytes 417800 | tf_op jit(solution)/shard_map/ppermute | solution.py:38
  25.2 13.9 %collective-permute-start.4 = (bf16[272,256]{1,0:T(8,128)(2,1)S(1)}, bf16[272,256]{1,0:T(8,128)(2,1)S(1)}, u32[]{:S(2)}, u32[]{:S(2)}) collective-permute-start(bf16[272,256]{1,0:T(8,128)(2,1)S(1)} %copy-done.17), channel_id=1, source_target_pairs={{48,0},{50,2},{0,16},{2,18},{16,32},{18,34},{32,48},{34,50},{49,1}... | collective-permute-start | bytes 417800 | tf_op jit(solution)/shard_map/ppermute | solution.py:38
  26.6 12.4 %collective-permute-start.3 = (bf16[272,256]{1,0:T(8,128)(2,1)S(1)}, bf16[272,256]{1,0:T(8,128)(2,1)S(1)}, u32[]{:S(2)}, u32[]{:S(2)}) collective-permute-start(bf16[272,256]{1,0:T(8,128)(2,1)S(1)} %copy-done.17), channel_id=1, source_target_pairs={{16,0},{18,2},{32,16},{34,18},{48,32},{50,34},{0,48},{2,50},{17,1}... | collective-permute-start | bytes 417800 | tf_op jit(solution)/shard_map/ppermute | solution.py:38
  39.1 56.9 %copy-start.15 = (bf16[4,1,272,256]{3,2,1,0:T(8,128)(2,1)}, bf16[4,1,272,256]{3,2,1,0:T(8,128)(2,1)S(1)}, u32[]{:S(2)}) copy-start(bf16[4,1,272,256]{3,2,1,0:T(8,128)(2,1)S(1)} %all-to-all-done.refs_0_) | copy-start | bytes 1671172
  40.7 5.0 %copy-start.20 = (bf16[288,256]{1,0:T(8,128)(2,1)S(1)}, bf16[288,256]{1,0:T(8,128)(2,1)}, u32[]{:S(2)}) copy-start(bf16[288,256]{1,0:T(8,128)(2,1)} %get-tuple-element.24) | copy-start | bytes 442372
  40.7 7.2 %copy-start.19 = (bf16[288,256]{1,0:T(8,128)(2,1)S(1)}, bf16[288,256]{1,0:T(8,128)(2,1)}, u32[]{:S(2)}) copy-start(bf16[288,256]{1,0:T(8,128)(2,1)} %get-tuple-element.25) | copy-start | bytes 442372
  40.7 9.7 %copy-start.18 = (bf16[288,256]{1,0:T(8,128)(2,1)S(1)}, bf16[288,256]{1,0:T(8,128)(2,1)}, u32[]{:S(2)}) copy-start(bf16[288,256]{1,0:T(8,128)(2,1)} %get-tuple-element.26) | copy-start | bytes 442372
  40.7 10.6 %copy-start.2 = (bf16[288,256]{1,0:T(8,128)(2,1)S(1)}, bf16[288,256]{1,0:T(8,128)(2,1)}, u32[]{:S(2)}) copy-start(bf16[288,256]{1,0:T(8,128)(2,1)} %get-tuple-element.23.c0) | copy-start | bytes 442372
  40.7 30.1 %all-to-all-start.1 = ((bf16[4,4,272,256]{3,2,1,0:T(8,128)(2,1)}), bf16[4,4,272,256]{3,2,1,0:T(8,128)(2,1)}, u32[]{:S(2)}, u32[]{:S(2)}) async-start(bf16[4,4,272,256]{3,2,1,0:T(8,128)(2,1)} %broadcast_in_dim.18), calls=%async_computation.1 | async-start | bytes 4456448 | tf_op jit(solution)/shard_map/all_to_all | solution.py:271
  45.6 11.4 %collective-permute-start = (bf16[288,256]{1,0:T(8,128)(2,1)S(1)}, bf16[288,256]{1,0:T(8,128)(2,1)S(1)}, u32[]{:S(2)}, u32[]{:S(2)}) collective-permute-start(bf16[288,256]{1,0:T(8,128)(2,1)S(1)} %copy-done.20), channel_id=1, source_target_pairs={{16,0},{18,2},{32,16},{34,18},{48,32},{50,34},{0,48},{2,50},{17,1}... | collective-permute-start | bytes 442376 | tf_op jit(solution)/shard_map/ppermute | solution.py:38
  47.9 14.2 %collective-permute-start.1 = (bf16[288,256]{1,0:T(8,128)(2,1)S(1)}, bf16[288,256]{1,0:T(8,128)(2,1)S(1)}, u32[]{:S(2)}, u32[]{:S(2)}) collective-permute-start(bf16[288,256]{1,0:T(8,128)(2,1)S(1)} %copy-done.19), channel_id=1, source_target_pairs={{32,0},{34,2},{48,16},{50,18},{0,32},{2,34},{16,48},{18,50},{33,1}... | collective-permute-start | bytes 442376 | tf_op jit(solution)/shard_map/ppermute | solution.py:38
  50.4 14.0 %collective-permute-start.2 = (bf16[288,256]{1,0:T(8,128)(2,1)S(1)}, bf16[288,256]{1,0:T(8,128)(2,1)S(1)}, u32[]{:S(2)}, u32[]{:S(2)}) collective-permute-start(bf16[288,256]{1,0:T(8,128)(2,1)S(1)} %copy-done.18), channel_id=1, source_target_pairs={{48,0},{50,2},{0,16},{2,18},{16,32},{18,34},{32,48},{34,50},{49,1}... | collective-permute-start | bytes 442376 | tf_op jit(solution)/shard_map/ppermute | solution.py:38
  51.4 19.5 %collective-permute-start.9 = (bf16[3,272,256]{2,1,0:T(8,128)(2,1)S(1)}, bf16[3,272,256]{2,1,0:T(8,128)(2,1)S(1)}, u32[]{:S(2)}, u32[]{:S(2)}) collective-permute-start(bf16[3,272,256]{2,1,0:T(8,128)(2,1)S(1)} %pad_maximum_fusion.1), channel_id=1, source_target_pairs={{2,0},{0,2},{18,16},{16,18},{34,32},{32,34},{50,48},{48,50},{3,1},... | collective-permute-start | bytes 1253384 | tf_op jit(solution)/shard_map/ppermute | solution.py:38
  57.0 65.5 %copy-start.3 = (bf16[288,256]{1,0:T(8,128)(2,1)}, bf16[288,256]{1,0:T(8,128)(2,1)S(1)}, u32[]{:S(2)}) copy-start(bf16[288,256]{1,0:T(8,128)(2,1)S(1)} %collective-permute-done.c1) | copy-start | bytes 442372
  62.0 60.5 %copy-start.5 = (bf16[288,256]{1,0:T(8,128)(2,1)}, bf16[288,256]{1,0:T(8,128)(2,1)S(1)}, u32[]{:S(2)}) copy-start(bf16[288,256]{1,0:T(8,128)(2,1)S(1)} %collective-permute-done.1.c2) | copy-start | bytes 442372
  64.5 58.1 %copy-start.7 = (bf16[288,256]{1,0:T(8,128)(2,1)}, bf16[288,256]{1,0:T(8,128)(2,1)S(1)}, u32[]{:S(2)}) copy-start(bf16[288,256]{1,0:T(8,128)(2,1)S(1)} %collective-permute-done.2.c3) | copy-start | bytes 442372
  72.1 23.9 %all-to-all-start.2 = ((bf16[4,3,272,256]{3,2,1,0:T(8,128)(2,1)}), bf16[4,3,272,256]{3,2,1,0:T(8,128)(2,1)}, u32[]{:S(2)}, u32[]{:S(2)}) async-start(bf16[4,3,272,256]{3,2,1,0:T(8,128)(2,1)} %broadcast_in_dim.19), calls=%async_computation.2 | async-start | bytes 3342336 | tf_op jit(solution)/shard_map/all_to_all | solution.py:271
  78.6 31.4 %all-gather.5.cloned.1.call-start = ((), (), s32[]{:S(2)}) async-start(), calls=%async_computation.11 | async-start | bytes 1966080 | tf_op jit(solution)/shard_map/all_gather | solution.py:278
  79.3 34.1 %collective-permute-start.8 = (bf16[4,4,272,256]{3,2,1,0:T(8,128)(2,1)}, bf16[4,4,272,256]{3,2,1,0:T(8,128)(2,1)}, u32[]{:S(2)}, u32[]{:S(2)}) collective-permute-start(bf16[4,4,272,256]{3,2,1,0:T(8,128)(2,1)} %all-to-all-done.1.refs_1_.refs_2_), channel_id=1, source_target_pairs={{0,1},{1,0},{2,3},{3,2},{4,5},{5,4},{6,7},{7,6},{8,9},{9,8},{10,11... | collective-permute-start | bytes 6684680 | tf_op jit(solution)/shard_map/ppermute | solution.py:42
  96.1 23.1 %collective-permute-start.10 = (bf16[4,3,272,256]{3,2,1,0:T(8,128)(2,1)}, bf16[4,3,272,256]{3,2,1,0:T(8,128)(2,1)}, u32[]{:S(2)}, u32[]{:S(2)}) collective-permute-start(bf16[4,3,272,256]{3,2,1,0:T(8,128)(2,1)} %all-to-all-done.2.refs_0_.refs_3_), channel_id=1, source_target_pairs={{0,1},{1,0},{2,3},{3,2},{4,5},{5,4},{6,7},{7,6},{8,9},{9,8},{10,11... | collective-permute-start | bytes 5013512 | tf_op jit(solution)/shard_map/ppermute | solution.py:42
  96.1 17.3 %collective-permute-start.7 = (bf16[4,1,272,256]{3,2,1,0:T(8,128)(2,1)S(1)}, bf16[4,1,272,256]{3,2,1,0:T(8,128)(2,1)S(1)}, u32[]{:S(2)}, u32[]{:S(2)}) collective-permute-start(bf16[4,1,272,256]{3,2,1,0:T(8,128)(2,1)S(1)} %all-to-all-done.refs_0_), channel_id=1, source_target_pairs={{0,1},{1,0},{2,3},{3,2},{4,5},{5,4},{6,7},{7,6},{8,9},{9,8},{10,11... | collective-permute-start | bytes 1671176 | tf_op jit(solution)/shard_map/ppermute | solution.py:42
  113.4 0.8 copy-start.16
  129.3 0.9 copy-start
  130.2 24.5 %all-to-all-start.3 = ((bf16[4,4,192,256]{3,2,1,0:T(8,128)(2,1)}), bf16[4,4,192,256]{3,2,1,0:T(8,128)(2,1)S(1)}, u32[]{:S(2)}, u32[]{:S(2)}) async-start(bf16[4,4,192,256]{3,2,1,0:T(8,128)(2,1)} %shard_map.98), calls=%async_computation.3 | async-start | bytes 3145728 | tf_op jit(solution)/shard_map/all_to_all | solution.py:326
  133.7 53.2 %all-gather.7.cloned.1.call-start = ((), (), s32[]{:S(2)}) async-start(), calls=%async_computation.12 | async-start | bytes 1966080 | tf_op jit(solution)/shard_map/all_gather | solution.py:333
  154.7 0.6 copy-start.10
  156.9 0.6 copy-start.13
  168.3 17.0 %all-to-all-start.5 = ((f32[16,8,128]{2,1,0:T(8,128)}), f32[16,8,128]{2,1,0:T(8,128)S(1)}, u32[]{:S(2)}, u32[]{:S(2)}) async-start(f32[16,8,128]{2,1,0:T(8,128)} %broadcast_in_dim.21), calls=%async_computation.5 | async-start | bytes 131072 | tf_op jit(solution)/shard_map/all_to_all | solution.py:251
  175.1 54.9 %reduce-scatter.2.cloned.1.call-start = ((), (), s32[]{:S(2)}) async-start(), calls=%async_computation.10 | async-start | bytes 1966080 | tf_op jit(solution)/shard_map/reduce_scatter | solution.py:354
  186.9 0.6 copy-start.11
  187.5 6.4 %copy-start.1 = (f32[4,192,256]{2,1,0:T(8,128)S(1)}, f32[4,192,256]{2,1,0:T(8,128)}, u32[]{:S(2)}) copy-start(f32[4,192,256]{2,1,0:T(8,128)} %copy-done) | copy-start | bytes 2359300
  187.5 6.4 %copy-start.4 = (bf16[288,256]{1,0:T(8,128)(2,1)S(1)}, bf16[288,256]{1,0:T(8,128)(2,1)}, u32[]{:S(2)}) copy-start(bf16[288,256]{1,0:T(8,128)(2,1)} %copy-done.3) | copy-start | bytes 442372
  187.5 6.4 %copy-start.6 = (bf16[288,256]{1,0:T(8,128)(2,1)S(1)}, bf16[288,256]{1,0:T(8,128)(2,1)}, u32[]{:S(2)}) copy-start(bf16[288,256]{1,0:T(8,128)(2,1)} %copy-done.5) | copy-start | bytes 442372
  187.5 6.4 %copy-start.8 = (bf16[288,256]{1,0:T(8,128)(2,1)S(1)}, bf16[288,256]{1,0:T(8,128)(2,1)}, u32[]{:S(2)}) copy-start(bf16[288,256]{1,0:T(8,128)(2,1)} %copy-done.7) | copy-start | bytes 442372
  201.5 47.7 %copy-start.12 = (s32[5]{0:T(128)S(1)}, s32[5]{0:T(128)}, u32[]{:S(2)}) copy-start(s32[5]{0:T(128)} %copy-done.9) | copy-start | bytes 64
  230.0 19.1 %all-to-all-start.8 = ((bf16[4,192,256]{2,1,0:T(8,128)(2,1)}), bf16[4,192,256]{2,1,0:T(8,128)(2,1)S(1)}, u32[]{:S(2)}, u32[]{:S(2)}) async-start(bf16[4,192,256]{2,1,0:T(8,128)(2,1)} %bitcast.45), calls=%async_computation.9 | async-start | bytes 786432 | tf_op jit(solution)/shard_map/all_to_all | solution.py:357
Sparse Core Ops, SparseCore 0:
  81.8 28.1 all-gather.4
  157.6 29.2 all-gather.6
  201.7 28.3 reduce-scatter.1

commit v4 on v3

--- a/solution.py
+++ b/solution.py
@@ -23,8 +23,7 @@
 
 GROUPS = (
     ((0, 0),),
-    ((0, 1),),
-    ((1, 0), (3, 0), (2, 0)),
+    ((1, 0), (3, 0), (2, 0), (0, 1)),
     ((1, 1), (3, 1), (2, 1)),
 )
 PLACE = {b: (g, i) for g, grp in enumerate(GROUPS) for i, b in enumerate(grp)}
@@ -54,7 +53,7 @@
         in_specs=in_specs,
         out_specs=out_specs,
         scratch_shapes=scratch,
-        compiler_params=pltpu.CompilerParams(vmem_limit_bytes=32 * 1024 * 1024),
+        compiler_params=pltpu.CompilerParams(vmem_limit_bytes=16 * 1024 * 1024),
         cost_estimate=pl.CostEstimate(flops=flops, bytes_accessed=nbytes, transcendentals=0),
     )
 
@@ -65,6 +64,10 @@
 
 def in_hbm(value):
     return pltpu.with_memory_space_constraint(value, pltpu.HBM)
+
+
+def in_vmem(value):
+    return pltpu.with_memory_space_constraint(value, pltpu.VMEM)
 
 
 SMEM = pl.BlockSpec(memory_space=pltpu.SMEM)
@@ -118,7 +121,7 @@
     scaled, sums, squares = {}, {}, {}
     for (grp, g), ref in zip(parts, toks):
         for i, (k, l) in enumerate(GROUPS[grp]):
-            tail = ref[0, i, BLK:PACK, :]
+            tail = ref[x, i, BLK:PACK, :]
             if (l, g) not in scaled:
                 gain = row(tail, 0)
                 at = (zl ^ l) * 2 + (c ^ g)
@@ -126,13 +129,18 @@
                 scaled[l, g] = (wv.astype(F32) * gain).astype(BF)
                 if gabs is not None:
                     gabs[x * 4 + at] = jnp.broadcast_to(gain, (8, BLK))
-            term = lax.dot_general(scaled[l, g], ref[0, i, 0:BLK, :], NT, preferred_element_type=F32)
-            sums[k] = sums[k] + term if k in sums else term
+            sums.setdefault(k, []).append((scaled[l, g], ref[x, i, 0:BLK, :]))
             s = row(tail, 3)
             squares[k] = squares[k] + s if k in squares else s
-    for k, total in sums.items():
-        out[k] += total
+    for k, pairs in sums.items():
+        out[k] += joined(pairs, 1, NT)
         sq[k] += jnp.broadcast_to(squares[k], (8, BLK))
+
+
+def joined(pairs, axis, dims):
+    left = jnp.concatenate([p[0] for p in pairs], axis=1)
+    right = jnp.concatenate([p[1] for p in pairs], axis=axis)
+    return lax.dot_general(left, right, dims, preferred_element_type=F32)
 
 
 def pre2_kernel(parts, ids, asc, mask, gabs, *refs):
@@ -150,10 +158,9 @@
                 at = (zl ^ l) * 2 + (c ^ g)
                 fb = x * 4 + at
                 scaled[l, g] = (asc[0, at].astype(F32) * mask_rows(mask[fb]) * gabs[fb][0:1]).astype(BF)
-            term = lax.dot_general(scaled[l, g], ref[0, i, 0:BLK, :], NT, preferred_element_type=F32)
-            sums[k] = sums[k] + term if k in sums else term
-    for k, total in sums.items():
-        out[k] += total
+            sums.setdefault(k, []).append((scaled[l, g], ref[x, i, 0:BLK, :]))
+    for k, pairs in sums.items():
+        out[k] += joined(pairs, 1, NT)
 
 
 def mask_rows(m):
@@ -184,14 +191,12 @@
 
 def outer_terms(parts, d, toks):
     where = {p: ref for p, ref in zip(parts, toks)}
+    x = pl.program_id(0)
     for l in range(2):
         for g in range(2):
-            total = None
-            for k in range(4):
-                grp, i = PLACE[k, l]
-                term = lax.dot_general(d[k], where[grp, g][0, i, 0:BLK, :], NN, preferred_element_type=F32)
-                total = term if total is None else total + term
-            yield l, g, total
+            places = [PLACE[k, l] for k in range(4)]
+            pairs = [(d[k], where[grp, g][x, i, 0:BLK, :]) for k, (grp, i) in enumerate(places)]
+            yield l, g, joined(pairs, 0, NN)
 
 
 def outer1_kernel(parts, ids, p0, p1, p2, s0, s1, s2, c0, c1, c2, c3, *refs):
@@ -270,7 +275,7 @@
     def over_x(value):
         return lax.all_to_all(jnp.broadcast_to(value[None], (4,) + value.shape), "x", 0, 0, tiled=True)
 
-    mids = [from_z(pack, k, 0) for k, _ in GROUPS[2]]
+    mids = [from_z(pack, k, 0) for k in (1, 3, 2)]
     near = from_z(pack, 0, 1)
     own_x = over_x(pack[None])
     pieces = [pieces[0]] + [from_z(pieces[k], k, 0) for k in range(1, 4)]
@@ -279,17 +284,14 @@
     mid_x = over_x(after(jnp.stack(mids + [near]), own_x))
     far = from_z(jnp.stack(mids), 0, 1)
     far_x = over_x(after(far, part_w, mid_x))
-    toks = {}
-    for g in range(2):
-        o, m, f = [in_hbm(other_core(v) if g else v) for v in (own_x, mid_x, far_x)]
-        toks.update({(0, g): o, (1, g): m, (2, g): m, (3, g): f})
+    mine = [in_vmem(v) for v in (own_x, mid_x)]
+    toks = {(grp, g): in_vmem(other_core(v)) if g else v for grp, v in enumerate(mine) for g in range(2)}
 
     pshape, sshape, gshape = shape((4, ROWS, BLK), F32), shape((4, 8, BLK), F32), shape((NB, 8, BLK), F32)
     wspec = by_x((4, ROWS, BLK))
 
     def tok_spec(grp):
-        at = 3 if grp == 1 else 0
-        return pl.BlockSpec((1, len(GROUPS[grp]), PACK, BLK), lambda i: (i, at, 0, 0))
+        return pl.BlockSpec(memory_space=pltpu.VMEM)
 
     def pre(parts, with_gain):
         outs = [pshape, sshape] + ([gshape] if with_gain else [])
@@ -304,9 +306,11 @@
             nbytes=blocks * 4 * 2 * PACK * BLK,
         )(ids, weights, *[toks[p] for p in parts])
 
-    p0, s0, gabs = pre(tuple((grp, g) for g in range(2) for grp in (0, 1, 2)), True)
-    p1, s1 = pre(((3, 0),), False)
-    p2, s2 = pre(((3, 1),), False)
+    p0, s0, gabs = pre(tuple((grp, g) for g in range(2) for grp in (0, 1)), True)
+    far_x = after(in_vmem(far_x), p0)
+    toks[2, 0], toks[2, 1] = far_x, in_vmem(other_core(far_x))
+    p1, s1 = pre(((2, 0),), False)
+    p2, s2 = pre(((2, 1),), False)
     parts = tuple((grp, g) for g in range(2) for grp in range(len(GROUPS)))
     tok_specs = [tok_spec(p[0]) for p in parts]
     tok_refs = [toks[p] for p in parts]

time: 258 us -> 252 us (0.977)
  waiting for transfers between devices: 102 us -> 92.9 us
    all_gather x1, waiting for transfers between devices: 13.5 us -> 1.01 us  [body(): weights = in_hbm(lax.all_gather(part_w, 'y', axis=0, tiled=False))]
    ppermute x8, waiting for transfers between devices: 28.3 us -> 31.9 us  [from_z(): return lax.ppermute(value, ('zh', 'zl'), pairs)]
    unnamed x42 -> x60, local copies, waits for them, and re-layouts: 4.21 us -> 6.57 us
  transfers between devices with their start and end apart: 20 -> 20, of which waited for: 13 -> 14; matrix products, arithmetic and copies ran while one was open for 2% -> 3% of each run, Pallas kernels for 3% -> 3%
where the time goes in v4:
time: 252 us; the launch traced here: 251 us
  waiting for transfers between devices  92.9 us (37%)
  starting transfers between devices  52.5 us (21%)
  Pallas kernels  37.8 us (15%)
  blocking collectives  34.9 us (14%)
  between operations  15.5 us (6%)
  local copies, waits for them, and re-layouts  12.8 us (5%)
  other arithmetic  4.67 us (2%)
    ppermute x8, waiting for transfers between devices, from_z(): return lax.ppermute(value, ('zh', 'zl'), pairs)  31.9 us
    all_to_all x2, blocking collectives, spread(): lax.all_to_all(jnp.broadcast_to(value[None], (n,) + value.shape), axes, 0...  26.3 us
    all_to_all x1, waiting for transfers between devices, body(): terms = lax.all_to_all(out1, 'y', 0, 0, tiled=True)  20.7 us
    all_to_all x3, starting transfers between devices, over_x(): lax.all_to_all(jnp.broadcast_to(value[None], (4,) + value.shape), 'x', 0,...  17.9 us
    ppermute x8, starting transfers between devices, from_z(): return lax.ppermute(value, ('zh', 'zl'), pairs)  17.2 us
    all_to_all x3, waiting for transfers between devices, over_x(): lax.all_to_all(jnp.broadcast_to(value[None], (4,) + value.shape), 'x', 0,...  15.4 us
    pallas_call x3, Pallas kernels, pre(): call(functools.partial(pre_kernel, parts, with_gain), outs, [SMEM, wspec]...  12.2 us
    all_to_all x1, waiting for transfers between devices, body(): sums = lax.all_to_all(sums, 'zh', 0, 0, tiled=True)  11.3 us
  transfers between devices with their start and end apart: 20, of which 14 were waited for; matrix products, arithmetic and copies ran while one was open for 3% of the time, Pallas kernels for 3%

profile of v4, /device:TPU:4, one launch (start us, length us, event | category | flops | bytes accessed | tf_op | source)
XLA Modules:
  0.0 251.0 jit_solution(12382262982808618286)
XLA Ops:
  7.9 2.4 shard_map.94
  10.3 1.8 broadcast_in_dim.17
  12.1 5.7 %all-to-all-start = ((bf16[4,1,272,256]{3,2,1,0:T(8,128)(2,1)}), bf16[4,1,272,256]{3,2,1,0:T(8,128)(2,1)S(1)}, u32[]{:S(2)}, u32[]{:S(2)}) async-start(bf16[4,1,272,256]{3,2,1,0:T(8,128)(2,1)} %broadcast_in_dim.17), calls=%async_computation | async-start | bytes 1114112 | tf_op jit(solution)/shard_map/all_to_all | solution.py:276
  17.8 1.0 collective-permute-start.6
  18.9 6.3 %collective-permute-start.5 = (bf16[272,256]{1,0:T(8,128)(2,1)S(1)}, bf16[272,256]{1,0:T(8,128)(2,1)S(1)}, u32[]{:S(2)}, u32[]{:S(2)}) collective-permute-start(bf16[272,256]{1,0:T(8,128)(2,1)S(1)} %copy-done.28), channel_id=1, source_target_pairs={{32,0},{34,2},{48,16},{50,18},{0,32},{2,34},{16,48},{18,50},{33,1}... | collective-permute-start | bytes 417800 | tf_op jit(solution)/shard_map/ppermute | solution.py:37
  25.1 1.5 collective-permute-start.4
  26.6 2.7 %collective-permute-start.3 = (bf16[272,256]{1,0:T(8,128)(2,1)S(1)}, bf16[272,256]{1,0:T(8,128)(2,1)S(1)}, u32[]{:S(2)}, u32[]{:S(2)}) collective-permute-start(bf16[272,256]{1,0:T(8,128)(2,1)S(1)} %copy-done.28), channel_id=1, source_target_pairs={{16,0},{18,2},{32,16},{34,18},{48,32},{50,34},{0,48},{2,50},{17,1}... | collective-permute-start | bytes 417800 | tf_op jit(solution)/shard_map/ppermute | solution.py:37
  29.3 8.7 %collective-permute-done.5 = bf16[272,256]{1,0:T(8,128)(2,1)S(1)} collective-permute-done((bf16[272,256]{1,0:T(8,128)(2,1)S(1)}, bf16[272,256]{1,0:T(8,128)(2,1)S(1)}, u32[]{:S(2)}, u32[]{:S(2)}) %collective-permute-start.5) | collective-permute-done | bytes 139296 | tf_op jit(solution)/shard_map/ppermute | solution.py:37
  38.0 1.1 collective-permute-done.4
  39.1 1.5 broadcast_in_dim.18
  40.7 4.9 %all-to-all-start.1 = ((bf16[4,4,272,256]{3,2,1,0:T(8,128)(2,1)}), bf16[4,4,272,256]{3,2,1,0:T(8,128)(2,1)S(1)}, u32[]{:S(2)}, u32[]{:S(2)}) async-start(bf16[4,4,272,256]{3,2,1,0:T(8,128)(2,1)} %broadcast_in_dim.18), calls=%async_computation.1 | async-start | bytes 4456448 | tf_op jit(solution)/shard_map/all_to_all | solution.py:276
  45.6 2.2 collective-permute-start
  47.8 2.4 collective-permute-start.1
  50.2 1.0 collective-permute-start.2
  51.2 6.7 %collective-permute-done.c1 = bf16[288,256]{1,0:T(8,128)(2,1)S(1)} collective-permute-done((bf16[288,256]{1,0:T(8,128)(2,1)}, bf16[288,256]{1,0:T(8,128)(2,1)S(1)}, u32[]{:S(2)}, u32[]{:S(2)}) %collective-permute-start) | collective-permute-done | bytes 147488 | tf_op jit(solution)/shard_map/ppermute | solution.py:37
  58.6 3.4 %collective-permute-done.1.c2 = bf16[288,256]{1,0:T(8,128)(2,1)S(1)} collective-permute-done((bf16[288,256]{1,0:T(8,128)(2,1)}, bf16[288,256]{1,0:T(8,128)(2,1)S(1)}, u32[]{:S(2)}, u32[]{:S(2)}) %collective-permute-start.1) | collective-permute-done | bytes 147488 | tf_op jit(solution)/shard_map/ppermute | solution.py:37
  63.3 0.8 pad_maximum_fusion.2
  64.1 4.8 %all-to-all-done.1.refs_1_ = bf16[4,4,272,256]{3,2,1,0:T(8,128)(2,1)S(1)} async-done(((bf16[4,4,272,256]{3,2,1,0:T(8,128)(2,1)}), bf16[4,4,272,256]{3,2,1,0:T(8,128)(2,1)S(1)}, u32[]{:S(2)}, u32[]{:S(2)}) %all-to-all-start.1) | async-done | bytes 2228256 | tf_op jit(solution)/shard_map/all_to_all | solution.py:276
  69.1 12.0 %collective-permute-done.9 = bf16[3,272,256]{2,1,0:T(8,128)(2,1)S(1)} collective-permute-done((bf16[3,272,256]{2,1,0:T(8,128)(2,1)S(1)}, bf16[3,272,256]{2,1,0:T(8,128)(2,1)S(1)}, u32[]{:S(2)}, u32[]{:S(2)}) %collective-permute-start.9) | collective-permute-done | bytes 417824 | tf_op jit(solution)/shard_map/ppermute | solution.py:37
  81.2 1.3 broadcast_in_dim.19
  82.5 7.3 %all-to-all-start.2 = ((bf16[4,3,272,256]{3,2,1,0:T(8,128)(2,1)}), bf16[4,3,272,256]{3,2,1,0:T(8,128)(2,1)}, u32[]{:S(2)}, u32[]{:S(2)}) async-start(bf16[4,3,272,256]{3,2,1,0:T(8,128)(2,1)} %broadcast_in_dim.19), calls=%async_computation.2 | async-start | bytes 3342336 | tf_op jit(solution)/shard_map/all_to_all | solution.py:276
  89.8 2.0 collective-permute-done.7.refs_2_.refs_3_
  91.8 1.0 all-gather.5.cloned.1.call-done
  92.8 4.7 %shard_map.95 = (f32[4,192,256]{2,1,0:T(8,128)S(1)}, f32[4,8,256]{2,1,0:T(8,128)S(1)}, f32[16,8,256]{2,1,0:T(8,128)S(1)}) custom-call(s32[5]{0:T(128)S(1)} %stack.59.ids, bf16[4,4,192,256]{3,2,1,0:T(8,128)(2,1)} %bitcast.33, bf16[4,1,272,256]{3,2,1,0:T(8,128)(2,1)S(1)} %all-to-all-done.refs_0_, bf16[4,4,272,256]{3,2,1,0:T(8,128)(2,1)S(1)} %all-to-all-done.1.refs_1_, ...), custom_call_target="tpu_custom_call" | custom-call | flops 1006632960 | bytes 5570560 | tf_op jit(solution)/shard_map/pallas_call | solution.py:299
  97.5 0.9 copy-done.3
  98.4 10.6 %all-to-all-done.2.refs_0_.refs_2_ = bf16[4,3,272,256]{3,2,1,0:T(8,128)(2,1)} async-done(((bf16[4,3,272,256]{3,2,1,0:T(8,128)(2,1)}), bf16[4,3,272,256]{3,2,1,0:T(8,128)(2,1)}, u32[]{:S(2)}, u32[]{:S(2)}) %all-to-all-start.2) | async-done | bytes 1671200 | tf_op jit(solution)/shard_map/all_to_all | solution.py:276
  109.0 3.6 %shard_map.96 = (f32[4,192,256]{2,1,0:T(8,128)S(1)}, f32[4,8,256]{2,1,0:T(8,128)S(1)}) custom-call(s32[5]{0:T(128)S(1)} %stack.59.ids, bf16[4,4,192,256]{3,2,1,0:T(8,128)(2,1)} %bitcast.34, bf16[4,3,272,256]{3,2,1,0:T(8,128)(2,1)} %all-to-all-done.2.refs_0_.refs_2_), custom_call_target="tpu_custom_call" | custom-call | flops 301989888 | bytes 1671168 | tf_op jit(solution)/shard_map/pallas_call | solution.py:299
  112.8 3.8 %shard_map.97 = (f32[4,192,256]{2,1,0:T(8,128)S(1)}, f32[4,8,256]{2,1,0:T(8,128)S(1)}) custom-call(s32[5]{0:T(128)S(1)} %stack.59.ids, bf16[4,4,192,256]{3,2,1,0:T(8,128)(2,1)} %bitcast.35, bf16[4,3,272,256]{3,2,1,0:T(8,128)(2,1)S(1)} %collective-permute-done.10.refs_0_.refs_5_), custom_call_target="tpu_custom_call" | custom-call | flops 301989888 | bytes 1671168 | tf_op jit(solution)/shard_map/pallas_call | solution.py:299
  116.7 6.1 %shard_map.98 = bf16[4,4,192,256]{3,2,1,0:T(8,128)(2,1)} custom-call(s32[5]{0:T(128)S(1)} %stack.59.ids, f32[4,192,256]{2,1,0:T(8,128)S(1)} %copy-done.4, f32[4,192,256]{2,1,0:T(8,128)S(1)} %get-tuple-element.33.p1, f32[4,192,256]{2,1,0:T(8,128)S(1)} %get-tuple-element.34.p2, f32[4,8,256]{2,1,0:T(8,128)S(1)} %get-tuple-element.35.s0, ...), custom_call_target="tpu_custom_call" | custom-call | flops 1610612736 | bytes 12000000 | tf_op jit(solution)/shard_map/pallas_call | solution.py:321
  122.7 0.9 copy-done.8
  123.7 4.5 %all-to-all-start.3 = ((bf16[4,4,192,256]{3,2,1,0:T(8,128)(2,1)}), bf16[4,4,192,256]{3,2,1,0:T(8,128)(2,1)}, u32[]{:S(2)}, u32[]{:S(2)}) async-start(bf16[4,4,192,256]{3,2,1,0:T(8,128)(2,1)} %shard_map.98), calls=%async_computation.3 | async-start | bytes 3145728 | tf_op jit(solution)/shard_map/all_to_all | solution.py:330
  128.2 0.8 convert_element_type.3
  128.9 20.7 %all-to-all-done.3.terms = bf16[4,4,192,256]{3,2,1,0:T(8,128)(2,1)} async-done(((bf16[4,4,192,256]{3,2,1,0:T(8,128)(2,1)}), bf16[4,4,192,256]{3,2,1,0:T(8,128)(2,1)}, u32[]{:S(2)}, u32[]{:S(2)}) %all-to-all-start.3) | async-done | bytes 1572896 | tf_op jit(solution)/shard_map/all_to_all | solution.py:330
  149.6 2.5 shard_map.99
  152.1 10.0 %all_to_all.50 = f32[16,8,128]{2,1,0:T(8,128)} all-to-all(f32[16,8,128]{2,1,0:T(8,128)S(1)} %broadcast_in_dim.20), channel_id=1, replica_groups=mesh['y'=4,'zh'=4,'x'=4,'zl'=2,'c'=2] {'x','zl','c'}, dimensions={0} | all-to-all | bytes 131072 | tf_op jit(solution)/shard_map/all_to_all | solution.py:256
  162.2 0.9 reduce_sum.36
  163.7 5.7 %all-to-all-start.5 = ((f32[16,8,128]{2,1,0:T(8,128)}), f32[16,8,128]{2,1,0:T(8,128)}, u32[]{:S(2)}, u32[]{:S(2)}) async-start(f32[16,8,128]{2,1,0:T(8,128)} %broadcast_in_dim.21), calls=%async_computation.5 | async-start | bytes 131072 | tf_op jit(solution)/shard_map/all_to_all | solution.py:256
  170.3 9.4 %all-to-all-done.5 = f32[16,8,128]{2,1,0:T(8,128)} async-done(((f32[16,8,128]{2,1,0:T(8,128)}), f32[16,8,128]{2,1,0:T(8,128)}, u32[]{:S(2)}, u32[]{:S(2)}) %all-to-all-start.5) | async-done | bytes 65568 | tf_op jit(solution)/shard_map/all_to_all | solution.py:256
  179.6 1.5 reduce_sum.37
  181.9 1.4 copy-done.1
  183.4 6.1 %shard_map.100.pa = f32[4,192,256]{2,1,0:T(8,128)S(1)} custom-call(s32[5]{0:T(128)S(1)} %stack.59.ids, bf16[4,4,192,256]{3,2,1,0:T(8,128)(2,1)} %bitcast.37, f32[16,2,256]{2,1,0:T(2,128)S(1)} %bitcast.29, f32[16,8,256]{2,1,0:T(8,128)S(1)} %get-tuple-element.38.gabs, bf16[4,1,272,256]{3,2,1,0:T(8,128)(2,1)S(1)} %all-to-all-done.refs_0_, ...), custom_call_target="tpu_custom_call" | custom-call | flops 1610612736 | bytes 12000000 | tf_op jit(solution)/shard_map/pallas_call | solution.py:341
  189.6 6.9 %shard_map.101 = (bf16[4,4,192,256]{3,2,1,0:T(8,128)(2,1)}, f32[16,256]{1,0:T(8,128)S(1)}) custom-call(f32[1]{0:T(128)} %bitcast.18.factor, s32[5]{0:T(128)S(1)} %stack.59.ids, f32[4,192,256]{2,1,0:T(8,128)S(1)} %copy-done.5, f32[4,192,256]{2,1,0:T(8,128)S(1)} %copy-done.7, f32[4,192,256]{2,1,0:T(8,128)S(1)} %copy-done.9, ...), custom_call_target="tpu_custom_call" | custom-call | flops 1610612736 | bytes 12000000 | tf_op jit(solution)/shard_map/pallas_call | solution.py:349
  197.9 8.6 %all_to_all.51 = f32[16,1,256]{2,1,0:T(1,128)S(1)} all-to-all(f32[16,1,256]{2,1,0:T(1,128)S(1)} %copy.12), channel_id=1, replica_groups=mesh['y'=4,'zh'=4,'x'=4,'zl'=2,'c'=2] {'x','zl','c'}, dimensions={0} | all-to-all | bytes 32768 | tf_op jit(solution)/shard_map/all_to_all | solution.py:359
  206.6 16.2 %all_to_all.52 = f32[16,1,256]{2,1,0:T(1,128)S(1)} all-to-all(f32[16,1,256]{2,1,0:T(1,128)S(1)} %broadcast_in_dim.23), channel_id=1, replica_groups=mesh['y'=4,'zh'=4,'x'=4,'zl'=2,'c'=2] {'y','zh'}, dimensions={0} | all-to-all | bytes 32768 | tf_op jit(solution)/shard_map/all_to_all | solution.py:256
  222.8 1.2 reduce-scatter.2.cloned.1.call-done
  224.0 7.0 %all-to-all-start.8 = ((bf16[4,192,256]{2,1,0:T(8,128)(2,1)}), bf16[4,192,256]{2,1,0:T(8,128)(2,1)S(1)}, u32[]{:S(2)}, u32[]{:S(2)}) async-start(bf16[4,192,256]{2,1,0:T(8,128)(2,1)} %bitcast.45), calls=%async_computation.9 | async-start | bytes 786432 | tf_op jit(solution)/shard_map/all_to_all | solution.py:361
  231.6 11.3 %all-to-all-done.8.sums = bf16[4,192,256]{2,1,0:T(8,128)(2,1)S(1)} async-done(((bf16[4,192,256]{2,1,0:T(8,128)(2,1)}), bf16[4,192,256]{2,1,0:T(8,128)(2,1)S(1)}, u32[]{:S(2)}, u32[]{:S(2)}) %all-to-all-start.8) | async-done | bytes 393248 | tf_op jit(solution)/shard_map/all_to_all | solution.py:361
  242.9 1.6 shard_map.102
  (87 shorter events, 6.0 us)
Async XLA Ops:
  7.3 0.7 copy-start.27
  10.3 7.5 %copy-start.28 = (bf16[272,256]{1,0:T(8,128)(2,1)S(1)}, bf16[272,256]{1,0:T(8,128)(2,1)}, u32[]{:S(2)}) copy-start(bf16[272,256]{1,0:T(8,128)(2,1)} %get-tuple-element.28) | copy-start | bytes 417796
  12.1 27.0 %all-to-all-start = ((bf16[4,1,272,256]{3,2,1,0:T(8,128)(2,1)}), bf16[4,1,272,256]{3,2,1,0:T(8,128)(2,1)S(1)}, u32[]{:S(2)}, u32[]{:S(2)}) async-start(bf16[4,1,272,256]{3,2,1,0:T(8,128)(2,1)} %broadcast_in_dim.17), calls=%async_computation | async-start | bytes 1114112 | tf_op jit(solution)/shard_map/all_to_all | solution.py:276
  17.8 11.5 %collective-permute-start.6 = (bf16[272,256]{1,0:T(8,128)(2,1)S(1)}, bf16[272,256]{1,0:T(8,128)(2,1)S(1)}, u32[]{:S(2)}, u32[]{:S(2)}) collective-permute-start(bf16[272,256]{1,0:T(8,128)(2,1)S(1)} %copy-done.28), channel_id=1, source_target_pairs={{2,0},{0,2},{18,16},{16,18},{34,32},{32,34},{50,48},{48,50},{3,1},... | collective-permute-start | bytes 417800 | tf_op jit(solution)/shard_map/ppermute | solution.py:37
  18.9 19.1 %collective-permute-start.5 = (bf16[272,256]{1,0:T(8,128)(2,1)S(1)}, bf16[272,256]{1,0:T(8,128)(2,1)S(1)}, u32[]{:S(2)}, u32[]{:S(2)}) collective-permute-start(bf16[272,256]{1,0:T(8,128)(2,1)S(1)} %copy-done.28), channel_id=1, source_target_pairs={{32,0},{34,2},{48,16},{50,18},{0,32},{2,34},{16,48},{18,50},{33,1}... | collective-permute-start | bytes 417800 | tf_op jit(solution)/shard_map/ppermute | solution.py:37
  25.1 13.9 %collective-permute-start.4 = (bf16[272,256]{1,0:T(8,128)(2,1)S(1)}, bf16[272,256]{1,0:T(8,128)(2,1)S(1)}, u32[]{:S(2)}, u32[]{:S(2)}) collective-permute-start(bf16[272,256]{1,0:T(8,128)(2,1)S(1)} %copy-done.28), channel_id=1, source_target_pairs={{48,0},{50,2},{0,16},{2,18},{16,32},{18,34},{32,48},{34,50},{49,1}... | collective-permute-start | bytes 417800 | tf_op jit(solution)/shard_map/ppermute | solution.py:37
  26.6 12.4 %collective-permute-start.3 = (bf16[272,256]{1,0:T(8,128)(2,1)S(1)}, bf16[272,256]{1,0:T(8,128)(2,1)S(1)}, u32[]{:S(2)}, u32[]{:S(2)}) collective-permute-start(bf16[272,256]{1,0:T(8,128)(2,1)S(1)} %copy-done.28), channel_id=1, source_target_pairs={{16,0},{18,2},{32,16},{34,18},{48,32},{50,34},{0,48},{2,50},{17,1}... | collective-permute-start | bytes 417800 | tf_op jit(solution)/shard_map/ppermute | solution.py:37
  40.7 9.6 %copy-start.29 = (bf16[288,256]{1,0:T(8,128)(2,1)S(1)}, bf16[288,256]{1,0:T(8,128)(2,1)}, u32[]{:S(2)}) copy-start(bf16[288,256]{1,0:T(8,128)(2,1)} %get-tuple-element.27) | copy-start | bytes 442372
  40.7 10.6 %copy-start.10 = (bf16[288,256]{1,0:T(8,128)(2,1)S(1)}, bf16[288,256]{1,0:T(8,128)(2,1)}, u32[]{:S(2)}) copy-start(bf16[288,256]{1,0:T(8,128)(2,1)} %get-tuple-element.24.c0) | copy-start | bytes 442372
  40.7 28.3 %all-to-all-start.1 = ((bf16[4,4,272,256]{3,2,1,0:T(8,128)(2,1)}), bf16[4,4,272,256]{3,2,1,0:T(8,128)(2,1)S(1)}, u32[]{:S(2)}, u32[]{:S(2)}) async-start(bf16[4,4,272,256]{3,2,1,0:T(8,128)(2,1)} %broadcast_in_dim.18), calls=%async_computation.1 | async-start | bytes 4456448 | tf_op jit(solution)/shard_map/all_to_all | solution.py:276
  45.6 47.2 %all-gather.5.cloned.1.call-start = ((), (), s32[]{:S(2)}) async-start(), calls=%async_computation.11 | async-start | bytes 1966080 | tf_op jit(solution)/shard_map/all_gather | solution.py:283
  45.6 12.4 %collective-permute-start = (bf16[288,256]{1,0:T(8,128)(2,1)}, bf16[288,256]{1,0:T(8,128)(2,1)S(1)}, u32[]{:S(2)}, u32[]{:S(2)}) collective-permute-start(bf16[288,256]{1,0:T(8,128)(2,1)} %get-tuple-element.25), channel_id=1, source_target_pairs={{16,0},{18,2},{32,16},{34,18},{48,32},{50,34},{0,48},{2,50},{17,1}... | collective-permute-start | bytes 442376 | tf_op jit(solution)/shard_map/ppermute | solution.py:37
  47.8 14.2 %collective-permute-start.1 = (bf16[288,256]{1,0:T(8,128)(2,1)}, bf16[288,256]{1,0:T(8,128)(2,1)S(1)}, u32[]{:S(2)}, u32[]{:S(2)}) collective-permute-start(bf16[288,256]{1,0:T(8,128)(2,1)} %get-tuple-element.26), channel_id=1, source_target_pairs={{32,0},{34,2},{48,16},{50,18},{0,32},{2,34},{16,48},{18,50},{33,1}... | collective-permute-start | bytes 442376 | tf_op jit(solution)/shard_map/ppermute | solution.py:37
  50.2 12.4 %collective-permute-start.2 = (bf16[288,256]{1,0:T(8,128)(2,1)S(1)}, bf16[288,256]{1,0:T(8,128)(2,1)S(1)}, u32[]{:S(2)}, u32[]{:S(2)}) collective-permute-start(bf16[288,256]{1,0:T(8,128)(2,1)S(1)} %copy-done.29), channel_id=1, source_target_pairs={{48,0},{50,2},{0,16},{2,18},{16,32},{18,34},{32,48},{34,50},{49,1}... | collective-permute-start | bytes 442376 | tf_op jit(solution)/shard_map/ppermute | solution.py:37
  62.0 0.7 copy-start.16
  62.7 0.7 copy-start.19
  69.0 23.8 %collective-permute-start.8 = (bf16[4,4,272,256]{3,2,1,0:T(8,128)(2,1)S(1)}, bf16[4,4,272,256]{3,2,1,0:T(8,128)(2,1)}, u32[]{:S(2)}, u32[]{:S(2)}) collective-permute-start(bf16[4,4,272,256]{3,2,1,0:T(8,128)(2,1)S(1)} %all-to-all-done.1.refs_1_), channel_id=1, source_target_pairs={{0,1},{1,0},{2,3},{3,2},{4,5},{5,4},{6,7},{7,6},{8,9},{9,8},{10,11... | collective-permute-start | bytes 6684680 | tf_op jit(solution)/shard_map/ppermute | solution.py:41
  69.0 12.1 %collective-permute-start.9 = (bf16[3,272,256]{2,1,0:T(8,128)(2,1)S(1)}, bf16[3,272,256]{2,1,0:T(8,128)(2,1)S(1)}, u32[]{:S(2)}, u32[]{:S(2)}) collective-permute-start(bf16[3,272,256]{2,1,0:T(8,128)(2,1)S(1)} %pad_maximum_fusion.1), channel_id=1, source_target_pairs={{2,0},{0,2},{18,16},{16,18},{34,32},{32,34},{50,48},{48,50},{3,1},... | collective-permute-start | bytes 1253384 | tf_op jit(solution)/shard_map/ppermute | solution.py:37
  82.5 26.5 %all-to-all-start.2 = ((bf16[4,3,272,256]{3,2,1,0:T(8,128)(2,1)}), bf16[4,3,272,256]{3,2,1,0:T(8,128)(2,1)}, u32[]{:S(2)}, u32[]{:S(2)}) async-start(bf16[4,3,272,256]{3,2,1,0:T(8,128)(2,1)} %broadcast_in_dim.19), calls=%async_computation.2 | async-start | bytes 3342336 | tf_op jit(solution)/shard_map/all_to_all | solution.py:276
  89.8 2.0 collective-permute-start.7
  97.5 0.9 copy-start.3
  109.0 3.8 %collective-permute-start.10 = (bf16[4,3,272,256]{3,2,1,0:T(8,128)(2,1)}, bf16[4,3,272,256]{3,2,1,0:T(8,128)(2,1)S(1)}, u32[]{:S(2)}, u32[]{:S(2)}) collective-permute-start(bf16[4,3,272,256]{3,2,1,0:T(8,128)(2,1)} %all-to-all-done.2.refs_0_.refs_2_), channel_id=1, source_target_pairs={{0,1},{1,0},{2,3},{3,2},{4,5},{5,4},{6,7},{7,6},{8,9},{9,8},{10,11... | collective-permute-start | bytes 5013512 | tf_op jit(solution)/shard_map/ppermute | solution.py:41
  112.6 4.0 %copy-start.6 = (f32[4,192,256]{2,1,0:T(8,128)}, f32[4,192,256]{2,1,0:T(8,128)S(1)}, u32[]{:S(2)}) copy-start(f32[4,192,256]{2,1,0:T(8,128)S(1)} %get-tuple-element.33.p1) | copy-start | bytes 2359300
  112.6 4.0 %copy-start.22 = (f32[4,8,256]{2,1,0:T(8,128)}, f32[4,8,256]{2,1,0:T(8,128)S(1)}, u32[]{:S(2)}) copy-start(f32[4,8,256]{2,1,0:T(8,128)S(1)} %get-tuple-element.36.s1) | copy-start | bytes 98308
  112.6 4.0 %copy-start.4 = (f32[4,192,256]{2,1,0:T(8,128)S(1)}, f32[4,192,256]{2,1,0:T(8,128)}, u32[]{:S(2)}) copy-start(f32[4,192,256]{2,1,0:T(8,128)} %copy-done.3) | copy-start | bytes 2359300
  112.6 4.0 %copy-start.11 = (bf16[288,256]{1,0:T(8,128)(2,1)S(1)}, bf16[288,256]{1,0:T(8,128)(2,1)}, u32[]{:S(2)}) copy-start(bf16[288,256]{1,0:T(8,128)(2,1)} %get-tuple-element.24.c0) | copy-start | bytes 442372
  112.7 4.0 %copy-start.14 = (bf16[288,256]{1,0:T(8,128)(2,1)S(1)}, bf16[288,256]{1,0:T(8,128)(2,1)}, u32[]{:S(2)}) copy-start(bf16[288,256]{1,0:T(8,128)(2,1)} %copy-done.13) | copy-start | bytes 442372
  112.7 4.0 %copy-start.17 = (bf16[288,256]{1,0:T(8,128)(2,1)S(1)}, bf16[288,256]{1,0:T(8,128)(2,1)}, u32[]{:S(2)}) copy-start(bf16[288,256]{1,0:T(8,128)(2,1)} %copy-done.16) | copy-start | bytes 442372
  112.7 4.0 %copy-start.20 = (bf16[288,256]{1,0:T(8,128)(2,1)S(1)}, bf16[288,256]{1,0:T(8,128)(2,1)}, u32[]{:S(2)}) copy-start(bf16[288,256]{1,0:T(8,128)(2,1)} %copy-done.19) | copy-start | bytes 442372
  112.7 3.9 %copy-start = (bf16[4,3,272,256]{3,2,1,0:T(8,128)(2,1)}, bf16[4,3,272,256]{3,2,1,0:T(8,128)(2,1)S(1)}, u32[]{:S(2)}) copy-start(bf16[4,3,272,256]{3,2,1,0:T(8,128)(2,1)S(1)} %collective-permute-done.10.refs_0_.refs_5_) | copy-start | bytes 5013508
  116.6 6.2 %copy-start.24 = (f32[4,8,256]{2,1,0:T(8,128)}, f32[4,8,256]{2,1,0:T(8,128)S(1)}, u32[]{:S(2)}) copy-start(f32[4,8,256]{2,1,0:T(8,128)S(1)} %get-tuple-element.37.s2) | copy-start | bytes 98308
  122.7 0.9 copy-start.8
  123.7 25.9 %all-to-all-start.3 = ((bf16[4,4,192,256]{3,2,1,0:T(8,128)(2,1)}), bf16[4,4,192,256]{3,2,1,0:T(8,128)(2,1)}, u32[]{:S(2)}, u32[]{:S(2)}) async-start(bf16[4,4,192,256]{3,2,1,0:T(8,128)(2,1)} %shard_map.98), calls=%async_computation.3 | async-start | bytes 3145728 | tf_op jit(solution)/shard_map/all_to_all | solution.py:330
  128.2 53.7 %all-gather.7.cloned.1.call-start = ((), (), s32[]{:S(2)}) async-start(), calls=%async_computation.12 | async-start | bytes 1966080 | tf_op jit(solution)/shard_map/all_gather | solution.py:337
  163.7 15.9 %all-to-all-start.5 = ((f32[16,8,128]{2,1,0:T(8,128)}), f32[16,8,128]{2,1,0:T(8,128)}, u32[]{:S(2)}, u32[]{:S(2)}) async-start(f32[16,8,128]{2,1,0:T(8,128)} %broadcast_in_dim.21), calls=%async_computation.5 | async-start | bytes 131072 | tf_op jit(solution)/shard_map/all_to_all | solution.py:256
  169.4 54.6 %reduce-scatter.2.cloned.1.call-start = ((), (), s32[]{:S(2)}) async-start(), calls=%async_computation.10 | async-start | bytes 1966080 | tf_op jit(solution)/shard_map/reduce_scatter | solution.py:358
  181.9 1.4 copy-start.1
  183.3 6.2 %copy-start.2 = (bf16[4,3,272,256]{3,2,1,0:T(8,128)(2,1)S(1)}, bf16[4,3,272,256]{3,2,1,0:T(8,128)(2,1)}, u32[]{:S(2)}) copy-start(bf16[4,3,272,256]{3,2,1,0:T(8,128)(2,1)} %copy-done) | copy-start | bytes 5013508
  183.3 6.2 %copy-start.5 = (f32[4,192,256]{2,1,0:T(8,128)S(1)}, f32[4,192,256]{2,1,0:T(8,128)}, u32[]{:S(2)}) copy-start(f32[4,192,256]{2,1,0:T(8,128)} %copy-done.3) | copy-start | bytes 2359300
  183.3 6.2 %copy-start.7 = (f32[4,192,256]{2,1,0:T(8,128)S(1)}, f32[4,192,256]{2,1,0:T(8,128)}, u32[]{:S(2)}) copy-start(f32[4,192,256]{2,1,0:T(8,128)} %copy-done.6) | copy-start | bytes 2359300
  183.3 6.3 %copy-start.9 = (f32[4,192,256]{2,1,0:T(8,128)S(1)}, f32[4,192,256]{2,1,0:T(8,128)}, u32[]{:S(2)}) copy-start(f32[4,192,256]{2,1,0:T(8,128)} %copy-done.8) | copy-start | bytes 2359300
  183.3 6.3 %copy-start.12 = (bf16[288,256]{1,0:T(8,128)(2,1)S(1)}, bf16[288,256]{1,0:T(8,128)(2,1)}, u32[]{:S(2)}) copy-start(bf16[288,256]{1,0:T(8,128)(2,1)} %get-tuple-element.24.c0) | copy-start | bytes 442372
  183.3 6.3 %copy-start.15 = (bf16[288,256]{1,0:T(8,128)(2,1)S(1)}, bf16[288,256]{1,0:T(8,128)(2,1)}, u32[]{:S(2)}) copy-start(bf16[288,256]{1,0:T(8,128)(2,1)} %copy-done.13) | copy-start | bytes 442372
  183.3 6.3 %copy-start.18 = (bf16[288,256]{1,0:T(8,128)(2,1)S(1)}, bf16[288,256]{1,0:T(8,128)(2,1)}, u32[]{:S(2)}) copy-start(bf16[288,256]{1,0:T(8,128)(2,1)} %copy-done.16) | copy-start | bytes 442372
  183.3 6.3 %copy-start.21 = (bf16[288,256]{1,0:T(8,128)(2,1)S(1)}, bf16[288,256]{1,0:T(8,128)(2,1)}, u32[]{:S(2)}) copy-start(bf16[288,256]{1,0:T(8,128)(2,1)} %copy-done.19) | copy-start | bytes 442372
  183.3 6.3 %copy-start.23 = (f32[4,8,256]{2,1,0:T(8,128)S(1)}, f32[4,8,256]{2,1,0:T(8,128)}, u32[]{:S(2)}) copy-start(f32[4,8,256]{2,1,0:T(8,128)} %copy-done.22) | copy-start | bytes 98308
  183.4 6.3 %copy-start.25 = (f32[4,8,256]{2,1,0:T(8,128)S(1)}, f32[4,8,256]{2,1,0:T(8,128)}, u32[]{:S(2)}) copy-start(f32[4,8,256]{2,1,0:T(8,128)} %copy-done.24) | copy-start | bytes 98308
  224.0 18.9 %all-to-all-start.8 = ((bf16[4,192,256]{2,1,0:T(8,128)(2,1)}), bf16[4,192,256]{2,1,0:T(8,128)(2,1)S(1)}, u32[]{:S(2)}, u32[]{:S(2)}) async-start(bf16[4,192,256]{2,1,0:T(8,128)(2,1)} %bitcast.45), calls=%async_computation.9 | async-start | bytes 786432 | tf_op jit(solution)/shard_map/all_to_all | solution.py:361
  (2 other events, 1.3 us)
Sparse Core Ops, SparseCore 0:
  64.3 28.4 all-gather.4
  152.3 27.7 all-gather.6
  197.3 26.6 reduce-scatter.1

commit v5 on v4

--- a/solution.py
+++ b/solution.py
@@ -66,10 +66,6 @@
     return pltpu.with_memory_space_constraint(value, pltpu.HBM)
 
 
-def in_vmem(value):
-    return pltpu.with_memory_space_constraint(value, pltpu.VMEM)
-
-
 SMEM = pl.BlockSpec(memory_space=pltpu.SMEM)
 
 
@@ -121,7 +117,7 @@
     scaled, sums, squares = {}, {}, {}
     for (grp, g), ref in zip(parts, toks):
         for i, (k, l) in enumerate(GROUPS[grp]):
-            tail = ref[x, i, BLK:PACK, :]
+            tail = ref[0, i, BLK:PACK, :]
             if (l, g) not in scaled:
                 gain = row(tail, 0)
                 at = (zl ^ l) * 2 + (c ^ g)
@@ -129,7 +125,7 @@
                 scaled[l, g] = (wv.astype(F32) * gain).astype(BF)
                 if gabs is not None:
                     gabs[x * 4 + at] = jnp.broadcast_to(gain, (8, BLK))
-            sums.setdefault(k, []).append((scaled[l, g], ref[x, i, 0:BLK, :]))
+            sums.setdefault(k, []).append((scaled[l, g], ref[0, i, 0:BLK, :]))
             s = row(tail, 3)
             squares[k] = squares[k] + s if k in squares else s
     for k, pairs in sums.items():
@@ -158,7 +154,7 @@
                 at = (zl ^ l) * 2 + (c ^ g)
                 fb = x * 4 + at
                 scaled[l, g] = (asc[0, at].astype(F32) * mask_rows(mask[fb]) * gabs[fb][0:1]).astype(BF)
-            sums.setdefault(k, []).append((scaled[l, g], ref[x, i, 0:BLK, :]))
+            sums.setdefault(k, []).append((scaled[l, g], ref[0, i, 0:BLK, :]))
     for k, pairs in sums.items():
         out[k] += joined(pairs, 1, NT)
 
@@ -180,45 +176,41 @@
     return jnp.concatenate([u * up * slope * r, u * act * r], axis=0).astype(BF)
 
 
-def fill_grads(ids, d, pres, sqs, pieces):
-    for k in range(4):
-        pre, sq = pres(k), sqs[0][k][0:1]
-        for s in sqs[1:]:
-            sq = sq + s[k][0:1]
-        r = lax.rsqrt(sq / (NB * BLK) + 1e-06)
-        d[k] = hidden_grads(pre, r, pieces[k][ROWS : ROWS + SUB, :])
-
-
 def outer_terms(parts, d, toks):
     where = {p: ref for p, ref in zip(parts, toks)}
-    x = pl.program_id(0)
     for l in range(2):
         for g in range(2):
             places = [PLACE[k, l] for k in range(4)]
-            pairs = [(d[k], where[grp, g][x, i, 0:BLK, :]) for k, (grp, i) in enumerate(places)]
+            pairs = [(d[k], where[grp, g][0, i, 0:BLK, :]) for k, (grp, i) in enumerate(places)]
             yield l, g, joined(pairs, 0, NN)
 
 
 def outer1_kernel(parts, ids, p0, p1, p2, s0, s1, s2, c0, c1, c2, c3, *refs):
-    toks, out, d = refs[: len(parts)], refs[len(parts)], refs[len(parts) + 1]
+    toks, (out, praw, rs, d) = refs[: len(parts)], refs[len(parts) :]
     zl, c = ids[3], ids[4]
 
     @pl.when(pl.program_id(0) == 0)
     def _():
-        fill_grads(ids, d, lambda k: p0[k] + p1[k] + p2[k], (s0, s1, s2), (c0, c1, c2, c3))
+        for k, cot in enumerate((c0, c1, c2, c3)):
+            r = lax.rsqrt((s0[k] + s1[k] + s2[k]) / (NB * BLK) + 1e-06)
+            pre = p0[k] + p1[k] + p2[k]
+            rs[k] = r
+            praw[k] = pre
+            d[k] = hidden_grads(pre, r[0:1], cot[ROWS : ROWS + SUB, :])
 
     for l, g, total in outer_terms(parts, d, toks):
         out[0, (zl ^ l) * 2 + (c ^ g)] = total.astype(BF)
 
 
-def outer2_kernel(parts, factor, ids, p0, p1, p2, s0, s1, s2, c0, c1, c2, c3, pa, w, asc, mask, *refs):
-    toks, out, dgp, d = refs[: len(parts)], refs[len(parts)], refs[len(parts) + 1], refs[len(parts) + 2]
+def outer2_kernel(parts, factor, ids, praw, rs, pa, c0, c1, c2, c3, w, asc, mask, *refs):
+    toks, (out, dgp, d) = refs[: len(parts)], refs[len(parts) :]
     x, zh, zl, c = pl.program_id(0), ids[1], ids[3], ids[4]
     f = factor[0]
 
     @pl.when(x == 0)
     def _():
-        fill_grads(ids, d, lambda k: p0[k] + p1[k] + p2[k] + f * pa[k], (s0, s1, s2), (c0, c1, c2, c3))
+        for k, cot in enumerate((c0, c1, c2, c3)):
+            d[k] = hidden_grads(praw[k] + f * pa[k], rs[k][0:1], cot[ROWS : ROWS + SUB, :])
 
     for l, g, total in outer_terms(parts, d, toks):
         at = (zl ^ l) * 2 + (c ^ g)
@@ -226,7 +218,7 @@
         fb = x * 4 + at
         wv = w[0, lax.rem(at - zh + 4, 4)].astype(F32)
         wv = wv + f * mask_rows(mask[fb]) * asc[0, at].astype(F32)
-        dgp[pl.ds(fb, 1), :] = jnp.sum(wv * total, axis=0, keepdims=True)
+        dgp[fb] = jnp.sum(wv * total, axis=0, keepdims=True)
 
 
 def ascent_kernel(ids, terms, gabs, mask, asc, part):
@@ -280,21 +272,21 @@
     own_x = over_x(pack[None])
     pieces = [pieces[0]] + [from_z(pieces[k], k, 0) for k in range(1, 4)]
     part_w = jnp.stack([p[:ROWS] for p in pieces])
-    weights = in_hbm(lax.all_gather(part_w, "y", axis=0, tiled=False))
     mid_x = over_x(after(jnp.stack(mids + [near]), own_x))
     far = from_z(jnp.stack(mids), 0, 1)
+    weights = in_hbm(lax.all_gather(after(part_w, far), "y", axis=0, tiled=False))
     far_x = over_x(after(far, part_w, mid_x))
-    mine = [in_vmem(v) for v in (own_x, mid_x)]
-    toks = {(grp, g): in_vmem(other_core(v)) if g else v for grp, v in enumerate(mine) for g in range(2)}
+    mine = [in_hbm(v) for v in (own_x, mid_x)]
+    toks = {(grp, g): in_hbm(other_core(v)) if g else v for grp, v in enumerate(mine) for g in range(2)}
 
     pshape, sshape, gshape = shape((4, ROWS, BLK), F32), shape((4, 8, BLK), F32), shape((NB, 8, BLK), F32)
     wspec = by_x((4, ROWS, BLK))
 
     def tok_spec(grp):
-        return pl.BlockSpec(memory_space=pltpu.VMEM)
+        return by_x((len(GROUPS[grp]), PACK, BLK))
 
     def pre(parts, with_gain):
-        outs = [pshape, sshape] + ([gshape] if with_gain else [])
+        outs = [hbm(pshape.shape, F32) if with_gain else pshape, sshape] + ([gshape] if with_gain else [])
         blocks = sum(len(GROUPS[p[0]]) for p in parts)
         return call(
             functools.partial(pre_kernel, parts, with_gain),
@@ -307,8 +299,8 @@
         )(ids, weights, *[toks[p] for p in parts])
 
     p0, s0, gabs = pre(tuple((grp, g) for g in range(2) for grp in (0, 1)), True)
-    far_x = after(in_vmem(far_x), p0)
-    toks[2, 0], toks[2, 1] = far_x, in_vmem(other_core(far_x))
+    far_x = after(far_x, p0)
+    toks[2, 0], toks[2, 1] = far_x, other_core(far_x)
     p1, s1 = pre(((2, 0),), False)
     p2, s2 = pre(((2, 1),), False)
     parts = tuple((grp, g) for g in range(2) for grp in range(len(GROUPS)))
@@ -316,13 +308,14 @@
     tok_refs = [toks[p] for p in parts]
     cost = {"flops": 64 * 2 * ROWS * BLK * BLK, "nbytes": 12 * 10**6}
     oshape = hbm((4, 4, ROWS, BLK), BF)
+    pspec, sspec = whole(pshape.shape), whole(sshape.shape)
+    pieces = [in_hbm(p) for p in pieces]
     dscratch = [pltpu.VMEM((4, ROWS, BLK), BF)]
-    first_specs = [whole(pshape.shape)] * 3 + [whole(sshape.shape)] * 3 + [whole(piece.shape)] * 4
-    out1 = call(
+    out1, praw, rs = call(
         functools.partial(outer1_kernel, parts),
-        oshape,
-        [SMEM] + first_specs + tok_specs,
-        by_x((4, ROWS, BLK)),
+        (oshape, hbm(pshape.shape, F32), hbm(sshape.shape, F32)),
+        [SMEM] + [pspec] * 3 + [sspec] * 3 + [whole(piece.shape)] * 4 + tok_specs,
+        (by_x((4, ROWS, BLK)), pspec, sspec),
         (4,),
         dscratch,
         **cost,
@@ -335,26 +328,26 @@
         (whole((4, ROWS, BLK)), whole((8, 128))),
     )(ids, terms, gabs, mask)
     ascs = in_hbm(lax.all_gather(asc, "y", axis=0, tiled=False))
-    part = jnp.sum(spread(part, MP), axis=0)
-    total = jnp.sum(spread(part, DP))
-    factor = (radius[0] / (jnp.sqrt(total) + 1e-12))[None]
+    part = spread(jnp.sum(spread(part, MP), axis=0), DP)
     pa = call(
         functools.partial(pre2_kernel, parts),
-        pshape,
+        hbm(pshape.shape, F32),
         [SMEM, wspec, whole((NB, 2, BLK)), whole(gshape.shape)] + tok_specs,
         whole(pshape.shape),
         (4,),
         **cost,
     )(ids, ascs, mask, gabs, *tok_refs)
+    total = jnp.sum(after(part, pa))
+    factor = (radius[0] / (jnp.sqrt(total) + 1e-12))[None]
     out2, dgp = call(
         functools.partial(outer2_kernel, parts),
-        (oshape, shape((NB, BLK), F32)),
-        [SMEM, SMEM] + first_specs + [whole(pshape.shape), wspec, wspec, whole((NB, 2, BLK))] + tok_specs,
-        (by_x((4, ROWS, BLK)), whole((NB, BLK))),
+        (oshape, hbm((NB, 1, BLK), F32)),
+        [SMEM, SMEM, pspec, sspec, pspec] + [whole(piece.shape)] * 4 + [wspec, wspec, whole((NB, 2, BLK))] + tok_specs,
+        (by_x((4, ROWS, BLK)), whole((NB, 1, BLK))),
         (4,),
         dscratch,
         **cost,
-    )(factor, ids, p0, p1, p2, s0, s1, s2, *pieces, pa, weights, ascs, mask, *tok_refs)
+    )(factor, ids, in_hbm(praw), in_hbm(rs), in_hbm(pa), *pieces, weights, ascs, mask, *tok_refs)
     sums = lax.psum_scatter(out2, "y", scatter_dimension=0, tiled=False)
     dg = jnp.sum(lax.all_to_all(dgp, MP, 0, 0, tiled=True), axis=0)
     grad_gain = jnp.sum(spread(dg, DP).reshape(16, BLK), axis=0)

time: 252 us -> 251 us (level)
  blocking collectives: 34.9 us -> 26.8 us
  waiting for transfers between devices: 92.9 us -> 100 us
  local copies, waits for them, and re-layouts: 12.8 us -> 6.92 us
  starting transfers between devices: 52.5 us -> 57.8 us
    all_gather x1, waiting for transfers between devices: 1.01 us -> 19.9 us  [body(): lax.all_gather(after(part_w, far), 'y', axis=0, tiled=False)]
    all_to_all x3, waiting for transfers between devices: 15.4 us -> 0.01 us  [over_x(): lax.all_to_all(jnp.broadcast_to(value[None], (4,) + value.shape), 'x', 0,...]
    all_gather x1, waiting for transfers between devices: 0.02 us -> 10.4 us  [body(): ascs = in_hbm(lax.all_gather(asc, 'y', axis=0, tiled=False))]
    all_to_all x2 -> x1, blocking collectives: 26.3 us -> 17.2 us  [spread(): lax.all_to_all(jnp.broadcast_to(value[None], (n,) + value.shape), axes, 0...]
    all_to_all x1 -> x2, starting transfers between devices: 5.68 us -> 12.7 us  [spread(): lax.all_to_all(jnp.broadcast_to(value[None], (n,) + value.shape), axes, 0...]
    all_to_all x1 -> x2, waiting for transfers between devices: 9.35 us -> 3.36 us  [spread(): lax.all_to_all(jnp.broadcast_to(value[None], (n,) + value.shape), axes, 0...]
    unnamed x60 -> x26, local copies, waits for them, and re-layouts: 6.57 us -> 0.72 us
  transfers between devices with their start and end apart: 20 -> 21, of which waited for: 14 -> 14; matrix products, arithmetic and copies ran while one was open for 3% -> 2% of each run, Pallas kernels for 3% -> 6%
where the time goes in v5:
time: 251 us; the launch traced here: 250 us
  waiting for transfers between devices  100 us (40%)
  starting transfers between devices  57.8 us (23%)
  Pallas kernels  39 us (16%)
  blocking collectives  26.8 us (11%)
  between operations  15.3 us (6%)
  local copies, waits for them, and re-layouts  6.92 us (3%)
  other arithmetic  3.9 us (2%)
    ppermute x8, waiting for transfers between devices, from_z(): return lax.ppermute(value, ('zh', 'zl'), pairs)  29.4 us
    all_to_all x1, waiting for transfers between devices, body(): terms = lax.all_to_all(out1, 'y', 0, 0, tiled=True)  21.3 us
    all_gather x1, waiting for transfers between devices, body(): lax.all_gather(after(part_w, far), 'y', axis=0, tiled=False)  19.9 us
    ppermute x8, starting transfers between devices, from_z(): return lax.ppermute(value, ('zh', 'zl'), pairs)  18 us
    all_to_all x1, blocking collectives, spread(): lax.all_to_all(jnp.broadcast_to(value[None], (n,) + value.shape), axes, 0...  17.2 us
    all_to_all x3, starting transfers between devices, over_x(): lax.all_to_all(jnp.broadcast_to(value[None], (4,) + value.shape), 'x', 0,...  15.4 us
    all_to_all x2, starting transfers between devices, spread(): lax.all_to_all(jnp.broadcast_to(value[None], (n,) + value.shape), axes, 0...  12.7 us
    pallas_call x3, Pallas kernels, pre(): call(functools.partial(pre_kernel, parts, with_gain), outs, [SMEM, wspec]...  11.9 us
  transfers between devices with their start and end apart: 21, of which 14 were waited for; matrix products, arithmetic and copies ran while one was open for 2% of the time, Pallas kernels for 6%

profile of v5, /device:TPU:4, one launch (start us, length us, event | category | flops | bytes accessed | tf_op | source)
XLA Modules:
  0.0 250.0 jit_solution(17068144853905950107)
XLA Ops:
  7.3 0.7 copy-done.1
  7.9 2.4 shard_map.94
  10.3 1.8 broadcast_in_dim.17
  12.1 5.7 %all-to-all-start = ((bf16[4,1,272,256]{3,2,1,0:T(8,128)(2,1)}), bf16[4,1,272,256]{3,2,1,0:T(8,128)(2,1)S(1)}, u32[]{:S(2)}, u32[]{:S(2)}) async-start(bf16[4,1,272,256]{3,2,1,0:T(8,128)(2,1)} %broadcast_in_dim.17), calls=%async_computation | async-start | bytes 1114112 | tf_op jit(solution)/shard_map/all_to_all | solution.py:268
  17.8 5.4 %collective-permute-start.3 = (bf16[272,256]{1,0:T(8,128)(2,1)S(1)}, bf16[272,256]{1,0:T(8,128)(2,1)S(1)}, u32[]{:S(2)}, u32[]{:S(2)}) collective-permute-start(bf16[272,256]{1,0:T(8,128)(2,1)S(1)} %copy-done.8), channel_id=1, source_target_pairs={{16,0},{18,2},{32,16},{34,18},{48,32},{50,34},{0,48},{2,50},{17,1}... | collective-permute-start | bytes 417800 | tf_op jit(solution)/shard_map/ppermute | solution.py:37
  23.2 3.8 %collective-permute-start.5 = (bf16[272,256]{1,0:T(8,128)(2,1)S(1)}, bf16[272,256]{1,0:T(8,128)(2,1)S(1)}, u32[]{:S(2)}, u32[]{:S(2)}) collective-permute-start(bf16[272,256]{1,0:T(8,128)(2,1)S(1)} %copy-done.8), channel_id=1, source_target_pairs={{32,0},{34,2},{48,16},{50,18},{0,32},{2,34},{16,48},{18,50},{33,1}... | collective-permute-start | bytes 417800 | tf_op jit(solution)/shard_map/ppermute | solution.py:37
  27.0 1.0 collective-permute-start.7
  28.1 5.2 %collective-permute-done.3 = bf16[272,256]{1,0:T(8,128)(2,1)S(1)} collective-permute-done((bf16[272,256]{1,0:T(8,128)(2,1)S(1)}, bf16[272,256]{1,0:T(8,128)(2,1)S(1)}, u32[]{:S(2)}, u32[]{:S(2)}) %collective-permute-start.3) | collective-permute-done | bytes 139296 | tf_op jit(solution)/shard_map/ppermute | solution.py:37
  33.2 2.7 %collective-permute-done.4 = bf16[272,256]{1,0:T(8,128)(2,1)S(1)} collective-permute-done((bf16[272,256]{1,0:T(8,128)(2,1)S(1)}, bf16[272,256]{1,0:T(8,128)(2,1)S(1)}, u32[]{:S(2)}, u32[]{:S(2)}) %collective-permute-start.4) | collective-permute-done | bytes 139296 | tf_op jit(solution)/shard_map/ppermute | solution.py:37
  36.0 4.0 %collective-permute-done.5 = bf16[272,256]{1,0:T(8,128)(2,1)S(1)} collective-permute-done((bf16[272,256]{1,0:T(8,128)(2,1)S(1)}, bf16[272,256]{1,0:T(8,128)(2,1)S(1)}, u32[]{:S(2)}, u32[]{:S(2)}) %collective-permute-start.5) | collective-permute-done | bytes 139296 | tf_op jit(solution)/shard_map/ppermute | solution.py:37
  40.1 1.6 broadcast_in_dim.18
  41.8 4.9 %all-to-all-start.1 = ((bf16[4,4,272,256]{3,2,1,0:T(8,128)(2,1)}), bf16[4,4,272,256]{3,2,1,0:T(8,128)(2,1)}, u32[]{:S(2)}, u32[]{:S(2)}) async-start(bf16[4,4,272,256]{3,2,1,0:T(8,128)(2,1)} %broadcast_in_dim.18), calls=%async_computation.1 | async-start | bytes 4456448 | tf_op jit(solution)/shard_map/all_to_all | solution.py:268
  46.7 1.9 collective-permute-start.2
  48.6 1.3 collective-permute-start.1
  49.9 2.4 collective-permute-start
  52.3 2.2 collective-permute-start.6
  54.5 6.4 %collective-permute-done.2.c3 = bf16[288,256]{1,0:T(8,128)(2,1)S(1)} collective-permute-done((bf16[288,256]{1,0:T(8,128)(2,1)S(1)}, bf16[288,256]{1,0:T(8,128)(2,1)S(1)}, u32[]{:S(2)}, u32[]{:S(2)}) %collective-permute-start.2) | collective-permute-done | bytes 147488 | tf_op jit(solution)/shard_map/ppermute | solution.py:37
  60.9 1.7 collective-permute-done.1.c2
  62.6 0.8 pad_maximum_fusion.2
  63.5 9.4 %collective-permute-done.6 = bf16[3,272,256]{2,1,0:T(8,128)(2,1)S(1)} collective-permute-done((bf16[3,272,256]{2,1,0:T(8,128)(2,1)S(1)}, bf16[3,272,256]{2,1,0:T(8,128)(2,1)S(1)}, u32[]{:S(2)}, u32[]{:S(2)}) %collective-permute-start.6) | collective-permute-done | bytes 417824 | tf_op jit(solution)/shard_map/ppermute | solution.py:37
  73.0 1.4 broadcast_in_dim.19
  74.3 4.8 %all-to-all-start.2 = ((bf16[4,3,272,256]{3,2,1,0:T(8,128)(2,1)}), bf16[4,3,272,256]{3,2,1,0:T(8,128)(2,1)S(1)}, u32[]{:S(2)}, u32[]{:S(2)}) async-start(bf16[4,3,272,256]{3,2,1,0:T(8,128)(2,1)} %broadcast_in_dim.19), calls=%async_computation.2 | async-start | bytes 3342336 | tf_op jit(solution)/shard_map/all_to_all | solution.py:268
  79.2 2.0 collective-permute-done.8.refs_2_.refs_3_
  81.1 19.9 %all-gather.5.cloned.1.call-done = bf16[16,192,256]{2,1,0:T(8,128)(2,1)} async-done(((bf16[4,192,256]{2,1,0:T(8,128)(2,1)}), bf16[16,192,256]{2,1,0:T(8,128)(2,1)}) %all-gather.5.cloned.1.call-update) | async-done | bytes 1572880 | tf_op jit(solution)/shard_map/all_gather | solution.py:277
  101.1 5.9 %shard_map.95 = (f32[4,192,256]{2,1,0:T(8,128)}, f32[4,8,256]{2,1,0:T(8,128)S(1)}, f32[16,8,256]{2,1,0:T(8,128)S(1)}) custom-call(s32[5]{0:T(128)S(1)} %stack.59.ids, bf16[4,4,192,256]{3,2,1,0:T(8,128)(2,1)} %bitcast.31, bf16[4,1,272,256]{3,2,1,0:T(8,128)(2,1)} %copy-done.2, bf16[4,4,272,256]{3,2,1,0:T(8,128)(2,1)} %all-to-all-done.1.refs_1_, ...), custom_call_target="tpu_custom_call" | custom-call | flops 1006632960 | bytes 5570560 | tf_op jit(solution)/shard_map/pallas_call | solution.py:291
  106.9 3.0 %shard_map.96 = (f32[4,192,256]{2,1,0:T(8,128)S(1)}, f32[4,8,256]{2,1,0:T(8,128)S(1)}) custom-call(s32[5]{0:T(128)S(1)} %stack.59.ids, bf16[4,4,192,256]{3,2,1,0:T(8,128)(2,1)} %bitcast.32, bf16[4,3,272,256]{3,2,1,0:T(8,128)(2,1)S(1)} %all-to-all-done.2.refs_0_.refs_2_), custom_call_target="tpu_custom_call" | custom-call | flops 301989888 | bytes 1671168 | tf_op jit(solution)/shard_map/pallas_call | solution.py:291
  110.5 3.0 %shard_map.97 = (f32[4,192,256]{2,1,0:T(8,128)S(1)}, f32[4,8,256]{2,1,0:T(8,128)S(1)}) custom-call(s32[5]{0:T(128)S(1)} %stack.59.ids, bf16[4,4,192,256]{3,2,1,0:T(8,128)(2,1)} %bitcast.33, bf16[4,3,272,256]{3,2,1,0:T(8,128)(2,1)S(1)} %collective-permute-done.10.refs_0_.refs_5_), custom_call_target="tpu_custom_call" | custom-call | flops 301989888 | bytes 1671168 | tf_op jit(solution)/shard_map/pallas_call | solution.py:291
  113.5 6.4 %shard_map.98 = (bf16[4,4,192,256]{3,2,1,0:T(8,128)(2,1)}, f32[4,192,256]{2,1,0:T(8,128)}, f32[4,8,256]{2,1,0:T(8,128)}) custom-call(s32[5]{0:T(128)S(1)} %stack.59.ids, f32[4,192,256]{2,1,0:T(8,128)S(1)} %copy-done, f32[4,192,256]{2,1,0:T(8,128)S(1)} %get-tuple-element.39.p1, f32[4,192,256]{2,1,0:T(8,128)S(1)} %get-tuple-element.40.p2, ...), custom_call_target="tpu_custom_call" | custom-call | flops 1610612736 | bytes 12000000 | tf_op jit(solution)/shard_map/pallas_call | solution.py:314
  120.0 4.4 %all-to-all-start.3 = ((bf16[4,4,192,256]{3,2,1,0:T(8,128)(2,1)}), bf16[4,4,192,256]{3,2,1,0:T(8,128)(2,1)}, u32[]{:S(2)}, u32[]{:S(2)}) async-start(bf16[4,4,192,256]{3,2,1,0:T(8,128)(2,1)} %get-tuple-element.44), calls=%async_computation.3 | async-start | bytes 3145728 | tf_op jit(solution)/shard_map/all_to_all | solution.py:323
  124.4 21.3 %all-to-all-done.3.terms = bf16[4,4,192,256]{3,2,1,0:T(8,128)(2,1)} async-done(((bf16[4,4,192,256]{3,2,1,0:T(8,128)(2,1)}), bf16[4,4,192,256]{3,2,1,0:T(8,128)(2,1)}, u32[]{:S(2)}, u32[]{:S(2)}) %all-to-all-start.3) | async-done | bytes 1572896 | tf_op jit(solution)/shard_map/all_to_all | solution.py:323
  145.8 2.5 shard_map.99
  148.3 0.6 broadcast_in_dim.20
  148.9 5.8 %all-to-all-start.4 = ((f32[16,8,128]{2,1,0:T(8,128)}), f32[16,8,128]{2,1,0:T(8,128)}, u32[]{:S(2)}, u32[]{:S(2)}) async-start(f32[16,8,128]{2,1,0:T(8,128)} %broadcast_in_dim.20), calls=%async_computation.4 | async-start | bytes 131072 | tf_op jit(solution)/shard_map/all_to_all | solution.py:248
  155.4 3.4 %all-to-all-done.4 = f32[16,8,128]{2,1,0:T(8,128)} async-done(((f32[16,8,128]{2,1,0:T(8,128)}), f32[16,8,128]{2,1,0:T(8,128)}, u32[]{:S(2)}, u32[]{:S(2)}) %all-to-all-start.4) | async-done | bytes 65568 | tf_op jit(solution)/shard_map/all_to_all | solution.py:248
  158.7 0.9 reduce_sum.36
  159.6 0.6 broadcast_in_dim.21
  160.2 6.9 %all-to-all-start.5 = ((f32[16,8,128]{2,1,0:T(8,128)}), f32[16,8,128]{2,1,0:T(8,128)}, u32[]{:S(2)}, u32[]{:S(2)}) async-start(f32[16,8,128]{2,1,0:T(8,128)} %broadcast_in_dim.21), calls=%async_computation.5 | async-start | bytes 131072 | tf_op jit(solution)/shard_map/all_to_all | solution.py:248
  167.3 10.4 %all-gather.7.cloned.1.call-done = bf16[16,192,256]{2,1,0:T(8,128)(2,1)} async-done(((bf16[4,192,256]{2,1,0:T(8,128)(2,1)}), bf16[16,192,256]{2,1,0:T(8,128)(2,1)}) %all-gather.7.cloned.1.call-update) | async-done | bytes 1572880 | tf_op jit(solution)/shard_map/all_gather | solution.py:330
  177.7 6.6 %shard_map.100.pa = f32[4,192,256]{2,1,0:T(8,128)} custom-call(s32[5]{0:T(128)S(1)} %stack.59.ids, bf16[4,4,192,256]{3,2,1,0:T(8,128)(2,1)} %bitcast.35, f32[16,2,256]{2,1,0:T(2,128)S(1)} %bitcast.28, f32[16,8,256]{2,1,0:T(8,128)S(1)} %get-tuple-element.45.gabs, bf16[4,1,272,256]{3,2,1,0:T(8,128)(2,1)} %copy-done.2, ...), custom_call_target="tpu_custom_call" | custom-call | flops 1610612736 | bytes 12000000 | tf_op jit(solution)/shard_map/pallas_call | solution.py:332
  184.3 1.5 reduce_sum.37
  186.5 7.6 %shard_map.101 = (bf16[4,4,192,256]{3,2,1,0:T(8,128)(2,1)}, f32[16,1,256]{2,1,0:T(1,128)}) custom-call(f32[1]{0:T(128)} %bitcast.20.factor, s32[5]{0:T(128)S(1)} %stack.59.ids, f32[4,192,256]{2,1,0:T(8,128)} %get-tuple-element.49.praw, f32[4,8,256]{2,1,0:T(8,128)} %get-tuple-element.50.rs, f32[4,192,256]{2,1,0:T(8,128)} %shard_map.100.pa, ...), custom_call_target="tpu_custom_call" | custom-call | flops 1610612736 | bytes 12000000 | tf_op jit(solution)/shard_map/pallas_call | solution.py:342
  194.1 9.6 %all_to_all.45 = f32[16,1,256]{2,1,0:T(1,128)S(1)} all-to-all(f32[16,1,256]{2,1,0:T(1,128)} %get-tuple-element.51), channel_id=1, replica_groups=mesh['y'=4,'zh'=4,'x'=4,'zl'=2,'c'=2] {'x','zl','c'}, dimensions={0} | all-to-all | bytes 32768 | tf_op jit(solution)/shard_map/all_to_all | solution.py:352
  203.8 17.2 %all_to_all.46 = f32[16,1,256]{2,1,0:T(1,128)S(1)} all-to-all(f32[16,1,256]{2,1,0:T(1,128)S(1)} %broadcast_in_dim.23), channel_id=1, replica_groups=mesh['y'=4,'zh'=4,'x'=4,'zl'=2,'c'=2] {'y','zh'}, dimensions={0} | all-to-all | bytes 32768 | tf_op jit(solution)/shard_map/all_to_all | solution.py:248
  221.0 1.8 reduce-scatter.2.cloned.1.call-done
  222.8 6.9 %all-to-all-start.8 = ((bf16[4,192,256]{2,1,0:T(8,128)(2,1)}), bf16[4,192,256]{2,1,0:T(8,128)(2,1)S(1)}, u32[]{:S(2)}, u32[]{:S(2)}) async-start(bf16[4,192,256]{2,1,0:T(8,128)(2,1)} %bitcast.43), calls=%async_computation.9 | async-start | bytes 786432 | tf_op jit(solution)/shard_map/all_to_all | solution.py:354
  229.7 0.6 reduce_sum.39
  230.3 11.6 %all-to-all-done.8.sums = bf16[4,192,256]{2,1,0:T(8,128)(2,1)S(1)} async-done(((bf16[4,192,256]{2,1,0:T(8,128)(2,1)}), bf16[4,192,256]{2,1,0:T(8,128)(2,1)S(1)}, u32[]{:S(2)}, u32[]{:S(2)}) %all-to-all-start.8) | async-done | bytes 393248 | tf_op jit(solution)/shard_map/all_to_all | solution.py:354
  241.9 1.6 shard_map.102
  (53 shorter events, 1.3 us)
Async XLA Ops:
  7.3 0.7 copy-start.1
  10.3 7.5 %copy-start.8 = (bf16[272,256]{1,0:T(8,128)(2,1)S(1)}, bf16[272,256]{1,0:T(8,128)(2,1)}, u32[]{:S(2)}) copy-start(bf16[272,256]{1,0:T(8,128)(2,1)} %get-tuple-element.33) | copy-start | bytes 417796
  12.1 28.0 %all-to-all-start = ((bf16[4,1,272,256]{3,2,1,0:T(8,128)(2,1)}), bf16[4,1,272,256]{3,2,1,0:T(8,128)(2,1)S(1)}, u32[]{:S(2)}, u32[]{:S(2)}) async-start(bf16[4,1,272,256]{3,2,1,0:T(8,128)(2,1)} %broadcast_in_dim.17), calls=%async_computation | async-start | bytes 1114112 | tf_op jit(solution)/shard_map/all_to_all | solution.py:268
  17.8 15.4 %collective-permute-start.3 = (bf16[272,256]{1,0:T(8,128)(2,1)S(1)}, bf16[272,256]{1,0:T(8,128)(2,1)S(1)}, u32[]{:S(2)}, u32[]{:S(2)}) collective-permute-start(bf16[272,256]{1,0:T(8,128)(2,1)S(1)} %copy-done.8), channel_id=1, source_target_pairs={{16,0},{18,2},{32,16},{34,18},{48,32},{50,34},{0,48},{2,50},{17,1}... | collective-permute-start | bytes 417800 | tf_op jit(solution)/shard_map/ppermute | solution.py:37
  23.2 12.7 %collective-permute-start.4 = (bf16[272,256]{1,0:T(8,128)(2,1)S(1)}, bf16[272,256]{1,0:T(8,128)(2,1)S(1)}, u32[]{:S(2)}, u32[]{:S(2)}) collective-permute-start(bf16[272,256]{1,0:T(8,128)(2,1)S(1)} %copy-done.8), channel_id=1, source_target_pairs={{48,0},{50,2},{0,16},{2,18},{16,32},{18,34},{32,48},{34,50},{49,1}... | collective-permute-start | bytes 417800 | tf_op jit(solution)/shard_map/ppermute | solution.py:37
  23.2 16.8 %collective-permute-start.5 = (bf16[272,256]{1,0:T(8,128)(2,1)S(1)}, bf16[272,256]{1,0:T(8,128)(2,1)S(1)}, u32[]{:S(2)}, u32[]{:S(2)}) collective-permute-start(bf16[272,256]{1,0:T(8,128)(2,1)S(1)} %copy-done.8), channel_id=1, source_target_pairs={{32,0},{34,2},{48,16},{50,18},{0,32},{2,34},{16,48},{18,50},{33,1}... | collective-permute-start | bytes 417800 | tf_op jit(solution)/shard_map/ppermute | solution.py:37
  27.0 13.0 %collective-permute-start.7 = (bf16[272,256]{1,0:T(8,128)(2,1)S(1)}, bf16[272,256]{1,0:T(8,128)(2,1)S(1)}, u32[]{:S(2)}, u32[]{:S(2)}) collective-permute-start(bf16[272,256]{1,0:T(8,128)(2,1)S(1)} %copy-done.8), channel_id=1, source_target_pairs={{2,0},{0,2},{18,16},{16,18},{34,32},{32,34},{50,48},{48,50},{3,1},... | collective-permute-start | bytes 417800 | tf_op jit(solution)/shard_map/ppermute | solution.py:37
  40.1 39.0 %copy-start.2 = (bf16[4,1,272,256]{3,2,1,0:T(8,128)(2,1)}, bf16[4,1,272,256]{3,2,1,0:T(8,128)(2,1)S(1)}, u32[]{:S(2)}) copy-start(bf16[4,1,272,256]{3,2,1,0:T(8,128)(2,1)S(1)} %all-to-all-done.refs_0_) | copy-start | bytes 1671172
  41.7 5.0 %copy-start.12 = (bf16[288,256]{1,0:T(8,128)(2,1)S(1)}, bf16[288,256]{1,0:T(8,128)(2,1)}, u32[]{:S(2)}) copy-start(bf16[288,256]{1,0:T(8,128)(2,1)} %get-tuple-element.32) | copy-start | bytes 442372
  41.7 6.8 %copy-start.11 = (bf16[288,256]{1,0:T(8,128)(2,1)S(1)}, bf16[288,256]{1,0:T(8,128)(2,1)}, u32[]{:S(2)}) copy-start(bf16[288,256]{1,0:T(8,128)(2,1)} %get-tuple-element.31) | copy-start | bytes 442372
  41.7 8.1 %copy-start.10 = (bf16[288,256]{1,0:T(8,128)(2,1)S(1)}, bf16[288,256]{1,0:T(8,128)(2,1)}, u32[]{:S(2)}) copy-start(bf16[288,256]{1,0:T(8,128)(2,1)} %get-tuple-element.30) | copy-start | bytes 442372
  41.7 10.5 %copy-start.4 = (bf16[288,256]{1,0:T(8,128)(2,1)S(1)}, bf16[288,256]{1,0:T(8,128)(2,1)}, u32[]{:S(2)}) copy-start(bf16[288,256]{1,0:T(8,128)(2,1)} %get-tuple-element.29.c0) | copy-start | bytes 442372
  41.8 31.1 %all-to-all-start.1 = ((bf16[4,4,272,256]{3,2,1,0:T(8,128)(2,1)}), bf16[4,4,272,256]{3,2,1,0:T(8,128)(2,1)}, u32[]{:S(2)}, u32[]{:S(2)}) async-start(bf16[4,4,272,256]{3,2,1,0:T(8,128)(2,1)} %broadcast_in_dim.18), calls=%async_computation.1 | async-start | bytes 4456448 | tf_op jit(solution)/shard_map/all_to_all | solution.py:268
  46.7 54.4 %all-gather.5.cloned.1.call-start = ((), (), s32[]{:S(2)}) async-start(), calls=%async_computation.11 | async-start | bytes 1966080 | tf_op jit(solution)/shard_map/all_gather | solution.py:277
  46.7 14.2 %collective-permute-start.2 = (bf16[288,256]{1,0:T(8,128)(2,1)S(1)}, bf16[288,256]{1,0:T(8,128)(2,1)S(1)}, u32[]{:S(2)}, u32[]{:S(2)}) collective-permute-start(bf16[288,256]{1,0:T(8,128)(2,1)S(1)} %copy-done.12), channel_id=1, source_target_pairs={{48,0},{50,2},{0,16},{2,18},{16,32},{18,34},{32,48},{34,50},{49,1}... | collective-permute-start | bytes 442376 | tf_op jit(solution)/shard_map/ppermute | solution.py:37
  48.6 14.0 %collective-permute-start.1 = (bf16[288,256]{1,0:T(8,128)(2,1)S(1)}, bf16[288,256]{1,0:T(8,128)(2,1)S(1)}, u32[]{:S(2)}, u32[]{:S(2)}) collective-permute-start(bf16[288,256]{1,0:T(8,128)(2,1)S(1)} %copy-done.11), channel_id=1, source_target_pairs={{32,0},{34,2},{48,16},{50,18},{0,32},{2,34},{16,48},{18,50},{33,1}... | collective-permute-start | bytes 442376 | tf_op jit(solution)/shard_map/ppermute | solution.py:37
  49.9 12.7 %collective-permute-start = (bf16[288,256]{1,0:T(8,128)(2,1)S(1)}, bf16[288,256]{1,0:T(8,128)(2,1)S(1)}, u32[]{:S(2)}, u32[]{:S(2)}) collective-permute-start(bf16[288,256]{1,0:T(8,128)(2,1)S(1)} %copy-done.10), channel_id=1, source_target_pairs={{16,0},{18,2},{32,16},{34,18},{48,32},{50,34},{0,48},{2,50},{17,1}... | collective-permute-start | bytes 442376 | tf_op jit(solution)/shard_map/ppermute | solution.py:37
  52.3 20.5 %collective-permute-start.6 = (bf16[3,272,256]{2,1,0:T(8,128)(2,1)S(1)}, bf16[3,272,256]{2,1,0:T(8,128)(2,1)S(1)}, u32[]{:S(2)}, u32[]{:S(2)}) collective-permute-start(bf16[3,272,256]{2,1,0:T(8,128)(2,1)S(1)} %pad_maximum_fusion.1), channel_id=1, source_target_pairs={{2,0},{0,2},{18,16},{16,18},{34,32},{32,34},{50,48},{48,50},{3,1},... | collective-permute-start | bytes 1253384 | tf_op jit(solution)/shard_map/ppermute | solution.py:37
  60.9 13.4 %copy-start.5 = (bf16[288,256]{1,0:T(8,128)(2,1)}, bf16[288,256]{1,0:T(8,128)(2,1)S(1)}, u32[]{:S(2)}) copy-start(bf16[288,256]{1,0:T(8,128)(2,1)S(1)} %collective-permute-done.2.c3) | copy-start | bytes 442372
  62.6 11.7 %copy-start.6 = (bf16[288,256]{1,0:T(8,128)(2,1)}, bf16[288,256]{1,0:T(8,128)(2,1)S(1)}, u32[]{:S(2)}) copy-start(bf16[288,256]{1,0:T(8,128)(2,1)S(1)} %collective-permute-done.1.c2) | copy-start | bytes 442372
  62.6 11.7 %copy-start.7 = (bf16[288,256]{1,0:T(8,128)(2,1)}, bf16[288,256]{1,0:T(8,128)(2,1)S(1)}, u32[]{:S(2)}) copy-start(bf16[288,256]{1,0:T(8,128)(2,1)S(1)} %collective-permute-done.c1) | copy-start | bytes 442372
  72.8 28.2 %collective-permute-start.9 = (bf16[4,4,272,256]{3,2,1,0:T(8,128)(2,1)}, bf16[4,4,272,256]{3,2,1,0:T(8,128)(2,1)}, u32[]{:S(2)}, u32[]{:S(2)}) collective-permute-start(bf16[4,4,272,256]{3,2,1,0:T(8,128)(2,1)} %all-to-all-done.1.refs_1_), channel_id=1, source_target_pairs={{0,1},{1,0},{2,3},{3,2},{4,5},{5,4},{6,7},{7,6},{8,9},{9,8},{10,11... | collective-permute-start | bytes 6684680 | tf_op jit(solution)/shard_map/ppermute | solution.py:41
  74.3 32.6 %all-to-all-start.2 = ((bf16[4,3,272,256]{3,2,1,0:T(8,128)(2,1)}), bf16[4,3,272,256]{3,2,1,0:T(8,128)(2,1)S(1)}, u32[]{:S(2)}, u32[]{:S(2)}) async-start(bf16[4,3,272,256]{3,2,1,0:T(8,128)(2,1)} %broadcast_in_dim.19), calls=%async_computation.2 | async-start | bytes 3342336 | tf_op jit(solution)/shard_map/all_to_all | solution.py:268
  79.2 2.0 collective-permute-start.8
  81.1 20.0 %copy-start.3 = (bf16[4,1,272,256]{3,2,1,0:T(8,128)(2,1)}, bf16[4,1,272,256]{3,2,1,0:T(8,128)(2,1)S(1)}, u32[]{:S(2)}) copy-start(bf16[4,1,272,256]{3,2,1,0:T(8,128)(2,1)S(1)} %collective-permute-done.8.refs_2_.refs_3_) | copy-start | bytes 1671172
  106.9 3.6 %collective-permute-start.10 = (bf16[4,3,272,256]{3,2,1,0:T(8,128)(2,1)S(1)}, bf16[4,3,272,256]{3,2,1,0:T(8,128)(2,1)S(1)}, u32[]{:S(2)}, u32[]{:S(2)}) collective-permute-start(bf16[4,3,272,256]{3,2,1,0:T(8,128)(2,1)S(1)} %all-to-all-done.2.refs_0_.refs_2_), channel_id=1, source_target_pairs={{0,1},{1,0},{2,3},{3,2},{4,5},{5,4},{6,7},{7,6},{8,9},{9,8},{10,11... | collective-permute-start | bytes 5013512 | tf_op jit(solution)/shard_map/ppermute | solution.py:41
  110.0 3.5 %copy-start = (f32[4,192,256]{2,1,0:T(8,128)S(1)}, f32[4,192,256]{2,1,0:T(8,128)}, u32[]{:S(2)}) copy-start(f32[4,192,256]{2,1,0:T(8,128)} %get-tuple-element.36.p0) | copy-start | bytes 2359300
  120.0 4.5 %copy-start.9 = (s32[2,4096]{1,0:T(2,128)S(1)}, s32[2,4096]{1,0:T(2,128)}, u32[]{:S(2)}) copy-start(s32[2,4096]{1,0:T(2,128)} %param.12) | copy-start | bytes 98308
  120.0 25.8 %all-to-all-start.3 = ((bf16[4,4,192,256]{3,2,1,0:T(8,128)(2,1)}), bf16[4,4,192,256]{3,2,1,0:T(8,128)(2,1)}, u32[]{:S(2)}, u32[]{:S(2)}) async-start(bf16[4,4,192,256]{3,2,1,0:T(8,128)(2,1)} %get-tuple-element.44), calls=%async_computation.3 | async-start | bytes 3145728 | tf_op jit(solution)/shard_map/all_to_all | solution.py:323
  124.4 53.3 %all-gather.7.cloned.1.call-start = ((), (), s32[]{:S(2)}) async-start(), calls=%async_computation.12 | async-start | bytes 1966080 | tf_op jit(solution)/shard_map/all_gather | solution.py:330
  148.9 9.8 %all-to-all-start.4 = ((f32[16,8,128]{2,1,0:T(8,128)}), f32[16,8,128]{2,1,0:T(8,128)}, u32[]{:S(2)}, u32[]{:S(2)}) async-start(f32[16,8,128]{2,1,0:T(8,128)} %broadcast_in_dim.20), calls=%async_computation.4 | async-start | bytes 131072 | tf_op jit(solution)/shard_map/all_to_all | solution.py:248
  160.2 24.1 %all-to-all-start.5 = ((f32[16,8,128]{2,1,0:T(8,128)}), f32[16,8,128]{2,1,0:T(8,128)}, u32[]{:S(2)}, u32[]{:S(2)}) async-start(f32[16,8,128]{2,1,0:T(8,128)} %broadcast_in_dim.21), calls=%async_computation.5 | async-start | bytes 131072 | tf_op jit(solution)/shard_map/all_to_all | solution.py:248
  167.1 55.7 %reduce-scatter.2.cloned.1.call-start = ((), (), s32[]{:S(2)}) async-start(), calls=%async_computation.10 | async-start | bytes 1966080 | tf_op jit(solution)/shard_map/reduce_scatter | solution.py:351
  222.8 19.1 %all-to-all-start.8 = ((bf16[4,192,256]{2,1,0:T(8,128)(2,1)}), bf16[4,192,256]{2,1,0:T(8,128)(2,1)S(1)}, u32[]{:S(2)}, u32[]{:S(2)}) async-start(bf16[4,192,256]{2,1,0:T(8,128)(2,1)} %bitcast.43), calls=%async_computation.9 | async-start | bytes 786432 | tf_op jit(solution)/shard_map/all_to_all | solution.py:354
Sparse Core Ops, SparseCore 0:
  73.0 28.0 all-gather.4
  148.4 29.2 all-gather.6
  194.2 28.4 reduce-scatter.1

commit v6 on v5

--- a/solution.py
+++ b/solution.py
@@ -89,13 +89,15 @@
     return rows[at : at + 1] + rows[at + 1 : at + 2] + rows[at + 2 : at + 3]
 
 
-def start_kernel(ids, tokens, gain, w_gate, w_up, cot, pack, p0, p1, p2, p3, turned):
+def start_kernel(ids, tokens, gain, w_gate, w_up, cot, pack, packs, p0, p1, p2, p3, turned):
     values = tokens[...].astype(F32)
     squares = jnp.sum((values * values).T, axis=0, keepdims=True)
     pack[0:BLK, :] = tokens[...]
     extra = split3(gain[...]) + split3(squares)
     tail = jnp.concatenate([e.astype(F32) for e in extra] + [jnp.zeros((10, BLK), F32)], axis=0)
     pack[BLK:PACK, :] = tail.astype(BF)
+    for i in range(4):
+        packs[i, 0] = pack[...]
     for i, ref in enumerate((w_gate, w_up, cot)):
         turned[i] = ref[...].astype(F32).T.astype(BF)
         for k, to in enumerate((p0, p1, p2, p3)):
@@ -253,11 +255,11 @@
     mask = decay_mask.astype(F32).reshape(2, NB, BLK).transpose(1, 0, 2)
 
     piece = hbm((3 * SUB, BLK), BF)
-    pack, *pieces = call(
+    pack, packs, *pieces = call(
         start_kernel,
-        (hbm((PACK, BLK), BF),) + (piece,) * 4,
+        (hbm((PACK, BLK), BF), hbm((4, 1, PACK, BLK), BF)) + (piece,) * 4,
         [SMEM, whole((BLK, BLK)), whole((1, BLK))] + [whole((BLK, 4 * SUB))] * 3,
-        (whole((PACK, BLK)),) + (whole(piece.shape),) * 4,
+        (whole((PACK, BLK)), whole((4, 1, PACK, BLK))) + (whole(piece.shape),) * 4,
         scratch=[pltpu.VMEM((3, 4 * SUB, BLK), BF)],
     )(ids, in_hbm(tokens), norm_gain[None, :], in_hbm(w_gate), in_hbm(w_up), in_hbm(cotangent))
 
@@ -269,14 +271,14 @@
 
     mids = [from_z(pack, k, 0) for k in (1, 3, 2)]
     near = from_z(pack, 0, 1)
-    own_x = over_x(pack[None])
+    own_x = lax.all_to_all(packs, "x", 0, 0, tiled=True)
     pieces = [pieces[0]] + [from_z(pieces[k], k, 0) for k in range(1, 4)]
     part_w = jnp.stack([p[:ROWS] for p in pieces])
     mid_x = over_x(after(jnp.stack(mids + [near]), own_x))
     far = from_z(jnp.stack(mids), 0, 1)
-    weights = in_hbm(lax.all_gather(after(part_w, far), "y", axis=0, tiled=False))
+    weights = in_hbm(lax.all_gather(part_w, "y", axis=0, tiled=False))
     far_x = over_x(after(far, part_w, mid_x))
-    mine = [in_hbm(v) for v in (own_x, mid_x)]
+    mine = [in_hbm(v) for v in (own_x, after(mid_x, far))]
     toks = {(grp, g): in_hbm(other_core(v)) if g else v for grp, v in enumerate(mine) for g in range(2)}
 
     pshape, sshape, gshape = shape((4, ROWS, BLK), F32), shape((4, 8, BLK), F32), shape((NB, 8, BLK), F32)

time: 251 us -> 244 us (0.972)
  waiting for transfers between devices: 100 us -> 94.7 us
    all_to_all x3 -> x2, starting transfers between devices: 15.4 us -> 9.74 us  [over_x(): lax.all_to_all(jnp.broadcast_to(value[None], (4,) + value.shape), 'x', 0,...]
    all_to_all x0 -> x1, starting transfers between devices: none -> 5.68 us  [body(): own_x = lax.all_to_all(packs, 'x', 0, 0, tiled=True)]
    all_gather x1, waiting for transfers between devices: 19.9 us -> 14.4 us  [body(): weights = in_hbm(lax.all_gather(part_w, 'y', axis=0, tiled=False))]
where the time goes in v6:
time: 244 us; the launch traced here: 243 us
  waiting for transfers between devices  94.7 us (39%)
  starting transfers between devices  57.6 us (24%)
  Pallas kernels  39.2 us (16%)
  blocking collectives  26.8 us (11%)
  between operations  15.3 us (6%)
  local copies, waits for them, and re-layouts  5.1 us (2%)
  other arithmetic  3.9 us (2%)
    ppermute x8, waiting for transfers between devices, from_z(): return lax.ppermute(value, ('zh', 'zl'), pairs)  29.4 us
    all_to_all x1, waiting for transfers between devices, body(): terms = lax.all_to_all(out1, 'y', 0, 0, tiled=True)  21.3 us
    ppermute x8, starting transfers between devices, from_z(): return lax.ppermute(value, ('zh', 'zl'), pairs)  17.9 us
    all_to_all x1, blocking collectives, spread(): lax.all_to_all(jnp.broadcast_to(value[None], (n,) + value.shape), axes, 0...  17.2 us
    all_gather x1, waiting for transfers between devices, body(): weights = in_hbm(lax.all_gather(part_w, 'y', axis=0, tiled=False))  14.4 us
    all_to_all x2, starting transfers between devices, spread(): lax.all_to_all(jnp.broadcast_to(value[None], (n,) + value.shape), axes, 0...  12.7 us
    pallas_call x3, Pallas kernels, pre(): call(functools.partial(pre_kernel, parts, with_gain), outs, [SMEM, wspec]...  11.9 us
    all_to_all x1, waiting for transfers between devices, body(): sums = lax.all_to_all(sums, 'zh', 0, 0, tiled=True)  11.7 us
  transfers between devices with their start and end apart: 21, of which 14 were waited for; matrix products, arithmetic and copies ran while one was open for 2% of the time, Pallas kernels for 6%

profile of v6, /device:TPU:4, one launch (start us, length us, event | category | flops | bytes accessed | tf_op | source)
XLA Modules:
  0.0 242.6 jit_solution(4761952457322291673)
XLA Ops:
  7.3 0.7 copy-done.1
  7.9 2.5 %shard_map.94 = (bf16[272,256]{1,0:T(8,128)(2,1)}, bf16[4,1,272,256]{3,2,1,0:T(8,128)(2,1)}, bf16[288,256]{1,0:T(8,128)(2,1)}, bf16[288,256]{1,0:T(8,128)(2,1)},...) custom-call(s32[5]{0:T(128)S(1)} %stack.59.ids, bf16[256,256]{1,0:T(8,128)(2,1)} %tokens.1, f32[1,256]{1,0:T(1,128)S(1)} %bitcast.30, ...), custom_call_target="tpu_custom_call" | custom-call | flops 1000000 | bytes 1000000 | tf_op jit(solution)/shard_map/pallas_call | solution.py:258
  10.4 5.7 %all-to-all-start = ((bf16[4,1,272,256]{3,2,1,0:T(8,128)(2,1)}), bf16[4,1,272,256]{3,2,1,0:T(8,128)(2,1)S(1)}, u32[]{:S(2)}, u32[]{:S(2)}) async-start(bf16[4,1,272,256]{3,2,1,0:T(8,128)(2,1)} %get-tuple-element.34), calls=%async_computation | async-start | bytes 1114112 | tf_op jit(solution)/shard_map/all_to_all | solution.py:274
  16.1 5.4 %collective-permute-start.3 = (bf16[272,256]{1,0:T(8,128)(2,1)}, bf16[272,256]{1,0:T(8,128)(2,1)S(1)}, u32[]{:S(2)}, u32[]{:S(2)}) collective-permute-start(bf16[272,256]{1,0:T(8,128)(2,1)} %get-tuple-element.35), channel_id=1, source_target_pairs={{16,0},{18,2},{32,16},{34,18},{48,32},{50,34},{0,48},{2,50},{17,1}... | collective-permute-start | bytes 417800 | tf_op jit(solution)/shard_map/ppermute | solution.py:37
  21.5 3.8 %collective-permute-start.5 = (bf16[272,256]{1,0:T(8,128)(2,1)}, bf16[272,256]{1,0:T(8,128)(2,1)S(1)}, u32[]{:S(2)}, u32[]{:S(2)}) collective-permute-start(bf16[272,256]{1,0:T(8,128)(2,1)} %get-tuple-element.35), channel_id=1, source_target_pairs={{32,0},{34,2},{48,16},{50,18},{0,32},{2,34},{16,48},{18,50},{33,1}... | collective-permute-start | bytes 417800 | tf_op jit(solution)/shard_map/ppermute | solution.py:37
  25.3 1.0 collective-permute-start.6
  26.4 5.5 %collective-permute-done.3 = bf16[272,256]{1,0:T(8,128)(2,1)S(1)} collective-permute-done((bf16[272,256]{1,0:T(8,128)(2,1)}, bf16[272,256]{1,0:T(8,128)(2,1)S(1)}, u32[]{:S(2)}, u32[]{:S(2)}) %collective-permute-start.3) | collective-permute-done | bytes 139296 | tf_op jit(solution)/shard_map/ppermute | solution.py:37
  31.9 2.6 %collective-permute-done.4 = bf16[272,256]{1,0:T(8,128)(2,1)S(1)} collective-permute-done((bf16[272,256]{1,0:T(8,128)(2,1)}, bf16[272,256]{1,0:T(8,128)(2,1)S(1)}, u32[]{:S(2)}, u32[]{:S(2)}) %collective-permute-start.4) | collective-permute-done | bytes 139296 | tf_op jit(solution)/shard_map/ppermute | solution.py:37
  34.5 4.2 %collective-permute-done.5 = bf16[272,256]{1,0:T(8,128)(2,1)S(1)} collective-permute-done((bf16[272,256]{1,0:T(8,128)(2,1)}, bf16[272,256]{1,0:T(8,128)(2,1)S(1)}, u32[]{:S(2)}, u32[]{:S(2)}) %collective-permute-start.5) | collective-permute-done | bytes 139296 | tf_op jit(solution)/shard_map/ppermute | solution.py:37
  38.8 1.6 broadcast_in_dim.15
  40.4 4.9 %all-to-all-start.1 = ((bf16[4,4,272,256]{3,2,1,0:T(8,128)(2,1)}), bf16[4,4,272,256]{3,2,1,0:T(8,128)(2,1)}, u32[]{:S(2)}, u32[]{:S(2)}) async-start(bf16[4,4,272,256]{3,2,1,0:T(8,128)(2,1)} %broadcast_in_dim.15), calls=%async_computation.1 | async-start | bytes 4456448 | tf_op jit(solution)/shard_map/all_to_all | solution.py:270
  45.3 1.7 collective-permute-start.2
  47.0 1.4 collective-permute-start.1
  48.5 2.2 collective-permute-start
  50.8 2.2 collective-permute-start.7
  53.0 6.0 %collective-permute-done.2.c3 = bf16[288,256]{1,0:T(8,128)(2,1)S(1)} collective-permute-done((bf16[288,256]{1,0:T(8,128)(2,1)S(1)}, bf16[288,256]{1,0:T(8,128)(2,1)S(1)}, u32[]{:S(2)}, u32[]{:S(2)}) %collective-permute-start.2) | collective-permute-done | bytes 147488 | tf_op jit(solution)/shard_map/ppermute | solution.py:37
  59.0 2.5 %collective-permute-done.1.c2 = bf16[288,256]{1,0:T(8,128)(2,1)S(1)} collective-permute-done((bf16[288,256]{1,0:T(8,128)(2,1)S(1)}, bf16[288,256]{1,0:T(8,128)(2,1)S(1)}, u32[]{:S(2)}, u32[]{:S(2)}) %collective-permute-start.1) | collective-permute-done | bytes 147488 | tf_op jit(solution)/shard_map/ppermute | solution.py:37
  61.6 0.8 pad_maximum_fusion.2
  62.4 8.7 %collective-permute-done.7 = bf16[3,272,256]{2,1,0:T(8,128)(2,1)S(1)} collective-permute-done((bf16[3,272,256]{2,1,0:T(8,128)(2,1)S(1)}, bf16[3,272,256]{2,1,0:T(8,128)(2,1)S(1)}, u32[]{:S(2)}, u32[]{:S(2)}) %collective-permute-start.7) | collective-permute-done | bytes 417824 | tf_op jit(solution)/shard_map/ppermute | solution.py:37
  71.1 1.4 broadcast_in_dim.16
  72.5 4.8 %all-to-all-start.2 = ((bf16[4,3,272,256]{3,2,1,0:T(8,128)(2,1)}), bf16[4,3,272,256]{3,2,1,0:T(8,128)(2,1)S(1)}, u32[]{:S(2)}, u32[]{:S(2)}) async-start(bf16[4,3,272,256]{3,2,1,0:T(8,128)(2,1)} %broadcast_in_dim.16), calls=%async_computation.2 | async-start | bytes 3342336 | tf_op jit(solution)/shard_map/all_to_all | solution.py:270
  77.3 2.0 collective-permute-done.8.refs_2_.refs_3_
  79.2 14.4 %all-gather.5.cloned.1.call-done = bf16[16,192,256]{2,1,0:T(8,128)(2,1)} async-done(((bf16[4,192,256]{2,1,0:T(8,128)(2,1)}), bf16[16,192,256]{2,1,0:T(8,128)(2,1)}) %all-gather.5.cloned.1.call-update) | async-done | bytes 1572880 | tf_op jit(solution)/shard_map/all_gather | solution.py:279
  93.6 5.9 %shard_map.95 = (f32[4,192,256]{2,1,0:T(8,128)}, f32[4,8,256]{2,1,0:T(8,128)S(1)}, f32[16,8,256]{2,1,0:T(8,128)S(1)}) custom-call(s32[5]{0:T(128)S(1)} %stack.59.ids, bf16[4,4,192,256]{3,2,1,0:T(8,128)(2,1)} %bitcast.31, bf16[4,1,272,256]{3,2,1,0:T(8,128)(2,1)} %copy-done.2, bf16[4,4,272,256]{3,2,1,0:T(8,128)(2,1)} %all-to-all-done.1.refs_1_, ...), custom_call_target="tpu_custom_call" | custom-call | flops 1006632960 | bytes 5570560 | tf_op jit(solution)/shard_map/pallas_call | solution.py:293
  99.5 3.0 %shard_map.96 = (f32[4,192,256]{2,1,0:T(8,128)S(1)}, f32[4,8,256]{2,1,0:T(8,128)S(1)}) custom-call(s32[5]{0:T(128)S(1)} %stack.59.ids, bf16[4,4,192,256]{3,2,1,0:T(8,128)(2,1)} %bitcast.32, bf16[4,3,272,256]{3,2,1,0:T(8,128)(2,1)S(1)} %all-to-all-done.2.refs_0_.refs_2_), custom_call_target="tpu_custom_call" | custom-call | flops 301989888 | bytes 1671168 | tf_op jit(solution)/shard_map/pallas_call | solution.py:293
  102.5 0.5 collective-permute-done.10.refs_0_.refs_5_
  103.0 3.0 %shard_map.97 = (f32[4,192,256]{2,1,0:T(8,128)S(1)}, f32[4,8,256]{2,1,0:T(8,128)S(1)}) custom-call(s32[5]{0:T(128)S(1)} %stack.59.ids, bf16[4,4,192,256]{3,2,1,0:T(8,128)(2,1)} %bitcast.33, bf16[4,3,272,256]{3,2,1,0:T(8,128)(2,1)S(1)} %collective-permute-done.10.refs_0_.refs_5_), custom_call_target="tpu_custom_call" | custom-call | flops 301989888 | bytes 1671168 | tf_op jit(solution)/shard_map/pallas_call | solution.py:293
  106.1 6.4 %shard_map.98 = (bf16[4,4,192,256]{3,2,1,0:T(8,128)(2,1)}, f32[4,192,256]{2,1,0:T(8,128)}, f32[4,8,256]{2,1,0:T(8,128)}) custom-call(s32[5]{0:T(128)S(1)} %stack.59.ids, f32[4,192,256]{2,1,0:T(8,128)S(1)} %copy-done, f32[4,192,256]{2,1,0:T(8,128)S(1)} %get-tuple-element.41.p1, f32[4,192,256]{2,1,0:T(8,128)S(1)} %get-tuple-element.42.p2, ...), custom_call_target="tpu_custom_call" | custom-call | flops 1610612736 | bytes 12000000 | tf_op jit(solution)/shard_map/pallas_call | solution.py:316
  112.5 4.4 %all-to-all-start.3 = ((bf16[4,4,192,256]{3,2,1,0:T(8,128)(2,1)}), bf16[4,4,192,256]{3,2,1,0:T(8,128)(2,1)}, u32[]{:S(2)}, u32[]{:S(2)}) async-start(bf16[4,4,192,256]{3,2,1,0:T(8,128)(2,1)} %get-tuple-element.46), calls=%async_computation.3 | async-start | bytes 3145728 | tf_op jit(solution)/shard_map/all_to_all | solution.py:325
  117.0 21.3 %all-to-all-done.3.terms = bf16[4,4,192,256]{3,2,1,0:T(8,128)(2,1)} async-done(((bf16[4,4,192,256]{3,2,1,0:T(8,128)(2,1)}), bf16[4,4,192,256]{3,2,1,0:T(8,128)(2,1)}, u32[]{:S(2)}, u32[]{:S(2)}) %all-to-all-start.3) | async-done | bytes 1572896 | tf_op jit(solution)/shard_map/all_to_all | solution.py:325
  138.3 2.5 %shard_map.99 = (bf16[4,192,256]{2,1,0:T(8,128)(2,1)}, f32[8,128]{1,0:T(8,128)S(1)}) custom-call(s32[5]{0:T(128)S(1)} %stack.59.ids, bf16[4,4,192,256]{3,2,1,0:T(8,128)(2,1)} %all-to-all-done.3.terms, f32[16,8,256]{2,1,0:T(8,128)S(1)} %get-tuple-element.47.gabs, f32[16,2,256]{2,1,0:T(2,128)S(1)} %bitcast.27), custom_call_target="tpu_custom_call" | custom-call | flops 1000000 | bytes 1000000 | tf_op jit(solution)/shard_map/pallas_call | solution.py:326
  140.9 0.6 broadcast_in_dim.17
  141.5 5.8 %all-to-all-start.4 = ((f32[16,8,128]{2,1,0:T(8,128)}), f32[16,8,128]{2,1,0:T(8,128)}, u32[]{:S(2)}, u32[]{:S(2)}) async-start(f32[16,8,128]{2,1,0:T(8,128)} %broadcast_in_dim.17), calls=%async_computation.4 | async-start | bytes 131072 | tf_op jit(solution)/shard_map/all_to_all | solution.py:250
  148.0 3.4 %all-to-all-done.4 = f32[16,8,128]{2,1,0:T(8,128)} async-done(((f32[16,8,128]{2,1,0:T(8,128)}), f32[16,8,128]{2,1,0:T(8,128)}, u32[]{:S(2)}, u32[]{:S(2)}) %all-to-all-start.4) | async-done | bytes 65568 | tf_op jit(solution)/shard_map/all_to_all | solution.py:250
  151.3 0.9 reduce_sum.36
  152.2 0.6 broadcast_in_dim.18
  152.8 6.9 %all-to-all-start.5 = ((f32[16,8,128]{2,1,0:T(8,128)}), f32[16,8,128]{2,1,0:T(8,128)}, u32[]{:S(2)}, u32[]{:S(2)}) async-start(f32[16,8,128]{2,1,0:T(8,128)} %broadcast_in_dim.18), calls=%async_computation.5 | async-start | bytes 131072 | tf_op jit(solution)/shard_map/all_to_all | solution.py:250
  159.9 10.4 %all-gather.7.cloned.1.call-done = bf16[16,192,256]{2,1,0:T(8,128)(2,1)} async-done(((bf16[4,192,256]{2,1,0:T(8,128)(2,1)}), bf16[16,192,256]{2,1,0:T(8,128)(2,1)}) %all-gather.7.cloned.1.call-update) | async-done | bytes 1572880 | tf_op jit(solution)/shard_map/all_gather | solution.py:332
  170.3 6.6 %shard_map.100.pa = f32[4,192,256]{2,1,0:T(8,128)} custom-call(s32[5]{0:T(128)S(1)} %stack.59.ids, bf16[4,4,192,256]{3,2,1,0:T(8,128)(2,1)} %bitcast.35, f32[16,2,256]{2,1,0:T(2,128)S(1)} %bitcast.28, f32[16,8,256]{2,1,0:T(8,128)S(1)} %get-tuple-element.47.gabs, bf16[4,1,272,256]{3,2,1,0:T(8,128)(2,1)} %copy-done.2, ...), custom_call_target="tpu_custom_call" | custom-call | flops 1610612736 | bytes 12000000 | tf_op jit(solution)/shard_map/pallas_call | solution.py:334
  176.9 1.5 reduce_sum.37
  179.1 7.6 %shard_map.101 = (bf16[4,4,192,256]{3,2,1,0:T(8,128)(2,1)}, f32[16,1,256]{2,1,0:T(1,128)}) custom-call(f32[1]{0:T(128)} %bitcast.20.factor, s32[5]{0:T(128)S(1)} %stack.59.ids, f32[4,192,256]{2,1,0:T(8,128)} %get-tuple-element.51.praw, f32[4,8,256]{2,1,0:T(8,128)} %get-tuple-element.52.rs, f32[4,192,256]{2,1,0:T(8,128)} %shard_map.100.pa, ...), custom_call_target="tpu_custom_call" | custom-call | flops 1610612736 | bytes 12000000 | tf_op jit(solution)/shard_map/pallas_call | solution.py:344
  186.7 9.6 %all_to_all.45 = f32[16,1,256]{2,1,0:T(1,128)S(1)} all-to-all(f32[16,1,256]{2,1,0:T(1,128)} %get-tuple-element.53), channel_id=1, replica_groups=mesh['y'=4,'zh'=4,'x'=4,'zl'=2,'c'=2] {'x','zl','c'}, dimensions={0} | all-to-all | bytes 32768 | tf_op jit(solution)/shard_map/all_to_all | solution.py:354
  196.4 17.2 %all_to_all.46 = f32[16,1,256]{2,1,0:T(1,128)S(1)} all-to-all(f32[16,1,256]{2,1,0:T(1,128)S(1)} %broadcast_in_dim.20), channel_id=1, replica_groups=mesh['y'=4,'zh'=4,'x'=4,'zl'=2,'c'=2] {'y','zh'}, dimensions={0} | all-to-all | bytes 32768 | tf_op jit(solution)/shard_map/all_to_all | solution.py:250
  213.6 1.7 reduce-scatter.2.cloned.1.call-done
  215.3 6.9 %all-to-all-start.8 = ((bf16[4,192,256]{2,1,0:T(8,128)(2,1)}), bf16[4,192,256]{2,1,0:T(8,128)(2,1)S(1)}, u32[]{:S(2)}, u32[]{:S(2)}) async-start(bf16[4,192,256]{2,1,0:T(8,128)(2,1)} %bitcast.43), calls=%async_computation.9 | async-start | bytes 786432 | tf_op jit(solution)/shard_map/all_to_all | solution.py:356
  222.2 0.6 reduce_sum.39
  222.8 11.7 %all-to-all-done.8.sums = bf16[4,192,256]{2,1,0:T(8,128)(2,1)S(1)} async-done(((bf16[4,192,256]{2,1,0:T(8,128)(2,1)}), bf16[4,192,256]{2,1,0:T(8,128)(2,1)S(1)}, u32[]{:S(2)}, u32[]{:S(2)}) %all-to-all-start.8) | async-done | bytes 393248 | tf_op jit(solution)/shard_map/all_to_all | solution.py:356
  234.5 1.6 shard_map.102
  (50 shorter events, 0.7 us)
Async XLA Ops:
  7.3 0.7 copy-start.1
  10.4 28.3 %all-to-all-start = ((bf16[4,1,272,256]{3,2,1,0:T(8,128)(2,1)}), bf16[4,1,272,256]{3,2,1,0:T(8,128)(2,1)S(1)}, u32[]{:S(2)}, u32[]{:S(2)}) async-start(bf16[4,1,272,256]{3,2,1,0:T(8,128)(2,1)} %get-tuple-element.34), calls=%async_computation | async-start | bytes 1114112 | tf_op jit(solution)/shard_map/all_to_all | solution.py:274
  16.1 15.7 %collective-permute-start.3 = (bf16[272,256]{1,0:T(8,128)(2,1)}, bf16[272,256]{1,0:T(8,128)(2,1)S(1)}, u32[]{:S(2)}, u32[]{:S(2)}) collective-permute-start(bf16[272,256]{1,0:T(8,128)(2,1)} %get-tuple-element.35), channel_id=1, source_target_pairs={{16,0},{18,2},{32,16},{34,18},{48,32},{50,34},{0,48},{2,50},{17,1}... | collective-permute-start | bytes 417800 | tf_op jit(solution)/shard_map/ppermute | solution.py:37
  21.5 12.9 %collective-permute-start.4 = (bf16[272,256]{1,0:T(8,128)(2,1)}, bf16[272,256]{1,0:T(8,128)(2,1)S(1)}, u32[]{:S(2)}, u32[]{:S(2)}) collective-permute-start(bf16[272,256]{1,0:T(8,128)(2,1)} %get-tuple-element.35), channel_id=1, source_target_pairs={{48,0},{50,2},{0,16},{2,18},{16,32},{18,34},{32,48},{34,50},{49,1}... | collective-permute-start | bytes 417800 | tf_op jit(solution)/shard_map/ppermute | solution.py:37
  21.5 17.1 %collective-permute-start.5 = (bf16[272,256]{1,0:T(8,128)(2,1)}, bf16[272,256]{1,0:T(8,128)(2,1)S(1)}, u32[]{:S(2)}, u32[]{:S(2)}) collective-permute-start(bf16[272,256]{1,0:T(8,128)(2,1)} %get-tuple-element.35), channel_id=1, source_target_pairs={{32,0},{34,2},{48,16},{50,18},{0,32},{2,34},{16,48},{18,50},{33,1}... | collective-permute-start | bytes 417800 | tf_op jit(solution)/shard_map/ppermute | solution.py:37
  25.3 13.3 %collective-permute-start.6 = (bf16[272,256]{1,0:T(8,128)(2,1)}, bf16[272,256]{1,0:T(8,128)(2,1)S(1)}, u32[]{:S(2)}, u32[]{:S(2)}) collective-permute-start(bf16[272,256]{1,0:T(8,128)(2,1)} %get-tuple-element.35), channel_id=1, source_target_pairs={{2,0},{0,2},{18,16},{16,18},{34,32},{32,34},{50,48},{48,50},{3,1},... | collective-permute-start | bytes 417800 | tf_op jit(solution)/shard_map/ppermute | solution.py:37
  38.7 38.5 %copy-start.2 = (bf16[4,1,272,256]{3,2,1,0:T(8,128)(2,1)}, bf16[4,1,272,256]{3,2,1,0:T(8,128)(2,1)S(1)}, u32[]{:S(2)}) copy-start(bf16[4,1,272,256]{3,2,1,0:T(8,128)(2,1)S(1)} %all-to-all-done.refs_0_) | copy-start | bytes 1671172
  40.4 5.0 %copy-start.11 = (bf16[288,256]{1,0:T(8,128)(2,1)S(1)}, bf16[288,256]{1,0:T(8,128)(2,1)}, u32[]{:S(2)}) copy-start(bf16[288,256]{1,0:T(8,128)(2,1)} %get-tuple-element.33) | copy-start | bytes 442372
  40.4 6.7 %copy-start.10 = (bf16[288,256]{1,0:T(8,128)(2,1)S(1)}, bf16[288,256]{1,0:T(8,128)(2,1)}, u32[]{:S(2)}) copy-start(bf16[288,256]{1,0:T(8,128)(2,1)} %get-tuple-element.32) | copy-start | bytes 442372
  40.4 8.1 %copy-start.9 = (bf16[288,256]{1,0:T(8,128)(2,1)S(1)}, bf16[288,256]{1,0:T(8,128)(2,1)}, u32[]{:S(2)}) copy-start(bf16[288,256]{1,0:T(8,128)(2,1)} %get-tuple-element.31) | copy-start | bytes 442372
  40.4 10.4 %copy-start.4 = (bf16[288,256]{1,0:T(8,128)(2,1)S(1)}, bf16[288,256]{1,0:T(8,128)(2,1)}, u32[]{:S(2)}) copy-start(bf16[288,256]{1,0:T(8,128)(2,1)} %get-tuple-element.30.c0) | copy-start | bytes 442372
  40.4 30.7 %all-to-all-start.1 = ((bf16[4,4,272,256]{3,2,1,0:T(8,128)(2,1)}), bf16[4,4,272,256]{3,2,1,0:T(8,128)(2,1)}, u32[]{:S(2)}, u32[]{:S(2)}) async-start(bf16[4,4,272,256]{3,2,1,0:T(8,128)(2,1)} %broadcast_in_dim.15), calls=%async_computation.1 | async-start | bytes 4456448 | tf_op jit(solution)/shard_map/all_to_all | solution.py:270
  45.3 48.3 %all-gather.5.cloned.1.call-start = ((), (), s32[]{:S(2)}) async-start(), calls=%async_computation.11 | async-start | bytes 1966080 | tf_op jit(solution)/shard_map/all_gather | solution.py:279
  45.3 13.7 %collective-permute-start.2 = (bf16[288,256]{1,0:T(8,128)(2,1)S(1)}, bf16[288,256]{1,0:T(8,128)(2,1)S(1)}, u32[]{:S(2)}, u32[]{:S(2)}) collective-permute-start(bf16[288,256]{1,0:T(8,128)(2,1)S(1)} %copy-done.11), channel_id=1, source_target_pairs={{48,0},{50,2},{0,16},{2,18},{16,32},{18,34},{32,48},{34,50},{49,1}... | collective-permute-start | bytes 442376 | tf_op jit(solution)/shard_map/ppermute | solution.py:37
  47.0 14.5 %collective-permute-start.1 = (bf16[288,256]{1,0:T(8,128)(2,1)S(1)}, bf16[288,256]{1,0:T(8,128)(2,1)S(1)}, u32[]{:S(2)}, u32[]{:S(2)}) collective-permute-start(bf16[288,256]{1,0:T(8,128)(2,1)S(1)} %copy-done.10), channel_id=1, source_target_pairs={{32,0},{34,2},{48,16},{50,18},{0,32},{2,34},{16,48},{18,50},{33,1}... | collective-permute-start | bytes 442376 | tf_op jit(solution)/shard_map/ppermute | solution.py:37
  48.5 13.0 %collective-permute-start = (bf16[288,256]{1,0:T(8,128)(2,1)S(1)}, bf16[288,256]{1,0:T(8,128)(2,1)S(1)}, u32[]{:S(2)}, u32[]{:S(2)}) collective-permute-start(bf16[288,256]{1,0:T(8,128)(2,1)S(1)} %copy-done.9), channel_id=1, source_target_pairs={{16,0},{18,2},{32,16},{34,18},{48,32},{50,34},{0,48},{2,50},{17,1}... | collective-permute-start | bytes 442376 | tf_op jit(solution)/shard_map/ppermute | solution.py:37
  50.8 20.3 %collective-permute-start.7 = (bf16[3,272,256]{2,1,0:T(8,128)(2,1)S(1)}, bf16[3,272,256]{2,1,0:T(8,128)(2,1)S(1)}, u32[]{:S(2)}, u32[]{:S(2)}) collective-permute-start(bf16[3,272,256]{2,1,0:T(8,128)(2,1)S(1)} %pad_maximum_fusion.1), channel_id=1, source_target_pairs={{2,0},{0,2},{18,16},{16,18},{34,32},{32,34},{50,48},{48,50},{3,1},... | collective-permute-start | bytes 1253384 | tf_op jit(solution)/shard_map/ppermute | solution.py:37
  59.0 13.5 %copy-start.5 = (bf16[288,256]{1,0:T(8,128)(2,1)}, bf16[288,256]{1,0:T(8,128)(2,1)S(1)}, u32[]{:S(2)}) copy-start(bf16[288,256]{1,0:T(8,128)(2,1)S(1)} %collective-permute-done.2.c3) | copy-start | bytes 442372
  61.5 11.0 %copy-start.6 = (bf16[288,256]{1,0:T(8,128)(2,1)}, bf16[288,256]{1,0:T(8,128)(2,1)S(1)}, u32[]{:S(2)}) copy-start(bf16[288,256]{1,0:T(8,128)(2,1)S(1)} %collective-permute-done.1.c2) | copy-start | bytes 442372
  61.5 10.9 %copy-start.7 = (bf16[288,256]{1,0:T(8,128)(2,1)}, bf16[288,256]{1,0:T(8,128)(2,1)S(1)}, u32[]{:S(2)}) copy-start(bf16[288,256]{1,0:T(8,128)(2,1)S(1)} %collective-permute-done.c1) | copy-start | bytes 442372
  71.1 22.5 %collective-permute-start.9 = (bf16[4,4,272,256]{3,2,1,0:T(8,128)(2,1)}, bf16[4,4,272,256]{3,2,1,0:T(8,128)(2,1)}, u32[]{:S(2)}, u32[]{:S(2)}) collective-permute-start(bf16[4,4,272,256]{3,2,1,0:T(8,128)(2,1)} %all-to-all-done.1.refs_1_), channel_id=1, source_target_pairs={{0,1},{1,0},{2,3},{3,2},{4,5},{5,4},{6,7},{7,6},{8,9},{9,8},{10,11... | collective-permute-start | bytes 6684680 | tf_op jit(solution)/shard_map/ppermute | solution.py:41
  72.5 27.0 %all-to-all-start.2 = ((bf16[4,3,272,256]{3,2,1,0:T(8,128)(2,1)}), bf16[4,3,272,256]{3,2,1,0:T(8,128)(2,1)S(1)}, u32[]{:S(2)}, u32[]{:S(2)}) async-start(bf16[4,3,272,256]{3,2,1,0:T(8,128)(2,1)} %broadcast_in_dim.16), calls=%async_computation.2 | async-start | bytes 3342336 | tf_op jit(solution)/shard_map/all_to_all | solution.py:270
  77.3 2.0 collective-permute-start.8
  79.2 14.4 %copy-start.3 = (bf16[4,1,272,256]{3,2,1,0:T(8,128)(2,1)}, bf16[4,1,272,256]{3,2,1,0:T(8,128)(2,1)S(1)}, u32[]{:S(2)}) copy-start(bf16[4,1,272,256]{3,2,1,0:T(8,128)(2,1)S(1)} %collective-permute-done.8.refs_2_.refs_3_) | copy-start | bytes 1671172
  99.5 3.6 %collective-permute-start.10 = (bf16[4,3,272,256]{3,2,1,0:T(8,128)(2,1)S(1)}, bf16[4,3,272,256]{3,2,1,0:T(8,128)(2,1)S(1)}, u32[]{:S(2)}, u32[]{:S(2)}) collective-permute-start(bf16[4,3,272,256]{3,2,1,0:T(8,128)(2,1)S(1)} %all-to-all-done.2.refs_0_.refs_2_), channel_id=1, source_target_pairs={{0,1},{1,0},{2,3},{3,2},{4,5},{5,4},{6,7},{7,6},{8,9},{9,8},{10,11... | collective-permute-start | bytes 5013512 | tf_op jit(solution)/shard_map/ppermute | solution.py:41
  102.5 3.5 %copy-start = (f32[4,192,256]{2,1,0:T(8,128)S(1)}, f32[4,192,256]{2,1,0:T(8,128)}, u32[]{:S(2)}) copy-start(f32[4,192,256]{2,1,0:T(8,128)} %get-tuple-element.38.p0) | copy-start | bytes 2359300
  112.5 4.5 %copy-start.8 = (s32[2,4096]{1,0:T(2,128)S(1)}, s32[2,4096]{1,0:T(2,128)}, u32[]{:S(2)}) copy-start(s32[2,4096]{1,0:T(2,128)} %param.12) | copy-start | bytes 98308
  112.5 25.8 %all-to-all-start.3 = ((bf16[4,4,192,256]{3,2,1,0:T(8,128)(2,1)}), bf16[4,4,192,256]{3,2,1,0:T(8,128)(2,1)}, u32[]{:S(2)}, u32[]{:S(2)}) async-start(bf16[4,4,192,256]{3,2,1,0:T(8,128)(2,1)} %get-tuple-element.46), calls=%async_computation.3 | async-start | bytes 3145728 | tf_op jit(solution)/shard_map/all_to_all | solution.py:325
  116.9 53.3 %all-gather.7.cloned.1.call-start = ((), (), s32[]{:S(2)}) async-start(), calls=%async_computation.12 | async-start | bytes 1966080 | tf_op jit(solution)/shard_map/all_gather | solution.py:332
  141.5 9.8 %all-to-all-start.4 = ((f32[16,8,128]{2,1,0:T(8,128)}), f32[16,8,128]{2,1,0:T(8,128)}, u32[]{:S(2)}, u32[]{:S(2)}) async-start(f32[16,8,128]{2,1,0:T(8,128)} %broadcast_in_dim.17), calls=%async_computation.4 | async-start | bytes 131072 | tf_op jit(solution)/shard_map/all_to_all | solution.py:250
  152.8 24.1 %all-to-all-start.5 = ((f32[16,8,128]{2,1,0:T(8,128)}), f32[16,8,128]{2,1,0:T(8,128)}, u32[]{:S(2)}, u32[]{:S(2)}) async-start(f32[16,8,128]{2,1,0:T(8,128)} %broadcast_in_dim.18), calls=%async_computation.5 | async-start | bytes 131072 | tf_op jit(solution)/shard_map/all_to_all | solution.py:250
  159.7 55.6 %reduce-scatter.2.cloned.1.call-start = ((), (), s32[]{:S(2)}) async-start(), calls=%async_computation.10 | async-start | bytes 1966080 | tf_op jit(solution)/shard_map/reduce_scatter | solution.py:353
  215.3 19.2 %all-to-all-start.8 = ((bf16[4,192,256]{2,1,0:T(8,128)(2,1)}), bf16[4,192,256]{2,1,0:T(8,128)(2,1)S(1)}, u32[]{:S(2)}, u32[]{:S(2)}) async-start(bf16[4,192,256]{2,1,0:T(8,128)(2,1)} %bitcast.43), calls=%async_computation.9 | async-start | bytes 786432 | tf_op jit(solution)/shard_map/all_to_all | solution.py:356
Sparse Core Ops, SparseCore 0:
  62.5 31.0 all-gather.4
  141.0 29.2 all-gather.6
  186.8 28.4 reduce-scatter.1

commit v7 on v6

--- a/solution.py
+++ b/solution.py
@@ -204,10 +204,11 @@
         out[0, (zl ^ l) * 2 + (c ^ g)] = total.astype(BF)
 
 
-def outer2_kernel(parts, factor, ids, praw, rs, pa, c0, c1, c2, c3, w, asc, mask, *refs):
+def outer2_kernel(parts, radius, ids, totals, praw, rs, pa, c0, c1, c2, c3, w, asc, mask, *refs):
     toks, (out, dgp, d) = refs[: len(parts)], refs[len(parts) :]
     x, zh, zl, c = pl.program_id(0), ids[1], ids[3], ids[4]
-    f = factor[0]
+    total = jnp.sum(jnp.sum(jnp.sum(totals[...], axis=0), axis=0, keepdims=True), axis=1, keepdims=True)
+    f = radius[0] / (jnp.sqrt(total) + 1e-12)
 
     @pl.when(x == 0)
     def _():
@@ -223,18 +224,30 @@
         dgp[fb] = jnp.sum(wv * total, axis=0, keepdims=True)
 
 
-def ascent_kernel(ids, terms, gabs, mask, asc, part):
-    y = ids[0]
-    acc = jnp.zeros((8, BLK), F32)
-    for h in range(4):
-        total = terms[0, h].astype(F32)
-        for j in range(1, 4):
-            total = total + terms[j, h].astype(F32)
-        low = (total * gabs[y * 4 + h][0:1]).astype(BF)
-        asc[h] = low
-        wide = low.astype(F32)
-        acc = acc + jnp.sum((mask_rows(mask[y * 4 + h]) * wide * wide).reshape(ROWS // 8, 8, BLK), axis=0)
-    part[...] = acc[:, 0:128] + acc[:, 128:256]
+def ascent_kernel(ids, terms, gabs, mask, asc, part, acc):
+    h = pl.program_id(0)
+    fb = ids[0] * 4 + h
+    total = terms[0, 0].astype(F32)
+    for j in range(1, 4):
+        total = total + terms[j, 0].astype(F32)
+    low = (total * gabs[fb][0:1]).astype(BF)
+    asc[0] = low
+    wide = low.astype(F32)
+    here = jnp.sum((mask_rows(mask[fb]) * wide * wide).reshape(ROWS // 8, 8, BLK), axis=0)
+    here = here[:, 0:128] + here[:, 128:256]
+
+    @pl.when(h == 0)
+    def _():
+        acc[...] = here
+
+    @pl.when(h > 0)
+    def _():
+        acc[...] += here
+
+    @pl.when(h == 3)
+    def _():
+        for i in range(16):
+            part[i] = acc[...]
 
 
 def final_kernel(ids, gabs, sums, gate, up):
@@ -261,7 +274,7 @@
         [SMEM, whole((BLK, BLK)), whole((1, BLK))] + [whole((BLK, 4 * SUB))] * 3,
         (whole((PACK, BLK)), whole((4, 1, PACK, BLK))) + (whole(piece.shape),) * 4,
         scratch=[pltpu.VMEM((3, 4 * SUB, BLK), BF)],
-    )(ids, in_hbm(tokens), norm_gain[None, :], in_hbm(w_gate), in_hbm(w_up), in_hbm(cotangent))
+    )(ids, in_hbm(tokens), in_hbm(norm_gain[None, :]), in_hbm(w_gate), in_hbm(w_up), in_hbm(cotangent))
 
     def after(value, *others):
         return lax.optimization_barrier((value,) + others)[0]
@@ -325,12 +338,20 @@
     terms = lax.all_to_all(out1, "y", 0, 0, tiled=True)
     asc, part = call(
         ascent_kernel,
-        (hbm((4, ROWS, BLK), BF), shape((8, 128), F32)),
-        [SMEM, whole(oshape.shape), whole(gshape.shape), whole((NB, 2, BLK))],
-        (whole((4, ROWS, BLK)), whole((8, 128))),
+        (hbm((4, ROWS, BLK), BF), hbm((16, 8, 128), F32)),
+        [
+            SMEM,
+            pl.BlockSpec((4, 1, ROWS, BLK), lambda h: (0, h, 0, 0)),
+            whole(gshape.shape),
+            whole((NB, 2, BLK)),
+        ],
+        (by_x((ROWS, BLK)), whole((16, 8, 128))),
+        (4,),
+        [pltpu.VMEM((8, 128), F32)],
     )(ids, terms, gabs, mask)
     ascs = in_hbm(lax.all_gather(asc, "y", axis=0, tiled=False))
-    part = spread(jnp.sum(spread(part, MP), axis=0), DP)
+    part = lax.all_to_all(part, MP, 0, 0, tiled=True)
+    part = spread(jnp.sum(part, axis=0), DP)
     pa = call(
         functools.partial(pre2_kernel, parts),
         hbm(pshape.shape, F32),
@@ -339,17 +360,15 @@
         (4,),
         **cost,
     )(ids, ascs, mask, gabs, *tok_refs)
-    total = jnp.sum(after(part, pa))
-    factor = (radius[0] / (jnp.sqrt(total) + 1e-12))[None]
     out2, dgp = call(
         functools.partial(outer2_kernel, parts),
         (oshape, hbm((NB, 1, BLK), F32)),
-        [SMEM, SMEM, pspec, sspec, pspec] + [whole(piece.shape)] * 4 + [wspec, wspec, whole((NB, 2, BLK))] + tok_specs,
+        [SMEM, SMEM, whole((16, 8, 128)), pspec, sspec, pspec] + [whole(piece.shape)] * 4 + [wspec, wspec, whole((NB, 2, BLK))] + tok_specs,
         (by_x((4, ROWS, BLK)), whole((NB, 1, BLK))),
         (4,),
         dscratch,
         **cost,
-    )(factor, ids, in_hbm(praw), in_hbm(rs), in_hbm(pa), *pieces, weights, ascs, mask, *tok_refs)
+    )(radius, ids, after(part, pa), in_hbm(praw), in_hbm(rs), in_hbm(pa), *pieces, weights, ascs, mask, *tok_refs)
     sums = lax.psum_scatter(out2, "y", scatter_dimension=0, tiled=False)
     dg = jnp.sum(lax.all_to_all(dgp, MP, 0, 0, tiled=True), axis=0)
     grad_gain = jnp.sum(spread(dg, DP).reshape(16, BLK), axis=0)

time: 244 us -> 242 us (level)
    all_to_all x0 -> x1, starting transfers between devices: none -> 5.82 us  [body(): part = lax.all_to_all(part, MP, 0, 0, tiled=True)]
    all_to_all x2 -> x1, starting transfers between devices: 12.7 us -> 6.87 us  [spread(): lax.all_to_all(jnp.broadcast_to(value[None], (n,) + value.shape), axes, 0...]
    all_to_all x0 -> x1, waiting for transfers between devices: none -> 3.35 us  [body(): part = lax.all_to_all(part, MP, 0, 0, tiled=True)]
    all_to_all x2 -> x1, waiting for transfers between devices: 3.36 us -> 0.01 us  [spread(): lax.all_to_all(jnp.broadcast_to(value[None], (n,) + value.shape), axes, 0...]
where the time goes in v7:
time: 242 us; the launch traced here: 241 us
  waiting for transfers between devices  95.2 us (39%)
  starting transfers between devices  57.6 us (24%)
  Pallas kernels  40.6 us (17%)
  blocking collectives  26.8 us (11%)
  between operations  14.6 us (6%)
  local copies, waits for them, and re-layouts  3.73 us (2%)
  other arithmetic  2.43 us (1%)
    ppermute x8, waiting for transfers between devices, from_z(): return lax.ppermute(value, ('zh', 'zl'), pairs)  29.4 us
    all_to_all x1, waiting for transfers between devices, body(): terms = lax.all_to_all(out1, 'y', 0, 0, tiled=True)  21.4 us
    ppermute x8, starting transfers between devices, from_z(): return lax.ppermute(value, ('zh', 'zl'), pairs)  17.9 us
    all_to_all x1, blocking collectives, spread(): lax.all_to_all(jnp.broadcast_to(value[None], (n,) + value.shape), axes, 0...  17.2 us
    all_gather x1, waiting for transfers between devices, body(): weights = in_hbm(lax.all_gather(part_w, 'y', axis=0, tiled=False))  14.4 us
    pallas_call x3, Pallas kernels, pre(): call(functools.partial(pre_kernel, parts, with_gain), outs, [SMEM, wspec]...  12 us
    all_to_all x1, waiting for transfers between devices, body(): sums = lax.all_to_all(sums, 'zh', 0, 0, tiled=True)  11.6 us
    all_gather x1, waiting for transfers between devices, body(): ascs = in_hbm(lax.all_gather(asc, 'y', axis=0, tiled=False))  11 us
  transfers between devices with their start and end apart: 21, of which 14 were waited for; matrix products, arithmetic and copies ran while one was open for 2% of the time, Pallas kernels for 6%

profile of v7, /device:TPU:4, one launch (start us, length us, event | category | flops | bytes accessed | tf_op | source)
XLA Modules:
  0.0 240.9 jit_solution(17345999211754902611)
XLA Ops:
  7.2 0.1 stack.59.ids
  7.3 2.5 %shard_map.94 = (bf16[272,256]{1,0:T(8,128)(2,1)}, bf16[4,1,272,256]{3,2,1,0:T(8,128)(2,1)}, bf16[288,256]{1,0:T(8,128)(2,1)}, bf16[288,256]{1,0:T(8,128)(2,1)},...) custom-call(s32[5]{0:T(128)S(1)} %stack.59.ids, bf16[256,256]{1,0:T(8,128)(2,1)} %tokens.1, f32[1,256]{1,0:T(1,128)} %bitcast.41, ...), custom_call_target="tpu_custom_call" | custom-call | flops 1000000 | bytes 1000000 | tf_op jit(solution)/shard_map/pallas_call | solution.py:271
  9.8 5.7 %all-to-all-start = ((bf16[4,1,272,256]{3,2,1,0:T(8,128)(2,1)}), bf16[4,1,272,256]{3,2,1,0:T(8,128)(2,1)S(1)}, u32[]{:S(2)}, u32[]{:S(2)}) async-start(bf16[4,1,272,256]{3,2,1,0:T(8,128)(2,1)} %get-tuple-element.34), calls=%async_computation | async-start | bytes 1114112 | tf_op jit(solution)/shard_map/all_to_all | solution.py:287
  15.5 5.4 %collective-permute-start.3 = (bf16[272,256]{1,0:T(8,128)(2,1)}, bf16[272,256]{1,0:T(8,128)(2,1)S(1)}, u32[]{:S(2)}, u32[]{:S(2)}) collective-permute-start(bf16[272,256]{1,0:T(8,128)(2,1)} %get-tuple-element.35), channel_id=1, source_target_pairs={{16,0},{18,2},{32,16},{34,18},{48,32},{50,34},{0,48},{2,50},{17,1}... | collective-permute-start | bytes 417800 | tf_op jit(solution)/shard_map/ppermute | solution.py:37
  20.9 3.8 %collective-permute-start.5 = (bf16[272,256]{1,0:T(8,128)(2,1)}, bf16[272,256]{1,0:T(8,128)(2,1)S(1)}, u32[]{:S(2)}, u32[]{:S(2)}) collective-permute-start(bf16[272,256]{1,0:T(8,128)(2,1)} %get-tuple-element.35), channel_id=1, source_target_pairs={{32,0},{34,2},{48,16},{50,18},{0,32},{2,34},{16,48},{18,50},{33,1}... | collective-permute-start | bytes 417800 | tf_op jit(solution)/shard_map/ppermute | solution.py:37
  24.7 1.0 collective-permute-start.6
  25.7 5.5 %collective-permute-done.3 = bf16[272,256]{1,0:T(8,128)(2,1)S(1)} collective-permute-done((bf16[272,256]{1,0:T(8,128)(2,1)}, bf16[272,256]{1,0:T(8,128)(2,1)S(1)}, u32[]{:S(2)}, u32[]{:S(2)}) %collective-permute-start.3) | collective-permute-done | bytes 139296 | tf_op jit(solution)/shard_map/ppermute | solution.py:37
  31.2 2.6 %collective-permute-done.4 = bf16[272,256]{1,0:T(8,128)(2,1)S(1)} collective-permute-done((bf16[272,256]{1,0:T(8,128)(2,1)}, bf16[272,256]{1,0:T(8,128)(2,1)S(1)}, u32[]{:S(2)}, u32[]{:S(2)}) %collective-permute-start.4) | collective-permute-done | bytes 139296 | tf_op jit(solution)/shard_map/ppermute | solution.py:37
  33.8 4.2 %collective-permute-done.5 = bf16[272,256]{1,0:T(8,128)(2,1)S(1)} collective-permute-done((bf16[272,256]{1,0:T(8,128)(2,1)}, bf16[272,256]{1,0:T(8,128)(2,1)S(1)}, u32[]{:S(2)}, u32[]{:S(2)}) %collective-permute-start.5) | collective-permute-done | bytes 139296 | tf_op jit(solution)/shard_map/ppermute | solution.py:37
  38.0 0.1 pad_maximum_fusion
  38.1 1.6 broadcast_in_dim.11
  39.7 4.9 %all-to-all-start.1 = ((bf16[4,4,272,256]{3,2,1,0:T(8,128)(2,1)}), bf16[4,4,272,256]{3,2,1,0:T(8,128)(2,1)}, u32[]{:S(2)}, u32[]{:S(2)}) async-start(bf16[4,4,272,256]{3,2,1,0:T(8,128)(2,1)} %broadcast_in_dim.11), calls=%async_computation.1 | async-start | bytes 4456448 | tf_op jit(solution)/shard_map/all_to_all | solution.py:283
  44.6 1.7 collective-permute-start.2
  46.3 1.4 collective-permute-start.1
  47.8 2.2 collective-permute-start
  50.1 2.2 collective-permute-start.7
  52.3 5.9 %collective-permute-done.2.c3 = bf16[288,256]{1,0:T(8,128)(2,1)S(1)} collective-permute-done((bf16[288,256]{1,0:T(8,128)(2,1)S(1)}, bf16[288,256]{1,0:T(8,128)(2,1)S(1)}, u32[]{:S(2)}, u32[]{:S(2)}) %collective-permute-start.2) | collective-permute-done | bytes 147488 | tf_op jit(solution)/shard_map/ppermute | solution.py:37
  58.2 2.6 %collective-permute-done.1.c2 = bf16[288,256]{1,0:T(8,128)(2,1)S(1)} collective-permute-done((bf16[288,256]{1,0:T(8,128)(2,1)S(1)}, bf16[288,256]{1,0:T(8,128)(2,1)S(1)}, u32[]{:S(2)}, u32[]{:S(2)}) %collective-permute-start.1) | collective-permute-done | bytes 147488 | tf_op jit(solution)/shard_map/ppermute | solution.py:37
  60.8 0.8 pad_maximum_fusion.2
  61.7 8.7 %collective-permute-done.7 = bf16[3,272,256]{2,1,0:T(8,128)(2,1)S(1)} collective-permute-done((bf16[3,272,256]{2,1,0:T(8,128)(2,1)S(1)}, bf16[3,272,256]{2,1,0:T(8,128)(2,1)S(1)}, u32[]{:S(2)}, u32[]{:S(2)}) %collective-permute-start.7) | collective-permute-done | bytes 417824 | tf_op jit(solution)/shard_map/ppermute | solution.py:37
  70.4 1.4 broadcast_in_dim.12
  71.7 4.8 %all-to-all-start.2 = ((bf16[4,3,272,256]{3,2,1,0:T(8,128)(2,1)}), bf16[4,3,272,256]{3,2,1,0:T(8,128)(2,1)S(1)}, u32[]{:S(2)}, u32[]{:S(2)}) async-start(bf16[4,3,272,256]{3,2,1,0:T(8,128)(2,1)} %broadcast_in_dim.12), calls=%async_computation.2 | async-start | bytes 3342336 | tf_op jit(solution)/shard_map/all_to_all | solution.py:283
  76.5 2.0 collective-permute-done.8.refs_2_.refs_3_
  78.5 14.4 %all-gather.5.cloned.1.call-done = bf16[16,192,256]{2,1,0:T(8,128)(2,1)} async-done(((bf16[4,192,256]{2,1,0:T(8,128)(2,1)}), bf16[16,192,256]{2,1,0:T(8,128)(2,1)}) %all-gather.5.cloned.1.call-update) | async-done | bytes 1572880 | tf_op jit(solution)/shard_map/all_gather | solution.py:292
  92.9 5.9 %shard_map.95 = (f32[4,192,256]{2,1,0:T(8,128)}, f32[4,8,256]{2,1,0:T(8,128)S(1)}, f32[16,8,256]{2,1,0:T(8,128)S(1)}) custom-call(s32[5]{0:T(128)S(1)} %stack.59.ids, bf16[4,4,192,256]{3,2,1,0:T(8,128)(2,1)} %bitcast.27, bf16[4,1,272,256]{3,2,1,0:T(8,128)(2,1)} %copy-done.1, bf16[4,4,272,256]{3,2,1,0:T(8,128)(2,1)} %all-to-all-done.1.refs_1_, ...), custom_call_target="tpu_custom_call" | custom-call | flops 1006632960 | bytes 5570560 | tf_op jit(solution)/shard_map/pallas_call | solution.py:306
  98.8 3.0 %shard_map.96 = (f32[4,192,256]{2,1,0:T(8,128)S(1)}, f32[4,8,256]{2,1,0:T(8,128)S(1)}) custom-call(s32[5]{0:T(128)S(1)} %stack.59.ids, bf16[4,4,192,256]{3,2,1,0:T(8,128)(2,1)} %bitcast.28, bf16[4,3,272,256]{3,2,1,0:T(8,128)(2,1)S(1)} %all-to-all-done.2.refs_0_.refs_2_), custom_call_target="tpu_custom_call" | custom-call | flops 301989888 | bytes 1671168 | tf_op jit(solution)/shard_map/pallas_call | solution.py:306
  101.9 0.5 collective-permute-done.10.refs_0_.refs_5_
  102.4 3.0 %shard_map.97 = (f32[4,192,256]{2,1,0:T(8,128)S(1)}, f32[4,8,256]{2,1,0:T(8,128)S(1)}) custom-call(s32[5]{0:T(128)S(1)} %stack.59.ids, bf16[4,4,192,256]{3,2,1,0:T(8,128)(2,1)} %bitcast.29, bf16[4,3,272,256]{3,2,1,0:T(8,128)(2,1)S(1)} %collective-permute-done.10.refs_0_.refs_5_), custom_call_target="tpu_custom_call" | custom-call | flops 301989888 | bytes 1671168 | tf_op jit(solution)/shard_map/pallas_call | solution.py:306
  105.4 6.5 %shard_map.98 = (bf16[4,4,192,256]{3,2,1,0:T(8,128)(2,1)}, f32[4,192,256]{2,1,0:T(8,128)}, f32[4,8,256]{2,1,0:T(8,128)}) custom-call(s32[5]{0:T(128)S(1)} %stack.59.ids, f32[4,192,256]{2,1,0:T(8,128)S(1)} %copy-done, f32[4,192,256]{2,1,0:T(8,128)S(1)} %get-tuple-element.41.p1, f32[4,192,256]{2,1,0:T(8,128)S(1)} %get-tuple-element.42.p2, ...), custom_call_target="tpu_custom_call" | custom-call | flops 1610612736 | bytes 12000000 | tf_op jit(solution)/shard_map/pallas_call | solution.py:329
  111.9 4.4 %all-to-all-start.3 = ((bf16[4,4,192,256]{3,2,1,0:T(8,128)(2,1)}), bf16[4,4,192,256]{3,2,1,0:T(8,128)(2,1)}, u32[]{:S(2)}, u32[]{:S(2)}) async-start(bf16[4,4,192,256]{3,2,1,0:T(8,128)(2,1)} %get-tuple-element.46), calls=%async_computation.3 | async-start | bytes 3145728 | tf_op jit(solution)/shard_map/all_to_all | solution.py:338
  116.4 21.4 %all-to-all-done.3.terms = bf16[4,4,192,256]{3,2,1,0:T(8,128)(2,1)} async-done(((bf16[4,4,192,256]{3,2,1,0:T(8,128)(2,1)}), bf16[4,4,192,256]{3,2,1,0:T(8,128)(2,1)}, u32[]{:S(2)}, u32[]{:S(2)}) %all-to-all-start.3) | async-done | bytes 1572896 | tf_op jit(solution)/shard_map/all_to_all | solution.py:338
  137.7 3.5 %shard_map.99 = (bf16[4,192,256]{2,1,0:T(8,128)(2,1)}, f32[16,8,128]{2,1,0:T(8,128)}) custom-call(s32[5]{0:T(128)S(1)} %stack.59.ids, bf16[4,4,192,256]{3,2,1,0:T(8,128)(2,1)} %all-to-all-done.3.terms, f32[16,8,256]{2,1,0:T(8,128)S(1)} %get-tuple-element.47.gabs, f32[16,2,256]{2,1,0:T(2,128)S(1)} %bitcast.24), custom_call_target="tpu_custom_call" | custom-call | flops 1000000 | bytes 1000000 | tf_op jit(solution)/shard_map/pallas_call | solution.py:339
  141.3 5.8 %all-to-all-start.4 = ((f32[16,8,128]{2,1,0:T(8,128)}), f32[16,8,128]{2,1,0:T(8,128)}, u32[]{:S(2)}, u32[]{:S(2)}) async-start(f32[16,8,128]{2,1,0:T(8,128)} %get-tuple-element.48), calls=%async_computation.4 | async-start | bytes 131072 | tf_op jit(solution)/shard_map/all_to_all | solution.py:353
  147.8 3.4 %all-to-all-done.4 = f32[16,8,128]{2,1,0:T(8,128)} async-done(((f32[16,8,128]{2,1,0:T(8,128)}), f32[16,8,128]{2,1,0:T(8,128)}, u32[]{:S(2)}, u32[]{:S(2)}) %all-to-all-start.4) | async-done | bytes 65568 | tf_op jit(solution)/shard_map/all_to_all | solution.py:353
  151.1 0.9 reduce_sum.27
  152.0 0.6 broadcast_in_dim.13
  152.6 6.9 %all-to-all-start.5 = ((f32[16,8,128]{2,1,0:T(8,128)}), f32[16,8,128]{2,1,0:T(8,128)}, u32[]{:S(2)}, u32[]{:S(2)}) async-start(f32[16,8,128]{2,1,0:T(8,128)} %broadcast_in_dim.13), calls=%async_computation.5 | async-start | bytes 131072 | tf_op jit(solution)/shard_map/all_to_all | solution.py:263
  159.5 0.2 reduce-scatter.2.cloned.1.call-start
  159.7 11.0 %all-gather.7.cloned.1.call-done = bf16[16,192,256]{2,1,0:T(8,128)(2,1)} async-done(((bf16[4,192,256]{2,1,0:T(8,128)(2,1)}), bf16[16,192,256]{2,1,0:T(8,128)(2,1)}) %all-gather.7.cloned.1.call-update) | async-done | bytes 1572880 | tf_op jit(solution)/shard_map/all_gather | solution.py:352
  170.7 6.6 %shard_map.100.pa = f32[4,192,256]{2,1,0:T(8,128)} custom-call(s32[5]{0:T(128)S(1)} %stack.59.ids, bf16[4,4,192,256]{3,2,1,0:T(8,128)(2,1)} %bitcast.31, f32[16,2,256]{2,1,0:T(2,128)S(1)} %bitcast.25, f32[16,8,256]{2,1,0:T(8,128)S(1)} %get-tuple-element.47.gabs, bf16[4,1,272,256]{3,2,1,0:T(8,128)(2,1)} %copy-done.1, ...), custom_call_target="tpu_custom_call" | custom-call | flops 1610612736 | bytes 12000000 | tf_op jit(solution)/shard_map/pallas_call | solution.py:355
  177.3 7.8 %shard_map.101 = (bf16[4,4,192,256]{3,2,1,0:T(8,128)(2,1)}, f32[16,1,256]{2,1,0:T(1,128)}) custom-call(f32[1]{0:T(128)S(6)} %copy.12.radius, s32[5]{0:T(128)S(1)} %stack.59.ids, f32[16,8,128]{2,1,0:T(8,128)} %all-to-all-done.5.totals, f32[4,192,256]{2,1,0:T(8,128)} %get-tuple-element.51.praw, f32[4,8,256]{2,1,0:T(8,128)} %get-tuple-element.52.rs, ...), custom_call_target="tpu_custom_call" | custom-call | flops 1610612736 | bytes 12000000 | tf_op jit(solution)/shard_map/pallas_call | solution.py:363
  185.2 9.6 %all_to_all.45 = f32[16,1,256]{2,1,0:T(1,128)S(1)} all-to-all(f32[16,1,256]{2,1,0:T(1,128)} %get-tuple-element.53), channel_id=1, replica_groups=mesh['y'=4,'zh'=4,'x'=4,'zl'=2,'c'=2] {'x','zl','c'}, dimensions={0} | all-to-all | bytes 32768 | tf_op jit(solution)/shard_map/all_to_all | solution.py:373
  194.9 17.2 %all_to_all.46 = f32[16,1,256]{2,1,0:T(1,128)S(1)} all-to-all(f32[16,1,256]{2,1,0:T(1,128)S(1)} %broadcast_in_dim.14), channel_id=1, replica_groups=mesh['y'=4,'zh'=4,'x'=4,'zl'=2,'c'=2] {'y','zh'}, dimensions={0} | all-to-all | bytes 32768 | tf_op jit(solution)/shard_map/all_to_all | solution.py:263
  212.1 1.6 reduce-scatter.2.cloned.1.call-done
  213.7 6.9 %all-to-all-start.8 = ((bf16[4,192,256]{2,1,0:T(8,128)(2,1)}), bf16[4,192,256]{2,1,0:T(8,128)(2,1)S(1)}, u32[]{:S(2)}, u32[]{:S(2)}) async-start(bf16[4,192,256]{2,1,0:T(8,128)(2,1)} %bitcast.39), calls=%async_computation.9 | async-start | bytes 786432 | tf_op jit(solution)/shard_map/all_to_all | solution.py:375
  220.6 0.6 reduce_sum.29
  221.2 11.6 %all-to-all-done.8.sums = bf16[4,192,256]{2,1,0:T(8,128)(2,1)S(1)} async-done(((bf16[4,192,256]{2,1,0:T(8,128)(2,1)}), bf16[4,192,256]{2,1,0:T(8,128)(2,1)S(1)}, u32[]{:S(2)}, u32[]{:S(2)}) %all-to-all-start.8) | async-done | bytes 393248 | tf_op jit(solution)/shard_map/all_to_all | solution.py:375
  232.8 1.6 shard_map.102
  (46 shorter events, 0.3 us)
Async XLA Ops:
  9.8 28.3 %all-to-all-start = ((bf16[4,1,272,256]{3,2,1,0:T(8,128)(2,1)}), bf16[4,1,272,256]{3,2,1,0:T(8,128)(2,1)S(1)}, u32[]{:S(2)}, u32[]{:S(2)}) async-start(bf16[4,1,272,256]{3,2,1,0:T(8,128)(2,1)} %get-tuple-element.34), calls=%async_computation | async-start | bytes 1114112 | tf_op jit(solution)/shard_map/all_to_all | solution.py:287
  15.5 15.7 %collective-permute-start.3 = (bf16[272,256]{1,0:T(8,128)(2,1)}, bf16[272,256]{1,0:T(8,128)(2,1)S(1)}, u32[]{:S(2)}, u32[]{:S(2)}) collective-permute-start(bf16[272,256]{1,0:T(8,128)(2,1)} %get-tuple-element.35), channel_id=1, source_target_pairs={{16,0},{18,2},{32,16},{34,18},{48,32},{50,34},{0,48},{2,50},{17,1}... | collective-permute-start | bytes 417800 | tf_op jit(solution)/shard_map/ppermute | solution.py:37
  20.9 12.9 %collective-permute-start.4 = (bf16[272,256]{1,0:T(8,128)(2,1)}, bf16[272,256]{1,0:T(8,128)(2,1)S(1)}, u32[]{:S(2)}, u32[]{:S(2)}) collective-permute-start(bf16[272,256]{1,0:T(8,128)(2,1)} %get-tuple-element.35), channel_id=1, source_target_pairs={{48,0},{50,2},{0,16},{2,18},{16,32},{18,34},{32,48},{34,50},{49,1}... | collective-permute-start | bytes 417800 | tf_op jit(solution)/shard_map/ppermute | solution.py:37
  20.9 17.1 %collective-permute-start.5 = (bf16[272,256]{1,0:T(8,128)(2,1)}, bf16[272,256]{1,0:T(8,128)(2,1)S(1)}, u32[]{:S(2)}, u32[]{:S(2)}) collective-permute-start(bf16[272,256]{1,0:T(8,128)(2,1)} %get-tuple-element.35), channel_id=1, source_target_pairs={{32,0},{34,2},{48,16},{50,18},{0,32},{2,34},{16,48},{18,50},{33,1}... | collective-permute-start | bytes 417800 | tf_op jit(solution)/shard_map/ppermute | solution.py:37
  24.7 13.3 %collective-permute-start.6 = (bf16[272,256]{1,0:T(8,128)(2,1)}, bf16[272,256]{1,0:T(8,128)(2,1)S(1)}, u32[]{:S(2)}, u32[]{:S(2)}) collective-permute-start(bf16[272,256]{1,0:T(8,128)(2,1)} %get-tuple-element.35), channel_id=1, source_target_pairs={{2,0},{0,2},{18,16},{16,18},{34,32},{32,34},{50,48},{48,50},{3,1},... | collective-permute-start | bytes 417800 | tf_op jit(solution)/shard_map/ppermute | solution.py:37
  38.1 38.5 %copy-start.1 = (bf16[4,1,272,256]{3,2,1,0:T(8,128)(2,1)}, bf16[4,1,272,256]{3,2,1,0:T(8,128)(2,1)S(1)}, u32[]{:S(2)}) copy-start(bf16[4,1,272,256]{3,2,1,0:T(8,128)(2,1)S(1)} %all-to-all-done.refs_0_) | copy-start | bytes 1671172
  39.6 5.0 %copy-start.10 = (bf16[288,256]{1,0:T(8,128)(2,1)S(1)}, bf16[288,256]{1,0:T(8,128)(2,1)}, u32[]{:S(2)}) copy-start(bf16[288,256]{1,0:T(8,128)(2,1)} %get-tuple-element.33) | copy-start | bytes 442372
  39.7 6.7 %copy-start.9 = (bf16[288,256]{1,0:T(8,128)(2,1)S(1)}, bf16[288,256]{1,0:T(8,128)(2,1)}, u32[]{:S(2)}) copy-start(bf16[288,256]{1,0:T(8,128)(2,1)} %get-tuple-element.32) | copy-start | bytes 442372
  39.7 8.1 %copy-start.8 = (bf16[288,256]{1,0:T(8,128)(2,1)S(1)}, bf16[288,256]{1,0:T(8,128)(2,1)}, u32[]{:S(2)}) copy-start(bf16[288,256]{1,0:T(8,128)(2,1)} %get-tuple-element.31) | copy-start | bytes 442372
  39.7 10.4 %copy-start.3 = (bf16[288,256]{1,0:T(8,128)(2,1)S(1)}, bf16[288,256]{1,0:T(8,128)(2,1)}, u32[]{:S(2)}) copy-start(bf16[288,256]{1,0:T(8,128)(2,1)} %get-tuple-element.30.c0) | copy-start | bytes 442372
  39.7 30.7 %all-to-all-start.1 = ((bf16[4,4,272,256]{3,2,1,0:T(8,128)(2,1)}), bf16[4,4,272,256]{3,2,1,0:T(8,128)(2,1)}, u32[]{:S(2)}, u32[]{:S(2)}) async-start(bf16[4,4,272,256]{3,2,1,0:T(8,128)(2,1)} %broadcast_in_dim.11), calls=%async_computation.1 | async-start | bytes 4456448 | tf_op jit(solution)/shard_map/all_to_all | solution.py:283
  44.6 48.3 %all-gather.5.cloned.1.call-start = ((), (), s32[]{:S(2)}) async-start(), calls=%async_computation.11 | async-start | bytes 1966080 | tf_op jit(solution)/shard_map/all_gather | solution.py:292
  44.6 13.6 %collective-permute-start.2 = (bf16[288,256]{1,0:T(8,128)(2,1)S(1)}, bf16[288,256]{1,0:T(8,128)(2,1)S(1)}, u32[]{:S(2)}, u32[]{:S(2)}) collective-permute-start(bf16[288,256]{1,0:T(8,128)(2,1)S(1)} %copy-done.10), channel_id=1, source_target_pairs={{48,0},{50,2},{0,16},{2,18},{16,32},{18,34},{32,48},{34,50},{49,1}... | collective-permute-start | bytes 442376 | tf_op jit(solution)/shard_map/ppermute | solution.py:37
  46.3 14.5 %collective-permute-start.1 = (bf16[288,256]{1,0:T(8,128)(2,1)S(1)}, bf16[288,256]{1,0:T(8,128)(2,1)S(1)}, u32[]{:S(2)}, u32[]{:S(2)}) collective-permute-start(bf16[288,256]{1,0:T(8,128)(2,1)S(1)} %copy-done.9), channel_id=1, source_target_pairs={{32,0},{34,2},{48,16},{50,18},{0,32},{2,34},{16,48},{18,50},{33,1}... | collective-permute-start | bytes 442376 | tf_op jit(solution)/shard_map/ppermute | solution.py:37
  47.8 13.0 %collective-permute-start = (bf16[288,256]{1,0:T(8,128)(2,1)S(1)}, bf16[288,256]{1,0:T(8,128)(2,1)S(1)}, u32[]{:S(2)}, u32[]{:S(2)}) collective-permute-start(bf16[288,256]{1,0:T(8,128)(2,1)S(1)} %copy-done.8), channel_id=1, source_target_pairs={{16,0},{18,2},{32,16},{34,18},{48,32},{50,34},{0,48},{2,50},{17,1}... | collective-permute-start | bytes 442376 | tf_op jit(solution)/shard_map/ppermute | solution.py:37
  50.1 20.3 %collective-permute-start.7 = (bf16[3,272,256]{2,1,0:T(8,128)(2,1)S(1)}, bf16[3,272,256]{2,1,0:T(8,128)(2,1)S(1)}, u32[]{:S(2)}, u32[]{:S(2)}) collective-permute-start(bf16[3,272,256]{2,1,0:T(8,128)(2,1)S(1)} %pad_maximum_fusion.1), channel_id=1, source_target_pairs={{2,0},{0,2},{18,16},{16,18},{34,32},{32,34},{50,48},{48,50},{3,1},... | collective-permute-start | bytes 1253384 | tf_op jit(solution)/shard_map/ppermute | solution.py:37
  58.2 13.5 %copy-start.4 = (bf16[288,256]{1,0:T(8,128)(2,1)}, bf16[288,256]{1,0:T(8,128)(2,1)S(1)}, u32[]{:S(2)}) copy-start(bf16[288,256]{1,0:T(8,128)(2,1)S(1)} %collective-permute-done.2.c3) | copy-start | bytes 442372
  60.8 10.9 %copy-start.5 = (bf16[288,256]{1,0:T(8,128)(2,1)}, bf16[288,256]{1,0:T(8,128)(2,1)S(1)}, u32[]{:S(2)}) copy-start(bf16[288,256]{1,0:T(8,128)(2,1)S(1)} %collective-permute-done.1.c2) | copy-start | bytes 442372
  60.8 10.9 %copy-start.6 = (bf16[288,256]{1,0:T(8,128)(2,1)}, bf16[288,256]{1,0:T(8,128)(2,1)S(1)}, u32[]{:S(2)}) copy-start(bf16[288,256]{1,0:T(8,128)(2,1)S(1)} %collective-permute-done.c1) | copy-start | bytes 442372
  70.4 22.5 %collective-permute-start.9 = (bf16[4,4,272,256]{3,2,1,0:T(8,128)(2,1)}, bf16[4,4,272,256]{3,2,1,0:T(8,128)(2,1)}, u32[]{:S(2)}, u32[]{:S(2)}) collective-permute-start(bf16[4,4,272,256]{3,2,1,0:T(8,128)(2,1)} %all-to-all-done.1.refs_1_), channel_id=1, source_target_pairs={{0,1},{1,0},{2,3},{3,2},{4,5},{5,4},{6,7},{7,6},{8,9},{9,8},{10,11... | collective-permute-start | bytes 6684680 | tf_op jit(solution)/shard_map/ppermute | solution.py:41
  71.7 27.1 %all-to-all-start.2 = ((bf16[4,3,272,256]{3,2,1,0:T(8,128)(2,1)}), bf16[4,3,272,256]{3,2,1,0:T(8,128)(2,1)S(1)}, u32[]{:S(2)}, u32[]{:S(2)}) async-start(bf16[4,3,272,256]{3,2,1,0:T(8,128)(2,1)} %broadcast_in_dim.12), calls=%async_computation.2 | async-start | bytes 3342336 | tf_op jit(solution)/shard_map/all_to_all | solution.py:283
  76.5 2.0 collective-permute-start.8
  78.5 14.4 %copy-start.2 = (bf16[4,1,272,256]{3,2,1,0:T(8,128)(2,1)}, bf16[4,1,272,256]{3,2,1,0:T(8,128)(2,1)S(1)}, u32[]{:S(2)}) copy-start(bf16[4,1,272,256]{3,2,1,0:T(8,128)(2,1)S(1)} %collective-permute-done.8.refs_2_.refs_3_) | copy-start | bytes 1671172
  98.8 3.6 %collective-permute-start.10 = (bf16[4,3,272,256]{3,2,1,0:T(8,128)(2,1)S(1)}, bf16[4,3,272,256]{3,2,1,0:T(8,128)(2,1)S(1)}, u32[]{:S(2)}, u32[]{:S(2)}) collective-permute-start(bf16[4,3,272,256]{3,2,1,0:T(8,128)(2,1)S(1)} %all-to-all-done.2.refs_0_.refs_2_), channel_id=1, source_target_pairs={{0,1},{1,0},{2,3},{3,2},{4,5},{5,4},{6,7},{7,6},{8,9},{9,8},{10,11... | collective-permute-start | bytes 5013512 | tf_op jit(solution)/shard_map/ppermute | solution.py:41
  101.9 3.5 %copy-start = (f32[4,192,256]{2,1,0:T(8,128)S(1)}, f32[4,192,256]{2,1,0:T(8,128)}, u32[]{:S(2)}) copy-start(f32[4,192,256]{2,1,0:T(8,128)} %get-tuple-element.38.p0) | copy-start | bytes 2359300
  111.9 4.5 %copy-start.7 = (s32[2,4096]{1,0:T(2,128)S(1)}, s32[2,4096]{1,0:T(2,128)}, u32[]{:S(2)}) copy-start(s32[2,4096]{1,0:T(2,128)} %param.12) | copy-start | bytes 98308
  111.9 25.8 %all-to-all-start.3 = ((bf16[4,4,192,256]{3,2,1,0:T(8,128)(2,1)}), bf16[4,4,192,256]{3,2,1,0:T(8,128)(2,1)}, u32[]{:S(2)}, u32[]{:S(2)}) async-start(bf16[4,4,192,256]{3,2,1,0:T(8,128)(2,1)} %get-tuple-element.46), calls=%async_computation.3 | async-start | bytes 3145728 | tf_op jit(solution)/shard_map/all_to_all | solution.py:338
  116.3 54.4 %all-gather.7.cloned.1.call-start = ((), (), s32[]{:S(2)}) async-start(), calls=%async_computation.12 | async-start | bytes 1966080 | tf_op jit(solution)/shard_map/all_gather | solution.py:352
  141.3 9.8 %all-to-all-start.4 = ((f32[16,8,128]{2,1,0:T(8,128)}), f32[16,8,128]{2,1,0:T(8,128)}, u32[]{:S(2)}, u32[]{:S(2)}) async-start(f32[16,8,128]{2,1,0:T(8,128)} %get-tuple-element.48), calls=%async_computation.4 | async-start | bytes 131072 | tf_op jit(solution)/shard_map/all_to_all | solution.py:353
  152.6 24.7 %all-to-all-start.5 = ((f32[16,8,128]{2,1,0:T(8,128)}), f32[16,8,128]{2,1,0:T(8,128)}, u32[]{:S(2)}, u32[]{:S(2)}) async-start(f32[16,8,128]{2,1,0:T(8,128)} %broadcast_in_dim.13), calls=%async_computation.5 | async-start | bytes 131072 | tf_op jit(solution)/shard_map/all_to_all | solution.py:263
  159.5 54.2 %reduce-scatter.2.cloned.1.call-start = ((), (), s32[]{:S(2)}) async-start(), calls=%async_computation.10 | async-start | bytes 1966080 | tf_op jit(solution)/shard_map/reduce_scatter | solution.py:372
  213.7 19.1 %all-to-all-start.8 = ((bf16[4,192,256]{2,1,0:T(8,128)(2,1)}), bf16[4,192,256]{2,1,0:T(8,128)(2,1)S(1)}, u32[]{:S(2)}, u32[]{:S(2)}) async-start(bf16[4,192,256]{2,1,0:T(8,128)(2,1)} %bitcast.39), calls=%async_computation.9 | async-start | bytes 786432 | tf_op jit(solution)/shard_map/all_to_all | solution.py:375
Sparse Core Ops, SparseCore 0:
  61.8 31.0 all-gather.4
  141.4 29.2 all-gather.6
  185.3 28.3 reduce-scatter.1

commit v8 on v7

--- a/solution.py
+++ b/solution.py
@@ -187,21 +187,35 @@
             yield l, g, joined(pairs, 0, NN)
 
 
-def outer1_kernel(parts, ids, p0, p1, p2, s0, s1, s2, c0, c1, c2, c3, *refs):
+def outer1_kernel(parts, ids, p0, p1, s0, s1, c0, c1, c2, c3, w, *refs):
     toks, (out, praw, rs, d) = refs[: len(parts)], refs[len(parts) :]
-    zl, c = ids[3], ids[4]
-
-    @pl.when(pl.program_id(0) == 0)
+    i, zh, zl, c = pl.program_id(0), ids[1], ids[3], ids[4]
+    grp, g = parts[-1]
+
+    @pl.when(i == 0)
+    def _():
+        praw[...] = p0[...] + p1[...]
+        rs[...] = s0[...] + s1[...]
+
+    @pl.when(i < 4)
+    def _():
+        wv = w[0, lax.rem((zl ^ 1) * 2 + (c ^ g) - zh + 4, 4)].astype(F32)
+        scaled = (wv * row(toks[-1][0, 0, BLK:PACK, :], 0)).astype(BF)
+        for j, (k, _) in enumerate(GROUPS[grp]):
+            praw[k] += lax.dot_general(scaled, toks[-1][0, j, 0:BLK, :], NT, preferred_element_type=F32)
+            rs[k] += jnp.broadcast_to(row(toks[-1][0, j, BLK:PACK, :], 3), (8, BLK))
+
+    @pl.when(i == 4)
     def _():
         for k, cot in enumerate((c0, c1, c2, c3)):
-            r = lax.rsqrt((s0[k] + s1[k] + s2[k]) / (NB * BLK) + 1e-06)
-            pre = p0[k] + p1[k] + p2[k]
+            r = lax.rsqrt(rs[k] / (NB * BLK) + 1e-06)
             rs[k] = r
-            praw[k] = pre
-            d[k] = hidden_grads(pre, r[0:1], cot[ROWS : ROWS + SUB, :])
-
-    for l, g, total in outer_terms(parts, d, toks):
-        out[0, (zl ^ l) * 2 + (c ^ g)] = total.astype(BF)
+            d[k] = hidden_grads(praw[k], r[0:1], cot[ROWS : ROWS + SUB, :])
+
+    @pl.when(i >= 4)
+    def _():
+        for l, h, total in outer_terms(parts, d, toks):
+            out[0, (zl ^ l) * 2 + (c ^ h)] = total.astype(BF)
 
 
 def outer2_kernel(parts, radius, ids, totals, praw, rs, pa, c0, c1, c2, c3, w, asc, mask, *refs):
@@ -317,7 +331,6 @@
     far_x = after(far_x, p0)
     toks[2, 0], toks[2, 1] = far_x, other_core(far_x)
     p1, s1 = pre(((2, 0),), False)
-    p2, s2 = pre(((2, 1),), False)
     parts = tuple((grp, g) for g in range(2) for grp in range(len(GROUPS)))
     tok_specs = [tok_spec(p[0]) for p in parts]
     tok_refs = [toks[p] for p in parts]
@@ -326,15 +339,21 @@
     pspec, sspec = whole(pshape.shape), whole(sshape.shape)
     pieces = [in_hbm(p) for p in pieces]
     dscratch = [pltpu.VMEM((4, ROWS, BLK), BF)]
+    def late(dims):
+        return pl.BlockSpec((1,) + dims, lambda i: (jnp.maximum(i - 4, 0),) + (0,) * len(dims))
+
+    late_specs = [late((len(GROUPS[p[0]]), PACK, BLK)) for p in parts[:-1]]
+    both_spec = pl.BlockSpec((1, len(GROUPS[2]), PACK, BLK), lambda i: (lax.rem(i, 4), 0, 0, 0))
+    early_w = pl.BlockSpec((1, 4, ROWS, BLK), lambda i: (jnp.minimum(i, 3), 0, 0, 0))
     out1, praw, rs = call(
         functools.partial(outer1_kernel, parts),
         (oshape, hbm(pshape.shape, F32), hbm(sshape.shape, F32)),
-        [SMEM] + [pspec] * 3 + [sspec] * 3 + [whole(piece.shape)] * 4 + tok_specs,
-        (by_x((4, ROWS, BLK)), pspec, sspec),
-        (4,),
+        [SMEM] + [pspec] * 2 + [sspec] * 2 + [whole(piece.shape)] * 4 + [early_w] + late_specs + [both_spec],
+        (late((4, ROWS, BLK)), pspec, sspec),
+        (8,),
         dscratch,
         **cost,
-    )(ids, p0, p1, p2, s0, s1, s2, *pieces, *tok_refs)
+    )(ids, p0, p1, s0, s1, *pieces, weights, *tok_refs)
     terms = lax.all_to_all(out1, "y", 0, 0, tiled=True)
     asc, part = call(
         ascent_kernel,

time: 242 us -> 240 us (level)
  waiting for transfers between devices: 95.2 us -> 92.4 us
    pallas_call x3 -> x2, Pallas kernels: 12 us -> 9 us  [pre(): call(functools.partial(pre_kernel, parts, with_gain), outs, [SMEM, wspec]...]
    pallas_call x1, Pallas kernels: 6.47 us -> 9.11 us  [body(): call(functools.partial(outer1_kernel, parts), (oshape, hbm(pshape.shape,...]
  transfers between devices with their start and end apart: 21 -> 21, of which waited for: 14 -> 14; matrix products, arithmetic and copies ran while one was open for 2% -> 2% of each run, Pallas kernels for 6% -> 7%
where the time goes in v8:
time: 240 us; the launch traced here: 238 us
  waiting for transfers between devices  92.4 us (38%)
  starting transfers between devices  58.1 us (24%)
  Pallas kernels  40.2 us (17%)
  blocking collectives  26.8 us (11%)
  between operations  14.5 us (6%)
  local copies, waits for them, and re-layouts  3.69 us (2%)
  other arithmetic  2.43 us (1%)
    ppermute x8, waiting for transfers between devices, from_z(): return lax.ppermute(value, ('zh', 'zl'), pairs)  28.5 us
    all_to_all x1, waiting for transfers between devices, body(): terms = lax.all_to_all(out1, 'y', 0, 0, tiled=True)  21.3 us
    ppermute x8, starting transfers between devices, from_z(): return lax.ppermute(value, ('zh', 'zl'), pairs)  17.2 us
    all_to_all x1, blocking collectives, spread(): lax.all_to_all(jnp.broadcast_to(value[None], (n,) + value.shape), axes, 0...  17.2 us
    all_gather x1, waiting for transfers between devices, body(): weights = in_hbm(lax.all_gather(part_w, 'y', axis=0, tiled=False))  13 us
    all_to_all x1, waiting for transfers between devices, body(): sums = lax.all_to_all(sums, 'zh', 0, 0, tiled=True)  11.5 us
    all_gather x1, waiting for transfers between devices, body(): ascs = in_hbm(lax.all_gather(asc, 'y', axis=0, tiled=False))  11 us
    all_to_all x2, starting transfers between devices, over_x(): lax.all_to_all(jnp.broadcast_to(value[None], (4,) + value.shape), 'x', 0,...  10.6 us
  transfers between devices with their start and end apart: 21, of which 14 were waited for; matrix products, arithmetic and copies ran while one was open for 2% of the time, Pallas kernels for 7%

profile of v8, /device:TPU:4, one launch (start us, length us, event | category | flops | bytes accessed | tf_op | source)
XLA Modules:
  0.0 238.3 jit_solution(6231183386253973812)
XLA Ops:
  7.3 2.5 %shard_map.94 = (bf16[272,256]{1,0:T(8,128)(2,1)}, bf16[4,1,272,256]{3,2,1,0:T(8,128)(2,1)}, bf16[288,256]{1,0:T(8,128)(2,1)}, bf16[288,256]{1,0:T(8,128)(2,1)},...) custom-call(s32[5]{0:T(128)S(1)} %stack.59.ids, bf16[256,256]{1,0:T(8,128)(2,1)} %tokens.1, f32[1,256]{1,0:T(1,128)} %bitcast.41, ...), custom_call_target="tpu_custom_call" | custom-call | flops 1000000 | bytes 1000000 | tf_op jit(solution)/shard_map/pallas_call | solution.py:285
  9.8 5.7 %all-to-all-start = ((bf16[4,1,272,256]{3,2,1,0:T(8,128)(2,1)}), bf16[4,1,272,256]{3,2,1,0:T(8,128)(2,1)S(1)}, u32[]{:S(2)}, u32[]{:S(2)}) async-start(bf16[4,1,272,256]{3,2,1,0:T(8,128)(2,1)} %get-tuple-element.32), calls=%async_computation | async-start | bytes 1114112 | tf_op jit(solution)/shard_map/all_to_all | solution.py:301
  15.5 1.0 collective-permute-start.6
  16.5 6.3 %collective-permute-start.5 = (bf16[272,256]{1,0:T(8,128)(2,1)}, bf16[272,256]{1,0:T(8,128)(2,1)S(1)}, u32[]{:S(2)}, u32[]{:S(2)}) collective-permute-start(bf16[272,256]{1,0:T(8,128)(2,1)} %get-tuple-element.33), channel_id=1, source_target_pairs={{32,0},{34,2},{48,16},{50,18},{0,32},{2,34},{16,48},{18,50},{33,1}... | collective-permute-start | bytes 417800 | tf_op jit(solution)/shard_map/ppermute | solution.py:37
  22.8 1.5 collective-permute-start.4
  24.3 2.7 %collective-permute-start.3 = (bf16[272,256]{1,0:T(8,128)(2,1)}, bf16[272,256]{1,0:T(8,128)(2,1)S(1)}, u32[]{:S(2)}, u32[]{:S(2)}) collective-permute-start(bf16[272,256]{1,0:T(8,128)(2,1)} %get-tuple-element.33), channel_id=1, source_target_pairs={{16,0},{18,2},{32,16},{34,18},{48,32},{50,34},{0,48},{2,50},{17,1}... | collective-permute-start | bytes 417800 | tf_op jit(solution)/shard_map/ppermute | solution.py:37
  26.9 8.9 %collective-permute-done.5 = bf16[272,256]{1,0:T(8,128)(2,1)S(1)} collective-permute-done((bf16[272,256]{1,0:T(8,128)(2,1)}, bf16[272,256]{1,0:T(8,128)(2,1)S(1)}, u32[]{:S(2)}, u32[]{:S(2)}) %collective-permute-start.5) | collective-permute-done | bytes 139296 | tf_op jit(solution)/shard_map/ppermute | solution.py:37
  35.8 1.1 collective-permute-done.4
  37.0 1.5 broadcast_in_dim.11
  38.5 4.9 %all-to-all-start.1 = ((bf16[4,4,272,256]{3,2,1,0:T(8,128)(2,1)}), bf16[4,4,272,256]{3,2,1,0:T(8,128)(2,1)}, u32[]{:S(2)}, u32[]{:S(2)}) async-start(bf16[4,4,272,256]{3,2,1,0:T(8,128)(2,1)} %broadcast_in_dim.11), calls=%async_computation.1 | async-start | bytes 4456448 | tf_op jit(solution)/shard_map/all_to_all | solution.py:297
  43.5 2.2 collective-permute-start
  45.7 2.5 %collective-permute-start.1 = (bf16[288,256]{1,0:T(8,128)(2,1)S(1)}, bf16[288,256]{1,0:T(8,128)(2,1)S(1)}, u32[]{:S(2)}, u32[]{:S(2)}) collective-permute-start(bf16[288,256]{1,0:T(8,128)(2,1)S(1)} %copy-done.9), channel_id=1, source_target_pairs={{32,0},{34,2},{48,16},{50,18},{0,32},{2,34},{16,48},{18,50},{33,1}... | collective-permute-start | bytes 442376 | tf_op jit(solution)/shard_map/ppermute | solution.py:37
  48.2 0.9 collective-permute-start.2
  49.2 0.1 collective-permute-start.7
  49.3 5.5 %collective-permute-done.c1 = bf16[288,256]{1,0:T(8,128)(2,1)S(1)} collective-permute-done((bf16[288,256]{1,0:T(8,128)(2,1)S(1)}, bf16[288,256]{1,0:T(8,128)(2,1)S(1)}, u32[]{:S(2)}, u32[]{:S(2)}) %collective-permute-start) | collective-permute-done | bytes 147488 | tf_op jit(solution)/shard_map/ppermute | solution.py:37
  54.8 5.0 %collective-permute-done.1.c2 = bf16[288,256]{1,0:T(8,128)(2,1)S(1)} collective-permute-done((bf16[288,256]{1,0:T(8,128)(2,1)S(1)}, bf16[288,256]{1,0:T(8,128)(2,1)S(1)}, u32[]{:S(2)}, u32[]{:S(2)}) %collective-permute-start.1) | collective-permute-done | bytes 147488 | tf_op jit(solution)/shard_map/ppermute | solution.py:37
  59.8 2.4 %collective-permute-done.2.c3 = bf16[288,256]{1,0:T(8,128)(2,1)S(1)} collective-permute-done((bf16[288,256]{1,0:T(8,128)(2,1)S(1)}, bf16[288,256]{1,0:T(8,128)(2,1)S(1)}, u32[]{:S(2)}, u32[]{:S(2)}) %collective-permute-start.2) | collective-permute-done | bytes 147488 | tf_op jit(solution)/shard_map/ppermute | solution.py:37
  62.3 0.8 pad_maximum_fusion.2
  63.1 5.5 %collective-permute-done.7 = bf16[3,272,256]{2,1,0:T(8,128)(2,1)S(1)} collective-permute-done((bf16[3,272,256]{2,1,0:T(8,128)(2,1)S(1)}, bf16[3,272,256]{2,1,0:T(8,128)(2,1)S(1)}, u32[]{:S(2)}, u32[]{:S(2)}) %collective-permute-start.7) | collective-permute-done | bytes 417824 | tf_op jit(solution)/shard_map/ppermute | solution.py:37
  68.7 1.3 broadcast_in_dim.12
  70.0 5.7 %all-to-all-start.2 = ((bf16[4,3,272,256]{3,2,1,0:T(8,128)(2,1)}), bf16[4,3,272,256]{3,2,1,0:T(8,128)(2,1)S(1)}, u32[]{:S(2)}, u32[]{:S(2)}) async-start(bf16[4,3,272,256]{3,2,1,0:T(8,128)(2,1)} %broadcast_in_dim.12), calls=%async_computation.2 | async-start | bytes 3342336 | tf_op jit(solution)/shard_map/all_to_all | solution.py:297
  75.7 0.2 collective-permute-start.8
  75.9 1.7 collective-permute-done.8.refs_2_.refs_3_
  77.7 13.0 %all-gather.5.cloned.1.call-done = bf16[16,192,256]{2,1,0:T(8,128)(2,1)} async-done(((bf16[4,192,256]{2,1,0:T(8,128)(2,1)}), bf16[16,192,256]{2,1,0:T(8,128)(2,1)}) %all-gather.5.cloned.1.call-update) | async-done | bytes 1572880 | tf_op jit(solution)/shard_map/all_gather | solution.py:306
  90.7 5.9 %shard_map.95 = (f32[4,192,256]{2,1,0:T(8,128)}, f32[4,8,256]{2,1,0:T(8,128)S(1)}, f32[16,8,256]{2,1,0:T(8,128)S(1)}) custom-call(s32[5]{0:T(128)S(1)} %stack.59.ids, bf16[4,4,192,256]{3,2,1,0:T(8,128)(2,1)} %bitcast.27, bf16[4,1,272,256]{3,2,1,0:T(8,128)(2,1)} %copy-done.1, bf16[4,4,272,256]{3,2,1,0:T(8,128)(2,1)} %all-to-all-done.1.refs_1_, ...), custom_call_target="tpu_custom_call" | custom-call | flops 1006632960 | bytes 5570560 | tf_op jit(solution)/shard_map/pallas_call | solution.py:320
  96.6 0.1 collective-permute-start.10
  96.7 3.1 %shard_map.96 = (f32[4,192,256]{2,1,0:T(8,128)S(1)}, f32[4,8,256]{2,1,0:T(8,128)S(1)}) custom-call(s32[5]{0:T(128)S(1)} %stack.59.ids, bf16[4,4,192,256]{3,2,1,0:T(8,128)(2,1)} %bitcast.28, bf16[4,3,272,256]{3,2,1,0:T(8,128)(2,1)S(1)} %all-to-all-done.2.refs_0_.refs_2_), custom_call_target="tpu_custom_call" | custom-call | flops 301989888 | bytes 1671168 | tf_op jit(solution)/shard_map/pallas_call | solution.py:320
  99.8 0.4 collective-permute-done.10.refs_5_
  100.2 9.1 %shard_map.97 = (bf16[4,4,192,256]{3,2,1,0:T(8,128)(2,1)}, f32[4,192,256]{2,1,0:T(8,128)}, f32[4,8,256]{2,1,0:T(8,128)}) custom-call(s32[5]{0:T(128)S(1)} %stack.59.ids, f32[4,192,256]{2,1,0:T(8,128)S(1)} %copy-done, f32[4,192,256]{2,1,0:T(8,128)S(1)} %get-tuple-element.39.p1, f32[4,8,256]{2,1,0:T(8,128)S(1)} %get-tuple-element.40.s0, ...), custom_call_target="tpu_custom_call" | custom-call | flops 1610612736 | bytes 12000000 | tf_op jit(solution)/shard_map/pallas_call | solution.py:348
  109.4 4.4 %all-to-all-start.3 = ((bf16[4,4,192,256]{3,2,1,0:T(8,128)(2,1)}), bf16[4,4,192,256]{3,2,1,0:T(8,128)(2,1)}, u32[]{:S(2)}, u32[]{:S(2)}) async-start(bf16[4,4,192,256]{3,2,1,0:T(8,128)(2,1)} %get-tuple-element.42), calls=%async_computation.3 | async-start | bytes 3145728 | tf_op jit(solution)/shard_map/all_to_all | solution.py:357
  113.8 21.3 %all-to-all-done.3.terms = bf16[4,4,192,256]{3,2,1,0:T(8,128)(2,1)} async-done(((bf16[4,4,192,256]{3,2,1,0:T(8,128)(2,1)}), bf16[4,4,192,256]{3,2,1,0:T(8,128)(2,1)}, u32[]{:S(2)}, u32[]{:S(2)}) %all-to-all-start.3) | async-done | bytes 1572896 | tf_op jit(solution)/shard_map/all_to_all | solution.py:357
  135.1 3.5 %shard_map.98 = (bf16[4,192,256]{2,1,0:T(8,128)(2,1)}, f32[16,8,128]{2,1,0:T(8,128)}) custom-call(s32[5]{0:T(128)S(1)} %stack.59.ids, bf16[4,4,192,256]{3,2,1,0:T(8,128)(2,1)} %all-to-all-done.3.terms, f32[16,8,256]{2,1,0:T(8,128)S(1)} %get-tuple-element.43.gabs, f32[16,2,256]{2,1,0:T(2,128)S(1)} %bitcast.24), custom_call_target="tpu_custom_call" | custom-call | flops 1000000 | bytes 1000000 | tf_op jit(solution)/shard_map/pallas_call | solution.py:358
  138.7 5.8 %all-to-all-start.4 = ((f32[16,8,128]{2,1,0:T(8,128)}), f32[16,8,128]{2,1,0:T(8,128)}, u32[]{:S(2)}, u32[]{:S(2)}) async-start(f32[16,8,128]{2,1,0:T(8,128)} %get-tuple-element.44), calls=%async_computation.4 | async-start | bytes 131072 | tf_op jit(solution)/shard_map/all_to_all | solution.py:372
  145.1 3.4 %all-to-all-done.4 = f32[16,8,128]{2,1,0:T(8,128)} async-done(((f32[16,8,128]{2,1,0:T(8,128)}), f32[16,8,128]{2,1,0:T(8,128)}, u32[]{:S(2)}, u32[]{:S(2)}) %all-to-all-start.4) | async-done | bytes 65568 | tf_op jit(solution)/shard_map/all_to_all | solution.py:372
  148.5 0.9 reduce_sum.27
  149.4 0.6 broadcast_in_dim.13
  150.0 6.9 %all-to-all-start.5 = ((f32[16,8,128]{2,1,0:T(8,128)}), f32[16,8,128]{2,1,0:T(8,128)}, u32[]{:S(2)}, u32[]{:S(2)}) async-start(f32[16,8,128]{2,1,0:T(8,128)} %broadcast_in_dim.13), calls=%async_computation.5 | async-start | bytes 131072 | tf_op jit(solution)/shard_map/all_to_all | solution.py:277
  156.9 0.2 reduce-scatter.2.cloned.1.call-start
  157.1 11.0 %all-gather.7.cloned.1.call-done = bf16[16,192,256]{2,1,0:T(8,128)(2,1)} async-done(((bf16[4,192,256]{2,1,0:T(8,128)(2,1)}), bf16[16,192,256]{2,1,0:T(8,128)(2,1)}) %all-gather.7.cloned.1.call-update) | async-done | bytes 1572880 | tf_op jit(solution)/shard_map/all_gather | solution.py:371
  168.1 6.6 %shard_map.99.pa = f32[4,192,256]{2,1,0:T(8,128)} custom-call(s32[5]{0:T(128)S(1)} %stack.59.ids, bf16[4,4,192,256]{3,2,1,0:T(8,128)(2,1)} %bitcast.31, f32[16,2,256]{2,1,0:T(2,128)S(1)} %bitcast.25, f32[16,8,256]{2,1,0:T(8,128)S(1)} %get-tuple-element.43.gabs, bf16[4,1,272,256]{3,2,1,0:T(8,128)(2,1)} %copy-done.1, ...), custom_call_target="tpu_custom_call" | custom-call | flops 1610612736 | bytes 12000000 | tf_op jit(solution)/shard_map/pallas_call | solution.py:374
  174.7 7.8 %shard_map.100 = (bf16[4,4,192,256]{3,2,1,0:T(8,128)(2,1)}, f32[16,1,256]{2,1,0:T(1,128)}) custom-call(f32[1]{0:T(128)S(6)} %copy.12.radius, s32[5]{0:T(128)S(1)} %stack.59.ids, f32[16,8,128]{2,1,0:T(8,128)} %all-to-all-done.5.totals, f32[4,192,256]{2,1,0:T(8,128)} %get-tuple-element.47.praw, f32[4,8,256]{2,1,0:T(8,128)} %get-tuple-element.48.rs, ...), custom_call_target="tpu_custom_call" | custom-call | flops 1610612736 | bytes 12000000 | tf_op jit(solution)/shard_map/pallas_call | solution.py:382
  182.6 9.6 %all_to_all.45 = f32[16,1,256]{2,1,0:T(1,128)S(1)} all-to-all(f32[16,1,256]{2,1,0:T(1,128)} %get-tuple-element.49), channel_id=1, replica_groups=mesh['y'=4,'zh'=4,'x'=4,'zl'=2,'c'=2] {'x','zl','c'}, dimensions={0} | all-to-all | bytes 32768 | tf_op jit(solution)/shard_map/all_to_all | solution.py:392
  192.3 17.2 %all_to_all.46 = f32[16,1,256]{2,1,0:T(1,128)S(1)} all-to-all(f32[16,1,256]{2,1,0:T(1,128)S(1)} %broadcast_in_dim.14), channel_id=1, replica_groups=mesh['y'=4,'zh'=4,'x'=4,'zl'=2,'c'=2] {'y','zh'}, dimensions={0} | all-to-all | bytes 32768 | tf_op jit(solution)/shard_map/all_to_all | solution.py:277
  209.4 1.6 reduce-scatter.2.cloned.1.call-done
  211.1 7.0 %all-to-all-start.8 = ((bf16[4,192,256]{2,1,0:T(8,128)(2,1)}), bf16[4,192,256]{2,1,0:T(8,128)(2,1)S(1)}, u32[]{:S(2)}, u32[]{:S(2)}) async-start(bf16[4,192,256]{2,1,0:T(8,128)(2,1)} %bitcast.39), calls=%async_computation.9 | async-start | bytes 786432 | tf_op jit(solution)/shard_map/all_to_all | solution.py:394
  218.0 0.6 reduce_sum.29
  218.6 11.5 %all-to-all-done.8.sums = bf16[4,192,256]{2,1,0:T(8,128)(2,1)S(1)} async-done(((bf16[4,192,256]{2,1,0:T(8,128)(2,1)}), bf16[4,192,256]{2,1,0:T(8,128)(2,1)S(1)}, u32[]{:S(2)}, u32[]{:S(2)}) %all-to-all-start.8) | async-done | bytes 393248 | tf_op jit(solution)/shard_map/all_to_all | solution.py:394
  230.2 1.6 shard_map.101
  (45 shorter events, 0.5 us)
Async XLA Ops:
  9.8 27.2 %all-to-all-start = ((bf16[4,1,272,256]{3,2,1,0:T(8,128)(2,1)}), bf16[4,1,272,256]{3,2,1,0:T(8,128)(2,1)S(1)}, u32[]{:S(2)}, u32[]{:S(2)}) async-start(bf16[4,1,272,256]{3,2,1,0:T(8,128)(2,1)} %get-tuple-element.32), calls=%async_computation | async-start | bytes 1114112 | tf_op jit(solution)/shard_map/all_to_all | solution.py:301
  15.5 11.5 %collective-permute-start.6 = (bf16[272,256]{1,0:T(8,128)(2,1)}, bf16[272,256]{1,0:T(8,128)(2,1)S(1)}, u32[]{:S(2)}, u32[]{:S(2)}) collective-permute-start(bf16[272,256]{1,0:T(8,128)(2,1)} %get-tuple-element.33), channel_id=1, source_target_pairs={{2,0},{0,2},{18,16},{16,18},{34,32},{32,34},{50,48},{48,50},{3,1},... | collective-permute-start | bytes 417800 | tf_op jit(solution)/shard_map/ppermute | solution.py:37
  16.5 19.3 %collective-permute-start.5 = (bf16[272,256]{1,0:T(8,128)(2,1)}, bf16[272,256]{1,0:T(8,128)(2,1)S(1)}, u32[]{:S(2)}, u32[]{:S(2)}) collective-permute-start(bf16[272,256]{1,0:T(8,128)(2,1)} %get-tuple-element.33), channel_id=1, source_target_pairs={{32,0},{34,2},{48,16},{50,18},{0,32},{2,34},{16,48},{18,50},{33,1}... | collective-permute-start | bytes 417800 | tf_op jit(solution)/shard_map/ppermute | solution.py:37
  22.8 14.1 %collective-permute-start.4 = (bf16[272,256]{1,0:T(8,128)(2,1)}, bf16[272,256]{1,0:T(8,128)(2,1)S(1)}, u32[]{:S(2)}, u32[]{:S(2)}) collective-permute-start(bf16[272,256]{1,0:T(8,128)(2,1)} %get-tuple-element.33), channel_id=1, source_target_pairs={{48,0},{50,2},{0,16},{2,18},{16,32},{18,34},{32,48},{34,50},{49,1}... | collective-permute-start | bytes 417800 | tf_op jit(solution)/shard_map/ppermute | solution.py:37
  24.3 12.6 %collective-permute-start.3 = (bf16[272,256]{1,0:T(8,128)(2,1)}, bf16[272,256]{1,0:T(8,128)(2,1)S(1)}, u32[]{:S(2)}, u32[]{:S(2)}) collective-permute-start(bf16[272,256]{1,0:T(8,128)(2,1)} %get-tuple-element.33), channel_id=1, source_target_pairs={{16,0},{18,2},{32,16},{34,18},{48,32},{50,34},{0,48},{2,50},{17,1}... | collective-permute-start | bytes 417800 | tf_op jit(solution)/shard_map/ppermute | solution.py:37
  37.0 38.8 %copy-start.1 = (bf16[4,1,272,256]{3,2,1,0:T(8,128)(2,1)}, bf16[4,1,272,256]{3,2,1,0:T(8,128)(2,1)S(1)}, u32[]{:S(2)}) copy-start(bf16[4,1,272,256]{3,2,1,0:T(8,128)(2,1)S(1)} %all-to-all-done.refs_0_) | copy-start | bytes 1671172
  38.5 5.0 %copy-start.10 = (bf16[288,256]{1,0:T(8,128)(2,1)S(1)}, bf16[288,256]{1,0:T(8,128)(2,1)}, u32[]{:S(2)}) copy-start(bf16[288,256]{1,0:T(8,128)(2,1)} %get-tuple-element.29) | copy-start | bytes 442372
  38.5 7.2 %copy-start.9 = (bf16[288,256]{1,0:T(8,128)(2,1)S(1)}, bf16[288,256]{1,0:T(8,128)(2,1)}, u32[]{:S(2)}) copy-start(bf16[288,256]{1,0:T(8,128)(2,1)} %get-tuple-element.30) | copy-start | bytes 442372
  38.5 9.7 %copy-start.8 = (bf16[288,256]{1,0:T(8,128)(2,1)S(1)}, bf16[288,256]{1,0:T(8,128)(2,1)}, u32[]{:S(2)}) copy-start(bf16[288,256]{1,0:T(8,128)(2,1)} %get-tuple-element.31) | copy-start | bytes 442372
  38.5 10.6 %copy-start.3 = (bf16[288,256]{1,0:T(8,128)(2,1)S(1)}, bf16[288,256]{1,0:T(8,128)(2,1)}, u32[]{:S(2)}) copy-start(bf16[288,256]{1,0:T(8,128)(2,1)} %get-tuple-element.28.c0) | copy-start | bytes 442372
  38.5 30.1 %all-to-all-start.1 = ((bf16[4,4,272,256]{3,2,1,0:T(8,128)(2,1)}), bf16[4,4,272,256]{3,2,1,0:T(8,128)(2,1)}, u32[]{:S(2)}, u32[]{:S(2)}) async-start(bf16[4,4,272,256]{3,2,1,0:T(8,128)(2,1)} %broadcast_in_dim.11), calls=%async_computation.1 | async-start | bytes 4456448 | tf_op jit(solution)/shard_map/all_to_all | solution.py:297
  43.5 47.2 %all-gather.5.cloned.1.call-start = ((), (), s32[]{:S(2)}) async-start(), calls=%async_computation.11 | async-start | bytes 1966080 | tf_op jit(solution)/shard_map/all_gather | solution.py:306
  43.5 11.3 %collective-permute-start = (bf16[288,256]{1,0:T(8,128)(2,1)S(1)}, bf16[288,256]{1,0:T(8,128)(2,1)S(1)}, u32[]{:S(2)}, u32[]{:S(2)}) collective-permute-start(bf16[288,256]{1,0:T(8,128)(2,1)S(1)} %copy-done.10), channel_id=1, source_target_pairs={{16,0},{18,2},{32,16},{34,18},{48,32},{50,34},{0,48},{2,50},{17,1}... | collective-permute-start | bytes 442376 | tf_op jit(solution)/shard_map/ppermute | solution.py:37
  45.7 14.1 %collective-permute-start.1 = (bf16[288,256]{1,0:T(8,128)(2,1)S(1)}, bf16[288,256]{1,0:T(8,128)(2,1)S(1)}, u32[]{:S(2)}, u32[]{:S(2)}) collective-permute-start(bf16[288,256]{1,0:T(8,128)(2,1)S(1)} %copy-done.9), channel_id=1, source_target_pairs={{32,0},{34,2},{48,16},{50,18},{0,32},{2,34},{16,48},{18,50},{33,1}... | collective-permute-start | bytes 442376 | tf_op jit(solution)/shard_map/ppermute | solution.py:37
  48.2 14.0 %collective-permute-start.2 = (bf16[288,256]{1,0:T(8,128)(2,1)S(1)}, bf16[288,256]{1,0:T(8,128)(2,1)S(1)}, u32[]{:S(2)}, u32[]{:S(2)}) collective-permute-start(bf16[288,256]{1,0:T(8,128)(2,1)S(1)} %copy-done.8), channel_id=1, source_target_pairs={{48,0},{50,2},{0,16},{2,18},{16,32},{18,34},{32,48},{34,50},{49,1}... | collective-permute-start | bytes 442376 | tf_op jit(solution)/shard_map/ppermute | solution.py:37
  49.2 19.5 %collective-permute-start.7 = (bf16[3,272,256]{2,1,0:T(8,128)(2,1)S(1)}, bf16[3,272,256]{2,1,0:T(8,128)(2,1)S(1)}, u32[]{:S(2)}, u32[]{:S(2)}) collective-permute-start(bf16[3,272,256]{2,1,0:T(8,128)(2,1)S(1)} %pad_maximum_fusion.1), channel_id=1, source_target_pairs={{2,0},{0,2},{18,16},{16,18},{34,32},{32,34},{50,48},{48,50},{3,1},... | collective-permute-start | bytes 1253384 | tf_op jit(solution)/shard_map/ppermute | solution.py:37
  54.8 15.2 %copy-start.4 = (bf16[288,256]{1,0:T(8,128)(2,1)}, bf16[288,256]{1,0:T(8,128)(2,1)S(1)}, u32[]{:S(2)}) copy-start(bf16[288,256]{1,0:T(8,128)(2,1)S(1)} %collective-permute-done.c1) | copy-start | bytes 442372
  59.8 10.2 %copy-start.5 = (bf16[288,256]{1,0:T(8,128)(2,1)}, bf16[288,256]{1,0:T(8,128)(2,1)S(1)}, u32[]{:S(2)}) copy-start(bf16[288,256]{1,0:T(8,128)(2,1)S(1)} %collective-permute-done.1.c2) | copy-start | bytes 442372
  62.3 7.7 %copy-start.6 = (bf16[288,256]{1,0:T(8,128)(2,1)}, bf16[288,256]{1,0:T(8,128)(2,1)S(1)}, u32[]{:S(2)}) copy-start(bf16[288,256]{1,0:T(8,128)(2,1)S(1)} %collective-permute-done.2.c3) | copy-start | bytes 442372
  68.7 22.0 %collective-permute-start.9 = (bf16[4,4,272,256]{3,2,1,0:T(8,128)(2,1)}, bf16[4,4,272,256]{3,2,1,0:T(8,128)(2,1)}, u32[]{:S(2)}, u32[]{:S(2)}) collective-permute-start(bf16[4,4,272,256]{3,2,1,0:T(8,128)(2,1)} %all-to-all-done.1.refs_1_), channel_id=1, source_target_pairs={{0,1},{1,0},{2,3},{3,2},{4,5},{5,4},{6,7},{7,6},{8,9},{9,8},{10,11... | collective-permute-start | bytes 6684680 | tf_op jit(solution)/shard_map/ppermute | solution.py:41
  70.0 26.6 %all-to-all-start.2 = ((bf16[4,3,272,256]{3,2,1,0:T(8,128)(2,1)}), bf16[4,3,272,256]{3,2,1,0:T(8,128)(2,1)S(1)}, u32[]{:S(2)}, u32[]{:S(2)}) async-start(bf16[4,3,272,256]{3,2,1,0:T(8,128)(2,1)} %broadcast_in_dim.12), calls=%async_computation.2 | async-start | bytes 3342336 | tf_op jit(solution)/shard_map/all_to_all | solution.py:297
  75.7 2.0 collective-permute-start.8
  77.7 13.0 %copy-start.2 = (bf16[4,1,272,256]{3,2,1,0:T(8,128)(2,1)}, bf16[4,1,272,256]{3,2,1,0:T(8,128)(2,1)S(1)}, u32[]{:S(2)}) copy-start(bf16[4,1,272,256]{3,2,1,0:T(8,128)(2,1)S(1)} %collective-permute-done.8.refs_2_.refs_3_) | copy-start | bytes 1671172
  96.6 3.6 %copy-start = (f32[4,192,256]{2,1,0:T(8,128)S(1)}, f32[4,192,256]{2,1,0:T(8,128)}, u32[]{:S(2)}) copy-start(f32[4,192,256]{2,1,0:T(8,128)} %get-tuple-element.36.p0) | copy-start | bytes 2359300
  96.6 3.6 %collective-permute-start.10 = (bf16[4,3,272,256]{3,2,1,0:T(8,128)(2,1)S(1)}, bf16[4,3,272,256]{3,2,1,0:T(8,128)(2,1)S(1)}, u32[]{:S(2)}, u32[]{:S(2)}) collective-permute-start(bf16[4,3,272,256]{3,2,1,0:T(8,128)(2,1)S(1)} %all-to-all-done.2.refs_0_.refs_2_), channel_id=1, source_target_pairs={{0,1},{1,0},{2,3},{3,2},{4,5},{5,4},{6,7},{7,6},{8,9},{9,8},{10,11... | collective-permute-start | bytes 5013512 | tf_op jit(solution)/shard_map/ppermute | solution.py:41
  109.4 4.5 %copy-start.7 = (s32[2,4096]{1,0:T(2,128)S(1)}, s32[2,4096]{1,0:T(2,128)}, u32[]{:S(2)}) copy-start(s32[2,4096]{1,0:T(2,128)} %param.12) | copy-start | bytes 98308
  109.4 25.7 %all-to-all-start.3 = ((bf16[4,4,192,256]{3,2,1,0:T(8,128)(2,1)}), bf16[4,4,192,256]{3,2,1,0:T(8,128)(2,1)}, u32[]{:S(2)}, u32[]{:S(2)}) async-start(bf16[4,4,192,256]{3,2,1,0:T(8,128)(2,1)} %get-tuple-element.42), calls=%async_computation.3 | async-start | bytes 3145728 | tf_op jit(solution)/shard_map/all_to_all | solution.py:357
  113.8 54.3 %all-gather.7.cloned.1.call-start = ((), (), s32[]{:S(2)}) async-start(), calls=%async_computation.12 | async-start | bytes 1966080 | tf_op jit(solution)/shard_map/all_gather | solution.py:371
  138.7 9.8 %all-to-all-start.4 = ((f32[16,8,128]{2,1,0:T(8,128)}), f32[16,8,128]{2,1,0:T(8,128)}, u32[]{:S(2)}, u32[]{:S(2)}) async-start(f32[16,8,128]{2,1,0:T(8,128)} %get-tuple-element.44), calls=%async_computation.4 | async-start | bytes 131072 | tf_op jit(solution)/shard_map/all_to_all | solution.py:372
  150.0 24.7 %all-to-all-start.5 = ((f32[16,8,128]{2,1,0:T(8,128)}), f32[16,8,128]{2,1,0:T(8,128)}, u32[]{:S(2)}, u32[]{:S(2)}) async-start(f32[16,8,128]{2,1,0:T(8,128)} %broadcast_in_dim.13), calls=%async_computation.5 | async-start | bytes 131072 | tf_op jit(solution)/shard_map/all_to_all | solution.py:277
  156.9 54.2 %reduce-scatter.2.cloned.1.call-start = ((), (), s32[]{:S(2)}) async-start(), calls=%async_computation.10 | async-start | bytes 1966080 | tf_op jit(solution)/shard_map/reduce_scatter | solution.py:391
  211.1 19.1 %all-to-all-start.8 = ((bf16[4,192,256]{2,1,0:T(8,128)(2,1)}), bf16[4,192,256]{2,1,0:T(8,128)(2,1)S(1)}, u32[]{:S(2)}, u32[]{:S(2)}) async-start(bf16[4,192,256]{2,1,0:T(8,128)(2,1)} %bitcast.39), calls=%async_computation.9 | async-start | bytes 786432 | tf_op jit(solution)/shard_map/all_to_all | solution.py:394
Sparse Core Ops, SparseCore 0:
  63.2 27.3 all-gather.4
  138.8 29.2 all-gather.6
  182.7 28.3 reduce-scatter.1

commit v9 on v8

--- a/solution.py
+++ b/solution.py
@@ -231,45 +231,37 @@
 
     for l, g, total in outer_terms(parts, d, toks):
         at = (zl ^ l) * 2 + (c ^ g)
-        out[0, at] = total.astype(BF)
+        out[0, lax.rem(at - zh + 4, 4)] = total.astype(BF)
         fb = x * 4 + at
         wv = w[0, lax.rem(at - zh + 4, 4)].astype(F32)
         wv = wv + f * mask_rows(mask[fb]) * asc[0, at].astype(F32)
         dgp[fb] = jnp.sum(wv * total, axis=0, keepdims=True)
 
 
-def ascent_kernel(ids, terms, gabs, mask, asc, part, acc):
-    h = pl.program_id(0)
-    fb = ids[0] * 4 + h
-    total = terms[0, 0].astype(F32)
-    for j in range(1, 4):
-        total = total + terms[j, 0].astype(F32)
-    low = (total * gabs[fb][0:1]).astype(BF)
-    asc[0] = low
-    wide = low.astype(F32)
-    here = jnp.sum((mask_rows(mask[fb]) * wide * wide).reshape(ROWS // 8, 8, BLK), axis=0)
-    here = here[:, 0:128] + here[:, 128:256]
-
-    @pl.when(h == 0)
-    def _():
-        acc[...] = here
-
-    @pl.when(h > 0)
-    def _():
-        acc[...] += here
-
-    @pl.when(h == 3)
-    def _():
-        for i in range(16):
-            part[i] = acc[...]
-
-
-def final_kernel(ids, gabs, sums, gate, up):
+def ascent_kernel(ids, terms, gabs, mask, asc, part):
+    acc = jnp.zeros((8, BLK), F32)
+    for h in range(4):
+        fb = ids[0] * 4 + h
+        total = terms[0, h].astype(F32)
+        for j in range(1, 4):
+            total = total + terms[j, h].astype(F32)
+        low = (total * gabs[fb][0:1]).astype(BF)
+        asc[h] = low
+        wide = low.astype(F32)
+        acc = acc + jnp.sum((mask_rows(mask[fb]) * wide * wide).reshape(ROWS // 8, 8, BLK), axis=0)
+    acc = acc[:, 0:128] + acc[:, 128:256]
+    for i in range(16):
+        part[i] = acc
+
+
+def final_kernel(ids, gabs, b0, b1, b2, b3, gate, up, tg, tu):
     g = gabs[ids[0] * 4 + ids[1]][0:1]
-    tg = jnp.concatenate([sums[q, 0:SUB, :].astype(F32) for q in range(4)], axis=0) * g
-    tu = jnp.concatenate([sums[q, SUB:ROWS, :].astype(F32) for q in range(4)], axis=0) * g
-    gate[...] = tg.T
-    up[...] = tu.T
+    for k, ref in enumerate((b0, b1, b2, b3)):
+        q = pl.multiple_of(lax.rem(ids[1] - k + 4, 4) * SUB, SUB)
+        tg[pl.ds(q, SUB), :] = ref[0:SUB, :].astype(F32) * g
+        tu[pl.ds(q, SUB), :] = ref[SUB:ROWS, :].astype(F32) * g
+    gate[...] = tg[...].T
+    up[...] = tu[...].T
 
 
 def spread(value, axes):
@@ -358,15 +350,8 @@
     asc, part = call(
         ascent_kernel,
         (hbm((4, ROWS, BLK), BF), hbm((16, 8, 128), F32)),
-        [
-            SMEM,
-            pl.BlockSpec((4, 1, ROWS, BLK), lambda h: (0, h, 0, 0)),
-            whole(gshape.shape),
-            whole((NB, 2, BLK)),
-        ],
-        (by_x((ROWS, BLK)), whole((16, 8, 128))),
-        (4,),
-        [pltpu.VMEM((8, 128), F32)],
+        [SMEM, whole(oshape.shape), whole(gshape.shape), whole((NB, 2, BLK))],
+        (whole((4, ROWS, BLK)), whole((16, 8, 128))),
     )(ids, terms, gabs, mask)
     ascs = in_hbm(lax.all_gather(asc, "y", axis=0, tiled=False))
     part = lax.all_to_all(part, MP, 0, 0, tiled=True)
@@ -391,14 +376,15 @@
     sums = lax.psum_scatter(out2, "y", scatter_dimension=0, tiled=False)
     dg = jnp.sum(lax.all_to_all(dgp, MP, 0, 0, tiled=True), axis=0)
     grad_gain = jnp.sum(spread(dg, DP).reshape(16, BLK), axis=0)
-    sums = lax.all_to_all(sums, "zh", 0, 0, tiled=True)
+    sums = [sums[0]] + [from_z(sums[k], 4 - k, 0) for k in range(1, 4)]
     out = hbm((BLK, 4 * SUB), F32)
     grad_gate, grad_up = call(
         final_kernel,
         (out, out),
-        [SMEM, whole(gshape.shape), whole((4, ROWS, BLK))],
+        [SMEM, whole(gshape.shape)] + [whole((ROWS, BLK))] * 4,
         (whole((BLK, 4 * SUB)), whole((BLK, 4 * SUB))),
-    )(ids, gabs, sums)
+        scratch=[pltpu.VMEM((4 * SUB, BLK), F32)] * 2,
+    )(ids, gabs, *sums)
     return grad_gain, grad_gate, grad_up
 
 

time: 240 us -> 254 us (1.058)
  waiting for transfers between devices: 92.4 us -> 108 us
  blocking collectives: 26.8 us -> 23.1 us
    reduce_scatter x1, waiting for transfers between devices: 1.62 us -> 28.4 us  [body(): sums = lax.psum_scatter(out2, 'y', scatter_dimension=0, tiled=False)]
    all_to_all x1 -> x0, waiting for transfers between devices: 11.5 us -> none  [body(): sums = lax.all_to_all(sums, 'zh', 0, 0, tiled=True)]
    ppermute x8 -> x11, starting transfers between devices: 17.2 us -> 25.9 us  [from_z(): return lax.ppermute(value, ('zh', 'zl'), pairs)]
    all_to_all x1 -> x0, starting transfers between devices: 6.95 us -> none  [body(): sums = lax.all_to_all(sums, 'zh', 0, 0, tiled=True)]
    all_to_all x1, blocking collectives: 17.2 us -> 14.5 us  [spread(): lax.all_to_all(jnp.broadcast_to(value[None], (n,) + value.shape), axes, 0...]
    ppermute x8 -> x11, waiting for transfers between devices: 28.5 us -> 28.5 us  [from_z(): return lax.ppermute(value, ('zh', 'zl'), pairs)]
  transfers between devices with their start and end apart: 21 -> 23, of which waited for: 14 -> 13; matrix products, arithmetic and copies ran while one was open for 2% -> 2% of each run, Pallas kernels for 7% -> 6%
where the time goes in v9:
time: 254 us; the launch traced here: 252 us
  waiting for transfers between devices  108 us (43%)
  starting transfers between devices  59.9 us (24%)
  Pallas kernels  39.2 us (15%)
  blocking collectives  23.1 us (9%)
  between operations  14.6 us (6%)
  local copies, waits for them, and re-layouts  4.79 us (2%)
    ppermute x11, waiting for transfers between devices, from_z(): return lax.ppermute(value, ('zh', 'zl'), pairs)  28.5 us
    reduce_scatter x1, waiting for transfers between devices, body(): sums = lax.psum_scatter(out2, 'y', scatter_dimension=0, tiled=False)  28.4 us
    ppermute x11, starting transfers between devices, from_z(): return lax.ppermute(value, ('zh', 'zl'), pairs)  25.9 us
    all_to_all x1, waiting for transfers between devices, body(): terms = lax.all_to_all(out1, 'y', 0, 0, tiled=True)  21.3 us
    all_to_all x1, blocking collectives, spread(): lax.all_to_all(jnp.broadcast_to(value[None], (n,) + value.shape), axes, 0...  14.5 us
    all_gather x1, waiting for transfers between devices, body(): weights = in_hbm(lax.all_gather(part_w, 'y', axis=0, tiled=False))  13 us
    all_gather x1, waiting for transfers between devices, body(): ascs = in_hbm(lax.all_gather(asc, 'y', axis=0, tiled=False))  11 us
    all_to_all x2, starting transfers between devices, over_x(): lax.all_to_all(jnp.broadcast_to(value[None], (4,) + value.shape), 'x', 0,...  10.6 us
  transfers between devices with their start and end apart: 23, of which 13 were waited for; matrix products, arithmetic and copies ran while one was open for 2% of the time, Pallas kernels for 6%

profile of v9, /device:TPU:4, one launch (start us, length us, event | category | flops | bytes accessed | tf_op | source)
XLA Modules:
  0.0 251.6 jit_solution(464125807769425102)
XLA Ops:
  7.3 2.5 shard_map.94
  9.8 5.7 %all-to-all-start = ((bf16[4,1,272,256]{3,2,1,0:T(8,128)(2,1)}), bf16[4,1,272,256]{3,2,1,0:T(8,128)(2,1)S(1)}, u32[]{:S(2)}, u32[]{:S(2)}) async-start(bf16[4,1,272,256]{3,2,1,0:T(8,128)(2,1)} %get-tuple-element.32), calls=%async_computation | async-start | bytes 1114112 | tf_op jit(solution)/shard_map/all_to_all | solution.py:293
  15.5 1.0 collective-permute-start.6
  16.5 6.3 %collective-permute-start.5 = (bf16[272,256]{1,0:T(8,128)(2,1)}, bf16[272,256]{1,0:T(8,128)(2,1)S(1)}, u32[]{:S(2)}, u32[]{:S(2)}) collective-permute-start(bf16[272,256]{1,0:T(8,128)(2,1)} %get-tuple-element.33), channel_id=1, source_target_pairs={{32,0},{34,2},{48,16},{50,18},{0,32},{2,34},{16,48},{18,50},{33,1}... | collective-permute-start | bytes 417800 | tf_op jit(solution)/shard_map/ppermute | solution.py:37
  22.8 1.5 collective-permute-start.4
  24.2 2.7 %collective-permute-start.3 = (bf16[272,256]{1,0:T(8,128)(2,1)}, bf16[272,256]{1,0:T(8,128)(2,1)S(1)}, u32[]{:S(2)}, u32[]{:S(2)}) collective-permute-start(bf16[272,256]{1,0:T(8,128)(2,1)} %get-tuple-element.33), channel_id=1, source_target_pairs={{16,0},{18,2},{32,16},{34,18},{48,32},{50,34},{0,48},{2,50},{17,1}... | collective-permute-start | bytes 417800 | tf_op jit(solution)/shard_map/ppermute | solution.py:37
  26.9 8.9 %collective-permute-done.5 = bf16[272,256]{1,0:T(8,128)(2,1)S(1)} collective-permute-done((bf16[272,256]{1,0:T(8,128)(2,1)}, bf16[272,256]{1,0:T(8,128)(2,1)S(1)}, u32[]{:S(2)}, u32[]{:S(2)}) %collective-permute-start.5) | collective-permute-done | bytes 139296 | tf_op jit(solution)/shard_map/ppermute | solution.py:37
  35.8 1.1 collective-permute-done.4
  37.0 1.6 broadcast_in_dim.11
  38.5 4.9 %all-to-all-start.1 = ((bf16[4,4,272,256]{3,2,1,0:T(8,128)(2,1)}), bf16[4,4,272,256]{3,2,1,0:T(8,128)(2,1)}, u32[]{:S(2)}, u32[]{:S(2)}) async-start(bf16[4,4,272,256]{3,2,1,0:T(8,128)(2,1)} %broadcast_in_dim.11), calls=%async_computation.1 | async-start | bytes 4456448 | tf_op jit(solution)/shard_map/all_to_all | solution.py:289
  43.5 2.2 collective-permute-start
  45.7 2.5 %collective-permute-start.1 = (bf16[288,256]{1,0:T(8,128)(2,1)S(1)}, bf16[288,256]{1,0:T(8,128)(2,1)S(1)}, u32[]{:S(2)}, u32[]{:S(2)}) collective-permute-start(bf16[288,256]{1,0:T(8,128)(2,1)S(1)} %copy-done.10), channel_id=1, source_target_pairs={{32,0},{34,2},{48,16},{50,18},{0,32},{2,34},{16,48},{18,50},{33,1}... | collective-permute-start | bytes 442376 | tf_op jit(solution)/shard_map/ppermute | solution.py:37
  48.2 0.9 collective-permute-start.2
  49.3 5.5 %collective-permute-done.c1 = bf16[288,256]{1,0:T(8,128)(2,1)S(1)} collective-permute-done((bf16[288,256]{1,0:T(8,128)(2,1)S(1)}, bf16[288,256]{1,0:T(8,128)(2,1)S(1)}, u32[]{:S(2)}, u32[]{:S(2)}) %collective-permute-start) | collective-permute-done | bytes 147488 | tf_op jit(solution)/shard_map/ppermute | solution.py:37
  54.8 5.1 %collective-permute-done.1.c2 = bf16[288,256]{1,0:T(8,128)(2,1)S(1)} collective-permute-done((bf16[288,256]{1,0:T(8,128)(2,1)S(1)}, bf16[288,256]{1,0:T(8,128)(2,1)S(1)}, u32[]{:S(2)}, u32[]{:S(2)}) %collective-permute-start.1) | collective-permute-done | bytes 147488 | tf_op jit(solution)/shard_map/ppermute | solution.py:37
  59.9 2.4 collective-permute-done.2.c3
  62.3 0.8 pad_maximum_fusion.2
  63.1 5.5 %collective-permute-done.7 = bf16[3,272,256]{2,1,0:T(8,128)(2,1)S(1)} collective-permute-done((bf16[3,272,256]{2,1,0:T(8,128)(2,1)S(1)}, bf16[3,272,256]{2,1,0:T(8,128)(2,1)S(1)}, u32[]{:S(2)}, u32[]{:S(2)}) %collective-permute-start.7) | collective-permute-done | bytes 417824 | tf_op jit(solution)/shard_map/ppermute | solution.py:37
  68.7 1.4 broadcast_in_dim.12
  70.0 5.7 %all-to-all-start.2 = ((bf16[4,3,272,256]{3,2,1,0:T(8,128)(2,1)}), bf16[4,3,272,256]{3,2,1,0:T(8,128)(2,1)S(1)}, u32[]{:S(2)}, u32[]{:S(2)}) async-start(bf16[4,3,272,256]{3,2,1,0:T(8,128)(2,1)} %broadcast_in_dim.12), calls=%async_computation.2 | async-start | bytes 3342336 | tf_op jit(solution)/shard_map/all_to_all | solution.py:289
  75.7 0.2 collective-permute-start.8
  76.0 1.7 collective-permute-done.8.refs_2_.refs_3_
  77.7 13.0 %all-gather.5.cloned.1.call-done = bf16[16,192,256]{2,1,0:T(8,128)(2,1)} async-done(((bf16[4,192,256]{2,1,0:T(8,128)(2,1)}), bf16[16,192,256]{2,1,0:T(8,128)(2,1)}) %all-gather.5.cloned.1.call-update) | async-done | bytes 1572880 | tf_op jit(solution)/shard_map/all_gather | solution.py:298
  90.7 5.9 %shard_map.95 = (f32[4,192,256]{2,1,0:T(8,128)}, f32[4,8,256]{2,1,0:T(8,128)S(1)}, f32[16,8,256]{2,1,0:T(8,128)S(1)}) custom-call(s32[5]{0:T(128)S(1)} %stack.59.ids, bf16[4,4,192,256]{3,2,1,0:T(8,128)(2,1)} %bitcast.34, bf16[4,1,272,256]{3,2,1,0:T(8,128)(2,1)} %copy-done.1, bf16[4,4,272,256]{3,2,1,0:T(8,128)(2,1)} %all-to-all-done.1.refs_1_, ...), custom_call_target="tpu_custom_call" | custom-call | flops 1006632960 | bytes 5570560 | tf_op jit(solution)/shard_map/pallas_call | solution.py:312
  96.7 3.1 %shard_map.96 = (f32[4,192,256]{2,1,0:T(8,128)S(1)}, f32[4,8,256]{2,1,0:T(8,128)S(1)}) custom-call(s32[5]{0:T(128)S(1)} %stack.59.ids, bf16[4,4,192,256]{3,2,1,0:T(8,128)(2,1)} %bitcast.35, bf16[4,3,272,256]{3,2,1,0:T(8,128)(2,1)S(1)} %all-to-all-done.2.refs_0_.refs_2_), custom_call_target="tpu_custom_call" | custom-call | flops 301989888 | bytes 1671168 | tf_op jit(solution)/shard_map/pallas_call | solution.py:312
  99.8 0.4 collective-permute-done.10.refs_5_
  100.2 9.1 %shard_map.97 = (bf16[4,4,192,256]{3,2,1,0:T(8,128)(2,1)}, f32[4,192,256]{2,1,0:T(8,128)}, f32[4,8,256]{2,1,0:T(8,128)}) custom-call(s32[5]{0:T(128)S(1)} %stack.59.ids, f32[4,192,256]{2,1,0:T(8,128)S(1)} %copy-done, f32[4,192,256]{2,1,0:T(8,128)S(1)} %get-tuple-element.39.p1, f32[4,8,256]{2,1,0:T(8,128)S(1)} %get-tuple-element.40.s0, ...), custom_call_target="tpu_custom_call" | custom-call | flops 1610612736 | bytes 12000000 | tf_op jit(solution)/shard_map/pallas_call | solution.py:340
  109.4 4.4 %all-to-all-start.3 = ((bf16[4,4,192,256]{3,2,1,0:T(8,128)(2,1)}), bf16[4,4,192,256]{3,2,1,0:T(8,128)(2,1)}, u32[]{:S(2)}, u32[]{:S(2)}) async-start(bf16[4,4,192,256]{3,2,1,0:T(8,128)(2,1)} %get-tuple-element.42), calls=%async_computation.3 | async-start | bytes 3145728 | tf_op jit(solution)/shard_map/all_to_all | solution.py:349
  113.9 21.3 %all-to-all-done.3.terms = bf16[4,4,192,256]{3,2,1,0:T(8,128)(2,1)} async-done(((bf16[4,4,192,256]{3,2,1,0:T(8,128)(2,1)}), bf16[4,4,192,256]{3,2,1,0:T(8,128)(2,1)}, u32[]{:S(2)}, u32[]{:S(2)}) %all-to-all-start.3) | async-done | bytes 1572896 | tf_op jit(solution)/shard_map/all_to_all | solution.py:349
  135.1 2.5 shard_map.98
  137.6 5.8 %all-to-all-start.4 = ((f32[16,8,128]{2,1,0:T(8,128)}), f32[16,8,128]{2,1,0:T(8,128)}, u32[]{:S(2)}, u32[]{:S(2)}) async-start(f32[16,8,128]{2,1,0:T(8,128)} %get-tuple-element.44), calls=%async_computation.4 | async-start | bytes 131072 | tf_op jit(solution)/shard_map/all_to_all | solution.py:357
  144.1 3.4 %all-to-all-done.4 = f32[16,8,128]{2,1,0:T(8,128)} async-done(((f32[16,8,128]{2,1,0:T(8,128)}), f32[16,8,128]{2,1,0:T(8,128)}, u32[]{:S(2)}, u32[]{:S(2)}) %all-to-all-start.4) | async-done | bytes 65568 | tf_op jit(solution)/shard_map/all_to_all | solution.py:357
  147.5 0.9 reduce_sum.27
  148.3 0.6 broadcast_in_dim.13
  149.0 6.9 %all-to-all-start.5 = ((f32[16,8,128]{2,1,0:T(8,128)}), f32[16,8,128]{2,1,0:T(8,128)}, u32[]{:S(2)}, u32[]{:S(2)}) async-start(f32[16,8,128]{2,1,0:T(8,128)} %broadcast_in_dim.13), calls=%async_computation.5 | async-start | bytes 131072 | tf_op jit(solution)/shard_map/all_to_all | solution.py:269
  155.9 0.2 reduce-scatter.2.cloned.1.call-start
  156.1 11.0 %all-gather.7.cloned.1.call-done = bf16[16,192,256]{2,1,0:T(8,128)(2,1)} async-done(((bf16[4,192,256]{2,1,0:T(8,128)(2,1)}), bf16[16,192,256]{2,1,0:T(8,128)(2,1)}) %all-gather.7.cloned.1.call-update) | async-done | bytes 1572880 | tf_op jit(solution)/shard_map/all_gather | solution.py:356
  167.1 6.6 %shard_map.99.pa = f32[4,192,256]{2,1,0:T(8,128)} custom-call(s32[5]{0:T(128)S(1)} %stack.59.ids, bf16[4,4,192,256]{3,2,1,0:T(8,128)(2,1)} %bitcast.38, f32[16,2,256]{2,1,0:T(2,128)S(1)} %bitcast.32, f32[16,8,256]{2,1,0:T(8,128)S(1)} %get-tuple-element.43.gabs, bf16[4,1,272,256]{3,2,1,0:T(8,128)(2,1)} %copy-done.1, ...), custom_call_target="tpu_custom_call" | custom-call | flops 1610612736 | bytes 12000000 | tf_op jit(solution)/shard_map/pallas_call | solution.py:359
  173.7 7.8 %shard_map.100 = (bf16[4,4,192,256]{3,2,1,0:T(8,128)(2,1)}, f32[16,1,256]{2,1,0:T(1,128)}) custom-call(f32[1]{0:T(128)S(6)} %copy.12.radius, s32[5]{0:T(128)S(1)} %stack.59.ids, f32[16,8,128]{2,1,0:T(8,128)} %all-to-all-done.5.totals, f32[4,192,256]{2,1,0:T(8,128)} %get-tuple-element.47.praw, f32[4,8,256]{2,1,0:T(8,128)} %get-tuple-element.48.rs, ...), custom_call_target="tpu_custom_call" | custom-call | flops 1610612736 | bytes 12000000 | tf_op jit(solution)/shard_map/pallas_call | solution.py:367
  181.5 28.4 %reduce-scatter.2.cloned.1.call-done = bf16[1,4,192,256]{3,2,1,0:T(8,128)(2,1)} async-done(((bf16[4,4,192,256]{3,2,1,0:T(8,128)(2,1)}), bf16[1,4,192,256]{3,2,1,0:T(8,128)(2,1)}) %reduce-scatter.2.cloned.1.call-update) | async-done | bytes 393232 | tf_op jit(solution)/shard_map/reduce_scatter | solution.py:376
  209.9 1.1 slice_bitcast_fusion
  211.0 4.2 %collective-permute-start.13 = (bf16[192,256]{1,0:T(8,128)(2,1)S(1)}, bf16[192,256]{1,0:T(8,128)(2,1)S(1)}, u32[]{:S(2)}, u32[]{:S(2)}) collective-permute-start(bf16[192,256]{1,0:T(8,128)(2,1)S(1)} %get-tuple-element.53), channel_id=1, source_target_pairs={{16,0},{18,2},{32,16},{34,18},{48,32},{50,34},{0,48},{2,50},{17,1}... | collective-permute-start | bytes 294920 | tf_op jit(solution)/shard_map/ppermute | solution.py:37
  215.2 2.0 collective-permute-start.12
  217.2 2.5 %collective-permute-start.11 = (bf16[192,256]{1,0:T(8,128)(2,1)S(1)}, bf16[192,256]{1,0:T(8,128)(2,1)S(1)}, u32[]{:S(2)}, u32[]{:S(2)}) collective-permute-start(bf16[192,256]{1,0:T(8,128)(2,1)S(1)} %get-tuple-element.55), channel_id=1, source_target_pairs={{48,0},{50,2},{0,16},{2,18},{16,32},{18,34},{32,48},{34,50},{49,1}... | collective-permute-start | bytes 294920 | tf_op jit(solution)/shard_map/ppermute | solution.py:37
  219.8 8.5 %all_to_all.40 = f32[16,1,256]{2,1,0:T(1,128)S(1)} all-to-all(f32[16,1,256]{2,1,0:T(1,128)S(1)} %copy-done.8), channel_id=1, replica_groups=mesh['y'=4,'zh'=4,'x'=4,'zl'=2,'c'=2] {'x','zl','c'}, dimensions={0} | all-to-all | bytes 32768 | tf_op jit(solution)/shard_map/all_to_all | solution.py:377
  228.3 14.5 %all_to_all.41 = f32[16,1,256]{2,1,0:T(1,128)S(1)} all-to-all(f32[16,1,256]{2,1,0:T(1,128)S(1)} %broadcast_in_dim.14), channel_id=1, replica_groups=mesh['y'=4,'zh'=4,'x'=4,'zl'=2,'c'=2] {'y','zh'}, dimensions={0} | all-to-all | bytes 32768 | tf_op jit(solution)/shard_map/all_to_all | solution.py:269
  242.9 0.6 reduce_sum.29
  243.5 1.6 shard_map.101
  (52 shorter events, 0.7 us)
Async XLA Ops:
  9.8 27.2 %all-to-all-start = ((bf16[4,1,272,256]{3,2,1,0:T(8,128)(2,1)}), bf16[4,1,272,256]{3,2,1,0:T(8,128)(2,1)S(1)}, u32[]{:S(2)}, u32[]{:S(2)}) async-start(bf16[4,1,272,256]{3,2,1,0:T(8,128)(2,1)} %get-tuple-element.32), calls=%async_computation | async-start | bytes 1114112 | tf_op jit(solution)/shard_map/all_to_all | solution.py:293
  15.5 11.5 %collective-permute-start.6 = (bf16[272,256]{1,0:T(8,128)(2,1)}, bf16[272,256]{1,0:T(8,128)(2,1)S(1)}, u32[]{:S(2)}, u32[]{:S(2)}) collective-permute-start(bf16[272,256]{1,0:T(8,128)(2,1)} %get-tuple-element.33), channel_id=1, source_target_pairs={{2,0},{0,2},{18,16},{16,18},{34,32},{32,34},{50,48},{48,50},{3,1},... | collective-permute-start | bytes 417800 | tf_op jit(solution)/shard_map/ppermute | solution.py:37
  16.5 19.3 %collective-permute-start.5 = (bf16[272,256]{1,0:T(8,128)(2,1)}, bf16[272,256]{1,0:T(8,128)(2,1)S(1)}, u32[]{:S(2)}, u32[]{:S(2)}) collective-permute-start(bf16[272,256]{1,0:T(8,128)(2,1)} %get-tuple-element.33), channel_id=1, source_target_pairs={{32,0},{34,2},{48,16},{50,18},{0,32},{2,34},{16,48},{18,50},{33,1}... | collective-permute-start | bytes 417800 | tf_op jit(solution)/shard_map/ppermute | solution.py:37
  22.8 14.1 %collective-permute-start.4 = (bf16[272,256]{1,0:T(8,128)(2,1)}, bf16[272,256]{1,0:T(8,128)(2,1)S(1)}, u32[]{:S(2)}, u32[]{:S(2)}) collective-permute-start(bf16[272,256]{1,0:T(8,128)(2,1)} %get-tuple-element.33), channel_id=1, source_target_pairs={{48,0},{50,2},{0,16},{2,18},{16,32},{18,34},{32,48},{34,50},{49,1}... | collective-permute-start | bytes 417800 | tf_op jit(solution)/shard_map/ppermute | solution.py:37
  24.2 12.6 %collective-permute-start.3 = (bf16[272,256]{1,0:T(8,128)(2,1)}, bf16[272,256]{1,0:T(8,128)(2,1)S(1)}, u32[]{:S(2)}, u32[]{:S(2)}) collective-permute-start(bf16[272,256]{1,0:T(8,128)(2,1)} %get-tuple-element.33), channel_id=1, source_target_pairs={{16,0},{18,2},{32,16},{34,18},{48,32},{50,34},{0,48},{2,50},{17,1}... | collective-permute-start | bytes 417800 | tf_op jit(solution)/shard_map/ppermute | solution.py:37
  37.0 38.8 %copy-start.1 = (bf16[4,1,272,256]{3,2,1,0:T(8,128)(2,1)}, bf16[4,1,272,256]{3,2,1,0:T(8,128)(2,1)S(1)}, u32[]{:S(2)}) copy-start(bf16[4,1,272,256]{3,2,1,0:T(8,128)(2,1)S(1)} %all-to-all-done.refs_0_) | copy-start | bytes 1671172
  38.5 5.0 %copy-start.11 = (bf16[288,256]{1,0:T(8,128)(2,1)S(1)}, bf16[288,256]{1,0:T(8,128)(2,1)}, u32[]{:S(2)}) copy-start(bf16[288,256]{1,0:T(8,128)(2,1)} %get-tuple-element.29) | copy-start | bytes 442372
  38.5 7.2 %copy-start.10 = (bf16[288,256]{1,0:T(8,128)(2,1)S(1)}, bf16[288,256]{1,0:T(8,128)(2,1)}, u32[]{:S(2)}) copy-start(bf16[288,256]{1,0:T(8,128)(2,1)} %get-tuple-element.30) | copy-start | bytes 442372
  38.5 9.7 %copy-start.9 = (bf16[288,256]{1,0:T(8,128)(2,1)S(1)}, bf16[288,256]{1,0:T(8,128)(2,1)}, u32[]{:S(2)}) copy-start(bf16[288,256]{1,0:T(8,128)(2,1)} %get-tuple-element.31) | copy-start | bytes 442372
  38.5 10.6 %copy-start.3 = (bf16[288,256]{1,0:T(8,128)(2,1)S(1)}, bf16[288,256]{1,0:T(8,128)(2,1)}, u32[]{:S(2)}) copy-start(bf16[288,256]{1,0:T(8,128)(2,1)} %get-tuple-element.28.c0) | copy-start | bytes 442372
  38.5 30.1 %all-to-all-start.1 = ((bf16[4,4,272,256]{3,2,1,0:T(8,128)(2,1)}), bf16[4,4,272,256]{3,2,1,0:T(8,128)(2,1)}, u32[]{:S(2)}, u32[]{:S(2)}) async-start(bf16[4,4,272,256]{3,2,1,0:T(8,128)(2,1)} %broadcast_in_dim.11), calls=%async_computation.1 | async-start | bytes 4456448 | tf_op jit(solution)/shard_map/all_to_all | solution.py:289
  43.5 47.2 %all-gather.5.cloned.1.call-start = ((), (), s32[]{:S(2)}) async-start(), calls=%async_computation.10 | async-start | bytes 1966080 | tf_op jit(solution)/shard_map/all_gather | solution.py:298
  43.5 11.3 %collective-permute-start = (bf16[288,256]{1,0:T(8,128)(2,1)S(1)}, bf16[288,256]{1,0:T(8,128)(2,1)S(1)}, u32[]{:S(2)}, u32[]{:S(2)}) collective-permute-start(bf16[288,256]{1,0:T(8,128)(2,1)S(1)} %copy-done.11), channel_id=1, source_target_pairs={{16,0},{18,2},{32,16},{34,18},{48,32},{50,34},{0,48},{2,50},{17,1}... | collective-permute-start | bytes 442376 | tf_op jit(solution)/shard_map/ppermute | solution.py:37
  45.7 14.1 %collective-permute-start.1 = (bf16[288,256]{1,0:T(8,128)(2,1)S(1)}, bf16[288,256]{1,0:T(8,128)(2,1)S(1)}, u32[]{:S(2)}, u32[]{:S(2)}) collective-permute-start(bf16[288,256]{1,0:T(8,128)(2,1)S(1)} %copy-done.10), channel_id=1, source_target_pairs={{32,0},{34,2},{48,16},{50,18},{0,32},{2,34},{16,48},{18,50},{33,1}... | collective-permute-start | bytes 442376 | tf_op jit(solution)/shard_map/ppermute | solution.py:37
  48.2 14.0 %collective-permute-start.2 = (bf16[288,256]{1,0:T(8,128)(2,1)S(1)}, bf16[288,256]{1,0:T(8,128)(2,1)S(1)}, u32[]{:S(2)}, u32[]{:S(2)}) collective-permute-start(bf16[288,256]{1,0:T(8,128)(2,1)S(1)} %copy-done.9), channel_id=1, source_target_pairs={{48,0},{50,2},{0,16},{2,18},{16,32},{18,34},{32,48},{34,50},{49,1}... | collective-permute-start | bytes 442376 | tf_op jit(solution)/shard_map/ppermute | solution.py:37
  49.2 19.5 %collective-permute-start.7 = (bf16[3,272,256]{2,1,0:T(8,128)(2,1)S(1)}, bf16[3,272,256]{2,1,0:T(8,128)(2,1)S(1)}, u32[]{:S(2)}, u32[]{:S(2)}) collective-permute-start(bf16[3,272,256]{2,1,0:T(8,128)(2,1)S(1)} %pad_maximum_fusion.1), channel_id=1, source_target_pairs={{2,0},{0,2},{18,16},{16,18},{34,32},{32,34},{50,48},{48,50},{3,1},... | collective-permute-start | bytes 1253384 | tf_op jit(solution)/shard_map/ppermute | solution.py:37
  54.8 15.3 %copy-start.4 = (bf16[288,256]{1,0:T(8,128)(2,1)}, bf16[288,256]{1,0:T(8,128)(2,1)S(1)}, u32[]{:S(2)}) copy-start(bf16[288,256]{1,0:T(8,128)(2,1)S(1)} %collective-permute-done.c1) | copy-start | bytes 442372
  59.9 10.2 %copy-start.5 = (bf16[288,256]{1,0:T(8,128)(2,1)}, bf16[288,256]{1,0:T(8,128)(2,1)S(1)}, u32[]{:S(2)}) copy-start(bf16[288,256]{1,0:T(8,128)(2,1)S(1)} %collective-permute-done.1.c2) | copy-start | bytes 442372
  62.3 7.8 %copy-start.6 = (bf16[288,256]{1,0:T(8,128)(2,1)}, bf16[288,256]{1,0:T(8,128)(2,1)S(1)}, u32[]{:S(2)}) copy-start(bf16[288,256]{1,0:T(8,128)(2,1)S(1)} %collective-permute-done.2.c3) | copy-start | bytes 442372
  68.7 22.0 %collective-permute-start.9 = (bf16[4,4,272,256]{3,2,1,0:T(8,128)(2,1)}, bf16[4,4,272,256]{3,2,1,0:T(8,128)(2,1)}, u32[]{:S(2)}, u32[]{:S(2)}) collective-permute-start(bf16[4,4,272,256]{3,2,1,0:T(8,128)(2,1)} %all-to-all-done.1.refs_1_), channel_id=1, source_target_pairs={{0,1},{1,0},{2,3},{3,2},{4,5},{5,4},{6,7},{7,6},{8,9},{9,8},{10,11... | collective-permute-start | bytes 6684680 | tf_op jit(solution)/shard_map/ppermute | solution.py:41
  70.0 26.6 %all-to-all-start.2 = ((bf16[4,3,272,256]{3,2,1,0:T(8,128)(2,1)}), bf16[4,3,272,256]{3,2,1,0:T(8,128)(2,1)S(1)}, u32[]{:S(2)}, u32[]{:S(2)}) async-start(bf16[4,3,272,256]{3,2,1,0:T(8,128)(2,1)} %broadcast_in_dim.12), calls=%async_computation.2 | async-start | bytes 3342336 | tf_op jit(solution)/shard_map/all_to_all | solution.py:289
  75.7 2.0 collective-permute-start.8
  77.7 13.0 %copy-start.2 = (bf16[4,1,272,256]{3,2,1,0:T(8,128)(2,1)}, bf16[4,1,272,256]{3,2,1,0:T(8,128)(2,1)S(1)}, u32[]{:S(2)}) copy-start(bf16[4,1,272,256]{3,2,1,0:T(8,128)(2,1)S(1)} %collective-permute-done.8.refs_2_.refs_3_) | copy-start | bytes 1671172
  96.6 3.6 %copy-start = (f32[4,192,256]{2,1,0:T(8,128)S(1)}, f32[4,192,256]{2,1,0:T(8,128)}, u32[]{:S(2)}) copy-start(f32[4,192,256]{2,1,0:T(8,128)} %get-tuple-element.36.p0) | copy-start | bytes 2359300
  96.6 3.6 %collective-permute-start.10 = (bf16[4,3,272,256]{3,2,1,0:T(8,128)(2,1)S(1)}, bf16[4,3,272,256]{3,2,1,0:T(8,128)(2,1)S(1)}, u32[]{:S(2)}, u32[]{:S(2)}) collective-permute-start(bf16[4,3,272,256]{3,2,1,0:T(8,128)(2,1)S(1)} %all-to-all-done.2.refs_0_.refs_2_), channel_id=1, source_target_pairs={{0,1},{1,0},{2,3},{3,2},{4,5},{5,4},{6,7},{7,6},{8,9},{9,8},{10,11... | collective-permute-start | bytes 5013512 | tf_op jit(solution)/shard_map/ppermute | solution.py:41
  109.3 4.5 %copy-start.7 = (s32[2,4096]{1,0:T(2,128)S(1)}, s32[2,4096]{1,0:T(2,128)}, u32[]{:S(2)}) copy-start(s32[2,4096]{1,0:T(2,128)} %param.12) | copy-start | bytes 98308
  109.4 25.8 %all-to-all-start.3 = ((bf16[4,4,192,256]{3,2,1,0:T(8,128)(2,1)}), bf16[4,4,192,256]{3,2,1,0:T(8,128)(2,1)}, u32[]{:S(2)}, u32[]{:S(2)}) async-start(bf16[4,4,192,256]{3,2,1,0:T(8,128)(2,1)} %get-tuple-element.42), calls=%async_computation.3 | async-start | bytes 3145728 | tf_op jit(solution)/shard_map/all_to_all | solution.py:349
  113.8 53.3 %all-gather.7.cloned.1.call-start = ((), (), s32[]{:S(2)}) async-start(), calls=%async_computation.11 | async-start | bytes 1966080 | tf_op jit(solution)/shard_map/all_gather | solution.py:356
  137.6 9.8 %all-to-all-start.4 = ((f32[16,8,128]{2,1,0:T(8,128)}), f32[16,8,128]{2,1,0:T(8,128)}, u32[]{:S(2)}, u32[]{:S(2)}) async-start(f32[16,8,128]{2,1,0:T(8,128)} %get-tuple-element.44), calls=%async_computation.4 | async-start | bytes 131072 | tf_op jit(solution)/shard_map/all_to_all | solution.py:357
  149.0 24.7 %all-to-all-start.5 = ((f32[16,8,128]{2,1,0:T(8,128)}), f32[16,8,128]{2,1,0:T(8,128)}, u32[]{:S(2)}, u32[]{:S(2)}) async-start(f32[16,8,128]{2,1,0:T(8,128)} %broadcast_in_dim.13), calls=%async_computation.5 | async-start | bytes 131072 | tf_op jit(solution)/shard_map/all_to_all | solution.py:269
  155.9 54.1 %reduce-scatter.2.cloned.1.call-start = ((), (), s32[]{:S(2)}) async-start(), calls=%async_computation.9 | async-start | bytes 1966080 | tf_op jit(solution)/shard_map/reduce_scatter | solution.py:376
  181.5 38.3 %copy-start.8 = (f32[16,1,256]{2,1,0:T(1,128)S(1)}, f32[16,1,256]{2,1,0:T(1,128)}, u32[]{:S(2)}) copy-start(f32[16,1,256]{2,1,0:T(1,128)} %get-tuple-element.49) | copy-start | bytes 49156
  211.0 32.5 %collective-permute-start.13 = (bf16[192,256]{1,0:T(8,128)(2,1)S(1)}, bf16[192,256]{1,0:T(8,128)(2,1)S(1)}, u32[]{:S(2)}, u32[]{:S(2)}) collective-permute-start(bf16[192,256]{1,0:T(8,128)(2,1)S(1)} %get-tuple-element.53), channel_id=1, source_target_pairs={{16,0},{18,2},{32,16},{34,18},{48,32},{50,34},{0,48},{2,50},{17,1}... | collective-permute-start | bytes 294920 | tf_op jit(solution)/shard_map/ppermute | solution.py:37
  215.2 28.3 %collective-permute-start.12 = (bf16[192,256]{1,0:T(8,128)(2,1)S(1)}, bf16[192,256]{1,0:T(8,128)(2,1)S(1)}, u32[]{:S(2)}, u32[]{:S(2)}) collective-permute-start(bf16[192,256]{1,0:T(8,128)(2,1)S(1)} %get-tuple-element.54), channel_id=1, source_target_pairs={{32,0},{34,2},{48,16},{50,18},{0,32},{2,34},{16,48},{18,50},{33,1}... | collective-permute-start | bytes 294920 | tf_op jit(solution)/shard_map/ppermute | solution.py:37
  217.2 26.3 %collective-permute-start.11 = (bf16[192,256]{1,0:T(8,128)(2,1)S(1)}, bf16[192,256]{1,0:T(8,128)(2,1)S(1)}, u32[]{:S(2)}, u32[]{:S(2)}) collective-permute-start(bf16[192,256]{1,0:T(8,128)(2,1)S(1)} %get-tuple-element.55), channel_id=1, source_target_pairs={{48,0},{50,2},{0,16},{2,18},{16,32},{18,34},{32,48},{34,50},{49,1}... | collective-permute-start | bytes 294920 | tf_op jit(solution)/shard_map/ppermute | solution.py:37
Sparse Core Ops, SparseCore 0:
  63.2 27.3 all-gather.4
  137.8 29.2 all-gather.6
  181.7 28.2 reduce-scatter.1

commit v10 on v9

--- a/solution.py
+++ b/solution.py
@@ -375,7 +375,9 @@
     )(radius, ids, after(part, pa), in_hbm(praw), in_hbm(rs), in_hbm(pa), *pieces, weights, ascs, mask, *tok_refs)
     sums = lax.psum_scatter(out2, "y", scatter_dimension=0, tiled=False)
     dg = jnp.sum(lax.all_to_all(dgp, MP, 0, 0, tiled=True), axis=0)
-    grad_gain = jnp.sum(spread(dg, DP).reshape(16, BLK), axis=0)
+    dg = spread(dg, DP)
+    sums = after(sums, dg)
+    grad_gain = jnp.sum(dg.reshape(16, BLK), axis=0)
     sums = [sums[0]] + [from_z(sums[k], 4 - k, 0) for k in range(1, 4)]
     out = hbm((BLK, 4 * SUB), F32)
     grad_gate, grad_up = call(

time: 254 us -> 237 us (0.933)
  waiting for transfers between devices: 108 us -> 86 us
  blocking collectives: 23.1 us -> 26.8 us
    reduce_scatter x1, waiting for transfers between devices: 28.4 us -> 1.64 us  [body(): sums = lax.psum_scatter(out2, 'y', scatter_dimension=0, tiled=False)]
    ppermute x11, waiting for transfers between devices: 28.5 us -> 33.6 us  [from_z(): return lax.ppermute(value, ('zh', 'zl'), pairs)]
    all_to_all x1, blocking collectives: 14.5 us -> 17.2 us  [spread(): lax.all_to_all(jnp.broadcast_to(value[None], (n,) + value.shape), axes, 0...]
  transfers between devices with their start and end apart: 23 -> 23, of which waited for: 13 -> 15; matrix products, arithmetic and copies ran while one was open for 2% -> 2% of each run, Pallas kernels for 6% -> 7%
where the time goes in v10:
time: 237 us; the launch traced here: 234 us
  waiting for transfers between devices  86 us (36%)
  starting transfers between devices  59.9 us (25%)
  Pallas kernels  39.2 us (17%)
  blocking collectives  26.8 us (11%)
  between operations  14.6 us (6%)
  local copies, waits for them, and re-layouts  4.78 us (2%)
  other arithmetic  2.43 us (1%)
    ppermute x11, waiting for transfers between devices, from_z(): return lax.ppermute(value, ('zh', 'zl'), pairs)  33.6 us
    ppermute x11, starting transfers between devices, from_z(): return lax.ppermute(value, ('zh', 'zl'), pairs)  25.8 us
    all_to_all x1, waiting for transfers between devices, body(): terms = lax.all_to_all(out1, 'y', 0, 0, tiled=True)  21.3 us
    all_to_all x1, blocking collectives, spread(): lax.all_to_all(jnp.broadcast_to(value[None], (n,) + value.shape), axes, 0...  17.2 us
    all_gather x1, waiting for transfers between devices, body(): weights = in_hbm(lax.all_gather(part_w, 'y', axis=0, tiled=False))  13 us
    all_gather x1, waiting for transfers between devices, body(): ascs = in_hbm(lax.all_gather(asc, 'y', axis=0, tiled=False))  11 us
    all_to_all x2, starting transfers between devices, over_x(): lax.all_to_all(jnp.broadcast_to(value[None], (4,) + value.shape), 'x', 0,...  10.6 us
    all_to_all x1, blocking collectives, body(): dg = jnp.sum(lax.all_to_all(dgp, MP, 0, 0, tiled=True), axis=0)  9.64 us
  transfers between devices with their start and end apart: 23, of which 15 were waited for; matrix products, arithmetic and copies ran while one was open for 2% of the time, Pallas kernels for 7%

profile of v10, /device:TPU:4, one launch (start us, length us, event | category | flops | bytes accessed | tf_op | source)
XLA Modules:
  0.0 233.7 jit_solution(15545750752328228809)
XLA Ops:
  7.3 2.5 %shard_map.94 = (bf16[272,256]{1,0:T(8,128)(2,1)}, bf16[4,1,272,256]{3,2,1,0:T(8,128)(2,1)}, bf16[288,256]{1,0:T(8,128)(2,1)}, bf16[288,256]{1,0:T(8,128)(2,1)},...) custom-call(s32[5]{0:T(128)S(1)} %stack.59.ids, bf16[256,256]{1,0:T(8,128)(2,1)} %tokens.1, f32[1,256]{1,0:T(1,128)} %bitcast.49, ...), custom_call_target="tpu_custom_call" | custom-call | flops 1000000 | bytes 1000000 | tf_op jit(solution)/shard_map/pallas_call | solution.py:277
  9.8 5.7 %all-to-all-start = ((bf16[4,1,272,256]{3,2,1,0:T(8,128)(2,1)}), bf16[4,1,272,256]{3,2,1,0:T(8,128)(2,1)S(1)}, u32[]{:S(2)}, u32[]{:S(2)}) async-start(bf16[4,1,272,256]{3,2,1,0:T(8,128)(2,1)} %get-tuple-element.33), calls=%async_computation | async-start | bytes 1114112 | tf_op jit(solution)/shard_map/all_to_all | solution.py:293
  15.5 1.0 collective-permute-start.6
  16.5 6.3 %collective-permute-start.5 = (bf16[272,256]{1,0:T(8,128)(2,1)}, bf16[272,256]{1,0:T(8,128)(2,1)S(1)}, u32[]{:S(2)}, u32[]{:S(2)}) collective-permute-start(bf16[272,256]{1,0:T(8,128)(2,1)} %get-tuple-element.34), channel_id=1, source_target_pairs={{32,0},{34,2},{48,16},{50,18},{0,32},{2,34},{16,48},{18,50},{33,1}... | collective-permute-start | bytes 417800 | tf_op jit(solution)/shard_map/ppermute | solution.py:37
  22.8 1.5 collective-permute-start.4
  24.2 2.7 %collective-permute-start.3 = (bf16[272,256]{1,0:T(8,128)(2,1)}, bf16[272,256]{1,0:T(8,128)(2,1)S(1)}, u32[]{:S(2)}, u32[]{:S(2)}) collective-permute-start(bf16[272,256]{1,0:T(8,128)(2,1)} %get-tuple-element.34), channel_id=1, source_target_pairs={{16,0},{18,2},{32,16},{34,18},{48,32},{50,34},{0,48},{2,50},{17,1}... | collective-permute-start | bytes 417800 | tf_op jit(solution)/shard_map/ppermute | solution.py:37
  26.9 8.9 %collective-permute-done.5 = bf16[272,256]{1,0:T(8,128)(2,1)S(1)} collective-permute-done((bf16[272,256]{1,0:T(8,128)(2,1)}, bf16[272,256]{1,0:T(8,128)(2,1)S(1)}, u32[]{:S(2)}, u32[]{:S(2)}) %collective-permute-start.5) | collective-permute-done | bytes 139296 | tf_op jit(solution)/shard_map/ppermute | solution.py:37
  35.8 1.1 collective-permute-done.4
  37.0 1.6 broadcast_in_dim.11
  38.5 4.9 %all-to-all-start.1 = ((bf16[4,4,272,256]{3,2,1,0:T(8,128)(2,1)}), bf16[4,4,272,256]{3,2,1,0:T(8,128)(2,1)}, u32[]{:S(2)}, u32[]{:S(2)}) async-start(bf16[4,4,272,256]{3,2,1,0:T(8,128)(2,1)} %broadcast_in_dim.11), calls=%async_computation.1 | async-start | bytes 4456448 | tf_op jit(solution)/shard_map/all_to_all | solution.py:289
  43.5 2.2 collective-permute-start
  45.7 2.5 %collective-permute-start.1 = (bf16[288,256]{1,0:T(8,128)(2,1)S(1)}, bf16[288,256]{1,0:T(8,128)(2,1)S(1)}, u32[]{:S(2)}, u32[]{:S(2)}) collective-permute-start(bf16[288,256]{1,0:T(8,128)(2,1)S(1)} %copy-done.9), channel_id=1, source_target_pairs={{32,0},{34,2},{48,16},{50,18},{0,32},{2,34},{16,48},{18,50},{33,1}... | collective-permute-start | bytes 442376 | tf_op jit(solution)/shard_map/ppermute | solution.py:37
  48.3 0.9 collective-permute-start.2
  49.3 5.5 %collective-permute-done.c1 = bf16[288,256]{1,0:T(8,128)(2,1)S(1)} collective-permute-done((bf16[288,256]{1,0:T(8,128)(2,1)S(1)}, bf16[288,256]{1,0:T(8,128)(2,1)S(1)}, u32[]{:S(2)}, u32[]{:S(2)}) %collective-permute-start) | collective-permute-done | bytes 147488 | tf_op jit(solution)/shard_map/ppermute | solution.py:37
  54.8 5.0 %collective-permute-done.1.c2 = bf16[288,256]{1,0:T(8,128)(2,1)S(1)} collective-permute-done((bf16[288,256]{1,0:T(8,128)(2,1)S(1)}, bf16[288,256]{1,0:T(8,128)(2,1)S(1)}, u32[]{:S(2)}, u32[]{:S(2)}) %collective-permute-start.1) | collective-permute-done | bytes 147488 | tf_op jit(solution)/shard_map/ppermute | solution.py:37
  59.9 2.4 %collective-permute-done.2.c3 = bf16[288,256]{1,0:T(8,128)(2,1)S(1)} collective-permute-done((bf16[288,256]{1,0:T(8,128)(2,1)S(1)}, bf16[288,256]{1,0:T(8,128)(2,1)S(1)}, u32[]{:S(2)}, u32[]{:S(2)}) %collective-permute-start.2) | collective-permute-done | bytes 147488 | tf_op jit(solution)/shard_map/ppermute | solution.py:37
  62.3 0.8 pad_maximum_fusion.2
  63.1 5.5 %collective-permute-done.7 = bf16[3,272,256]{2,1,0:T(8,128)(2,1)S(1)} collective-permute-done((bf16[3,272,256]{2,1,0:T(8,128)(2,1)S(1)}, bf16[3,272,256]{2,1,0:T(8,128)(2,1)S(1)}, u32[]{:S(2)}, u32[]{:S(2)}) %collective-permute-start.7) | collective-permute-done | bytes 417824 | tf_op jit(solution)/shard_map/ppermute | solution.py:37
  68.7 1.4 broadcast_in_dim.12
  70.0 5.7 %all-to-all-start.2 = ((bf16[4,3,272,256]{3,2,1,0:T(8,128)(2,1)}), bf16[4,3,272,256]{3,2,1,0:T(8,128)(2,1)S(1)}, u32[]{:S(2)}, u32[]{:S(2)}) async-start(bf16[4,3,272,256]{3,2,1,0:T(8,128)(2,1)} %broadcast_in_dim.12), calls=%async_computation.2 | async-start | bytes 3342336 | tf_op jit(solution)/shard_map/all_to_all | solution.py:289
  76.0 1.7 collective-permute-done.8.refs_2_.refs_3_
  77.7 13.0 %all-gather.5.cloned.1.call-done = bf16[16,192,256]{2,1,0:T(8,128)(2,1)} async-done(((bf16[4,192,256]{2,1,0:T(8,128)(2,1)}), bf16[16,192,256]{2,1,0:T(8,128)(2,1)}) %all-gather.5.cloned.1.call-update) | async-done | bytes 1572880 | tf_op jit(solution)/shard_map/all_gather | solution.py:298
  90.7 5.9 %shard_map.95 = (f32[4,192,256]{2,1,0:T(8,128)}, f32[4,8,256]{2,1,0:T(8,128)S(1)}, f32[16,8,256]{2,1,0:T(8,128)S(1)}) custom-call(s32[5]{0:T(128)S(1)} %stack.59.ids, bf16[4,4,192,256]{3,2,1,0:T(8,128)(2,1)} %bitcast.35, bf16[4,1,272,256]{3,2,1,0:T(8,128)(2,1)} %copy-done.1, bf16[4,4,272,256]{3,2,1,0:T(8,128)(2,1)} %all-to-all-done.1.refs_1_, ...), custom_call_target="tpu_custom_call" | custom-call | flops 1006632960 | bytes 5570560 | tf_op jit(solution)/shard_map/pallas_call | solution.py:312
  96.7 3.1 %shard_map.96 = (f32[4,192,256]{2,1,0:T(8,128)S(1)}, f32[4,8,256]{2,1,0:T(8,128)S(1)}) custom-call(s32[5]{0:T(128)S(1)} %stack.59.ids, bf16[4,4,192,256]{3,2,1,0:T(8,128)(2,1)} %bitcast.36, bf16[4,3,272,256]{3,2,1,0:T(8,128)(2,1)S(1)} %all-to-all-done.2.refs_0_.refs_2_), custom_call_target="tpu_custom_call" | custom-call | flops 301989888 | bytes 1671168 | tf_op jit(solution)/shard_map/pallas_call | solution.py:312
  99.8 0.4 collective-permute-done.10.refs_5_
  100.3 9.1 %shard_map.97 = (bf16[4,4,192,256]{3,2,1,0:T(8,128)(2,1)}, f32[4,192,256]{2,1,0:T(8,128)}, f32[4,8,256]{2,1,0:T(8,128)}) custom-call(s32[5]{0:T(128)S(1)} %stack.59.ids, f32[4,192,256]{2,1,0:T(8,128)S(1)} %copy-done, f32[4,192,256]{2,1,0:T(8,128)S(1)} %get-tuple-element.40.p1, f32[4,8,256]{2,1,0:T(8,128)S(1)} %get-tuple-element.41.s0, ...), custom_call_target="tpu_custom_call" | custom-call | flops 1610612736 | bytes 12000000 | tf_op jit(solution)/shard_map/pallas_call | solution.py:340
  109.4 4.4 %all-to-all-start.3 = ((bf16[4,4,192,256]{3,2,1,0:T(8,128)(2,1)}), bf16[4,4,192,256]{3,2,1,0:T(8,128)(2,1)}, u32[]{:S(2)}, u32[]{:S(2)}) async-start(bf16[4,4,192,256]{3,2,1,0:T(8,128)(2,1)} %get-tuple-element.43), calls=%async_computation.3 | async-start | bytes 3145728 | tf_op jit(solution)/shard_map/all_to_all | solution.py:349
  113.9 21.3 %all-to-all-done.3.terms = bf16[4,4,192,256]{3,2,1,0:T(8,128)(2,1)} async-done(((bf16[4,4,192,256]{3,2,1,0:T(8,128)(2,1)}), bf16[4,4,192,256]{3,2,1,0:T(8,128)(2,1)}, u32[]{:S(2)}, u32[]{:S(2)}) %all-to-all-start.3) | async-done | bytes 1572896 | tf_op jit(solution)/shard_map/all_to_all | solution.py:349
  135.1 2.5 %shard_map.98 = (bf16[4,192,256]{2,1,0:T(8,128)(2,1)}, f32[16,8,128]{2,1,0:T(8,128)}) custom-call(s32[5]{0:T(128)S(1)} %stack.59.ids, bf16[4,4,192,256]{3,2,1,0:T(8,128)(2,1)} %all-to-all-done.3.terms, f32[16,8,256]{2,1,0:T(8,128)S(1)} %get-tuple-element.44.gabs, f32[16,2,256]{2,1,0:T(2,128)S(1)} %bitcast.32), custom_call_target="tpu_custom_call" | custom-call | flops 1000000 | bytes 1000000 | tf_op jit(solution)/shard_map/pallas_call | solution.py:350
  137.7 5.8 %all-to-all-start.4 = ((f32[16,8,128]{2,1,0:T(8,128)}), f32[16,8,128]{2,1,0:T(8,128)}, u32[]{:S(2)}, u32[]{:S(2)}) async-start(f32[16,8,128]{2,1,0:T(8,128)} %get-tuple-element.45), calls=%async_computation.4 | async-start | bytes 131072 | tf_op jit(solution)/shard_map/all_to_all | solution.py:357
  144.1 3.4 %all-to-all-done.4 = f32[16,8,128]{2,1,0:T(8,128)} async-done(((f32[16,8,128]{2,1,0:T(8,128)}), f32[16,8,128]{2,1,0:T(8,128)}, u32[]{:S(2)}, u32[]{:S(2)}) %all-to-all-start.4) | async-done | bytes 65568 | tf_op jit(solution)/shard_map/all_to_all | solution.py:357
  147.5 0.9 reduce_sum.27
  148.4 0.6 broadcast_in_dim.13
  149.0 6.9 %all-to-all-start.5 = ((f32[16,8,128]{2,1,0:T(8,128)}), f32[16,8,128]{2,1,0:T(8,128)}, u32[]{:S(2)}, u32[]{:S(2)}) async-start(f32[16,8,128]{2,1,0:T(8,128)} %broadcast_in_dim.13), calls=%async_computation.5 | async-start | bytes 131072 | tf_op jit(solution)/shard_map/all_to_all | solution.py:269
  156.1 11.0 %all-gather.7.cloned.1.call-done = bf16[16,192,256]{2,1,0:T(8,128)(2,1)} async-done(((bf16[4,192,256]{2,1,0:T(8,128)(2,1)}), bf16[16,192,256]{2,1,0:T(8,128)(2,1)}) %all-gather.7.cloned.1.call-update) | async-done | bytes 1572880 | tf_op jit(solution)/shard_map/all_gather | solution.py:356
  167.1 6.6 %shard_map.99.pa = f32[4,192,256]{2,1,0:T(8,128)} custom-call(s32[5]{0:T(128)S(1)} %stack.59.ids, bf16[4,4,192,256]{3,2,1,0:T(8,128)(2,1)} %bitcast.39, f32[16,2,256]{2,1,0:T(2,128)S(1)} %bitcast.33, f32[16,8,256]{2,1,0:T(8,128)S(1)} %get-tuple-element.44.gabs, bf16[4,1,272,256]{3,2,1,0:T(8,128)(2,1)} %copy-done.1, ...), custom_call_target="tpu_custom_call" | custom-call | flops 1610612736 | bytes 12000000 | tf_op jit(solution)/shard_map/pallas_call | solution.py:359
  173.7 7.8 %shard_map.100 = (bf16[4,4,192,256]{3,2,1,0:T(8,128)(2,1)}, f32[16,1,256]{2,1,0:T(1,128)}) custom-call(f32[1]{0:T(128)S(6)} %copy.12.radius, s32[5]{0:T(128)S(1)} %stack.59.ids, f32[16,8,128]{2,1,0:T(8,128)} %all-to-all-done.5.totals, f32[4,192,256]{2,1,0:T(8,128)} %get-tuple-element.48.praw, f32[4,8,256]{2,1,0:T(8,128)} %get-tuple-element.49.rs, ...), custom_call_target="tpu_custom_call" | custom-call | flops 1610612736 | bytes 12000000 | tf_op jit(solution)/shard_map/pallas_call | solution.py:367
  181.5 9.6 %all_to_all.40 = f32[16,1,256]{2,1,0:T(1,128)S(1)} all-to-all(f32[16,1,256]{2,1,0:T(1,128)} %get-tuple-element.50), channel_id=1, replica_groups=mesh['y'=4,'zh'=4,'x'=4,'zl'=2,'c'=2] {'x','zl','c'}, dimensions={0} | all-to-all | bytes 32768 | tf_op jit(solution)/shard_map/all_to_all | solution.py:377
  191.2 17.2 %all_to_all.41 = f32[16,1,256]{2,1,0:T(1,128)S(1)} all-to-all(f32[16,1,256]{2,1,0:T(1,128)S(1)} %broadcast_in_dim.14), channel_id=1, replica_groups=mesh['y'=4,'zh'=4,'x'=4,'zl'=2,'c'=2] {'y','zh'}, dimensions={0} | all-to-all | bytes 32768 | tf_op jit(solution)/shard_map/all_to_all | solution.py:269
  208.4 1.6 reduce-scatter.2.cloned.1.call-done
  210.1 1.1 slice_bitcast_fusion.3
  211.1 4.3 %collective-permute-start.13 = (bf16[192,256]{1,0:T(8,128)(2,1)S(1)}, bf16[192,256]{1,0:T(8,128)(2,1)S(1)}, u32[]{:S(2)}, u32[]{:S(2)}) collective-permute-start(bf16[192,256]{1,0:T(8,128)(2,1)S(1)} %get-tuple-element.55), channel_id=1, source_target_pairs={{16,0},{18,2},{32,16},{34,18},{48,32},{50,34},{0,48},{2,50},{17,1}... | collective-permute-start | bytes 294920 | tf_op jit(solution)/shard_map/ppermute | solution.py:37
  215.4 2.0 collective-permute-start.12
  217.3 2.4 %collective-permute-start.11 = (bf16[192,256]{1,0:T(8,128)(2,1)S(1)}, bf16[192,256]{1,0:T(8,128)(2,1)S(1)}, u32[]{:S(2)}, u32[]{:S(2)}) collective-permute-start(bf16[192,256]{1,0:T(8,128)(2,1)S(1)} %get-tuple-element.57), channel_id=1, source_target_pairs={{48,0},{50,2},{0,16},{2,18},{16,32},{18,34},{32,48},{34,50},{49,1}... | collective-permute-start | bytes 294920 | tf_op jit(solution)/shard_map/ppermute | solution.py:37
  219.8 0.6 reduce_sum.29
  220.4 2.8 %collective-permute-done.13.b3 = bf16[192,256]{1,0:T(8,128)(2,1)S(1)} collective-permute-done((bf16[192,256]{1,0:T(8,128)(2,1)S(1)}, bf16[192,256]{1,0:T(8,128)(2,1)S(1)}, u32[]{:S(2)}, u32[]{:S(2)}) %collective-permute-start.13) | collective-permute-done | bytes 98336 | tf_op jit(solution)/shard_map/ppermute | solution.py:37
  223.2 2.4 %collective-permute-done.12.b2 = bf16[192,256]{1,0:T(8,128)(2,1)S(1)} collective-permute-done((bf16[192,256]{1,0:T(8,128)(2,1)S(1)}, bf16[192,256]{1,0:T(8,128)(2,1)S(1)}, u32[]{:S(2)}, u32[]{:S(2)}) %collective-permute-start.12) | collective-permute-done | bytes 98336 | tf_op jit(solution)/shard_map/ppermute | solution.py:37
  225.5 1.6 shard_map.101
  (50 shorter events, 1.1 us)
Async XLA Ops:
  9.8 27.2 %all-to-all-start = ((bf16[4,1,272,256]{3,2,1,0:T(8,128)(2,1)}), bf16[4,1,272,256]{3,2,1,0:T(8,128)(2,1)S(1)}, u32[]{:S(2)}, u32[]{:S(2)}) async-start(bf16[4,1,272,256]{3,2,1,0:T(8,128)(2,1)} %get-tuple-element.33), calls=%async_computation | async-start | bytes 1114112 | tf_op jit(solution)/shard_map/all_to_all | solution.py:293
  15.5 11.5 %collective-permute-start.6 = (bf16[272,256]{1,0:T(8,128)(2,1)}, bf16[272,256]{1,0:T(8,128)(2,1)S(1)}, u32[]{:S(2)}, u32[]{:S(2)}) collective-permute-start(bf16[272,256]{1,0:T(8,128)(2,1)} %get-tuple-element.34), channel_id=1, source_target_pairs={{2,0},{0,2},{18,16},{16,18},{34,32},{32,34},{50,48},{48,50},{3,1},... | collective-permute-start | bytes 417800 | tf_op jit(solution)/shard_map/ppermute | solution.py:37
  16.5 19.3 %collective-permute-start.5 = (bf16[272,256]{1,0:T(8,128)(2,1)}, bf16[272,256]{1,0:T(8,128)(2,1)S(1)}, u32[]{:S(2)}, u32[]{:S(2)}) collective-permute-start(bf16[272,256]{1,0:T(8,128)(2,1)} %get-tuple-element.34), channel_id=1, source_target_pairs={{32,0},{34,2},{48,16},{50,18},{0,32},{2,34},{16,48},{18,50},{33,1}... | collective-permute-start | bytes 417800 | tf_op jit(solution)/shard_map/ppermute | solution.py:37
  22.8 14.1 %collective-permute-start.4 = (bf16[272,256]{1,0:T(8,128)(2,1)}, bf16[272,256]{1,0:T(8,128)(2,1)S(1)}, u32[]{:S(2)}, u32[]{:S(2)}) collective-permute-start(bf16[272,256]{1,0:T(8,128)(2,1)} %get-tuple-element.34), channel_id=1, source_target_pairs={{48,0},{50,2},{0,16},{2,18},{16,32},{18,34},{32,48},{34,50},{49,1}... | collective-permute-start | bytes 417800 | tf_op jit(solution)/shard_map/ppermute | solution.py:37
  24.2 12.6 %collective-permute-start.3 = (bf16[272,256]{1,0:T(8,128)(2,1)}, bf16[272,256]{1,0:T(8,128)(2,1)S(1)}, u32[]{:S(2)}, u32[]{:S(2)}) collective-permute-start(bf16[272,256]{1,0:T(8,128)(2,1)} %get-tuple-element.34), channel_id=1, source_target_pairs={{16,0},{18,2},{32,16},{34,18},{48,32},{50,34},{0,48},{2,50},{17,1}... | collective-permute-start | bytes 417800 | tf_op jit(solution)/shard_map/ppermute | solution.py:37
  36.9 38.8 %copy-start.1 = (bf16[4,1,272,256]{3,2,1,0:T(8,128)(2,1)}, bf16[4,1,272,256]{3,2,1,0:T(8,128)(2,1)S(1)}, u32[]{:S(2)}) copy-start(bf16[4,1,272,256]{3,2,1,0:T(8,128)(2,1)S(1)} %all-to-all-done.refs_0_) | copy-start | bytes 1671172
  38.5 5.0 %copy-start.10 = (bf16[288,256]{1,0:T(8,128)(2,1)S(1)}, bf16[288,256]{1,0:T(8,128)(2,1)}, u32[]{:S(2)}) copy-start(bf16[288,256]{1,0:T(8,128)(2,1)} %get-tuple-element.30) | copy-start | bytes 442372
  38.5 7.2 %copy-start.9 = (bf16[288,256]{1,0:T(8,128)(2,1)S(1)}, bf16[288,256]{1,0:T(8,128)(2,1)}, u32[]{:S(2)}) copy-start(bf16[288,256]{1,0:T(8,128)(2,1)} %get-tuple-element.31) | copy-start | bytes 442372
  38.5 9.7 %copy-start.8 = (bf16[288,256]{1,0:T(8,128)(2,1)S(1)}, bf16[288,256]{1,0:T(8,128)(2,1)}, u32[]{:S(2)}) copy-start(bf16[288,256]{1,0:T(8,128)(2,1)} %get-tuple-element.32) | copy-start | bytes 442372
  38.5 10.6 %copy-start.3 = (bf16[288,256]{1,0:T(8,128)(2,1)S(1)}, bf16[288,256]{1,0:T(8,128)(2,1)}, u32[]{:S(2)}) copy-start(bf16[288,256]{1,0:T(8,128)(2,1)} %get-tuple-element.29.c0) | copy-start | bytes 442372
  38.5 30.1 %all-to-all-start.1 = ((bf16[4,4,272,256]{3,2,1,0:T(8,128)(2,1)}), bf16[4,4,272,256]{3,2,1,0:T(8,128)(2,1)}, u32[]{:S(2)}, u32[]{:S(2)}) async-start(bf16[4,4,272,256]{3,2,1,0:T(8,128)(2,1)} %broadcast_in_dim.11), calls=%async_computation.1 | async-start | bytes 4456448 | tf_op jit(solution)/shard_map/all_to_all | solution.py:289
  43.5 47.2 %all-gather.5.cloned.1.call-start = ((), (), s32[]{:S(2)}) async-start(), calls=%async_computation.10 | async-start | bytes 1966080 | tf_op jit(solution)/shard_map/all_gather | solution.py:298
  43.5 11.3 %collective-permute-start = (bf16[288,256]{1,0:T(8,128)(2,1)S(1)}, bf16[288,256]{1,0:T(8,128)(2,1)S(1)}, u32[]{:S(2)}, u32[]{:S(2)}) collective-permute-start(bf16[288,256]{1,0:T(8,128)(2,1)S(1)} %copy-done.10), channel_id=1, source_target_pairs={{16,0},{18,2},{32,16},{34,18},{48,32},{50,34},{0,48},{2,50},{17,1}... | collective-permute-start | bytes 442376 | tf_op jit(solution)/shard_map/ppermute | solution.py:37
  45.7 14.1 %collective-permute-start.1 = (bf16[288,256]{1,0:T(8,128)(2,1)S(1)}, bf16[288,256]{1,0:T(8,128)(2,1)S(1)}, u32[]{:S(2)}, u32[]{:S(2)}) collective-permute-start(bf16[288,256]{1,0:T(8,128)(2,1)S(1)} %copy-done.9), channel_id=1, source_target_pairs={{32,0},{34,2},{48,16},{50,18},{0,32},{2,34},{16,48},{18,50},{33,1}... | collective-permute-start | bytes 442376 | tf_op jit(solution)/shard_map/ppermute | solution.py:37
  48.3 14.0 %collective-permute-start.2 = (bf16[288,256]{1,0:T(8,128)(2,1)S(1)}, bf16[288,256]{1,0:T(8,128)(2,1)S(1)}, u32[]{:S(2)}, u32[]{:S(2)}) collective-permute-start(bf16[288,256]{1,0:T(8,128)(2,1)S(1)} %copy-done.8), channel_id=1, source_target_pairs={{48,0},{50,2},{0,16},{2,18},{16,32},{18,34},{32,48},{34,50},{49,1}... | collective-permute-start | bytes 442376 | tf_op jit(solution)/shard_map/ppermute | solution.py:37
  49.2 19.5 %collective-permute-start.7 = (bf16[3,272,256]{2,1,0:T(8,128)(2,1)S(1)}, bf16[3,272,256]{2,1,0:T(8,128)(2,1)S(1)}, u32[]{:S(2)}, u32[]{:S(2)}) collective-permute-start(bf16[3,272,256]{2,1,0:T(8,128)(2,1)S(1)} %pad_maximum_fusion.1), channel_id=1, source_target_pairs={{2,0},{0,2},{18,16},{16,18},{34,32},{32,34},{50,48},{48,50},{3,1},... | collective-permute-start | bytes 1253384 | tf_op jit(solution)/shard_map/ppermute | solution.py:37
  54.8 15.3 %copy-start.4 = (bf16[288,256]{1,0:T(8,128)(2,1)}, bf16[288,256]{1,0:T(8,128)(2,1)S(1)}, u32[]{:S(2)}) copy-start(bf16[288,256]{1,0:T(8,128)(2,1)S(1)} %collective-permute-done.c1) | copy-start | bytes 442372
  59.8 10.2 %copy-start.5 = (bf16[288,256]{1,0:T(8,128)(2,1)}, bf16[288,256]{1,0:T(8,128)(2,1)S(1)}, u32[]{:S(2)}) copy-start(bf16[288,256]{1,0:T(8,128)(2,1)S(1)} %collective-permute-done.1.c2) | copy-start | bytes 442372
  62.3 7.7 %copy-start.6 = (bf16[288,256]{1,0:T(8,128)(2,1)}, bf16[288,256]{1,0:T(8,128)(2,1)S(1)}, u32[]{:S(2)}) copy-start(bf16[288,256]{1,0:T(8,128)(2,1)S(1)} %collective-permute-done.2.c3) | copy-start | bytes 442372
  68.7 22.0 %collective-permute-start.9 = (bf16[4,4,272,256]{3,2,1,0:T(8,128)(2,1)}, bf16[4,4,272,256]{3,2,1,0:T(8,128)(2,1)}, u32[]{:S(2)}, u32[]{:S(2)}) collective-permute-start(bf16[4,4,272,256]{3,2,1,0:T(8,128)(2,1)} %all-to-all-done.1.refs_1_), channel_id=1, source_target_pairs={{0,1},{1,0},{2,3},{3,2},{4,5},{5,4},{6,7},{7,6},{8,9},{9,8},{10,11... | collective-permute-start | bytes 6684680 | tf_op jit(solution)/shard_map/ppermute | solution.py:41
  70.0 26.6 %all-to-all-start.2 = ((bf16[4,3,272,256]{3,2,1,0:T(8,128)(2,1)}), bf16[4,3,272,256]{3,2,1,0:T(8,128)(2,1)S(1)}, u32[]{:S(2)}, u32[]{:S(2)}) async-start(bf16[4,3,272,256]{3,2,1,0:T(8,128)(2,1)} %broadcast_in_dim.12), calls=%async_computation.2 | async-start | bytes 3342336 | tf_op jit(solution)/shard_map/all_to_all | solution.py:289
  75.7 2.0 collective-permute-start.8
  77.7 13.0 %copy-start.2 = (bf16[4,1,272,256]{3,2,1,0:T(8,128)(2,1)}, bf16[4,1,272,256]{3,2,1,0:T(8,128)(2,1)S(1)}, u32[]{:S(2)}) copy-start(bf16[4,1,272,256]{3,2,1,0:T(8,128)(2,1)S(1)} %collective-permute-done.8.refs_2_.refs_3_) | copy-start | bytes 1671172
  96.6 3.6 %copy-start = (f32[4,192,256]{2,1,0:T(8,128)S(1)}, f32[4,192,256]{2,1,0:T(8,128)}, u32[]{:S(2)}) copy-start(f32[4,192,256]{2,1,0:T(8,128)} %get-tuple-element.37.p0) | copy-start | bytes 2359300
  96.6 3.6 %collective-permute-start.10 = (bf16[4,3,272,256]{3,2,1,0:T(8,128)(2,1)S(1)}, bf16[4,3,272,256]{3,2,1,0:T(8,128)(2,1)S(1)}, u32[]{:S(2)}, u32[]{:S(2)}) collective-permute-start(bf16[4,3,272,256]{3,2,1,0:T(8,128)(2,1)S(1)} %all-to-all-done.2.refs_0_.refs_2_), channel_id=1, source_target_pairs={{0,1},{1,0},{2,3},{3,2},{4,5},{5,4},{6,7},{7,6},{8,9},{9,8},{10,11... | collective-permute-start | bytes 5013512 | tf_op jit(solution)/shard_map/ppermute | solution.py:41
  109.4 4.5 %copy-start.7 = (s32[2,4096]{1,0:T(2,128)S(1)}, s32[2,4096]{1,0:T(2,128)}, u32[]{:S(2)}) copy-start(s32[2,4096]{1,0:T(2,128)} %param.12) | copy-start | bytes 98308
  109.4 25.8 %all-to-all-start.3 = ((bf16[4,4,192,256]{3,2,1,0:T(8,128)(2,1)}), bf16[4,4,192,256]{3,2,1,0:T(8,128)(2,1)}, u32[]{:S(2)}, u32[]{:S(2)}) async-start(bf16[4,4,192,256]{3,2,1,0:T(8,128)(2,1)} %get-tuple-element.43), calls=%async_computation.3 | async-start | bytes 3145728 | tf_op jit(solution)/shard_map/all_to_all | solution.py:349
  113.8 53.3 %all-gather.7.cloned.1.call-start = ((), (), s32[]{:S(2)}) async-start(), calls=%async_computation.11 | async-start | bytes 1966080 | tf_op jit(solution)/shard_map/all_gather | solution.py:356
  137.7 9.8 %all-to-all-start.4 = ((f32[16,8,128]{2,1,0:T(8,128)}), f32[16,8,128]{2,1,0:T(8,128)}, u32[]{:S(2)}, u32[]{:S(2)}) async-start(f32[16,8,128]{2,1,0:T(8,128)} %get-tuple-element.45), calls=%async_computation.4 | async-start | bytes 131072 | tf_op jit(solution)/shard_map/all_to_all | solution.py:357
  149.0 24.7 %all-to-all-start.5 = ((f32[16,8,128]{2,1,0:T(8,128)}), f32[16,8,128]{2,1,0:T(8,128)}, u32[]{:S(2)}, u32[]{:S(2)}) async-start(f32[16,8,128]{2,1,0:T(8,128)} %broadcast_in_dim.13), calls=%async_computation.5 | async-start | bytes 131072 | tf_op jit(solution)/shard_map/all_to_all | solution.py:269
  155.9 54.2 %reduce-scatter.2.cloned.1.call-start = ((), (), s32[]{:S(2)}) async-start(), calls=%async_computation.9 | async-start | bytes 1966080 | tf_op jit(solution)/shard_map/reduce_scatter | solution.py:376
  211.1 12.0 %collective-permute-start.13 = (bf16[192,256]{1,0:T(8,128)(2,1)S(1)}, bf16[192,256]{1,0:T(8,128)(2,1)S(1)}, u32[]{:S(2)}, u32[]{:S(2)}) collective-permute-start(bf16[192,256]{1,0:T(8,128)(2,1)S(1)} %get-tuple-element.55), channel_id=1, source_target_pairs={{16,0},{18,2},{32,16},{34,18},{48,32},{50,34},{0,48},{2,50},{17,1}... | collective-permute-start | bytes 294920 | tf_op jit(solution)/shard_map/ppermute | solution.py:37
  215.4 10.1 %collective-permute-start.12 = (bf16[192,256]{1,0:T(8,128)(2,1)S(1)}, bf16[192,256]{1,0:T(8,128)(2,1)S(1)}, u32[]{:S(2)}, u32[]{:S(2)}) collective-permute-start(bf16[192,256]{1,0:T(8,128)(2,1)S(1)} %get-tuple-element.56), channel_id=1, source_target_pairs={{32,0},{34,2},{48,16},{50,18},{0,32},{2,34},{16,48},{18,50},{33,1}... | collective-permute-start | bytes 294920 | tf_op jit(solution)/shard_map/ppermute | solution.py:37
  217.3 8.2 %collective-permute-start.11 = (bf16[192,256]{1,0:T(8,128)(2,1)S(1)}, bf16[192,256]{1,0:T(8,128)(2,1)S(1)}, u32[]{:S(2)}, u32[]{:S(2)}) collective-permute-start(bf16[192,256]{1,0:T(8,128)(2,1)S(1)} %get-tuple-element.57), channel_id=1, source_target_pairs={{48,0},{50,2},{0,16},{2,18},{16,32},{18,34},{32,48},{34,50},{49,1}... | collective-permute-start | bytes 294920 | tf_op jit(solution)/shard_map/ppermute | solution.py:37
Sparse Core Ops, SparseCore 0:
  63.3 27.3 all-gather.4
  137.8 29.2 all-gather.6
  181.7 28.3 reduce-scatter.1

commit v11 on v10

--- a/solution.py
+++ b/solution.py
@@ -89,7 +89,7 @@
     return rows[at : at + 1] + rows[at + 1 : at + 2] + rows[at + 2 : at + 3]
 
 
-def start_kernel(ids, tokens, gain, w_gate, w_up, cot, pack, packs, p0, p1, p2, p3, turned):
+def pack_kernel(tokens, gain, pack, packs):
     values = tokens[...].astype(F32)
     squares = jnp.sum((values * values).T, axis=0, keepdims=True)
     pack[0:BLK, :] = tokens[...]
@@ -98,6 +98,9 @@
     pack[BLK:PACK, :] = tail.astype(BF)
     for i in range(4):
         packs[i, 0] = pack[...]
+
+
+def quarter_kernel(ids, w_gate, w_up, cot, p0, p1, p2, p3, turned):
     for i, ref in enumerate((w_gate, w_up, cot)):
         turned[i] = ref[...].astype(F32).T.astype(BF)
         for k, to in enumerate((p0, p1, p2, p3)):
@@ -274,13 +277,19 @@
     mask = decay_mask.astype(F32).reshape(2, NB, BLK).transpose(1, 0, 2)
 
     piece = hbm((3 * SUB, BLK), BF)
-    pack, packs, *pieces = call(
-        start_kernel,
-        (hbm((PACK, BLK), BF), hbm((4, 1, PACK, BLK), BF)) + (piece,) * 4,
-        [SMEM, whole((BLK, BLK)), whole((1, BLK))] + [whole((BLK, 4 * SUB))] * 3,
-        (whole((PACK, BLK)), whole((4, 1, PACK, BLK))) + (whole(piece.shape),) * 4,
+    pack, packs = call(
+        pack_kernel,
+        (hbm((PACK, BLK), BF), hbm((4, 1, PACK, BLK), BF)),
+        [whole((BLK, BLK)), whole((1, BLK))],
+        (whole((PACK, BLK)), whole((4, 1, PACK, BLK))),
+    )(in_hbm(tokens), in_hbm(norm_gain[None, :]))
+    pieces = call(
+        quarter_kernel,
+        (piece,) * 4,
+        [SMEM] + [whole((BLK, 4 * SUB))] * 3,
+        (whole(piece.shape),) * 4,
         scratch=[pltpu.VMEM((3, 4 * SUB, BLK), BF)],
-    )(ids, in_hbm(tokens), in_hbm(norm_gain[None, :]), in_hbm(w_gate), in_hbm(w_up), in_hbm(cotangent))
+    )(ids, in_hbm(w_gate), in_hbm(w_up), in_hbm(cotangent))
 
     def after(value, *others):
         return lax.optimization_barrier((value,) + others)[0]
@@ -293,7 +302,7 @@
     own_x = lax.all_to_all(packs, "x", 0, 0, tiled=True)
     pieces = [pieces[0]] + [from_z(pieces[k], k, 0) for k in range(1, 4)]
     part_w = jnp.stack([p[:ROWS] for p in pieces])
-    mid_x = over_x(after(jnp.stack(mids + [near]), own_x))
+    mid_x = over_x(after(jnp.stack(mids + [near]), own_x, pieces[0]))
     far = from_z(jnp.stack(mids), 0, 1)
     weights = in_hbm(lax.all_gather(part_w, "y", axis=0, tiled=False))
     far_x = over_x(after(far, part_w, mid_x))

time: 237 us -> 236 us (level)
  transfers between devices with their start and end apart: 23 -> 23, of which waited for: 15 -> 15; matrix products, arithmetic and copies ran while one was open for 2% -> 2% of each run, Pallas kernels for 7% -> 8%
where the time goes in v11:
time: 236 us; the launch traced here: 233 us
  waiting for transfers between devices  83.7 us (35%)
  starting transfers between devices  59.9 us (25%)
  Pallas kernels  40.8 us (17%)
  blocking collectives  26.9 us (11%)
  between operations  14.5 us (6%)
  local copies, waits for them, and re-layouts  4.79 us (2%)
  other arithmetic  2.43 us (1%)
    ppermute x11, waiting for transfers between devices, from_z(): return lax.ppermute(value, ('zh', 'zl'), pairs)  31.3 us
    ppermute x11, starting transfers between devices, from_z(): return lax.ppermute(value, ('zh', 'zl'), pairs)  25.9 us
    all_to_all x1, waiting for transfers between devices, body(): terms = lax.all_to_all(out1, 'y', 0, 0, tiled=True)  21.3 us
    all_to_all x1, blocking collectives, spread(): lax.all_to_all(jnp.broadcast_to(value[None], (n,) + value.shape), axes, 0...  17.2 us
    all_gather x1, waiting for transfers between devices, body(): weights = in_hbm(lax.all_gather(part_w, 'y', axis=0, tiled=False))  13 us
    all_gather x1, waiting for transfers between devices, body(): ascs = in_hbm(lax.all_gather(asc, 'y', axis=0, tiled=False))  11 us
    all_to_all x2, starting transfers between devices, over_x(): lax.all_to_all(jnp.broadcast_to(value[None], (4,) + value.shape), 'x', 0,...  10.6 us
    all_to_all x1, blocking collectives, body(): dg = jnp.sum(lax.all_to_all(dgp, MP, 0, 0, tiled=True), axis=0)  9.64 us
  transfers between devices with their start and end apart: 23, of which 15 were waited for; matrix products, arithmetic and copies ran while one was open for 2% of the time, Pallas kernels for 8%

profile of v11, /device:TPU:4, one launch (start us, length us, event | category | flops | bytes accessed | tf_op | source)
XLA Modules:
  0.0 233.0 jit_solution(1155385598826316210)
XLA Ops:
  7.2 1.9 shard_map.95
  9.1 5.7 %all-to-all-start = ((bf16[4,1,272,256]{3,2,1,0:T(8,128)(2,1)}), bf16[4,1,272,256]{3,2,1,0:T(8,128)(2,1)S(1)}, u32[]{:S(2)}, u32[]{:S(2)}) async-start(bf16[4,1,272,256]{3,2,1,0:T(8,128)(2,1)} %get-tuple-element.33), calls=%async_computation | async-start | bytes 1114112 | tf_op jit(solution)/shard_map/all_to_all | solution.py:302
  14.8 1.0 collective-permute-start.6
  15.8 6.3 %collective-permute-start.5 = (bf16[272,256]{1,0:T(8,128)(2,1)}, bf16[272,256]{1,0:T(8,128)(2,1)S(1)}, u32[]{:S(2)}, u32[]{:S(2)}) collective-permute-start(bf16[272,256]{1,0:T(8,128)(2,1)} %get-tuple-element.34), channel_id=1, source_target_pairs={{32,0},{34,2},{48,16},{50,18},{0,32},{2,34},{16,48},{18,50},{33,1}... | collective-permute-start | bytes 417800 | tf_op jit(solution)/shard_map/ppermute | solution.py:37
  22.1 1.5 collective-permute-start.4
  23.6 2.7 %collective-permute-start.3 = (bf16[272,256]{1,0:T(8,128)(2,1)}, bf16[272,256]{1,0:T(8,128)(2,1)S(1)}, u32[]{:S(2)}, u32[]{:S(2)}) collective-permute-start(bf16[272,256]{1,0:T(8,128)(2,1)} %get-tuple-element.34), channel_id=1, source_target_pairs={{16,0},{18,2},{32,16},{34,18},{48,32},{50,34},{0,48},{2,50},{17,1}... | collective-permute-start | bytes 417800 | tf_op jit(solution)/shard_map/ppermute | solution.py:37
  26.3 2.2 shard_map.94
  28.5 6.6 %collective-permute-done.5 = bf16[272,256]{1,0:T(8,128)(2,1)S(1)} collective-permute-done((bf16[272,256]{1,0:T(8,128)(2,1)}, bf16[272,256]{1,0:T(8,128)(2,1)S(1)}, u32[]{:S(2)}, u32[]{:S(2)}) %collective-permute-start.5) | collective-permute-done | bytes 139296 | tf_op jit(solution)/shard_map/ppermute | solution.py:37
  35.1 1.1 collective-permute-done.4
  36.3 1.6 broadcast_in_dim.11
  37.8 4.9 %all-to-all-start.1 = ((bf16[4,4,272,256]{3,2,1,0:T(8,128)(2,1)}), bf16[4,4,272,256]{3,2,1,0:T(8,128)(2,1)}, u32[]{:S(2)}, u32[]{:S(2)}) async-start(bf16[4,4,272,256]{3,2,1,0:T(8,128)(2,1)} %broadcast_in_dim.11), calls=%async_computation.1 | async-start | bytes 4456448 | tf_op jit(solution)/shard_map/all_to_all | solution.py:298
  42.8 2.2 collective-permute-start
  45.0 2.5 %collective-permute-start.1 = (bf16[288,256]{1,0:T(8,128)(2,1)S(1)}, bf16[288,256]{1,0:T(8,128)(2,1)S(1)}, u32[]{:S(2)}, u32[]{:S(2)}) collective-permute-start(bf16[288,256]{1,0:T(8,128)(2,1)S(1)} %copy-done.9), channel_id=1, source_target_pairs={{32,0},{34,2},{48,16},{50,18},{0,32},{2,34},{16,48},{18,50},{33,1}... | collective-permute-start | bytes 442376 | tf_op jit(solution)/shard_map/ppermute | solution.py:37
  47.5 0.9 collective-permute-start.2
  48.6 5.5 %collective-permute-done.c1 = bf16[288,256]{1,0:T(8,128)(2,1)S(1)} collective-permute-done((bf16[288,256]{1,0:T(8,128)(2,1)S(1)}, bf16[288,256]{1,0:T(8,128)(2,1)S(1)}, u32[]{:S(2)}, u32[]{:S(2)}) %collective-permute-start) | collective-permute-done | bytes 147488 | tf_op jit(solution)/shard_map/ppermute | solution.py:37
  54.1 5.1 %collective-permute-done.1.c2 = bf16[288,256]{1,0:T(8,128)(2,1)S(1)} collective-permute-done((bf16[288,256]{1,0:T(8,128)(2,1)S(1)}, bf16[288,256]{1,0:T(8,128)(2,1)S(1)}, u32[]{:S(2)}, u32[]{:S(2)}) %collective-permute-start.1) | collective-permute-done | bytes 147488 | tf_op jit(solution)/shard_map/ppermute | solution.py:37
  59.2 2.4 %collective-permute-done.2.c3 = bf16[288,256]{1,0:T(8,128)(2,1)S(1)} collective-permute-done((bf16[288,256]{1,0:T(8,128)(2,1)S(1)}, bf16[288,256]{1,0:T(8,128)(2,1)S(1)}, u32[]{:S(2)}, u32[]{:S(2)}) %collective-permute-start.2) | collective-permute-done | bytes 147488 | tf_op jit(solution)/shard_map/ppermute | solution.py:37
  61.6 0.8 pad_maximum_fusion.2
  62.4 5.5 %collective-permute-done.7 = bf16[3,272,256]{2,1,0:T(8,128)(2,1)S(1)} collective-permute-done((bf16[3,272,256]{2,1,0:T(8,128)(2,1)S(1)}, bf16[3,272,256]{2,1,0:T(8,128)(2,1)S(1)}, u32[]{:S(2)}, u32[]{:S(2)}) %collective-permute-start.7) | collective-permute-done | bytes 417824 | tf_op jit(solution)/shard_map/ppermute | solution.py:37
  68.0 1.4 broadcast_in_dim.12
  69.3 5.7 %all-to-all-start.2 = ((bf16[4,3,272,256]{3,2,1,0:T(8,128)(2,1)}), bf16[4,3,272,256]{3,2,1,0:T(8,128)(2,1)S(1)}, u32[]{:S(2)}, u32[]{:S(2)}) async-start(bf16[4,3,272,256]{3,2,1,0:T(8,128)(2,1)} %broadcast_in_dim.12), calls=%async_computation.2 | async-start | bytes 3342336 | tf_op jit(solution)/shard_map/all_to_all | solution.py:298
  75.3 1.7 collective-permute-done.8.refs_2_.refs_3_
  77.0 13.0 %all-gather.5.cloned.1.call-done = bf16[16,192,256]{2,1,0:T(8,128)(2,1)} async-done(((bf16[4,192,256]{2,1,0:T(8,128)(2,1)}), bf16[16,192,256]{2,1,0:T(8,128)(2,1)}) %all-gather.5.cloned.1.call-update) | async-done | bytes 1572880 | tf_op jit(solution)/shard_map/all_gather | solution.py:307
  90.0 5.9 %shard_map.96 = (f32[4,192,256]{2,1,0:T(8,128)}, f32[4,8,256]{2,1,0:T(8,128)S(1)}, f32[16,8,256]{2,1,0:T(8,128)S(1)}) custom-call(s32[5]{0:T(128)S(1)} %stack.59.ids, bf16[4,4,192,256]{3,2,1,0:T(8,128)(2,1)} %bitcast.35, bf16[4,1,272,256]{3,2,1,0:T(8,128)(2,1)} %copy-done.1, bf16[4,4,272,256]{3,2,1,0:T(8,128)(2,1)} %all-to-all-done.1.refs_1_, ...), custom_call_target="tpu_custom_call" | custom-call | flops 1006632960 | bytes 5570560 | tf_op jit(solution)/shard_map/pallas_call | solution.py:321
  96.0 3.1 %shard_map.97 = (f32[4,192,256]{2,1,0:T(8,128)S(1)}, f32[4,8,256]{2,1,0:T(8,128)S(1)}) custom-call(s32[5]{0:T(128)S(1)} %stack.59.ids, bf16[4,4,192,256]{3,2,1,0:T(8,128)(2,1)} %bitcast.36, bf16[4,3,272,256]{3,2,1,0:T(8,128)(2,1)S(1)} %all-to-all-done.2.refs_0_.refs_2_), custom_call_target="tpu_custom_call" | custom-call | flops 301989888 | bytes 1671168 | tf_op jit(solution)/shard_map/pallas_call | solution.py:321
  99.6 9.1 %shard_map.98 = (bf16[4,4,192,256]{3,2,1,0:T(8,128)(2,1)}, f32[4,192,256]{2,1,0:T(8,128)}, f32[4,8,256]{2,1,0:T(8,128)}) custom-call(s32[5]{0:T(128)S(1)} %stack.59.ids, f32[4,192,256]{2,1,0:T(8,128)S(1)} %copy-done, f32[4,192,256]{2,1,0:T(8,128)S(1)} %get-tuple-element.40.p1, f32[4,8,256]{2,1,0:T(8,128)S(1)} %get-tuple-element.41.s0, ...), custom_call_target="tpu_custom_call" | custom-call | flops 1610612736 | bytes 12000000 | tf_op jit(solution)/shard_map/pallas_call | solution.py:349
  108.7 4.4 %all-to-all-start.3 = ((bf16[4,4,192,256]{3,2,1,0:T(8,128)(2,1)}), bf16[4,4,192,256]{3,2,1,0:T(8,128)(2,1)}, u32[]{:S(2)}, u32[]{:S(2)}) async-start(bf16[4,4,192,256]{3,2,1,0:T(8,128)(2,1)} %get-tuple-element.43), calls=%async_computation.3 | async-start | bytes 3145728 | tf_op jit(solution)/shard_map/all_to_all | solution.py:358
  113.2 21.3 %all-to-all-done.3.terms = bf16[4,4,192,256]{3,2,1,0:T(8,128)(2,1)} async-done(((bf16[4,4,192,256]{3,2,1,0:T(8,128)(2,1)}), bf16[4,4,192,256]{3,2,1,0:T(8,128)(2,1)}, u32[]{:S(2)}, u32[]{:S(2)}) %all-to-all-start.3) | async-done | bytes 1572896 | tf_op jit(solution)/shard_map/all_to_all | solution.py:358
  134.4 2.5 %shard_map.99 = (bf16[4,192,256]{2,1,0:T(8,128)(2,1)}, f32[16,8,128]{2,1,0:T(8,128)}) custom-call(s32[5]{0:T(128)S(1)} %stack.59.ids, bf16[4,4,192,256]{3,2,1,0:T(8,128)(2,1)} %all-to-all-done.3.terms, f32[16,8,256]{2,1,0:T(8,128)S(1)} %get-tuple-element.44.gabs, f32[16,2,256]{2,1,0:T(2,128)S(1)} %bitcast.32), custom_call_target="tpu_custom_call" | custom-call | flops 1000000 | bytes 1000000 | tf_op jit(solution)/shard_map/pallas_call | solution.py:359
  136.9 5.8 %all-to-all-start.4 = ((f32[16,8,128]{2,1,0:T(8,128)}), f32[16,8,128]{2,1,0:T(8,128)}, u32[]{:S(2)}, u32[]{:S(2)}) async-start(f32[16,8,128]{2,1,0:T(8,128)} %get-tuple-element.45), calls=%async_computation.4 | async-start | bytes 131072 | tf_op jit(solution)/shard_map/all_to_all | solution.py:366
  143.4 3.4 %all-to-all-done.4 = f32[16,8,128]{2,1,0:T(8,128)} async-done(((f32[16,8,128]{2,1,0:T(8,128)}), f32[16,8,128]{2,1,0:T(8,128)}, u32[]{:S(2)}, u32[]{:S(2)}) %all-to-all-start.4) | async-done | bytes 65568 | tf_op jit(solution)/shard_map/all_to_all | solution.py:366
  146.8 0.9 reduce_sum.27
  147.6 0.6 broadcast_in_dim.13
  148.3 6.9 %all-to-all-start.5 = ((f32[16,8,128]{2,1,0:T(8,128)}), f32[16,8,128]{2,1,0:T(8,128)}, u32[]{:S(2)}, u32[]{:S(2)}) async-start(f32[16,8,128]{2,1,0:T(8,128)} %broadcast_in_dim.13), calls=%async_computation.5 | async-start | bytes 131072 | tf_op jit(solution)/shard_map/all_to_all | solution.py:272
  155.4 11.0 %all-gather.7.cloned.1.call-done = bf16[16,192,256]{2,1,0:T(8,128)(2,1)} async-done(((bf16[4,192,256]{2,1,0:T(8,128)(2,1)}), bf16[16,192,256]{2,1,0:T(8,128)(2,1)}) %all-gather.7.cloned.1.call-update) | async-done | bytes 1572880 | tf_op jit(solution)/shard_map/all_gather | solution.py:365
  166.4 6.6 %shard_map.100.pa = f32[4,192,256]{2,1,0:T(8,128)} custom-call(s32[5]{0:T(128)S(1)} %stack.59.ids, bf16[4,4,192,256]{3,2,1,0:T(8,128)(2,1)} %bitcast.39, f32[16,2,256]{2,1,0:T(2,128)S(1)} %bitcast.33, f32[16,8,256]{2,1,0:T(8,128)S(1)} %get-tuple-element.44.gabs, bf16[4,1,272,256]{3,2,1,0:T(8,128)(2,1)} %copy-done.1, ...), custom_call_target="tpu_custom_call" | custom-call | flops 1610612736 | bytes 12000000 | tf_op jit(solution)/shard_map/pallas_call | solution.py:368
  173.0 7.8 %shard_map.101 = (bf16[4,4,192,256]{3,2,1,0:T(8,128)(2,1)}, f32[16,1,256]{2,1,0:T(1,128)}) custom-call(f32[1]{0:T(128)S(6)} %copy.12.radius, s32[5]{0:T(128)S(1)} %stack.59.ids, f32[16,8,128]{2,1,0:T(8,128)} %all-to-all-done.5.totals, f32[4,192,256]{2,1,0:T(8,128)} %get-tuple-element.48.praw, f32[4,8,256]{2,1,0:T(8,128)} %get-tuple-element.49.rs, ...), custom_call_target="tpu_custom_call" | custom-call | flops 1610612736 | bytes 12000000 | tf_op jit(solution)/shard_map/pallas_call | solution.py:376
  180.8 9.6 %all_to_all.40 = f32[16,1,256]{2,1,0:T(1,128)S(1)} all-to-all(f32[16,1,256]{2,1,0:T(1,128)} %get-tuple-element.50), channel_id=1, replica_groups=mesh['y'=4,'zh'=4,'x'=4,'zl'=2,'c'=2] {'x','zl','c'}, dimensions={0} | all-to-all | bytes 32768 | tf_op jit(solution)/shard_map/all_to_all | solution.py:386
  190.5 17.2 %all_to_all.41 = f32[16,1,256]{2,1,0:T(1,128)S(1)} all-to-all(f32[16,1,256]{2,1,0:T(1,128)S(1)} %broadcast_in_dim.14), channel_id=1, replica_groups=mesh['y'=4,'zh'=4,'x'=4,'zl'=2,'c'=2] {'y','zh'}, dimensions={0} | all-to-all | bytes 32768 | tf_op jit(solution)/shard_map/all_to_all | solution.py:272
  207.7 1.6 reduce-scatter.2.cloned.1.call-done
  209.3 1.1 slice_bitcast_fusion.3
  210.4 4.2 %collective-permute-start.13 = (bf16[192,256]{1,0:T(8,128)(2,1)S(1)}, bf16[192,256]{1,0:T(8,128)(2,1)S(1)}, u32[]{:S(2)}, u32[]{:S(2)}) collective-permute-start(bf16[192,256]{1,0:T(8,128)(2,1)S(1)} %get-tuple-element.55), channel_id=1, source_target_pairs={{16,0},{18,2},{32,16},{34,18},{48,32},{50,34},{0,48},{2,50},{17,1}... | collective-permute-start | bytes 294920 | tf_op jit(solution)/shard_map/ppermute | solution.py:37
  214.7 2.0 collective-permute-start.12
  216.6 2.4 %collective-permute-start.11 = (bf16[192,256]{1,0:T(8,128)(2,1)S(1)}, bf16[192,256]{1,0:T(8,128)(2,1)S(1)}, u32[]{:S(2)}, u32[]{:S(2)}) collective-permute-start(bf16[192,256]{1,0:T(8,128)(2,1)S(1)} %get-tuple-element.57), channel_id=1, source_target_pairs={{48,0},{50,2},{0,16},{2,18},{16,32},{18,34},{32,48},{34,50},{49,1}... | collective-permute-start | bytes 294920 | tf_op jit(solution)/shard_map/ppermute | solution.py:37
  219.1 0.6 reduce_sum.29
  219.7 2.7 %collective-permute-done.13.b3 = bf16[192,256]{1,0:T(8,128)(2,1)S(1)} collective-permute-done((bf16[192,256]{1,0:T(8,128)(2,1)S(1)}, bf16[192,256]{1,0:T(8,128)(2,1)S(1)}, u32[]{:S(2)}, u32[]{:S(2)}) %collective-permute-start.13) | collective-permute-done | bytes 98336 | tf_op jit(solution)/shard_map/ppermute | solution.py:37
  222.4 2.4 %collective-permute-done.12.b2 = bf16[192,256]{1,0:T(8,128)(2,1)S(1)} collective-permute-done((bf16[192,256]{1,0:T(8,128)(2,1)S(1)}, bf16[192,256]{1,0:T(8,128)(2,1)S(1)}, u32[]{:S(2)}, u32[]{:S(2)}) %collective-permute-start.12) | collective-permute-done | bytes 98336 | tf_op jit(solution)/shard_map/ppermute | solution.py:37
  224.8 1.6 shard_map.102
  (51 shorter events, 1.5 us)
Async XLA Ops:
  9.1 27.2 %all-to-all-start = ((bf16[4,1,272,256]{3,2,1,0:T(8,128)(2,1)}), bf16[4,1,272,256]{3,2,1,0:T(8,128)(2,1)S(1)}, u32[]{:S(2)}, u32[]{:S(2)}) async-start(bf16[4,1,272,256]{3,2,1,0:T(8,128)(2,1)} %get-tuple-element.33), calls=%async_computation | async-start | bytes 1114112 | tf_op jit(solution)/shard_map/all_to_all | solution.py:302
  14.8 13.8 %collective-permute-start.6 = (bf16[272,256]{1,0:T(8,128)(2,1)}, bf16[272,256]{1,0:T(8,128)(2,1)S(1)}, u32[]{:S(2)}, u32[]{:S(2)}) collective-permute-start(bf16[272,256]{1,0:T(8,128)(2,1)} %get-tuple-element.34), channel_id=1, source_target_pairs={{2,0},{0,2},{18,16},{16,18},{34,32},{32,34},{50,48},{48,50},{3,1},... | collective-permute-start | bytes 417800 | tf_op jit(solution)/shard_map/ppermute | solution.py:37
  15.8 19.3 %collective-permute-start.5 = (bf16[272,256]{1,0:T(8,128)(2,1)}, bf16[272,256]{1,0:T(8,128)(2,1)S(1)}, u32[]{:S(2)}, u32[]{:S(2)}) collective-permute-start(bf16[272,256]{1,0:T(8,128)(2,1)} %get-tuple-element.34), channel_id=1, source_target_pairs={{32,0},{34,2},{48,16},{50,18},{0,32},{2,34},{16,48},{18,50},{33,1}... | collective-permute-start | bytes 417800 | tf_op jit(solution)/shard_map/ppermute | solution.py:37
  22.1 14.1 %collective-permute-start.4 = (bf16[272,256]{1,0:T(8,128)(2,1)}, bf16[272,256]{1,0:T(8,128)(2,1)S(1)}, u32[]{:S(2)}, u32[]{:S(2)}) collective-permute-start(bf16[272,256]{1,0:T(8,128)(2,1)} %get-tuple-element.34), channel_id=1, source_target_pairs={{48,0},{50,2},{0,16},{2,18},{16,32},{18,34},{32,48},{34,50},{49,1}... | collective-permute-start | bytes 417800 | tf_op jit(solution)/shard_map/ppermute | solution.py:37
  23.6 12.6 %collective-permute-start.3 = (bf16[272,256]{1,0:T(8,128)(2,1)}, bf16[272,256]{1,0:T(8,128)(2,1)S(1)}, u32[]{:S(2)}, u32[]{:S(2)}) collective-permute-start(bf16[272,256]{1,0:T(8,128)(2,1)} %get-tuple-element.34), channel_id=1, source_target_pairs={{16,0},{18,2},{32,16},{34,18},{48,32},{50,34},{0,48},{2,50},{17,1}... | collective-permute-start | bytes 417800 | tf_op jit(solution)/shard_map/ppermute | solution.py:37
  36.3 38.8 %copy-start.1 = (bf16[4,1,272,256]{3,2,1,0:T(8,128)(2,1)}, bf16[4,1,272,256]{3,2,1,0:T(8,128)(2,1)S(1)}, u32[]{:S(2)}) copy-start(bf16[4,1,272,256]{3,2,1,0:T(8,128)(2,1)S(1)} %all-to-all-done.refs_0_) | copy-start | bytes 1671172
  37.8 5.0 %copy-start.10 = (bf16[288,256]{1,0:T(8,128)(2,1)S(1)}, bf16[288,256]{1,0:T(8,128)(2,1)}, u32[]{:S(2)}) copy-start(bf16[288,256]{1,0:T(8,128)(2,1)} %get-tuple-element.30) | copy-start | bytes 442372
  37.8 7.2 %copy-start.9 = (bf16[288,256]{1,0:T(8,128)(2,1)S(1)}, bf16[288,256]{1,0:T(8,128)(2,1)}, u32[]{:S(2)}) copy-start(bf16[288,256]{1,0:T(8,128)(2,1)} %get-tuple-element.31) | copy-start | bytes 442372
  37.8 9.7 %copy-start.8 = (bf16[288,256]{1,0:T(8,128)(2,1)S(1)}, bf16[288,256]{1,0:T(8,128)(2,1)}, u32[]{:S(2)}) copy-start(bf16[288,256]{1,0:T(8,128)(2,1)} %get-tuple-element.32) | copy-start | bytes 442372
  37.8 10.6 %copy-start.3 = (bf16[288,256]{1,0:T(8,128)(2,1)S(1)}, bf16[288,256]{1,0:T(8,128)(2,1)}, u32[]{:S(2)}) copy-start(bf16[288,256]{1,0:T(8,128)(2,1)} %get-tuple-element.29.c0) | copy-start | bytes 442372
  37.8 30.1 %all-to-all-start.1 = ((bf16[4,4,272,256]{3,2,1,0:T(8,128)(2,1)}), bf16[4,4,272,256]{3,2,1,0:T(8,128)(2,1)}, u32[]{:S(2)}, u32[]{:S(2)}) async-start(bf16[4,4,272,256]{3,2,1,0:T(8,128)(2,1)} %broadcast_in_dim.11), calls=%async_computation.1 | async-start | bytes 4456448 | tf_op jit(solution)/shard_map/all_to_all | solution.py:298
  42.8 47.2 %all-gather.5.cloned.1.call-start = ((), (), s32[]{:S(2)}) async-start(), calls=%async_computation.10 | async-start | bytes 1966080 | tf_op jit(solution)/shard_map/all_gather | solution.py:307
  42.8 11.3 %collective-permute-start = (bf16[288,256]{1,0:T(8,128)(2,1)S(1)}, bf16[288,256]{1,0:T(8,128)(2,1)S(1)}, u32[]{:S(2)}, u32[]{:S(2)}) collective-permute-start(bf16[288,256]{1,0:T(8,128)(2,1)S(1)} %copy-done.10), channel_id=1, source_target_pairs={{16,0},{18,2},{32,16},{34,18},{48,32},{50,34},{0,48},{2,50},{17,1}... | collective-permute-start | bytes 442376 | tf_op jit(solution)/shard_map/ppermute | solution.py:37
  45.0 14.1 %collective-permute-start.1 = (bf16[288,256]{1,0:T(8,128)(2,1)S(1)}, bf16[288,256]{1,0:T(8,128)(2,1)S(1)}, u32[]{:S(2)}, u32[]{:S(2)}) collective-permute-start(bf16[288,256]{1,0:T(8,128)(2,1)S(1)} %copy-done.9), channel_id=1, source_target_pairs={{32,0},{34,2},{48,16},{50,18},{0,32},{2,34},{16,48},{18,50},{33,1}... | collective-permute-start | bytes 442376 | tf_op jit(solution)/shard_map/ppermute | solution.py:37
  47.5 14.0 %collective-permute-start.2 = (bf16[288,256]{1,0:T(8,128)(2,1)S(1)}, bf16[288,256]{1,0:T(8,128)(2,1)S(1)}, u32[]{:S(2)}, u32[]{:S(2)}) collective-permute-start(bf16[288,256]{1,0:T(8,128)(2,1)S(1)} %copy-done.8), channel_id=1, source_target_pairs={{48,0},{50,2},{0,16},{2,18},{16,32},{18,34},{32,48},{34,50},{49,1}... | collective-permute-start | bytes 442376 | tf_op jit(solution)/shard_map/ppermute | solution.py:37
  48.5 19.5 %collective-permute-start.7 = (bf16[3,272,256]{2,1,0:T(8,128)(2,1)S(1)}, bf16[3,272,256]{2,1,0:T(8,128)(2,1)S(1)}, u32[]{:S(2)}, u32[]{:S(2)}) collective-permute-start(bf16[3,272,256]{2,1,0:T(8,128)(2,1)S(1)} %pad_maximum_fusion.1), channel_id=1, source_target_pairs={{2,0},{0,2},{18,16},{16,18},{34,32},{32,34},{50,48},{48,50},{3,1},... | collective-permute-start | bytes 1253384 | tf_op jit(solution)/shard_map/ppermute | solution.py:37
  54.1 15.3 %copy-start.4 = (bf16[288,256]{1,0:T(8,128)(2,1)}, bf16[288,256]{1,0:T(8,128)(2,1)S(1)}, u32[]{:S(2)}) copy-start(bf16[288,256]{1,0:T(8,128)(2,1)S(1)} %collective-permute-done.c1) | copy-start | bytes 442372
  59.2 10.2 %copy-start.5 = (bf16[288,256]{1,0:T(8,128)(2,1)}, bf16[288,256]{1,0:T(8,128)(2,1)S(1)}, u32[]{:S(2)}) copy-start(bf16[288,256]{1,0:T(8,128)(2,1)S(1)} %collective-permute-done.1.c2) | copy-start | bytes 442372
  61.6 7.8 %copy-start.6 = (bf16[288,256]{1,0:T(8,128)(2,1)}, bf16[288,256]{1,0:T(8,128)(2,1)S(1)}, u32[]{:S(2)}) copy-start(bf16[288,256]{1,0:T(8,128)(2,1)S(1)} %collective-permute-done.2.c3) | copy-start | bytes 442372
  68.0 22.0 %collective-permute-start.9 = (bf16[4,4,272,256]{3,2,1,0:T(8,128)(2,1)}, bf16[4,4,272,256]{3,2,1,0:T(8,128)(2,1)}, u32[]{:S(2)}, u32[]{:S(2)}) collective-permute-start(bf16[4,4,272,256]{3,2,1,0:T(8,128)(2,1)} %all-to-all-done.1.refs_1_), channel_id=1, source_target_pairs={{0,1},{1,0},{2,3},{3,2},{4,5},{5,4},{6,7},{7,6},{8,9},{9,8},{10,11... | collective-permute-start | bytes 6684680 | tf_op jit(solution)/shard_map/ppermute | solution.py:41
  69.3 26.6 %all-to-all-start.2 = ((bf16[4,3,272,256]{3,2,1,0:T(8,128)(2,1)}), bf16[4,3,272,256]{3,2,1,0:T(8,128)(2,1)S(1)}, u32[]{:S(2)}, u32[]{:S(2)}) async-start(bf16[4,3,272,256]{3,2,1,0:T(8,128)(2,1)} %broadcast_in_dim.12), calls=%async_computation.2 | async-start | bytes 3342336 | tf_op jit(solution)/shard_map/all_to_all | solution.py:298
  75.0 2.0 collective-permute-start.8
  77.0 13.0 %copy-start.2 = (bf16[4,1,272,256]{3,2,1,0:T(8,128)(2,1)}, bf16[4,1,272,256]{3,2,1,0:T(8,128)(2,1)S(1)}, u32[]{:S(2)}) copy-start(bf16[4,1,272,256]{3,2,1,0:T(8,128)(2,1)S(1)} %collective-permute-done.8.refs_2_.refs_3_) | copy-start | bytes 1671172
  95.9 3.6 %copy-start = (f32[4,192,256]{2,1,0:T(8,128)S(1)}, f32[4,192,256]{2,1,0:T(8,128)}, u32[]{:S(2)}) copy-start(f32[4,192,256]{2,1,0:T(8,128)} %get-tuple-element.37.p0) | copy-start | bytes 2359300
  95.9 3.6 %collective-permute-start.10 = (bf16[4,3,272,256]{3,2,1,0:T(8,128)(2,1)S(1)}, bf16[4,3,272,256]{3,2,1,0:T(8,128)(2,1)S(1)}, u32[]{:S(2)}, u32[]{:S(2)}) collective-permute-start(bf16[4,3,272,256]{3,2,1,0:T(8,128)(2,1)S(1)} %all-to-all-done.2.refs_0_.refs_2_), channel_id=1, source_target_pairs={{0,1},{1,0},{2,3},{3,2},{4,5},{5,4},{6,7},{7,6},{8,9},{9,8},{10,11... | collective-permute-start | bytes 5013512 | tf_op jit(solution)/shard_map/ppermute | solution.py:41
  108.6 4.5 %copy-start.7 = (s32[2,4096]{1,0:T(2,128)S(1)}, s32[2,4096]{1,0:T(2,128)}, u32[]{:S(2)}) copy-start(s32[2,4096]{1,0:T(2,128)} %param.12) | copy-start | bytes 98308
  108.7 25.8 %all-to-all-start.3 = ((bf16[4,4,192,256]{3,2,1,0:T(8,128)(2,1)}), bf16[4,4,192,256]{3,2,1,0:T(8,128)(2,1)}, u32[]{:S(2)}, u32[]{:S(2)}) async-start(bf16[4,4,192,256]{3,2,1,0:T(8,128)(2,1)} %get-tuple-element.43), calls=%async_computation.3 | async-start | bytes 3145728 | tf_op jit(solution)/shard_map/all_to_all | solution.py:358
  113.1 53.3 %all-gather.7.cloned.1.call-start = ((), (), s32[]{:S(2)}) async-start(), calls=%async_computation.11 | async-start | bytes 1966080 | tf_op jit(solution)/shard_map/all_gather | solution.py:365
  136.9 9.8 %all-to-all-start.4 = ((f32[16,8,128]{2,1,0:T(8,128)}), f32[16,8,128]{2,1,0:T(8,128)}, u32[]{:S(2)}, u32[]{:S(2)}) async-start(f32[16,8,128]{2,1,0:T(8,128)} %get-tuple-element.45), calls=%async_computation.4 | async-start | bytes 131072 | tf_op jit(solution)/shard_map/all_to_all | solution.py:366
  148.3 24.7 %all-to-all-start.5 = ((f32[16,8,128]{2,1,0:T(8,128)}), f32[16,8,128]{2,1,0:T(8,128)}, u32[]{:S(2)}, u32[]{:S(2)}) async-start(f32[16,8,128]{2,1,0:T(8,128)} %broadcast_in_dim.13), calls=%async_computation.5 | async-start | bytes 131072 | tf_op jit(solution)/shard_map/all_to_all | solution.py:272
  155.2 54.2 %reduce-scatter.2.cloned.1.call-start = ((), (), s32[]{:S(2)}) async-start(), calls=%async_computation.9 | async-start | bytes 1966080 | tf_op jit(solution)/shard_map/reduce_scatter | solution.py:385
  210.4 12.0 %collective-permute-start.13 = (bf16[192,256]{1,0:T(8,128)(2,1)S(1)}, bf16[192,256]{1,0:T(8,128)(2,1)S(1)}, u32[]{:S(2)}, u32[]{:S(2)}) collective-permute-start(bf16[192,256]{1,0:T(8,128)(2,1)S(1)} %get-tuple-element.55), channel_id=1, source_target_pairs={{16,0},{18,2},{32,16},{34,18},{48,32},{50,34},{0,48},{2,50},{17,1}... | collective-permute-start | bytes 294920 | tf_op jit(solution)/shard_map/ppermute | solution.py:37
  214.7 10.1 %collective-permute-start.12 = (bf16[192,256]{1,0:T(8,128)(2,1)S(1)}, bf16[192,256]{1,0:T(8,128)(2,1)S(1)}, u32[]{:S(2)}, u32[]{:S(2)}) collective-permute-start(bf16[192,256]{1,0:T(8,128)(2,1)S(1)} %get-tuple-element.56), channel_id=1, source_target_pairs={{32,0},{34,2},{48,16},{50,18},{0,32},{2,34},{16,48},{18,50},{33,1}... | collective-permute-start | bytes 294920 | tf_op jit(solution)/shard_map/ppermute | solution.py:37
  216.6 8.2 %collective-permute-start.11 = (bf16[192,256]{1,0:T(8,128)(2,1)S(1)}, bf16[192,256]{1,0:T(8,128)(2,1)S(1)}, u32[]{:S(2)}, u32[]{:S(2)}) collective-permute-start(bf16[192,256]{1,0:T(8,128)(2,1)S(1)} %get-tuple-element.57), channel_id=1, source_target_pairs={{48,0},{50,2},{0,16},{2,18},{16,32},{18,34},{32,48},{34,50},{49,1}... | collective-permute-start | bytes 294920 | tf_op jit(solution)/shard_map/ppermute | solution.py:37
Sparse Core Ops, SparseCore 0:
  62.6 27.3 all-gather.4
  137.1 29.2 all-gather.6
  180.9 28.3 reduce-scatter.1

commit v12 on v11

--- a/solution.py
+++ b/solution.py
@@ -236,9 +236,12 @@
         at = (zl ^ l) * 2 + (c ^ g)
         out[0, lax.rem(at - zh + 4, 4)] = total.astype(BF)
         fb = x * 4 + at
-        wv = w[0, lax.rem(at - zh + 4, 4)].astype(F32)
-        wv = wv + f * mask_rows(mask[fb]) * asc[0, at].astype(F32)
-        dgp[fb] = jnp.sum(wv * total, axis=0, keepdims=True)
+        by_w = jnp.sum(w[0, lax.rem(at - zh + 4, 4)].astype(F32) * total, axis=0, keepdims=True)
+        by_asc = asc[0, at].astype(F32) * total
+        m = mask[fb]
+        by_gate = m[0:1] * jnp.sum(by_asc[0:SUB], axis=0, keepdims=True)
+        by_up = m[1:2] * jnp.sum(by_asc[SUB:ROWS], axis=0, keepdims=True)
+        dgp[fb] = by_w + f * (by_gate + by_up)
 
 
 def ascent_kernel(ids, terms, gabs, mask, asc, part):
@@ -333,7 +336,7 @@
     toks[2, 0], toks[2, 1] = far_x, other_core(far_x)
     p1, s1 = pre(((2, 0),), False)
     parts = tuple((grp, g) for g in range(2) for grp in range(len(GROUPS)))
-    tok_specs = [tok_spec(p[0]) for p in parts]
+    tok_specs = [by_x((len(GROUPS[p[0]]), BLK, BLK)) for p in parts]
     tok_refs = [toks[p] for p in parts]
     cost = {"flops": 64 * 2 * ROWS * BLK * BLK, "nbytes": 12 * 10**6}
     oshape = hbm((4, 4, ROWS, BLK), BF)
@@ -343,7 +346,7 @@
     def late(dims):
         return pl.BlockSpec((1,) + dims, lambda i: (jnp.maximum(i - 4, 0),) + (0,) * len(dims))
 
-    late_specs = [late((len(GROUPS[p[0]]), PACK, BLK)) for p in parts[:-1]]
+    late_specs = [late((len(GROUPS[p[0]]), BLK, BLK)) for p in parts[:-1]]
     both_spec = pl.BlockSpec((1, len(GROUPS[2]), PACK, BLK), lambda i: (lax.rem(i, 4), 0, 0, 0))
     early_w = pl.BlockSpec((1, 4, ROWS, BLK), lambda i: (jnp.minimum(i, 3), 0, 0, 0))
     out1, praw, rs = call(

time: 236 us -> 236 us (level)
  no operation moved by 1% of the time
where the time goes in v12:
time: 236 us; the launch traced here: 233 us
  waiting for transfers between devices  83.7 us (35%)
  starting transfers between devices  59.8 us (25%)
  Pallas kernels  40.6 us (17%)
  blocking collectives  26.8 us (11%)
  between operations  14.5 us (6%)
  local copies, waits for them, and re-layouts  4.78 us (2%)
  other arithmetic  2.43 us (1%)
    ppermute x11, waiting for transfers between devices, from_z(): return lax.ppermute(value, ('zh', 'zl'), pairs)  31.3 us
    ppermute x11, starting transfers between devices, from_z(): return lax.ppermute(value, ('zh', 'zl'), pairs)  25.8 us
    all_to_all x1, waiting for transfers between devices, body(): terms = lax.all_to_all(out1, 'y', 0, 0, tiled=True)  21.3 us
    all_to_all x1, blocking collectives, spread(): lax.all_to_all(jnp.broadcast_to(value[None], (n,) + value.shape), axes, 0...  17.2 us
    all_gather x1, waiting for transfers between devices, body(): weights = in_hbm(lax.all_gather(part_w, 'y', axis=0, tiled=False))  13 us
    all_gather x1, waiting for transfers between devices, body(): ascs = in_hbm(lax.all_gather(asc, 'y', axis=0, tiled=False))  11 us
    all_to_all x2, starting transfers between devices, over_x(): lax.all_to_all(jnp.broadcast_to(value[None], (4,) + value.shape), 'x', 0,...  10.6 us
    all_to_all x1, blocking collectives, body(): dg = jnp.sum(lax.all_to_all(dgp, MP, 0, 0, tiled=True), axis=0)  9.64 us
  transfers between devices with their start and end apart: 23, of which 15 were waited for; matrix products, arithmetic and copies ran while one was open for 2% of the time, Pallas kernels for 8%

profile of v12, /device:TPU:4, one launch (start us, length us, event | category | flops | bytes accessed | tf_op | source)
XLA Modules:
  0.0 232.8 jit_solution(1114787773870504433)
XLA Ops:
  7.2 1.9 shard_map.95
  9.1 5.7 %all-to-all-start = ((bf16[4,1,272,256]{3,2,1,0:T(8,128)(2,1)}), bf16[4,1,272,256]{3,2,1,0:T(8,128)(2,1)S(1)}, u32[]{:S(2)}, u32[]{:S(2)}) async-start(bf16[4,1,272,256]{3,2,1,0:T(8,128)(2,1)} %get-tuple-element.33), calls=%async_computation | async-start | bytes 1114112 | tf_op jit(solution)/shard_map/all_to_all | solution.py:305
  14.8 1.0 collective-permute-start.6
  15.8 6.3 %collective-permute-start.5 = (bf16[272,256]{1,0:T(8,128)(2,1)}, bf16[272,256]{1,0:T(8,128)(2,1)S(1)}, u32[]{:S(2)}, u32[]{:S(2)}) collective-permute-start(bf16[272,256]{1,0:T(8,128)(2,1)} %get-tuple-element.34), channel_id=1, source_target_pairs={{32,0},{34,2},{48,16},{50,18},{0,32},{2,34},{16,48},{18,50},{33,1}... | collective-permute-start | bytes 417800 | tf_op jit(solution)/shard_map/ppermute | solution.py:37
  22.1 1.5 collective-permute-start.4
  23.6 2.7 %collective-permute-start.3 = (bf16[272,256]{1,0:T(8,128)(2,1)}, bf16[272,256]{1,0:T(8,128)(2,1)S(1)}, u32[]{:S(2)}, u32[]{:S(2)}) collective-permute-start(bf16[272,256]{1,0:T(8,128)(2,1)} %get-tuple-element.34), channel_id=1, source_target_pairs={{16,0},{18,2},{32,16},{34,18},{48,32},{50,34},{0,48},{2,50},{17,1}... | collective-permute-start | bytes 417800 | tf_op jit(solution)/shard_map/ppermute | solution.py:37
  26.3 2.2 shard_map.94
  28.5 6.6 %collective-permute-done.5 = bf16[272,256]{1,0:T(8,128)(2,1)S(1)} collective-permute-done((bf16[272,256]{1,0:T(8,128)(2,1)}, bf16[272,256]{1,0:T(8,128)(2,1)S(1)}, u32[]{:S(2)}, u32[]{:S(2)}) %collective-permute-start.5) | collective-permute-done | bytes 139296 | tf_op jit(solution)/shard_map/ppermute | solution.py:37
  35.1 1.1 collective-permute-done.4
  36.3 1.6 broadcast_in_dim.11
  37.8 4.9 %all-to-all-start.1 = ((bf16[4,4,272,256]{3,2,1,0:T(8,128)(2,1)}), bf16[4,4,272,256]{3,2,1,0:T(8,128)(2,1)}, u32[]{:S(2)}, u32[]{:S(2)}) async-start(bf16[4,4,272,256]{3,2,1,0:T(8,128)(2,1)} %broadcast_in_dim.11), calls=%async_computation.1 | async-start | bytes 4456448 | tf_op jit(solution)/shard_map/all_to_all | solution.py:301
  42.8 2.2 collective-permute-start
  45.0 2.5 %collective-permute-start.1 = (bf16[288,256]{1,0:T(8,128)(2,1)S(1)}, bf16[288,256]{1,0:T(8,128)(2,1)S(1)}, u32[]{:S(2)}, u32[]{:S(2)}) collective-permute-start(bf16[288,256]{1,0:T(8,128)(2,1)S(1)} %copy-done.9), channel_id=1, source_target_pairs={{32,0},{34,2},{48,16},{50,18},{0,32},{2,34},{16,48},{18,50},{33,1}... | collective-permute-start | bytes 442376 | tf_op jit(solution)/shard_map/ppermute | solution.py:37
  47.5 0.9 collective-permute-start.2
  48.6 5.5 %collective-permute-done.c1 = bf16[288,256]{1,0:T(8,128)(2,1)S(1)} collective-permute-done((bf16[288,256]{1,0:T(8,128)(2,1)S(1)}, bf16[288,256]{1,0:T(8,128)(2,1)S(1)}, u32[]{:S(2)}, u32[]{:S(2)}) %collective-permute-start) | collective-permute-done | bytes 147488 | tf_op jit(solution)/shard_map/ppermute | solution.py:37
  54.1 5.1 %collective-permute-done.1.c2 = bf16[288,256]{1,0:T(8,128)(2,1)S(1)} collective-permute-done((bf16[288,256]{1,0:T(8,128)(2,1)S(1)}, bf16[288,256]{1,0:T(8,128)(2,1)S(1)}, u32[]{:S(2)}, u32[]{:S(2)}) %collective-permute-start.1) | collective-permute-done | bytes 147488 | tf_op jit(solution)/shard_map/ppermute | solution.py:37
  59.2 2.4 %collective-permute-done.2.c3 = bf16[288,256]{1,0:T(8,128)(2,1)S(1)} collective-permute-done((bf16[288,256]{1,0:T(8,128)(2,1)S(1)}, bf16[288,256]{1,0:T(8,128)(2,1)S(1)}, u32[]{:S(2)}, u32[]{:S(2)}) %collective-permute-start.2) | collective-permute-done | bytes 147488 | tf_op jit(solution)/shard_map/ppermute | solution.py:37
  61.6 0.8 pad_maximum_fusion.2
  62.4 5.5 %collective-permute-done.7 = bf16[3,272,256]{2,1,0:T(8,128)(2,1)S(1)} collective-permute-done((bf16[3,272,256]{2,1,0:T(8,128)(2,1)S(1)}, bf16[3,272,256]{2,1,0:T(8,128)(2,1)S(1)}, u32[]{:S(2)}, u32[]{:S(2)}) %collective-permute-start.7) | collective-permute-done | bytes 417824 | tf_op jit(solution)/shard_map/ppermute | solution.py:37
  68.0 1.4 broadcast_in_dim.12
  69.3 5.7 %all-to-all-start.2 = ((bf16[4,3,272,256]{3,2,1,0:T(8,128)(2,1)}), bf16[4,3,272,256]{3,2,1,0:T(8,128)(2,1)S(1)}, u32[]{:S(2)}, u32[]{:S(2)}) async-start(bf16[4,3,272,256]{3,2,1,0:T(8,128)(2,1)} %broadcast_in_dim.12), calls=%async_computation.2 | async-start | bytes 3342336 | tf_op jit(solution)/shard_map/all_to_all | solution.py:301
  75.3 1.7 collective-permute-done.8.refs_2_.refs_3_
  77.0 13.0 %all-gather.5.cloned.1.call-done = bf16[16,192,256]{2,1,0:T(8,128)(2,1)} async-done(((bf16[4,192,256]{2,1,0:T(8,128)(2,1)}), bf16[16,192,256]{2,1,0:T(8,128)(2,1)}) %all-gather.5.cloned.1.call-update) | async-done | bytes 1572880 | tf_op jit(solution)/shard_map/all_gather | solution.py:310
  90.0 5.9 %shard_map.96 = (f32[4,192,256]{2,1,0:T(8,128)}, f32[4,8,256]{2,1,0:T(8,128)S(1)}, f32[16,8,256]{2,1,0:T(8,128)S(1)}) custom-call(s32[5]{0:T(128)S(1)} %stack.59.ids, bf16[4,4,192,256]{3,2,1,0:T(8,128)(2,1)} %bitcast.35, bf16[4,1,272,256]{3,2,1,0:T(8,128)(2,1)} %copy-done.1, bf16[4,4,272,256]{3,2,1,0:T(8,128)(2,1)} %all-to-all-done.1.refs_1_, ...), custom_call_target="tpu_custom_call" | custom-call | flops 1006632960 | bytes 5570560 | tf_op jit(solution)/shard_map/pallas_call | solution.py:324
  96.0 3.1 %shard_map.97 = (f32[4,192,256]{2,1,0:T(8,128)S(1)}, f32[4,8,256]{2,1,0:T(8,128)S(1)}) custom-call(s32[5]{0:T(128)S(1)} %stack.59.ids, bf16[4,4,192,256]{3,2,1,0:T(8,128)(2,1)} %bitcast.36, bf16[4,3,272,256]{3,2,1,0:T(8,128)(2,1)S(1)} %all-to-all-done.2.refs_0_.refs_2_), custom_call_target="tpu_custom_call" | custom-call | flops 301989888 | bytes 1671168 | tf_op jit(solution)/shard_map/pallas_call | solution.py:324
  99.6 9.1 %shard_map.98 = (bf16[4,4,192,256]{3,2,1,0:T(8,128)(2,1)}, f32[4,192,256]{2,1,0:T(8,128)}, f32[4,8,256]{2,1,0:T(8,128)}) custom-call(s32[5]{0:T(128)S(1)} %stack.59.ids, f32[4,192,256]{2,1,0:T(8,128)S(1)} %copy-done, f32[4,192,256]{2,1,0:T(8,128)S(1)} %get-tuple-element.40.p1, f32[4,8,256]{2,1,0:T(8,128)S(1)} %get-tuple-element.41.s0, ...), custom_call_target="tpu_custom_call" | custom-call | flops 1610612736 | bytes 12000000 | tf_op jit(solution)/shard_map/pallas_call | solution.py:352
  108.7 4.4 %all-to-all-start.3 = ((bf16[4,4,192,256]{3,2,1,0:T(8,128)(2,1)}), bf16[4,4,192,256]{3,2,1,0:T(8,128)(2,1)}, u32[]{:S(2)}, u32[]{:S(2)}) async-start(bf16[4,4,192,256]{3,2,1,0:T(8,128)(2,1)} %get-tuple-element.43), calls=%async_computation.3 | async-start | bytes 3145728 | tf_op jit(solution)/shard_map/all_to_all | solution.py:361
  113.1 21.3 %all-to-all-done.3.terms = bf16[4,4,192,256]{3,2,1,0:T(8,128)(2,1)} async-done(((bf16[4,4,192,256]{3,2,1,0:T(8,128)(2,1)}), bf16[4,4,192,256]{3,2,1,0:T(8,128)(2,1)}, u32[]{:S(2)}, u32[]{:S(2)}) %all-to-all-start.3) | async-done | bytes 1572896 | tf_op jit(solution)/shard_map/all_to_all | solution.py:361
  134.4 2.5 %shard_map.99 = (bf16[4,192,256]{2,1,0:T(8,128)(2,1)}, f32[16,8,128]{2,1,0:T(8,128)}) custom-call(s32[5]{0:T(128)S(1)} %stack.59.ids, bf16[4,4,192,256]{3,2,1,0:T(8,128)(2,1)} %all-to-all-done.3.terms, f32[16,8,256]{2,1,0:T(8,128)S(1)} %get-tuple-element.44.gabs, f32[16,2,256]{2,1,0:T(2,128)S(1)} %bitcast.32), custom_call_target="tpu_custom_call" | custom-call | flops 1000000 | bytes 1000000 | tf_op jit(solution)/shard_map/pallas_call | solution.py:362
  136.9 5.8 %all-to-all-start.4 = ((f32[16,8,128]{2,1,0:T(8,128)}), f32[16,8,128]{2,1,0:T(8,128)}, u32[]{:S(2)}, u32[]{:S(2)}) async-start(f32[16,8,128]{2,1,0:T(8,128)} %get-tuple-element.45), calls=%async_computation.4 | async-start | bytes 131072 | tf_op jit(solution)/shard_map/all_to_all | solution.py:369
  143.4 3.4 %all-to-all-done.4 = f32[16,8,128]{2,1,0:T(8,128)} async-done(((f32[16,8,128]{2,1,0:T(8,128)}), f32[16,8,128]{2,1,0:T(8,128)}, u32[]{:S(2)}, u32[]{:S(2)}) %all-to-all-start.4) | async-done | bytes 65568 | tf_op jit(solution)/shard_map/all_to_all | solution.py:369
  146.8 0.9 reduce_sum.27
  147.6 0.6 broadcast_in_dim.13
  148.3 6.9 %all-to-all-start.5 = ((f32[16,8,128]{2,1,0:T(8,128)}), f32[16,8,128]{2,1,0:T(8,128)}, u32[]{:S(2)}, u32[]{:S(2)}) async-start(f32[16,8,128]{2,1,0:T(8,128)} %broadcast_in_dim.13), calls=%async_computation.5 | async-start | bytes 131072 | tf_op jit(solution)/shard_map/all_to_all | solution.py:275
  155.4 11.0 %all-gather.7.cloned.1.call-done = bf16[16,192,256]{2,1,0:T(8,128)(2,1)} async-done(((bf16[4,192,256]{2,1,0:T(8,128)(2,1)}), bf16[16,192,256]{2,1,0:T(8,128)(2,1)}) %all-gather.7.cloned.1.call-update) | async-done | bytes 1572880 | tf_op jit(solution)/shard_map/all_gather | solution.py:368
  166.3 6.5 %shard_map.100.pa = f32[4,192,256]{2,1,0:T(8,128)} custom-call(s32[5]{0:T(128)S(1)} %stack.59.ids, bf16[4,4,192,256]{3,2,1,0:T(8,128)(2,1)} %bitcast.39, f32[16,2,256]{2,1,0:T(2,128)S(1)} %bitcast.33, f32[16,8,256]{2,1,0:T(8,128)S(1)} %get-tuple-element.44.gabs, bf16[4,1,272,256]{3,2,1,0:T(8,128)(2,1)} %copy-done.1, ...), custom_call_target="tpu_custom_call" | custom-call | flops 1610612736 | bytes 12000000 | tf_op jit(solution)/shard_map/pallas_call | solution.py:371
  172.9 7.7 %shard_map.101 = (bf16[4,4,192,256]{3,2,1,0:T(8,128)(2,1)}, f32[16,1,256]{2,1,0:T(1,128)}) custom-call(f32[1]{0:T(128)S(6)} %copy.12.radius, s32[5]{0:T(128)S(1)} %stack.59.ids, f32[16,8,128]{2,1,0:T(8,128)} %all-to-all-done.5.totals, f32[4,192,256]{2,1,0:T(8,128)} %get-tuple-element.48.praw, f32[4,8,256]{2,1,0:T(8,128)} %get-tuple-element.49.rs, ...), custom_call_target="tpu_custom_call" | custom-call | flops 1610612736 | bytes 12000000 | tf_op jit(solution)/shard_map/pallas_call | solution.py:379
  180.6 9.6 %all_to_all.40 = f32[16,1,256]{2,1,0:T(1,128)S(1)} all-to-all(f32[16,1,256]{2,1,0:T(1,128)} %get-tuple-element.50), channel_id=1, replica_groups=mesh['y'=4,'zh'=4,'x'=4,'zl'=2,'c'=2] {'x','zl','c'}, dimensions={0} | all-to-all | bytes 32768 | tf_op jit(solution)/shard_map/all_to_all | solution.py:389
  190.3 17.2 %all_to_all.41 = f32[16,1,256]{2,1,0:T(1,128)S(1)} all-to-all(f32[16,1,256]{2,1,0:T(1,128)S(1)} %broadcast_in_dim.14), channel_id=1, replica_groups=mesh['y'=4,'zh'=4,'x'=4,'zl'=2,'c'=2] {'y','zh'}, dimensions={0} | all-to-all | bytes 32768 | tf_op jit(solution)/shard_map/all_to_all | solution.py:275
  207.5 1.7 reduce-scatter.2.cloned.1.call-done
  209.2 1.1 slice_bitcast_fusion.3
  210.3 4.2 %collective-permute-start.13 = (bf16[192,256]{1,0:T(8,128)(2,1)S(1)}, bf16[192,256]{1,0:T(8,128)(2,1)S(1)}, u32[]{:S(2)}, u32[]{:S(2)}) collective-permute-start(bf16[192,256]{1,0:T(8,128)(2,1)S(1)} %get-tuple-element.55), channel_id=1, source_target_pairs={{16,0},{18,2},{32,16},{34,18},{48,32},{50,34},{0,48},{2,50},{17,1}... | collective-permute-start | bytes 294920 | tf_op jit(solution)/shard_map/ppermute | solution.py:37
  214.5 2.0 collective-permute-start.12
  216.5 2.4 %collective-permute-start.11 = (bf16[192,256]{1,0:T(8,128)(2,1)S(1)}, bf16[192,256]{1,0:T(8,128)(2,1)S(1)}, u32[]{:S(2)}, u32[]{:S(2)}) collective-permute-start(bf16[192,256]{1,0:T(8,128)(2,1)S(1)} %get-tuple-element.57), channel_id=1, source_target_pairs={{48,0},{50,2},{0,16},{2,18},{16,32},{18,34},{32,48},{34,50},{49,1}... | collective-permute-start | bytes 294920 | tf_op jit(solution)/shard_map/ppermute | solution.py:37
  218.9 0.6 reduce_sum.29
  219.5 2.7 %collective-permute-done.13.b3 = bf16[192,256]{1,0:T(8,128)(2,1)S(1)} collective-permute-done((bf16[192,256]{1,0:T(8,128)(2,1)S(1)}, bf16[192,256]{1,0:T(8,128)(2,1)S(1)}, u32[]{:S(2)}, u32[]{:S(2)}) %collective-permute-start.13) | collective-permute-done | bytes 98336 | tf_op jit(solution)/shard_map/ppermute | solution.py:37
  222.2 2.4 %collective-permute-done.12.b2 = bf16[192,256]{1,0:T(8,128)(2,1)S(1)} collective-permute-done((bf16[192,256]{1,0:T(8,128)(2,1)S(1)}, bf16[192,256]{1,0:T(8,128)(2,1)S(1)}, u32[]{:S(2)}, u32[]{:S(2)}) %collective-permute-start.12) | collective-permute-done | bytes 98336 | tf_op jit(solution)/shard_map/ppermute | solution.py:37
  224.6 1.6 shard_map.102
  (51 shorter events, 1.5 us)
Async XLA Ops:
  9.1 27.2 %all-to-all-start = ((bf16[4,1,272,256]{3,2,1,0:T(8,128)(2,1)}), bf16[4,1,272,256]{3,2,1,0:T(8,128)(2,1)S(1)}, u32[]{:S(2)}, u32[]{:S(2)}) async-start(bf16[4,1,272,256]{3,2,1,0:T(8,128)(2,1)} %get-tuple-element.33), calls=%async_computation | async-start | bytes 1114112 | tf_op jit(solution)/shard_map/all_to_all | solution.py:305
  14.8 13.8 %collective-permute-start.6 = (bf16[272,256]{1,0:T(8,128)(2,1)}, bf16[272,256]{1,0:T(8,128)(2,1)S(1)}, u32[]{:S(2)}, u32[]{:S(2)}) collective-permute-start(bf16[272,256]{1,0:T(8,128)(2,1)} %get-tuple-element.34), channel_id=1, source_target_pairs={{2,0},{0,2},{18,16},{16,18},{34,32},{32,34},{50,48},{48,50},{3,1},... | collective-permute-start | bytes 417800 | tf_op jit(solution)/shard_map/ppermute | solution.py:37
  15.8 19.3 %collective-permute-start.5 = (bf16[272,256]{1,0:T(8,128)(2,1)}, bf16[272,256]{1,0:T(8,128)(2,1)S(1)}, u32[]{:S(2)}, u32[]{:S(2)}) collective-permute-start(bf16[272,256]{1,0:T(8,128)(2,1)} %get-tuple-element.34), channel_id=1, source_target_pairs={{32,0},{34,2},{48,16},{50,18},{0,32},{2,34},{16,48},{18,50},{33,1}... | collective-permute-start | bytes 417800 | tf_op jit(solution)/shard_map/ppermute | solution.py:37
  22.1 14.1 %collective-permute-start.4 = (bf16[272,256]{1,0:T(8,128)(2,1)}, bf16[272,256]{1,0:T(8,128)(2,1)S(1)}, u32[]{:S(2)}, u32[]{:S(2)}) collective-permute-start(bf16[272,256]{1,0:T(8,128)(2,1)} %get-tuple-element.34), channel_id=1, source_target_pairs={{48,0},{50,2},{0,16},{2,18},{16,32},{18,34},{32,48},{34,50},{49,1}... | collective-permute-start | bytes 417800 | tf_op jit(solution)/shard_map/ppermute | solution.py:37
  23.6 12.6 %collective-permute-start.3 = (bf16[272,256]{1,0:T(8,128)(2,1)}, bf16[272,256]{1,0:T(8,128)(2,1)S(1)}, u32[]{:S(2)}, u32[]{:S(2)}) collective-permute-start(bf16[272,256]{1,0:T(8,128)(2,1)} %get-tuple-element.34), channel_id=1, source_target_pairs={{16,0},{18,2},{32,16},{34,18},{48,32},{50,34},{0,48},{2,50},{17,1}... | collective-permute-start | bytes 417800 | tf_op jit(solution)/shard_map/ppermute | solution.py:37
  36.3 38.8 %copy-start.1 = (bf16[4,1,272,256]{3,2,1,0:T(8,128)(2,1)}, bf16[4,1,272,256]{3,2,1,0:T(8,128)(2,1)S(1)}, u32[]{:S(2)}) copy-start(bf16[4,1,272,256]{3,2,1,0:T(8,128)(2,1)S(1)} %all-to-all-done.refs_0_) | copy-start | bytes 1671172
  37.8 5.0 %copy-start.10 = (bf16[288,256]{1,0:T(8,128)(2,1)S(1)}, bf16[288,256]{1,0:T(8,128)(2,1)}, u32[]{:S(2)}) copy-start(bf16[288,256]{1,0:T(8,128)(2,1)} %get-tuple-element.30) | copy-start | bytes 442372
  37.8 7.2 %copy-start.9 = (bf16[288,256]{1,0:T(8,128)(2,1)S(1)}, bf16[288,256]{1,0:T(8,128)(2,1)}, u32[]{:S(2)}) copy-start(bf16[288,256]{1,0:T(8,128)(2,1)} %get-tuple-element.31) | copy-start | bytes 442372
  37.8 9.7 %copy-start.8 = (bf16[288,256]{1,0:T(8,128)(2,1)S(1)}, bf16[288,256]{1,0:T(8,128)(2,1)}, u32[]{:S(2)}) copy-start(bf16[288,256]{1,0:T(8,128)(2,1)} %get-tuple-element.32) | copy-start | bytes 442372
  37.8 10.6 %copy-start.3 = (bf16[288,256]{1,0:T(8,128)(2,1)S(1)}, bf16[288,256]{1,0:T(8,128)(2,1)}, u32[]{:S(2)}) copy-start(bf16[288,256]{1,0:T(8,128)(2,1)} %get-tuple-element.29.c0) | copy-start | bytes 442372
  37.8 30.1 %all-to-all-start.1 = ((bf16[4,4,272,256]{3,2,1,0:T(8,128)(2,1)}), bf16[4,4,272,256]{3,2,1,0:T(8,128)(2,1)}, u32[]{:S(2)}, u32[]{:S(2)}) async-start(bf16[4,4,272,256]{3,2,1,0:T(8,128)(2,1)} %broadcast_in_dim.11), calls=%async_computation.1 | async-start | bytes 4456448 | tf_op jit(solution)/shard_map/all_to_all | solution.py:301
  42.8 47.2 %all-gather.5.cloned.1.call-start = ((), (), s32[]{:S(2)}) async-start(), calls=%async_computation.10 | async-start | bytes 1966080 | tf_op jit(solution)/shard_map/all_gather | solution.py:310
  42.8 11.3 %collective-permute-start = (bf16[288,256]{1,0:T(8,128)(2,1)S(1)}, bf16[288,256]{1,0:T(8,128)(2,1)S(1)}, u32[]{:S(2)}, u32[]{:S(2)}) collective-permute-start(bf16[288,256]{1,0:T(8,128)(2,1)S(1)} %copy-done.10), channel_id=1, source_target_pairs={{16,0},{18,2},{32,16},{34,18},{48,32},{50,34},{0,48},{2,50},{17,1}... | collective-permute-start | bytes 442376 | tf_op jit(solution)/shard_map/ppermute | solution.py:37
  45.0 14.1 %collective-permute-start.1 = (bf16[288,256]{1,0:T(8,128)(2,1)S(1)}, bf16[288,256]{1,0:T(8,128)(2,1)S(1)}, u32[]{:S(2)}, u32[]{:S(2)}) collective-permute-start(bf16[288,256]{1,0:T(8,128)(2,1)S(1)} %copy-done.9), channel_id=1, source_target_pairs={{32,0},{34,2},{48,16},{50,18},{0,32},{2,34},{16,48},{18,50},{33,1}... | collective-permute-start | bytes 442376 | tf_op jit(solution)/shard_map/ppermute | solution.py:37
  47.5 14.0 %collective-permute-start.2 = (bf16[288,256]{1,0:T(8,128)(2,1)S(1)}, bf16[288,256]{1,0:T(8,128)(2,1)S(1)}, u32[]{:S(2)}, u32[]{:S(2)}) collective-permute-start(bf16[288,256]{1,0:T(8,128)(2,1)S(1)} %copy-done.8), channel_id=1, source_target_pairs={{48,0},{50,2},{0,16},{2,18},{16,32},{18,34},{32,48},{34,50},{49,1}... | collective-permute-start | bytes 442376 | tf_op jit(solution)/shard_map/ppermute | solution.py:37
  48.5 19.5 %collective-permute-start.7 = (bf16[3,272,256]{2,1,0:T(8,128)(2,1)S(1)}, bf16[3,272,256]{2,1,0:T(8,128)(2,1)S(1)}, u32[]{:S(2)}, u32[]{:S(2)}) collective-permute-start(bf16[3,272,256]{2,1,0:T(8,128)(2,1)S(1)} %pad_maximum_fusion.1), channel_id=1, source_target_pairs={{2,0},{0,2},{18,16},{16,18},{34,32},{32,34},{50,48},{48,50},{3,1},... | collective-permute-start | bytes 1253384 | tf_op jit(solution)/shard_map/ppermute | solution.py:37
  54.1 15.3 %copy-start.4 = (bf16[288,256]{1,0:T(8,128)(2,1)}, bf16[288,256]{1,0:T(8,128)(2,1)S(1)}, u32[]{:S(2)}) copy-start(bf16[288,256]{1,0:T(8,128)(2,1)S(1)} %collective-permute-done.c1) | copy-start | bytes 442372
  59.2 10.2 %copy-start.5 = (bf16[288,256]{1,0:T(8,128)(2,1)}, bf16[288,256]{1,0:T(8,128)(2,1)S(1)}, u32[]{:S(2)}) copy-start(bf16[288,256]{1,0:T(8,128)(2,1)S(1)} %collective-permute-done.1.c2) | copy-start | bytes 442372
  61.6 7.8 %copy-start.6 = (bf16[288,256]{1,0:T(8,128)(2,1)}, bf16[288,256]{1,0:T(8,128)(2,1)S(1)}, u32[]{:S(2)}) copy-start(bf16[288,256]{1,0:T(8,128)(2,1)S(1)} %collective-permute-done.2.c3) | copy-start | bytes 442372
  68.0 22.0 %collective-permute-start.9 = (bf16[4,4,272,256]{3,2,1,0:T(8,128)(2,1)}, bf16[4,4,272,256]{3,2,1,0:T(8,128)(2,1)}, u32[]{:S(2)}, u32[]{:S(2)}) collective-permute-start(bf16[4,4,272,256]{3,2,1,0:T(8,128)(2,1)} %all-to-all-done.1.refs_1_), channel_id=1, source_target_pairs={{0,1},{1,0},{2,3},{3,2},{4,5},{5,4},{6,7},{7,6},{8,9},{9,8},{10,11... | collective-permute-start | bytes 6684680 | tf_op jit(solution)/shard_map/ppermute | solution.py:41
  69.3 26.6 %all-to-all-start.2 = ((bf16[4,3,272,256]{3,2,1,0:T(8,128)(2,1)}), bf16[4,3,272,256]{3,2,1,0:T(8,128)(2,1)S(1)}, u32[]{:S(2)}, u32[]{:S(2)}) async-start(bf16[4,3,272,256]{3,2,1,0:T(8,128)(2,1)} %broadcast_in_dim.12), calls=%async_computation.2 | async-start | bytes 3342336 | tf_op jit(solution)/shard_map/all_to_all | solution.py:301
  75.0 2.0 collective-permute-start.8
  77.0 13.0 %copy-start.2 = (bf16[4,1,272,256]{3,2,1,0:T(8,128)(2,1)}, bf16[4,1,272,256]{3,2,1,0:T(8,128)(2,1)S(1)}, u32[]{:S(2)}) copy-start(bf16[4,1,272,256]{3,2,1,0:T(8,128)(2,1)S(1)} %collective-permute-done.8.refs_2_.refs_3_) | copy-start | bytes 1671172
  95.9 3.6 %copy-start = (f32[4,192,256]{2,1,0:T(8,128)S(1)}, f32[4,192,256]{2,1,0:T(8,128)}, u32[]{:S(2)}) copy-start(f32[4,192,256]{2,1,0:T(8,128)} %get-tuple-element.37.p0) | copy-start | bytes 2359300
  95.9 3.6 %collective-permute-start.10 = (bf16[4,3,272,256]{3,2,1,0:T(8,128)(2,1)S(1)}, bf16[4,3,272,256]{3,2,1,0:T(8,128)(2,1)S(1)}, u32[]{:S(2)}, u32[]{:S(2)}) collective-permute-start(bf16[4,3,272,256]{3,2,1,0:T(8,128)(2,1)S(1)} %all-to-all-done.2.refs_0_.refs_2_), channel_id=1, source_target_pairs={{0,1},{1,0},{2,3},{3,2},{4,5},{5,4},{6,7},{7,6},{8,9},{9,8},{10,11... | collective-permute-start | bytes 5013512 | tf_op jit(solution)/shard_map/ppermute | solution.py:41
  108.6 4.5 %copy-start.7 = (s32[2,4096]{1,0:T(2,128)S(1)}, s32[2,4096]{1,0:T(2,128)}, u32[]{:S(2)}) copy-start(s32[2,4096]{1,0:T(2,128)} %param.12) | copy-start | bytes 98308
  108.7 25.8 %all-to-all-start.3 = ((bf16[4,4,192,256]{3,2,1,0:T(8,128)(2,1)}), bf16[4,4,192,256]{3,2,1,0:T(8,128)(2,1)}, u32[]{:S(2)}, u32[]{:S(2)}) async-start(bf16[4,4,192,256]{3,2,1,0:T(8,128)(2,1)} %get-tuple-element.43), calls=%async_computation.3 | async-start | bytes 3145728 | tf_op jit(solution)/shard_map/all_to_all | solution.py:361
  113.1 53.3 %all-gather.7.cloned.1.call-start = ((), (), s32[]{:S(2)}) async-start(), calls=%async_computation.11 | async-start | bytes 1966080 | tf_op jit(solution)/shard_map/all_gather | solution.py:368
  136.9 9.8 %all-to-all-start.4 = ((f32[16,8,128]{2,1,0:T(8,128)}), f32[16,8,128]{2,1,0:T(8,128)}, u32[]{:S(2)}, u32[]{:S(2)}) async-start(f32[16,8,128]{2,1,0:T(8,128)} %get-tuple-element.45), calls=%async_computation.4 | async-start | bytes 131072 | tf_op jit(solution)/shard_map/all_to_all | solution.py:369
  148.3 24.6 %all-to-all-start.5 = ((f32[16,8,128]{2,1,0:T(8,128)}), f32[16,8,128]{2,1,0:T(8,128)}, u32[]{:S(2)}, u32[]{:S(2)}) async-start(f32[16,8,128]{2,1,0:T(8,128)} %broadcast_in_dim.13), calls=%async_computation.5 | async-start | bytes 131072 | tf_op jit(solution)/shard_map/all_to_all | solution.py:275
  155.1 54.1 %reduce-scatter.2.cloned.1.call-start = ((), (), s32[]{:S(2)}) async-start(), calls=%async_computation.9 | async-start | bytes 1966080 | tf_op jit(solution)/shard_map/reduce_scatter | solution.py:388
  210.3 11.9 %collective-permute-start.13 = (bf16[192,256]{1,0:T(8,128)(2,1)S(1)}, bf16[192,256]{1,0:T(8,128)(2,1)S(1)}, u32[]{:S(2)}, u32[]{:S(2)}) collective-permute-start(bf16[192,256]{1,0:T(8,128)(2,1)S(1)} %get-tuple-element.55), channel_id=1, source_target_pairs={{16,0},{18,2},{32,16},{34,18},{48,32},{50,34},{0,48},{2,50},{17,1}... | collective-permute-start | bytes 294920 | tf_op jit(solution)/shard_map/ppermute | solution.py:37
  214.5 10.1 %collective-permute-start.12 = (bf16[192,256]{1,0:T(8,128)(2,1)S(1)}, bf16[192,256]{1,0:T(8,128)(2,1)S(1)}, u32[]{:S(2)}, u32[]{:S(2)}) collective-permute-start(bf16[192,256]{1,0:T(8,128)(2,1)S(1)} %get-tuple-element.56), channel_id=1, source_target_pairs={{32,0},{34,2},{48,16},{50,18},{0,32},{2,34},{16,48},{18,50},{33,1}... | collective-permute-start | bytes 294920 | tf_op jit(solution)/shard_map/ppermute | solution.py:37
  216.5 8.1 %collective-permute-start.11 = (bf16[192,256]{1,0:T(8,128)(2,1)S(1)}, bf16[192,256]{1,0:T(8,128)(2,1)S(1)}, u32[]{:S(2)}, u32[]{:S(2)}) collective-permute-start(bf16[192,256]{1,0:T(8,128)(2,1)S(1)} %get-tuple-element.57), channel_id=1, source_target_pairs={{48,0},{50,2},{0,16},{2,18},{16,32},{18,34},{32,48},{34,50},{49,1}... | collective-permute-start | bytes 294920 | tf_op jit(solution)/shard_map/ppermute | solution.py:37
Sparse Core Ops, SparseCore 0:
  62.6 27.3 all-gather.4
  137.1 29.2 all-gather.6
  180.8 28.3 reduce-scatter.1
